TPU v7x, 32 devices: a whole 2x2x4 slice. The times are simulated.
32 devices in a mesh: dp: 16 (over z, y, core), seq: 2 (over x).
Axes of the slice: x: 2, y: 2, z: 4, core: 2. Of those that a mesh axis runs over, the one named last changes fastest.
Arguments:
- inputs: bfloat16 [16, 2, 256, 2048], P('dp', 'seq'), may hold values from -6 to 6
- cotangent: bfloat16 [16, 2, 256, 2048], P('dp', 'seq'), may hold values from -6 to 6
- adapter_ids: int32 [16], P('dp'), may hold values from 0 to 7
- block_index: int32 [16, 2], P('dp'), may hold values from 0 to 1, each once within a row
- gain_first: bfloat16 [2048], P(('dp', 'seq')), may hold values from 0.25 to 1.75
- gain_second: bfloat16 [2048], P(('dp', 'seq')), may hold values from 0.25 to 1.75
- w_query: bfloat16 [2048, 2048], P(('dp', 'seq')), may hold values from -0.125 to 0.125
- w_key: bfloat16 [2048, 256], P(('dp', 'seq')), may hold values from -0.125 to 0.125
- w_value: bfloat16 [2048, 256], P(('dp', 'seq')), may hold values from -0.125 to 0.125
- w_output: bfloat16 [2048, 2048], P(('dp', 'seq')), may hold values from -1 to 1
- w_gate_up: bfloat16 [2, 2048, 5632], P(None, None, ('dp', 'seq')), may hold values from -0.125 to 0.125
- w_down: bfloat16 [5632, 2048], P(('dp', 'seq')), may hold values from -0.15625 to 0.15625
- reduce_attention: bfloat16 [3, 128, 2048], P(None, ('dp', 'seq')), may hold values from -0.125 to 0.125
- raise_query: bfloat16 [128, 2048], P(('dp', 'seq')), may hold values from -0.75 to 0.75
- raise_keyvalue: bfloat16 [2, 128, 256], P(None, ('dp', 'seq')), may hold values from -0.75 to 0.75
- reduce_output: bfloat16 [128, 2048], P(('dp', 'seq')), may hold values from -1 to 1
- raise_output: bfloat16 [128, 2048], P(('dp', 'seq')), may hold values from -0.75 to 0.75
- reduce_gate_up: bfloat16 [2, 128, 2048], P(None, ('dp', 'seq')), may hold values from -0.125 to 0.125
- raise_gate_up: bfloat16 [2, 128, 5632], P(None, ('dp', 'seq')), may hold values from -0.75 to 0.75
- reduce_down: bfloat16 [128, 5632], P(('dp', 'seq')), may hold values from -0.15625 to 0.15625
- raise_down: bfloat16 [128, 2048], P(('dp', 'seq')), may hold values from -0.75 to 0.75
Outputs:
- output: bfloat16 [16, 2, 256, 2048], P('dp', 'seq')
- input_grad: float32 [16, 2, 256, 2048], P('dp', 'seq')
- gradient_gain_first: float32 [2048], P(('dp', 'seq'))
- gradient_gain_second: float32 [2048], P(('dp', 'seq'))
- gradient_reduce_attention: float32 [3, 128, 2048], P(None, ('dp', 'seq'))
- gradient_raise_query: float32 [128, 2048], P(('dp', 'seq'))
- gradient_raise_keyvalue: float32 [2, 128, 256], P(None, ('dp', 'seq'))
- gradient_reduce_output: float32 [128, 2048], P(('dp', 'seq'))
- gradient_raise_output: float32 [128, 2048], P(('dp', 'seq'))
- gradient_reduce_gate_up: float32 [2, 128, 2048], P(None, ('dp', 'seq'))
- gradient_raise_gate_up: float32 [2, 128, 5632], P(None, ('dp', 'seq'))
- gradient_reduce_down: float32 [128, 5632], P(('dp', 'seq'))
- gradient_raise_down: float32 [128, 2048], P(('dp', 'seq'))
Inputs may be any that keep to these rules, and one draw needn't show every extreme that they name: `block_index`: each row is an ordering of 0 to 1.
All inputs are finite; a program needn't handle non-finite values.
Results may differ from a plain program's by a relative error of at most 0.019.
Values may be sent and summed in bfloat16 or wider, within the bound.
No kernel may reach another device: no remote copies, remote signals or barrier semaphores. Data moves between devices by JAX's collectives and lax.ppermute only.
A program may use at most 256 MiB of HBM per device.

v0:
```python
import jax
import jax.numpy as jnp
from jax import lax
from jax.sharding import PartitionSpec as P

HEADS = 32
KV_HEADS = 4
HEAD_DIM = 64
ADAPTERS = 8
RANK = 16


EPS = 1e-05
THETA = 10000.0


def rotary_tables(positions, head_size):
    split_at = head_size // 2
    speeds = THETA ** (-jnp.arange(split_at, dtype=jnp.float32) * (2.0 / head_size))
    angles = positions.astype(jnp.float32)[..., None] * speeds
    angles = jnp.concatenate([angles, angles], -1)
    return (jnp.cos(angles), jnp.sin(angles))


def rotate(values, cosine, sine_values):
    split_at = values.shape[-1] // 2
    turned = jnp.concatenate([-values[..., split_at:], values[..., :split_at]], -1)
    return values * cosine[..., None, :] + turned * sine_values[..., None, :]


def unrotate(grads, cosine, sine_values):
    split_at = grads.shape[-1] // 2
    scaled = grads * sine_values[..., None, :]
    turned = jnp.concatenate([scaled[..., split_at:], -scaled[..., :split_at]], -1)
    return grads * cosine[..., None, :] + turned


def choose_rows(onehot, table):
    shaped = table.reshape(ADAPTERS, RANK, table.shape[-1])
    return jnp.einsum("sa,arw->srw", onehot, shaped, preferred_element_type=jnp.float32).astype(
        jnp.bfloat16
    )


def choose_stacked(onehot, table):
    shaped = table.reshape(table.shape[0], ADAPTERS, RANK, table.shape[-1])
    return jnp.einsum("sa,karw->skrw", onehot, shaped, preferred_element_type=jnp.float32).astype(
        jnp.bfloat16
    )


def table_rows(onehot, per_seq):
    summed = jnp.einsum("sa,srw->arw", onehot, per_seq, precision=lax.Precision.HIGHEST)
    return summed.reshape(ADAPTERS * RANK, per_seq.shape[-1])


def table_stacked(onehot, per_seq):
    summed = jnp.einsum("sa,skrw->karw", onehot, per_seq, precision=lax.Precision.HIGHEST)
    return summed.reshape(per_seq.shape[1], ADAPTERS * RANK, per_seq.shape[-1])


def norm_forward(values, gain):
    scale = lax.rsqrt(jnp.mean(values * values, -1, keepdims=True) + EPS)
    return (scale, (values * scale * gain).astype(jnp.bfloat16))


def norm_backward(values, scale, gain, grad):
    weighted = grad * gain
    gain_grad = jnp.sum(grad * values * scale, axis=(0, 1))
    back = scale * weighted - values * scale * scale * scale * jnp.mean(
        weighted * values, -1, keepdims=True
    )
    return (back, gain_grad)


def per_device(
    inputs,
    cotangent,
    adapter_ids,
    block_index,
    gain_first,
    gain_second,
    w_query,
    w_key,
    w_value,
    w_output,
    w_gate_up,
    w_down,
    reduce_attention,
    raise_query,
    raise_keyvalue,
    reduce_output,
    raise_output,
    reduce_gate_up,
    raise_gate_up,
    reduce_down,
    raise_down,
):
    gathered = (
        lax.all_gather(gain_first, ("dp", "seq"), axis=0, tiled=True),
        lax.all_gather(gain_second, ("dp", "seq"), axis=0, tiled=True),
        lax.all_gather(w_query, ("dp", "seq"), axis=0, tiled=True),
        lax.all_gather(w_key, ("dp", "seq"), axis=0, tiled=True),
        lax.all_gather(w_value, ("dp", "seq"), axis=0, tiled=True),
        lax.all_gather(w_output, ("dp", "seq"), axis=0, tiled=True),
        lax.all_gather(reduce_attention, ("dp", "seq"), axis=1, tiled=True),
        lax.all_gather(raise_query, ("dp", "seq"), axis=0, tiled=True),
        lax.all_gather(raise_keyvalue, ("dp", "seq"), axis=1, tiled=True),
        lax.all_gather(reduce_output, ("dp", "seq"), axis=0, tiled=True),
        lax.all_gather(raise_output, ("dp", "seq"), axis=0, tiled=True),
        lax.all_gather(reduce_gate_up, ("dp", "seq"), axis=1, tiled=True),
        lax.all_gather(raise_gate_up, ("dp", "seq"), axis=1, tiled=True),
        lax.all_gather(reduce_down, ("dp", "seq"), axis=0, tiled=True),
        lax.all_gather(raise_down, ("dp", "seq"), axis=0, tiled=True),
    )
    (
        whole_gain_one,
        whole_gain_two,
        whole_query,
        whole_key,
        whole_value,
        whole_output,
        whole_reduce_att,
        whole_raise_query,
        whole_raise_kv,
        whole_reduce_out,
        whole_raise_out,
        whole_reduce_gu,
        whole_raise_gu,
        whole_reduce_down,
        whole_raise_down,
    ) = gathered
    sequences, blocks_dev, block_size, width = inputs.shape
    rows_dev = blocks_dev * block_size
    length_seq = block_index.shape[1] * block_size
    groups = HEADS // KV_HEADS
    kv_width = KV_HEADS * HEAD_DIM
    attn_scale = HEAD_DIM ** (-0.5)
    gain_one = whole_gain_one.astype(jnp.float32)
    gain_two = whole_gain_two.astype(jnp.float32)
    onehot_f = (adapter_ids[:, None] == jnp.arange(ADAPTERS, dtype=jnp.int32)[None, :]).astype(
        jnp.float32
    )
    onehot_b = onehot_f.astype(jnp.bfloat16)
    here = lax.axis_index("seq")
    own_blocks = lax.dynamic_slice_in_dim(block_index, here * blocks_dev, blocks_dev, 1)
    offsets = jnp.arange(block_size, dtype=jnp.int32)
    query_pos = (own_blocks[:, :, None] * block_size + offsets).reshape(sequences, rows_dev)
    key_pos = (block_index[:, :, None] * block_size + offsets).reshape(sequences, length_seq)
    visible = query_pos[:, :, None] >= key_pos[:, None, :]
    cosine, sine_values = rotary_tables(query_pos, HEAD_DIM)
    tokens = inputs.astype(jnp.float32).reshape(sequences, rows_dev, width)
    scale_one, normed_one = norm_forward(tokens, gain_one)
    sel_reduce_att = choose_stacked(onehot_b, whole_reduce_att)
    lows_att = jnp.einsum(
        "smd,skrd->skmr", normed_one, sel_reduce_att, preferred_element_type=jnp.float32
    ).astype(jnp.bfloat16)
    sel_raise_query = choose_rows(onehot_b, whole_raise_query)
    sel_raise_kv = choose_stacked(onehot_b, whole_raise_kv)
    query = jnp.einsum(
        "smd,dq->smq", normed_one, whole_query, preferred_element_type=jnp.float32
    ) + jnp.einsum(
        "smr,srq->smq", lows_att[:, 0], sel_raise_query, preferred_element_type=jnp.float32
    )
    key = jnp.einsum(
        "smd,dk->smk", normed_one, whole_key, preferred_element_type=jnp.float32
    ) + jnp.einsum(
        "smr,srk->smk", lows_att[:, 1], sel_raise_kv[:, 0], preferred_element_type=jnp.float32
    )
    value = (
        jnp.einsum("smd,dk->smk", normed_one, whole_value, preferred_element_type=jnp.float32)
        + jnp.einsum(
            "smr,srk->smk", lows_att[:, 2], sel_raise_kv[:, 1], preferred_element_type=jnp.float32
        )
    ).astype(jnp.bfloat16)
    query_rot = rotate(
        query.reshape(sequences, rows_dev, HEADS, HEAD_DIM), cosine, sine_values
    ).astype(jnp.bfloat16)
    key_rot = rotate(
        key.reshape(sequences, rows_dev, KV_HEADS, HEAD_DIM), cosine, sine_values
    ).astype(jnp.bfloat16)
    key_all, value_all = (
        lax.all_gather(
            key_rot.reshape(sequences, blocks_dev, block_size, kv_width), "seq", axis=1, tiled=True
        ),
        lax.all_gather(
            value.reshape(sequences, blocks_dev, block_size, kv_width), "seq", axis=1, tiled=True
        ),
    )
    key_heads = jnp.moveaxis(key_all.reshape(sequences, length_seq, KV_HEADS, HEAD_DIM), 2, 0)
    value_heads = jnp.moveaxis(value_all.reshape(sequences, length_seq, KV_HEADS, HEAD_DIM), 2, 0)
    query_heads = jnp.moveaxis(
        query_rot.reshape(sequences, rows_dev, KV_HEADS, groups, HEAD_DIM), 2, 0
    )

    def attend(packed):
        query_here, key_here, value_here = packed
        scores = (
            jnp.einsum("smgd,std->sgmt", query_here, key_here, preferred_element_type=jnp.float32)
            * attn_scale
        )
        scores = jnp.where(visible[:, None], scores, -1e30)
        peak = jnp.max(scores, -1, keepdims=True)
        weights = jnp.exp(scores - peak)
        total = jnp.sum(weights, -1, keepdims=True)
        probs = (weights / total).astype(jnp.bfloat16)
        mixed = jnp.einsum("sgmt,std->smgd", probs, value_here, preferred_element_type=jnp.float32)
        return (mixed, (peak + jnp.log(total))[..., 0])

    mixed, logsum = lax.map(attend, (query_heads, key_heads, value_heads))
    attended = (
        jnp.moveaxis(mixed, 0, 2)
        .reshape(sequences, rows_dev, HEADS * HEAD_DIM)
        .astype(jnp.bfloat16)
    )
    sel_reduce_out = choose_rows(onehot_b, whole_reduce_out)
    sel_raise_out = choose_rows(onehot_b, whole_raise_out)
    low_out = jnp.einsum(
        "smq,srq->smr", attended, sel_reduce_out, preferred_element_type=jnp.float32
    ).astype(jnp.bfloat16)
    branch_one = jnp.einsum(
        "smq,qd->smd", attended, whole_output, preferred_element_type=jnp.float32
    ) + jnp.einsum("smr,srd->smd", low_out, sel_raise_out, preferred_element_type=jnp.float32)
    middle = tokens + branch_one
    scale_two, normed_two = norm_forward(middle, gain_two)
    sel_reduce_gu = choose_stacked(onehot_b, whole_reduce_gu)
    sel_raise_gu = choose_stacked(onehot_b, whole_raise_gu)
    lows_gu = jnp.einsum(
        "smd,skrd->skmr", normed_two, sel_reduce_gu, preferred_element_type=jnp.float32
    ).astype(jnp.bfloat16)
    main_gu = jnp.einsum(
        "smd,kdf->skmf",
        normed_two,
        lax.all_gather(w_gate_up, ("dp", "seq"), axis=2, tiled=True),
        preferred_element_type=jnp.float32,
    )
    gate_up = main_gu + jnp.einsum(
        "skmr,skrf->skmf", lows_gu, sel_raise_gu, preferred_element_type=jnp.float32
    )
    gate = gate_up[:, 0]
    up_part = gate_up[:, 1]
    hidden = (jax.nn.silu(gate) * up_part).astype(jnp.bfloat16)
    branch_two = jnp.einsum(
        "smf,fd->smd",
        hidden,
        lax.all_gather(w_down, ("dp", "seq"), axis=0, tiled=True),
        preferred_element_type=jnp.float32,
    )
    sel_reduce_down = choose_rows(onehot_b, whole_reduce_down)
    sel_raise_down = choose_rows(onehot_b, whole_raise_down)
    low_down = jnp.einsum(
        "smf,srf->smr", hidden, sel_reduce_down, preferred_element_type=jnp.float32
    ).astype(jnp.bfloat16)
    branch_two = branch_two + jnp.einsum(
        "smr,srd->smd", low_down, sel_raise_down, preferred_element_type=jnp.float32
    )
    output = (middle + branch_two).astype(jnp.bfloat16).reshape(inputs.shape)
    grad_out = cotangent.reshape(sequences, rows_dev, width)
    grad_low_down = jnp.einsum(
        "smd,srd->smr", grad_out, sel_raise_down, preferred_element_type=jnp.float32
    ).astype(jnp.bfloat16)
    seq_raise_down = jnp.einsum(
        "smr,smd->srd", low_down, grad_out, preferred_element_type=jnp.float32
    )
    seq_reduce_down = jnp.einsum(
        "smr,smf->srf", grad_low_down, hidden, preferred_element_type=jnp.float32
    )
    grad_hidden = jnp.einsum(
        "smd,fd->smf",
        grad_out,
        lax.all_gather(w_down, ("dp", "seq"), axis=0, tiled=True),
        preferred_element_type=jnp.float32,
    )
    grad_hidden = grad_hidden + jnp.einsum(
        "smr,srf->smf", grad_low_down, sel_reduce_down, preferred_element_type=jnp.float32
    )
    sigmoid_gate = jax.nn.sigmoid(gate)
    grad_gate = grad_hidden * up_part * sigmoid_gate * (1.0 + gate * (1.0 - sigmoid_gate))
    grad_up = grad_hidden * (gate * sigmoid_gate)
    grad_gu = jnp.stack([grad_gate, grad_up], 1).astype(jnp.bfloat16)
    seq_raise_gu = jnp.einsum(
        "skmr,skmf->skrf", lows_gu, grad_gu, preferred_element_type=jnp.float32
    )
    grad_low_gu = jnp.einsum(
        "skmf,skrf->skmr", grad_gu, sel_raise_gu, preferred_element_type=jnp.float32
    ).astype(jnp.bfloat16)
    seq_reduce_gu = jnp.einsum(
        "skmr,smd->skrd", grad_low_gu, normed_two, preferred_element_type=jnp.float32
    )
    grad_normed_two = jnp.einsum(
        "skmf,kdf->smd",
        grad_gu,
        lax.all_gather(w_gate_up, ("dp", "seq"), axis=2, tiled=True),
        preferred_element_type=jnp.float32,
    )
    grad_normed_two = grad_normed_two + jnp.einsum(
        "skmr,skrd->smd", grad_low_gu, sel_reduce_gu, preferred_element_type=jnp.float32
    )
    back_two, gain_grad_two = norm_backward(middle, scale_two, gain_two, grad_normed_two)
    grad_middle = grad_out.astype(jnp.float32) + back_two
    grad_branch_one = grad_middle.astype(jnp.bfloat16)
    grad_low_out = jnp.einsum(
        "smd,srd->smr", grad_branch_one, sel_raise_out, preferred_element_type=jnp.float32
    ).astype(jnp.bfloat16)
    seq_raise_out = jnp.einsum(
        "smr,smd->srd", low_out, grad_branch_one, preferred_element_type=jnp.float32
    )
    seq_reduce_out = jnp.einsum(
        "smr,smq->srq", grad_low_out, attended, preferred_element_type=jnp.float32
    )
    back_query, back_key, back_value, back_output = (
        lax.all_gather(w_query, ("dp", "seq"), axis=0, tiled=True),
        lax.all_gather(w_key, ("dp", "seq"), axis=0, tiled=True),
        lax.all_gather(w_value, ("dp", "seq"), axis=0, tiled=True),
        lax.all_gather(w_output, ("dp", "seq"), axis=0, tiled=True),
    )
    grad_attended = (
        jnp.einsum("smd,qd->smq", grad_branch_one, back_output, preferred_element_type=jnp.float32)
        + jnp.einsum(
            "smr,srq->smq", grad_low_out, sel_reduce_out, preferred_element_type=jnp.float32
        )
    ).astype(jnp.bfloat16)
    grad_heads = jnp.moveaxis(
        grad_attended.reshape(sequences, rows_dev, KV_HEADS, groups, HEAD_DIM), 2, 0
    )

    def attend_back(packed):
        query_here, key_here, value_here, grad_here, logsum_here = packed
        scores = (
            jnp.einsum("smgd,std->sgmt", query_here, key_here, preferred_element_type=jnp.float32)
            * attn_scale
        )
        scores = jnp.where(visible[:, None], scores, -1e30)
        probs = jnp.exp(scores - logsum_here[..., None])
        probs_low = probs.astype(jnp.bfloat16)
        grad_probs = jnp.einsum(
            "smgd,std->sgmt", grad_here, value_here, preferred_element_type=jnp.float32
        )
        inner = jnp.sum(probs * grad_probs, -1, keepdims=True)
        grad_scores = (probs * (grad_probs - inner)).astype(jnp.bfloat16)
        grad_query_here = (
            jnp.einsum("sgmt,std->smgd", grad_scores, key_here, preferred_element_type=jnp.float32)
            * attn_scale
        )
        grad_key_here = (
            jnp.einsum(
                "sgmt,smgd->std", grad_scores, query_here, preferred_element_type=jnp.float32
            )
            * attn_scale
        )
        grad_value_here = jnp.einsum(
            "sgmt,smgd->std", probs_low, grad_here, preferred_element_type=jnp.float32
        )
        return (grad_query_here, grad_key_here, grad_value_here)

    grad_query_rot, grad_key_all, grad_value_all = lax.map(
        attend_back, (query_heads, key_heads, value_heads, grad_heads, logsum)
    )
    grad_key_all = jnp.moveaxis(grad_key_all, 0, 2).reshape(
        sequences, length_seq // block_size, block_size, kv_width
    )
    grad_value_all = jnp.moveaxis(grad_value_all, 0, 2).reshape(
        sequences, length_seq // block_size, block_size, kv_width
    )
    grad_key_own, grad_value_own = (
        lax.psum_scatter(
            grad_key_all.astype(jnp.bfloat16), "seq", scatter_dimension=1, tiled=True
        ).astype(jnp.float32),
        lax.psum_scatter(
            grad_value_all.astype(jnp.bfloat16), "seq", scatter_dimension=1, tiled=True
        ).astype(jnp.float32),
    )
    grad_query = (
        unrotate(
            jnp.moveaxis(grad_query_rot, 0, 2).reshape(sequences, rows_dev, HEADS, HEAD_DIM),
            cosine,
            sine_values,
        )
        .reshape(sequences, rows_dev, HEADS * HEAD_DIM)
        .astype(jnp.bfloat16)
    )
    grad_key = (
        unrotate(grad_key_own.reshape(sequences, rows_dev, KV_HEADS, HEAD_DIM), cosine, sine_values)
        .reshape(sequences, rows_dev, kv_width)
        .astype(jnp.bfloat16)
    )
    grad_value = grad_value_own.reshape(sequences, rows_dev, kv_width).astype(jnp.bfloat16)
    grad_low_query = jnp.einsum(
        "smq,srq->smr", grad_query, sel_raise_query, preferred_element_type=jnp.float32
    )
    grad_low_key = jnp.einsum(
        "smk,srk->smr", grad_key, sel_raise_kv[:, 0], preferred_element_type=jnp.float32
    )
    grad_low_value = jnp.einsum(
        "smk,srk->smr", grad_value, sel_raise_kv[:, 1], preferred_element_type=jnp.float32
    )
    grad_low_att = jnp.stack([grad_low_query, grad_low_key, grad_low_value], 1).astype(jnp.bfloat16)
    seq_raise_query = jnp.einsum(
        "smr,smq->srq", lows_att[:, 0], grad_query, preferred_element_type=jnp.float32
    )
    seq_raise_kv = jnp.stack(
        [
            jnp.einsum(
                "smr,smk->srk", lows_att[:, 1], grad_key, preferred_element_type=jnp.float32
            ),
            jnp.einsum(
                "smr,smk->srk", lows_att[:, 2], grad_value, preferred_element_type=jnp.float32
            ),
        ],
        1,
    )
    seq_reduce_att = jnp.einsum(
        "skmr,smd->skrd", grad_low_att, normed_one, preferred_element_type=jnp.float32
    )
    grad_normed_one = jnp.einsum(
        "smq,dq->smd", grad_query, back_query, preferred_element_type=jnp.float32
    )
    grad_normed_one = grad_normed_one + jnp.einsum(
        "smk,dk->smd", grad_key, back_key, preferred_element_type=jnp.float32
    )
    grad_normed_one = grad_normed_one + jnp.einsum(
        "smk,dk->smd", grad_value, back_value, preferred_element_type=jnp.float32
    )
    grad_normed_one = grad_normed_one + jnp.einsum(
        "skmr,skrd->smd", grad_low_att, sel_reduce_att, preferred_element_type=jnp.float32
    )
    back_one, gain_grad_one = norm_backward(tokens, scale_one, gain_one, grad_normed_one)
    input_grad = (grad_middle + back_one).reshape(inputs.shape)
    summed = (
        lax.psum_scatter(gain_grad_one, ("dp", "seq"), scatter_dimension=0, tiled=True),
        lax.psum_scatter(gain_grad_two, ("dp", "seq"), scatter_dimension=0, tiled=True),
        lax.psum_scatter(
            table_stacked(onehot_f, seq_reduce_att), ("dp", "seq"), scatter_dimension=1, tiled=True
        ),
        lax.psum_scatter(
            table_rows(onehot_f, seq_raise_query), ("dp", "seq"), scatter_dimension=0, tiled=True
        ),
        lax.psum_scatter(
            table_stacked(onehot_f, seq_raise_kv), ("dp", "seq"), scatter_dimension=1, tiled=True
        ),
        lax.psum_scatter(
            table_rows(onehot_f, seq_reduce_out), ("dp", "seq"), scatter_dimension=0, tiled=True
        ),
        lax.psum_scatter(
            table_rows(onehot_f, seq_raise_out), ("dp", "seq"), scatter_dimension=0, tiled=True
        ),
        lax.psum_scatter(
            table_stacked(onehot_f, seq_reduce_gu), ("dp", "seq"), scatter_dimension=1, tiled=True
        ),
        lax.psum_scatter(
            table_stacked(onehot_f, seq_raise_gu), ("dp", "seq"), scatter_dimension=1, tiled=True
        ),
        lax.psum_scatter(
            table_rows(onehot_f, seq_reduce_down), ("dp", "seq"), scatter_dimension=0, tiled=True
        ),
        lax.psum_scatter(
            table_rows(onehot_f, seq_raise_down), ("dp", "seq"), scatter_dimension=0, tiled=True
        ),
    )
    return (
        output,
        input_grad,
        summed[0],
        summed[1],
        summed[2],
        summed[3],
        summed[4],
        summed[5],
        summed[6],
        summed[7],
        summed[8],
        summed[9],
        summed[10],
    )


def solution(mesh):
    placed = (
        P("dp", "seq", None, None),
        P("dp", "seq", None, None),
        P("dp"),
        P("dp", None),
        P(("dp", "seq")),
        P(("dp", "seq")),
        P(("dp", "seq"), None),
        P(("dp", "seq"), None),
        P(("dp", "seq"), None),
        P(("dp", "seq"), None),
        P(None, None, ("dp", "seq")),
        P(("dp", "seq"), None),
        P(None, ("dp", "seq"), None),
        P(("dp", "seq"), None),
        P(None, ("dp", "seq"), None),
        P(("dp", "seq"), None),
        P(("dp", "seq"), None),
        P(None, ("dp", "seq"), None),
        P(None, ("dp", "seq"), None),
        P(("dp", "seq"), None),
        P(("dp", "seq"), None),
    )
    return jax.shard_map(
        per_device,
        mesh=mesh,
        in_specs=placed,
        out_specs=(
            P("dp", "seq", None, None),
            P("dp", "seq", None, None),
            P(("dp", "seq")),
            P(("dp", "seq")),
            P(None, ("dp", "seq"), None),
            P(("dp", "seq"), None),
            P(None, ("dp", "seq"), None),
            P(("dp", "seq"), None),
            P(("dp", "seq"), None),
            P(None, ("dp", "seq"), None),
            P(None, ("dp", "seq"), None),
            P(("dp", "seq"), None),
            P(("dp", "seq"), None),
        ),
        check_vma=False,
    )
```

profile of v0, /device:TPU:0, one launch (start us, length us, event | category | flops | bytes accessed | tf_op | source)
XLA Modules:
  0.0 1397.7 jit_solution(11443015997541219129)
XLA Ops:
  12.4 1.6 copy.89
  17.5 42.1 %all-reduce.15 = (bf16[2048]{0:T(1024)(128)(2,1)S(1)}, bf16[2048]{0:T(1024)(128)(2,1)S(1)}) all-reduce(bf16[2048]{0:T(1024)(128)(2,1)S(1)} %dynamic-update-slice, bf16[2048]{0:T(1024)(128)(2,1)S(1)} %dynamic-update-slice.1), channel_id=1, replica_groups=mesh['dp'=16,'seq'=2] {'dp','seq'}, use_global_device_ids=true, to_apply=%add | all-reduce | flops 4096 | bytes 16384
  60.3 66.6 %all_gather.66 = bf16[2,128,256]{2,0,1:T(2,128)(2,1)S(1)} all-gather(bf16[2,4,256]{2,0,1:T(2,128)(2,1)S(1)} %copy.81), channel_id=1, replica_groups=mesh['dp'=16,'seq'=2] {'dp','seq'}, dimensions={1}, use_global_device_ids=true | all-gather | bytes 135168 | tf_op jit(solution)/shard_map/all_gather | solution.py:108
  127.8 66.8 %all-gather.2 = bf16[32,4,2048]{2,1,0:T(4,128)(2,1)S(1)} all-gather(bf16[1,4,2048]{2,1,0:T(4,128)(2,1)S(1)} %bitcast.716), channel_id=1, replica_groups=mesh['dp'=16,'seq'=2] {'dp','seq'}, dimensions={0}, use_global_device_ids=true | all-gather | bytes 540672 | tf_op jit(solution)/shard_map/all_gather | solution.py:107
  195.4 69.2 %all-gather.3 = bf16[32,4,2048]{2,1,0:T(4,128)(2,1)S(1)} all-gather(bf16[1,4,2048]{2,1,0:T(4,128)(2,1)S(1)} %bitcast.717), channel_id=1, replica_groups=mesh['dp'=16,'seq'=2] {'dp','seq'}, dimensions={0}, use_global_device_ids=true | all-gather | bytes 540672 | tf_op jit(solution)/shard_map/all_gather | solution.py:109
  265.5 67.2 %all-gather.4 = bf16[32,4,2048]{2,1,0:T(4,128)(2,1)S(1)} all-gather(bf16[1,4,2048]{2,1,0:T(4,128)(2,1)S(1)} %bitcast.718), channel_id=1, replica_groups=mesh['dp'=16,'seq'=2] {'dp','seq'}, dimensions={0}, use_global_device_ids=true | all-gather | bytes 540672 | tf_op jit(solution)/shard_map/all_gather | solution.py:110
  334.2 69.5 %all-gather.6 = bf16[32,4,2048]{2,1,0:T(4,128)(2,1)S(1)} all-gather(bf16[1,4,2048]{2,1,0:T(4,128)(2,1)S(1)} %bitcast.719), channel_id=1, replica_groups=mesh['dp'=16,'seq'=2] {'dp','seq'}, dimensions={0}, use_global_device_ids=true | all-gather | bytes 540672 | tf_op jit(solution)/shard_map/all_gather | solution.py:114
  409.0 2.3 fusion.148
  411.4 2.1 fusion.146
  416.7 3.2 fusion.140
  420.0 2.4 fusion.209
  422.4 2.6 fusion.206
  425.0 2.6 reshape.1401
  427.6 2.5 fusion.118
  430.1 3.5 fusion.116
  435.2 5.6 all-gather
  442.2 6.1 all-gather.1
  448.3 6.1 fusion.85
  454.4 5.8 fusion.204
  460.2 2.5 convolution_add_fusion.4
  462.7 1.9 copy.84
  465.9 2.1 fusion.131
  468.0 18.2 %while.30 = (s32[]{:T(128)}, bf16[4,1,256,8,64]{2,4,3,1,0:T(8,128)(2,1)S(1)}, f32[4,1,8,256]{3,2,1,0:T(8,128)}, bf16[4,1,512,64]{2,3,1,0:T(8,128)(2,1)}, bf16[4,...) while((s32[]{:T(128)}, ...), condition=%wide.region_4.5_spmd.clone.clone, body=%wide.region_1.4_spmd.clone.sunk.clone | while | flops 281147392 | bytes 14095457 | solution.py:210
  469.9 2.1 fusion.299
  474.4 2.1 fusion.299
  478.9 2.1 fusion.299
  483.5 2.1 fusion.299
  486.4 34.7 %all-gather.26.cloned.1.call-done = bf16[2048,2048]{1,0:T(8,128)(2,1)} async-done(((bf16[64,2048]{1,0:T(8,128)(2,1)}), bf16[2048,2048]{1,0:T(8,128)(2,1)}) %all-gather.26.cloned.1.call-update) | async-done | bytes 8388624 | tf_op jit(solution)/shard_map/all_gather | solution.py:105
  521.2 5.8 fusion.214
  530.4 136.9 %all-gather.34.cloned.1.call-done = bf16[5632,2048]{1,0:T(8,128)(2,1)} async-done(((bf16[176,2048]{1,0:T(8,128)(2,1)}), bf16[5632,2048]{1,0:T(8,128)(2,1)}) %all-gather.34.cloned.1.call-update) | async-done | bytes 23068688 | tf_op jit(solution)/shard_map/all_gather | solution.py:246
  667.3 12.7 fusion.135
  680.0 243.7 %all-gather.28.cloned.1.call-done = bf16[2,2048,5632]{1,2,0:T(8,128)(2,1)} async-done(((bf16[2,2048,176]{1,2,0:T(8,128)(2,1)}), bf16[2,2048,5632]{1,2,0:T(8,128)(2,1)}) %all-gather.28.cloned.1.call-update) | async-done | bytes 46137360 | tf_op jit(solution)/shard_map/all_gather | solution.py:234
  923.7 22.5 %fusion.215 = f32[256,2,5632]{2,0,1:T(8,128)} fusion(bf16[256,2048,1]{1,0,2:T(8,128)(2,1)} %copy-done.7, bf16[2,2048,5632]{1,2,0:T(8,128)(2,1)} %all-gather.28.cloned.1.call-done), kind=kOutput, calls=%fused_computation.312 | convolution fusion | flops 11811160064 | bytes 58720256 | tf_op jit(solution)/shard_map/smd,kdf->skmf/dot_general | solution.py:231
  946.2 6.2 bitcast_add_fusion
  952.4 1.6 multiply_convert_fusion.1
  954.1 2.7 copy-done
  956.8 5.2 fusion.87
  962.1 1.6 fusion.122
  964.5 20.4 %multiply_reduce_fusion = (f32[2048]{0:T(1024)}, f32[256]{0:T(256)S(1)}, f32[256,2048]{1,0:T(8,128)S(1)}) fusion(f32[256,2048]{1,0:T(8,128)S(1)} %get-tuple-element.295, f32[256]{0:T(256)S(1)} %copy-done.73, f32[2048]{0:T(1024)S(1)} %copy-done.60, f32[256,2048]{1,0:T(8,128)S(1)} %convolution_bitcast_fusion.2, ...), kind=kOutput, calls=%fused_computation.140 | convolution fusion | flops 11817711616 | bytes 58214400 | tf_op jit(solution)/shard_map/skmf,kdf->smd/dot_general | solution.py:290
  984.9 2.5 subtract_add_fusion
  989.8 1.8 fusion.114
  994.8 2.4 fusion.200
  998.6 2.3 copy.90
  1000.9 35.6 %while.31 = (s32[]{:T(128)}, f32[4,1,256,8,64]{2,4,3,1,0:T(8,128)}, bf16[4,1,512,64]{2,3,1,0:T(8,128)(2,1)}, bf16[4,1,512,64]{2,3,1,0:T(8,128)(2,1)}, bf16[4,1,5...) while((s32[]{:T(128)}, f32[4,1,256,8,64]{2,4,3,1,0:T(8,128)}, ...), condition=%wide.region_9.10_spmd.clone.clone, body=%wide.region_7.9_spmd.clone.sunk.clone | while | flops 687110144 | bytes 42467588 | solution.py:356
  1002.5 2.1 fusion.309
  1011.4 2.1 fusion.309
  1020.3 2.1 fusion.309
  1029.3 2.1 fusion.309
  1038.6 1.7 broadcast_multiply_fusion.4
  1046.0 3.2 broadcast_multiply_fusion
  1049.2 2.0 broadcast_multiply_fusion.2
  1052.4 1.7 broadcast_multiply_fusion.3
  1054.1 3.3 broadcast_multiply_fusion.5
  1059.5 4.6 reduce-scatter.9.cloned.1.call-done
  1065.7 2.1 broadcast_multiply_fusion.1
  1068.8 15.6 %fusion.79 = f32[256,2048]{1,0:T(8,128)S(1)} fusion(bf16[5632,2048]{1,0:T(8,128)(2,1)} %all-gather.34.cloned.1.call-done, f32[1,2,256,5632]{3,2,1,0:T(8,128)} %copy-done), kind=kOutput, calls=%fused_computation.90 | convolution fusion | flops 5914230784 | bytes 36700160 | tf_op jit(solution)/shard_map/smf,fd->smd/dot_general | solution.py:243
  1085.9 5.9 fusion.216
  1094.4 2.3 fusion.108
  1096.7 40.6 %all-reduce.13 = (f32[2048]{0:T(1024)S(1)}, f32[2048]{0:T(1024)S(1)}) all-reduce(f32[2048]{0:T(1024)S(1)} %get-tuple-element.215, f32[2048]{0:T(1024)S(1)} %copy-done.74), channel_id=6, replica_groups=mesh['dp'=16,'seq'=2] {'dp','seq'}, use_global_device_ids=true, to_apply=%region_14.15.clone | all-reduce | flops 4096 | bytes 32768
  1138.4 3.7 fusion.105
  1142.1 237.9 %all-reduce.18.cloned.1.call-done = (f32[3,128,2048]{2,1,0:T(8,128)}, f32[128,2048]{1,0:T(8,128)}, f32[2,128,256]{2,1,0:T(8,128)}, f32[128,2048]{1,0:T(8,128)}, ...) async-done(((f32[3,128,2048]{2,1,0:T(8,128)}, f32[128,2048]{1,0:T(8,128)}, ...) | async-done | bytes 18350096
  1380.0 1.6 constant_dynamic-slice_fusion.8
  1384.4 1.7 constant_dynamic-slice_fusion.2
  1386.1 1.6 constant_dynamic-slice_fusion.1
  (371 shorter events, 97.5 us)
Async XLA Ops:
  7.2 9.8 copy-start.77
  7.2 10.0 copy-start.78
  7.2 53.0 %copy-start.75 = (bf16[2,4,256]{2,1,0:T(4,128)(2,1)S(1)}, bf16[2,4,256]{2,1,0:T(4,128)(2,1)}, u32[]{:S(2)}) copy-start(bf16[2,4,256]{2,1,0:T(4,128)(2,1)} %param.39) | copy-start | bytes 12292
  7.2 120.6 %copy-start.64 = (bf16[4,2048]{1,0:T(4,128)(2,1)S(1)}, bf16[4,2048]{1,0:T(4,128)(2,1)}, u32[]{:S(2)}) copy-start(bf16[4,2048]{1,0:T(4,128)(2,1)} %param.38) | copy-start | bytes 49156
  7.2 188.2 %copy-start.65 = (bf16[4,2048]{1,0:T(4,128)(2,1)S(1)}, bf16[4,2048]{1,0:T(4,128)(2,1)}, u32[]{:S(2)}) copy-start(bf16[4,2048]{1,0:T(4,128)(2,1)} %param.40) | copy-start | bytes 49156
  7.2 409.5 %all-gather.30.cloned.1.call-start = ((), (), s32[]{:S(2)}) async-start(), calls=%async_computation.8 | async-start | bytes 1081344 | tf_op jit(solution)/shard_map/all_gather | solution.py:111
  8.7 411.2 %all-gather.18.cloned.1.call-start = ((), (), s32[]{:S(2)}) async-start(), calls=%async_computation.2 | async-start | bytes 1081344 | tf_op jit(solution)/shard_map/all_gather | solution.py:104
  9.5 412.9 %all-gather.22.cloned.1.call-start = ((), (), s32[]{:S(2)}) async-start(), calls=%async_computation.4 | async-start | bytes 1081344 | tf_op jit(solution)/shard_map/all_gather | solution.py:103
  10.2 414.8 %all-gather.36.cloned.1.call-start = ((), (), s32[]{:S(2)}) async-start(), calls=%async_computation.13 | async-start | bytes 1486848 | tf_op jit(solution)/shard_map/all_gather | solution.py:113
  10.8 419.3 %all-gather.20.cloned.1.call-start = ((), (), s32[]{:S(2)}) async-start(), calls=%async_computation.3 | async-start | bytes 2162688 | tf_op jit(solution)/shard_map/all_gather | solution.py:106
  12.3 435.9 %all-gather.32.cloned.1.call-start = ((), (), s32[]{:S(2)}) async-start(), calls=%async_computation.9 | async-start | bytes 2973696 | tf_op jit(solution)/shard_map/all_gather | solution.py:112
  14.0 440.4 %all-gather.24.cloned.1.call-start = ((), (), s32[]{:S(2)}) async-start(), calls=%async_computation.5 | async-start | bytes 8650752 | tf_op jit(solution)/shard_map/all_gather | solution.py:102
  14.7 506.4 %all-gather.26.cloned.1.call-start = ((), (), s32[]{:S(2)}) async-start(), calls=%async_computation.6 | async-start | bytes 8650752 | tf_op jit(solution)/shard_map/all_gather | solution.py:105
  15.5 250.1 %copy-start.66 = (bf16[4,2048]{1,0:T(4,128)(2,1)S(1)}, bf16[4,2048]{1,0:T(4,128)(2,1)}, u32[]{:S(2)}) copy-start(bf16[4,2048]{1,0:T(4,128)(2,1)} %param.41) | copy-start | bytes 49156
  15.5 651.8 %all-gather.34.cloned.1.call-start = ((), (), s32[]{:S(2)}) async-start(), calls=%async_computation.10 | async-start | bytes 23789568 | tf_op jit(solution)/shard_map/all_gather | solution.py:246
  16.2 907.4 %all-gather.28.cloned.1.call-start = ((), (), s32[]{:S(2)}) async-start(), calls=%async_computation.7 | async-start | bytes 47579136 | tf_op jit(solution)/shard_map/all_gather | solution.py:234
  16.8 317.4 %copy-start.67 = (bf16[4,2048]{1,0:T(4,128)(2,1)S(1)}, bf16[4,2048]{1,0:T(4,128)(2,1)}, u32[]{:S(2)}) copy-start(bf16[4,2048]{1,0:T(4,128)(2,1)} %param.45) | copy-start | bytes 49156
  16.8 1040.6 %reduce-scatter.7.cloned.1.call-start = ((), (), s32[]{:S(2)}) async-start(), calls=%async_computation.11 | async-start | bytes 393216 | tf_op jit(solution)/shard_map/reduce_scatter | solution.py:366
  59.6 394.8 %copy-start.57 = (f32[2048]{0:T(1024)}, f32[2048]{0:T(1024)S(1)}, u32[]{:S(2)}) copy-start(f32[2048]{0:T(1024)S(1)} %convert_element_type.427) | copy-start | bytes 24580
  194.5 210.2 %copy-start.79 = (s32[1,2]{1,0:T(1,128)S(1)}, s32[1,2]{1,0:T(1,128)}, u32[]{:S(2)}) copy-start(s32[1,2]{1,0:T(1,128)} %param.28) | copy-start | bytes 28
  264.6 144.1 %copy-start.9 = (bf16[1,1,256,2048]{3,2,1,0:T(8,128)(2,1)S(1)}, bf16[1,1,256,2048]{3,2,1,0:T(8,128)(2,1)}, u32[]{:S(2)}) copy-start(bf16[1,1,256,2048]{3,2,1,0:T(8,128)(2,1)} %param.25) | copy-start | bytes 3145732
  403.8 12.0 copy-start.12
  404.7 8.8 copy-start.20
  404.7 9.9 copy-start.21
  409.0 13.4 copy-start.69
  430.1 4.9 copy-start.52
  430.1 4.9 copy-start.53
  430.1 11.7 copy-start.51
  433.6 8.5 copy-start.18
  433.6 8.5 copy-start.22
  435.0 7.1 copy-start.55
  442.0 12.4 copy-start.70
  454.4 5.8 copy-start.37
  468.0 18.2 %copy-start.41 = (bf16[1,16,2048]{2,0,1:T(2,128)(2,1)S(1)}, bf16[1,16,2048]{2,0,1:T(2,128)(2,1)}, u32[]{:S(2)}) copy-start(bf16[1,16,2048]{2,0,1:T(2,128)(2,1)} %fusion.146) | copy-start | bytes 196612
  486.2 35.0 %copy-start.3 = (bf16[4,1,256,8,64]{2,4,3,1,0:T(8,128)(2,1)}, bf16[4,1,256,8,64]{2,4,3,1,0:T(8,128)(2,1)S(1)}, u32[]{:S(2)}) copy-start(bf16[4,1,256,8,64]{2,4,3,1,0:T(8,128)(2,1)S(1)} %get-tuple-element.105) | copy-start | bytes 3145732
  486.4 40.6 %copy-start.39 = (bf16[1,16,2048]{2,0,1:T(2,128)(2,1)S(1)}, bf16[1,16,2048]{2,0,1:T(2,128)(2,1)}, u32[]{:S(2)}) copy-start(bf16[1,16,2048]{2,0,1:T(2,128)(2,1)} %fusion.144) | copy-start | bytes 196612
  521.2 5.8 copy-start.10
  527.7 436.4 %copy-start.1 = (f32[256,2048]{1,0:T(8,128)}, f32[256,2048]{1,0:T(8,128)S(1)}, u32[]{:S(2)}) copy-start(f32[256,2048]{1,0:T(8,128)S(1)} %get-tuple-element.295) | copy-start | bytes 6291460
  952.4 4.3 copy-start
  952.4 4.3 copy-start.35
  952.4 4.3 copy-start.62
  956.8 5.2 copy-start.24
  964.5 20.4 %copy-start.13 = (bf16[1,1,256,2048]{3,2,1,0:T(8,128)(2,1)S(1)}, bf16[1,1,256,2048]{3,2,1,0:T(8,128)(2,1)}, u32[]{:S(2)}) copy-start(bf16[1,1,256,2048]{3,2,1,0:T(8,128)(2,1)} %param.26) | copy-start | bytes 3145732
  984.9 4.8 copy-start.83
  987.8 6.9 slice-start
  989.8 5.0 slice-start.1
  1000.9 37.7 %copy-start.23 = (f32[256,64]{0,1:T(8,128)S(1)}, f32[256,64]{0,1:T(8,128)}, u32[]{:S(2)}) copy-start(f32[256,64]{0,1:T(8,128)} %get-tuple-element.289) | copy-start | bytes 196612
  1038.3 25.7 %reduce-scatter.9.cloned.1.call-start = ((), (), s32[]{:S(2)}) async-start(), calls=%async_computation.12 | async-start | bytes 393216 | tf_op jit(solution)/shard_map/reduce_scatter | solution.py:369
  1042.6 3.3 copy-start.36
  1042.7 3.3 copy-start.68
  1043.9 7.3 copy-start.16
  1046.0 3.2 copy-start.25
  1049.1 3.2 copy-start.30
  1054.0 5.1 copy-start.54
  1054.1 11.1 copy-start.11
  1054.1 11.1 copy-start.58
  1054.1 11.1 copy-start.71
  1054.1 325.9 %all-reduce.18.cloned.1.call-start = ((), (), s32[]{:S(2)}) async-start(), calls=%async_computation.14 | async-start | bytes 36700160
  1064.0 3.8 copy-start.26
  1068.8 15.7 %copy-start.2 = (f32[256,2048]{1,0:T(8,128)S(1)}, f32[256,2048]{1,0:T(8,128)}, u32[]{:S(2)}) copy-start(f32[256,2048]{1,0:T(8,128)} %copy-done.1) | copy-start | bytes 6291460
  1068.8 15.7 %copy-start.45 = (bf16[1,16,2048]{2,0,1:T(2,128)(2,1)S(1)}, bf16[1,16,2048]{2,0,1:T(2,128)(2,1)}, u32[]{:S(2)}) copy-start(bf16[1,16,2048]{2,0,1:T(2,128)(2,1)} %copy-done.44) | copy-start | bytes 196612
  1085.9 6.0 copy-start.31
  1085.9 6.0 copy-start.43
  1085.9 6.0 copy-start.34
  (50 other events, 84.3 us)
Sparse Core Ops, SparseCore 0:
  11.5 56.6 all-gather.29
  71.1 52.5 all-gather.17
  126.6 53.3 all-gather.21
  182.7 54.6 all-gather.35
  240.8 55.7 all-gather.19
  299.9 58.1 all-gather.31
  361.0 81.6 all-gather.23
  445.7 75.4 all-gather.25
  524.1 143.1 all-gather.33
  670.1 253.5 all-gather.27
  1038.5 9.8 reduce-scatter.6
  1054.2 9.8 reduce-scatter.8
  1070.4 309.4 all-reduce.17
where the time goes:
time: 1400 us
  waiting for transfers between devices  662 us (47%)
  blocking collectives  434 us (31%)
  matrix products  192 us (14%)
  local copies, waits for them, and re-layouts  47.7 us (3%)
  other arithmetic  44.7 us (3%)
  between operations  16 us (1%)
    all_gather x1, waiting for transfers between devices, per_device(): lax.all_gather(w_gate_up, ('dp', 'seq'), axis=2, tiled=True)  244 us
    unnamed x14, waiting for transfers between devices  242 us
    all_gather x1, waiting for transfers between devices, per_device(): lax.all_gather(w_down, ('dp', 'seq'), axis=0, tiled=True)  137 us
    unnamed x2, blocking collectives  82.7 us
    all_gather x1, blocking collectives, per_device(): lax.all_gather(raise_down, ('dp', 'seq'), axis=0, tiled=True)  69.5 us
    all_gather x1, blocking collectives, per_device(): lax.all_gather(reduce_output, ('dp', 'seq'), axis=0, tiled=True)  69.2 us
    all_gather x1, blocking collectives, per_device(): lax.all_gather(raise_output, ('dp', 'seq'), axis=0, tiled=True)  67.2 us
    all_gather x1, blocking collectives, per_device(): lax.all_gather(raise_query, ('dp', 'seq'), axis=0, tiled=True)  66.8 us
  transfers between devices with their start and end apart: 13, of which 5 were waited for; matrix products, arithmetic and copies ran while one was open for 10% of the time, Pallas kernels for 0%

commit v1 on v0

v1 whole, which is shorter than its diff:
```python
import functools

import jax
import jax.numpy as jnp
from jax import lax
from jax.experimental import pallas as pl
from jax.experimental.pallas import tpu as pltpu
from jax.sharding import PartitionSpec as P

HEADS = 32
KV_HEADS = 4
HEAD_DIM = 64
ADAPTERS = 8
RANK = 16
TABLE = ADAPTERS * RANK

EPS = 1e-05
THETA = 10000.0

ALL = ("dp", "seq")
X, C, Y = 1, 2, 4
BF = jnp.bfloat16
F32 = jnp.float32


def dot(a, b, dims):
    return lax.dot_general(a, b, (dims, ((), ())), preferred_element_type=F32)


def nn(a, b):
    return dot(a, b, ((1,), (0,)))


def nt(a, b):
    return dot(a, b, ((1,), (1,)))


def tn(a, b):
    return dot(a, b, ((0,), (0,)))


def exchange(value, mask, n):
    return lax.ppermute(value, ALL, [(i, i ^ mask) for i in range(n)])


def rotary_tables(positions):
    half = HEAD_DIM // 2
    speeds = THETA ** (-jnp.arange(half, dtype=F32) * (2.0 / HEAD_DIM))
    angles = positions.astype(F32)[..., None] * speeds
    angles = jnp.concatenate([angles, angles], -1)
    return (jnp.cos(angles), jnp.sin(angles))


def rotate(values, cosine, sine):
    half = values.shape[-1] // 2
    turned = jnp.concatenate([-values[..., half:], values[..., :half]], -1)
    return values * cosine[:, None, :] + turned * sine[:, None, :]


def unrotate(grads, cosine, sine):
    half = grads.shape[-1] // 2
    scaled = grads * sine[:, None, :]
    turned = jnp.concatenate([scaled[..., half:], -scaled[..., :half]], -1)
    return grads * cosine[:, None, :] + turned


def norm_forward(values, gain):
    scale = lax.rsqrt(jnp.mean(values * values, -1, keepdims=True) + EPS)
    return (scale, (values * scale * gain).astype(BF))


def norm_backward(values, scale, gain, grad):
    weighted = grad * gain
    gain_grad = jnp.sum(grad * values * scale, axis=0)
    back = scale * weighted - values * (scale * scale * scale) * jnp.mean(
        weighted * values, -1, keepdims=True
    )
    return (back, gain_grad)


def outer_bits(n):
    bits, bit = [], 8
    while bit < n:
        bits.append(bit)
        bit *= 2
    return bits


class Outer:
    def __init__(self, value, n):
        self.n = n
        self.held = {0: value}
        self.offsets = sorted(range(8, n, 8), key=lambda offset: (bin(offset).count("1"), -offset))

    def step(self):
        level = bin(self.offsets[0]).count("1")
        while self.offsets and bin(self.offsets[0]).count("1") == level:
            offset = self.offsets.pop(0)
            low = offset & -offset
            self.held[offset] = exchange(self.held[offset ^ low], low, self.n)
        return bool(self.offsets)

    def pass_through(self, order, *others):
        keys = sorted(self.held)
        passed = order.point(*[self.held[k] for k in keys], *others)
        self.held = dict(zip(keys, passed))
        return passed[len(keys) :]

    def parts(self):
        return [self.held[offset] for offset in sorted(self.held)]


def sum_outer(parts, n):
    held = {8 * i: part for i, part in enumerate(parts)}
    for bit in outer_bits(n):
        for offset in sorted(held):
            if offset & bit:
                held[offset ^ bit] = held[offset ^ bit] + exchange(held.pop(offset), bit, n)
    return held[0]


def place_kernel(count, outer, width, me_ref, *refs):
    pieces, out, held, sems, last = refs[:count], *refs[count:]
    me = me_ref[0]
    z, y, c, x = me // 8, (me // 4) % 2, (me // 2) % 2, me % 2
    copies = []
    for i in range(count):
        part, dc, dy, dx = i // 8, (i // 4) % 2, (i // 2) % 2, i % 2
        for dz in range(outer):
            block = (((z ^ dz) * 2 + (y ^ dy)) * 2 + (c ^ dc)) * 2 + (x ^ dx)
            copies.append(
                pltpu.make_async_copy(
                    pieces[i].at[dz],
                    held.at[block, :, pl.ds(part * width, width)],
                    sems.at[len(copies)],
                )
            )
    for copy in copies:
        copy.start()
    for copy in copies:
        copy.wait()
    copy = pltpu.make_async_copy(held, out, last)
    copy.start()
    copy.wait()


class Rows(Outer):
    def __init__(self, shard, n):
        super().__init__(shard, n)
        self.shape = shard.shape
        self.outer = n // 8

    def start_plane(self):
        half = self.shape[1] // 2
        pieces = self.parts()
        first = jnp.stack([p[:, :half] for p in pieces])
        second = jnp.stack([p[:, half:] for p in pieces])
        self.near = [first, exchange(first, X, self.n), exchange(first, Y, self.n)]
        self.near += [second, exchange(second, X, self.n), exchange(second, Y, self.n)]

    def end_plane(self):
        first, first_x, first_y, second, second_x, second_y = self.near
        first_xy = exchange(first_x, Y, self.n)
        second_xy = exchange(second_y, X, self.n)
        self.near = [first, first_x, first_y, first_xy, second, second_x, second_y, second_xy]

    def place(self, me):
        n, outer = self.n, self.outer
        rows, width = self.shape
        far = [exchange(v, C, n) for v in self.near]
        held = self.near[:4] + far[:4] + self.near[4:] + far[4:]
        whole = pl.pallas_call(
            functools.partial(place_kernel, len(held), outer, width // 2),
            out_shape=jax.ShapeDtypeStruct((n, rows, width), held[0].dtype),
            in_specs=[pl.BlockSpec(memory_space=pltpu.SMEM)]
            + [pl.BlockSpec(memory_space=pl.ANY)] * len(held),
            out_specs=pl.BlockSpec(memory_space=pl.ANY),
            scratch_shapes=[
                pltpu.VMEM((n, rows, width), held[0].dtype),
                pltpu.SemaphoreType.DMA((len(held) * outer,)),
                pltpu.SemaphoreType.DMA(()),
            ],
            compiler_params=pltpu.CompilerParams(vmem_limit_bytes=16 << 20),
            name="place",
        )(me.reshape(1), *held)
        return whole.reshape(n * rows, width)


class Plane:
    def __init__(self, value, n):
        self.n = n
        half = value.shape[0] // 2
        first, second = value[:half], value[half:]
        self.value = value
        self.near = [exchange(first, X, n), exchange(second, Y, n)]
        self.near += [exchange(second, X, n), exchange(first, Y, n)]
        self.other = exchange(value, C, n)

    def end(self):
        first_x, second_y, second_x, first_y = self.near
        first_xy = exchange(first_x, Y, self.n)
        second_xy = exchange(second_y, X, self.n)
        near = [first_x, second_x, first_y, second_y]
        self.far = [exchange(v, C, self.n) for v in near]
        self.near = near + [first_xy, second_xy]

    def all(self):
        far = self.far + [exchange(v, C, self.n) for v in self.near[4:]]
        return jnp.concatenate([self.value] + self.near + [self.other] + far, 0)


class Order:
    def __init__(self):
        self.token = jnp.zeros((), F32)

    def point(self, *values):
        *values, self.token = lax.optimization_barrier((*values, self.token))
        return values[0] if len(values) == 1 else values


def half_of(block, part):
    half = block.shape[0] // 2
    return block[part * half : (part + 1) * half].astype(F32)


def sum_plane(mine, other, n):
    recv = exchange(other, C, n)
    held = lambda block, part: half_of(mine[block], part) + half_of(recv[block], part)
    x_first = exchange(held(1, 0).astype(BF), X, n)
    y_second = exchange(held(2, 1).astype(BF), Y, n)
    xy_first = exchange(held(3, 0).astype(BF), X, n)
    xy_second = exchange(held(3, 1).astype(BF), Y, n)
    last_first = exchange((held(2, 0) + xy_first.astype(F32)).astype(BF), Y, n)
    last_second = exchange((held(1, 1) + xy_second.astype(F32)).astype(BF), X, n)
    return jnp.concatenate(
        [
            held(0, 0) + x_first.astype(F32) + last_first.astype(F32),
            held(0, 1) + y_second.astype(F32) + last_second.astype(F32),
        ],
        0,
    )


def load_feed(pieces, shard, slots, sems):
    copies = []
    for i, piece in enumerate(pieces):
        for kind, slot in enumerate(slots):
            copies.append(
                pltpu.make_async_copy(
                    piece.at[pl.ds(kind * shard, shard)],
                    slot.at[pl.ds(i * shard, shard)],
                    sems.at[len(copies)],
                )
            )
    return copies


def lift_of(adapter, place):
    row = lax.broadcasted_iota(jnp.int32, (TABLE, TABLE), 0) - place * RANK
    col = lax.broadcasted_iota(jnp.int32, (TABLE, TABLE), 1) - adapter * RANK
    return ((row == col) & (row >= 0) & (row < RANK)).astype(F32).astype(BF)


def hidden_kernel(count, shard, width, ids_ref, normed_ref, cot_ref, *refs):
    pieces = refs[:count]
    hidden_ref, gate_ref, up_ref, grads_ref, w_gate, w_up, w_down, sems = refs[count:]
    group = pl.program_id(0)
    copies = load_feed(pieces, shard, (w_gate, w_up, w_down), sems)

    @pl.when(group == 0)
    def _():
        for copy in copies:
            copy.start()
        grads_ref[...] = jnp.zeros_like(grads_ref)
        for copy in copies:
            copy.wait()

    adapter = ids_ref[group]
    lows = normed_ref[:, width:]
    low_gate = nn(lows, lift_of(adapter, 0)).astype(BF)
    low_up = nn(lows, lift_of(adapter, 1)).astype(BF)
    low_cot = nn(lows, lift_of(adapter, 2)).astype(BF)
    normed = normed_ref[:, :width]
    gate = nt(normed, w_gate[:, :width]) + nt(low_gate, w_gate[:, width:])
    up = nt(normed, w_up[:, :width]) + nt(low_up, w_up[:, width:])
    grad = nt(cot_ref[...], w_down[:, :width]) + nt(low_cot, w_down[:, width:])
    sigmoid = 1.0 / (1.0 + jnp.exp(-gate))
    silu = gate * sigmoid
    hidden = (silu * up).astype(BF)
    grad_gate = (grad * up * sigmoid * (1.0 + gate * (1.0 - sigmoid))).astype(BF)
    grad_up = (grad * silu).astype(BF)
    hidden_ref[...] = hidden
    gate_ref[...] = grad_gate
    up_ref[...] = grad_up
    grads_ref[0] += tn(low_gate, grad_gate)
    grads_ref[1] += tn(low_up, grad_up)
    grads_ref[2] += tn(low_cot, hidden)


def hidden_stage(ids, normed, cot, pieces, shard):
    tokens, wide = normed.shape
    width = wide - TABLE
    count = len(pieces)
    cols = count * shard
    block = tokens // 4
    out = jax.ShapeDtypeStruct((tokens, cols), BF)
    tile = pl.BlockSpec((block, cols), lambda i: (i, 0))
    return pl.pallas_call(
        functools.partial(hidden_kernel, count, shard, width),
        grid=(4,),
        out_shape=(out, out, out, jax.ShapeDtypeStruct((3, TABLE, cols), F32)),
        in_specs=[
            pl.BlockSpec(memory_space=pltpu.SMEM),
            pl.BlockSpec((block, wide), lambda i: (i, 0)),
            pl.BlockSpec((block, width), lambda i: (i, 0)),
        ]
        + [pl.BlockSpec(memory_space=pl.ANY)] * count,
        out_specs=(tile, tile, tile, pl.BlockSpec((3, TABLE, cols), lambda i: (0, 0, 0))),
        scratch_shapes=[pltpu.VMEM((cols, wide), BF)] * 3
        + [pltpu.SemaphoreType.DMA((3 * count,))],
        compiler_params=pltpu.CompilerParams(vmem_limit_bytes=40 << 20),
        cost_estimate=pl.CostEstimate(
            flops=6 * tokens * wide * cols,
            bytes_accessed=2 * (tokens * (wide + width + 3 * cols) + 3 * cols * wide),
            transcendentals=tokens * cols,
        ),
        name="hidden",
    )(ids, normed, cot, *pieces)


def grad_kernel(count, parts, shard, width, *refs):
    acts, refs = refs[: 2 * parts], refs[2 * parts :]
    pieces, (out_ref, w_gate, w_up, sems) = refs[:count], refs[count:]
    copies = load_feed(pieces, shard, (w_gate, w_up), sems)

    @pl.when(pl.program_id(0) == 0)
    def _():
        for copy in copies:
            copy.start()
        for copy in copies:
            copy.wait()

    cols = acts[0].shape[1]
    main, low_gate, low_up = 0.0, 0.0, 0.0
    for i in range(parts):
        own = pl.ds(i * cols, cols)
        gate, up = acts[i][...], acts[parts + i][...]
        main += nn(gate, w_gate[own, :width]) + nn(up, w_up[own, :width])
        low_gate += nn(gate, w_gate[own, width:])
        low_up += nn(up, w_up[own, width:])
    out_ref[:, :width] = main.astype(BF)
    out_ref[:, width : width + TABLE] = low_gate.astype(BF)
    out_ref[:, width + TABLE :] = low_up.astype(BF)


def grad_stage(gates, ups, pieces, shard, first, groups):
    tokens, cols = gates[0].shape
    wide = pieces[0].shape[1]
    width = wide - TABLE
    count, parts = len(pieces), len(gates)
    block = tokens // 4
    tile = pl.BlockSpec((block, cols), lambda i: (i + first, 0))
    return pl.pallas_call(
        functools.partial(grad_kernel, count, parts, shard, width),
        grid=(groups,),
        out_shape=jax.ShapeDtypeStruct((groups * block, wide + TABLE), BF),
        in_specs=[tile] * (2 * parts) + [pl.BlockSpec(memory_space=pl.ANY)] * count,
        out_specs=pl.BlockSpec((block, wide + TABLE), lambda i: (i, 0)),
        scratch_shapes=[pltpu.VMEM((count * shard, wide), BF)] * 2
        + [pltpu.SemaphoreType.DMA((2 * count,))],
        compiler_params=pltpu.CompilerParams(vmem_limit_bytes=40 << 20),
        cost_estimate=pl.CostEstimate(
            flops=4 * groups * block * wide * cols * parts,
            bytes_accessed=2 * (groups * block * (2 * parts * cols + wide) + 2 * count * shard * wide),
            transcendentals=0,
        ),
        name="grad",
    )(*gates, *ups, *pieces)


def down_kernel(count, parts, shard, *refs):
    acts, refs = refs[:parts], refs[parts:]
    pieces, (out_ref, w_down, sems) = refs[:count], refs[count:]
    copies = [
        pltpu.make_async_copy(
            piece.at[pl.ds(2 * shard, shard)], w_down.at[pl.ds(i * shard, shard)], sems.at[i]
        )
        for i, piece in enumerate(pieces)
    ]

    @pl.when(pl.program_id(0) == 0)
    def _():
        for copy in copies:
            copy.start()
        for copy in copies:
            copy.wait()

    cols = acts[0].shape[1]
    total = 0.0
    for i in range(parts):
        total += nn(acts[i][...], w_down[pl.ds(i * cols, cols), :])
    out_ref[...] = total.astype(BF)


def down_stage(hiddens, pieces, shard):
    tokens, cols = hiddens[0].shape
    wide = pieces[0].shape[1]
    count, parts = len(pieces), len(hiddens)
    block = tokens // 4
    return pl.pallas_call(
        functools.partial(down_kernel, count, parts, shard),
        grid=(4,),
        out_shape=jax.ShapeDtypeStruct((tokens, wide), BF),
        in_specs=[pl.BlockSpec((block, cols), lambda i: (i, 0))] * parts
        + [pl.BlockSpec(memory_space=pl.ANY)] * count,
        out_specs=pl.BlockSpec((block, wide), lambda i: (i, 0)),
        scratch_shapes=[
            pltpu.VMEM((count * shard, wide), BF),
            pltpu.SemaphoreType.DMA((count,)),
        ],
        compiler_params=pltpu.CompilerParams(vmem_limit_bytes=40 << 20),
        cost_estimate=pl.CostEstimate(
            flops=2 * tokens * wide * cols * parts,
            bytes_accessed=2 * (tokens * (parts * cols + wide) + count * shard * wide),
            transcendentals=0,
        ),
        name="down",
    )(*hiddens, *pieces)


def per_device(
    n,
    inputs,
    cotangent,
    adapter_ids,
    block_index,
    gain_first,
    gain_second,
    w_query,
    w_key,
    w_value,
    w_output,
    w_gate_up,
    w_down,
    reduce_attention,
    raise_query,
    raise_keyvalue,
    reduce_output,
    raise_output,
    reduce_gate_up,
    raise_gate_up,
    reduce_down,
    raise_down,
):
    width = inputs.shape[-1]
    rows = inputs.shape[-2]
    shard = w_down.shape[0]
    own_rows = raise_down.shape[0]
    gains = gain_first.shape[0]
    kv_width = KV_HEADS * HEAD_DIM
    groups = HEADS // KV_HEADS
    attn_scale = HEAD_DIM ** (-0.5)
    side = lax.axis_index("seq")
    me = lax.axis_index(ALL).astype(jnp.int32)
    tokens = inputs.reshape(rows, width).astype(F32)
    grad_out = cotangent.reshape(rows, width)

    order = Order()
    qkv_rows = Rows(jnp.concatenate([w_query, w_key, w_value], 1), n)
    qkv_rows.step()
    cot_plane = Plane(grad_out, n)

    table_width = 10 * width
    chunk = table_width // n
    table = jnp.concatenate(
        [reduce_attention[0], reduce_attention[1], reduce_attention[2], raise_query]
        + [reduce_output, raise_output, reduce_gate_up[0], reduce_gate_up[1], raise_down]
        + [raise_keyvalue[0], raise_keyvalue[1]],
        1,
    )
    table = jnp.pad(table, ((0, 0), (0, table_width - table.shape[1])))
    table = jnp.moveaxis(table.reshape(own_rows, n, chunk), 1, 0)
    hidden_table = jnp.stack([raise_gate_up[0], raise_gate_up[1], reduce_down])
    hidden_table = hidden_table.reshape(3, own_rows, n, shard).transpose(2, 1, 0, 3)
    hidden_table = hidden_table.reshape(n, own_rows, 3 * shard)
    small = jnp.concatenate([gain_first, gain_second, adapter_ids.astype(BF)])
    used = chunk + 3 * shard
    sent = -(-(used + small.shape[0]) // 128) * 128
    small = jnp.pad(small, (0, sent - used - small.shape[0]))
    small = jnp.broadcast_to(small, (n, own_rows, small.shape[0]))
    came = lax.all_to_all(jnp.concatenate([table, hidden_table, small], -1), ALL, 0, 0, tiled=True)
    gain_one = came[:, 0, used : used + gains].reshape(width).astype(F32)
    gain_two = came[:, 0, used + gains : used + 2 * gains].reshape(width).astype(F32)
    ids = came[:, 0, used + 2 * gains].astype(jnp.int32)
    columns = came[:, :, :chunk].reshape(ADAPTERS, RANK, chunk)
    hidden_cols = came[:, :, chunk:used].reshape(TABLE, 3, shard)
    own = lax.all_to_all(jnp.take(columns, ids, axis=0), ALL, 0, 0, tiled=True)
    own = jnp.moveaxis(own, 0, 1).reshape(RANK, table_width)
    (a_query, a_key, a_value, b_query, a_out, b_out, a_gate, a_up, b_down) = [
        own[:, i * width : (i + 1) * width] for i in range(9)
    ]
    b_key = own[:, 9 * width : 9 * width + kv_width]
    b_value = own[:, 9 * width + kv_width : 9 * width + 2 * kv_width]
    lift = (
        jnp.arange(TABLE, dtype=jnp.int32)[None, :]
        == adapter_ids[0] * RANK + jnp.arange(RANK, dtype=jnp.int32)[:, None]
    ).astype(BF)

    (w_output,) = qkv_rows.pass_through(order, w_output)
    more = True
    while more:
        more = qkv_rows.step()
    out_rows = Rows(w_output, n)
    out_rows.step()
    feed = jnp.stack([w_gate_up[0].T, w_gate_up[1].T, w_down])
    feed = jnp.concatenate([feed, hidden_cols.transpose(1, 2, 0)], 2)
    padded = -(-shard // 16) * 16
    feed = jnp.pad(feed, ((0, 0), (0, padded - shard), (0, 0))).reshape(3 * padded, -1)
    (feed, *cot_plane.near) = qkv_rows.pass_through(order, feed, *cot_plane.near)
    qkv_rows.start_plane()
    (feed,) = out_rows.pass_through(order, feed)
    more = True
    while more:
        more = out_rows.step()
    cot_plane.end()
    feed_rows = Outer(feed, n)
    feed_rows.step()

    positions_of = lambda block: block * rows + jnp.arange(rows, dtype=jnp.int32)
    own_block = lax.dynamic_index_in_dim(block_index[0], side, 0, keepdims=False)
    other_block = lax.dynamic_index_in_dim(block_index[0], 1 - side, 0, keepdims=False)
    query_pos = positions_of(own_block)
    key_pos = jnp.concatenate([query_pos, positions_of(other_block)])
    visible = query_pos[:, None] >= key_pos[None, :]
    cosine, sine = rotary_tables(query_pos)

    scale_one, normed_one = norm_forward(tokens, gain_one)
    low_att = nt(normed_one, jnp.concatenate([a_query, a_key, a_value], 0)).astype(BF)
    low_query, low_key, low_value = [low_att[:, i * RANK : (i + 1) * RANK] for i in range(3)]
    qkv_rows.near = list(order.point(*qkv_rows.near))
    qkv_rows.end_plane()
    qkv_rows.near = list(order.point(*qkv_rows.near))
    w_qkv = qkv_rows.place(me)
    out_rows.pass_through(order)
    out_rows.start_plane()
    qkv = nn(normed_one, w_qkv)
    query = qkv[:, :width] + nn(low_query, b_query)
    key = qkv[:, width : width + kv_width] + nn(low_key, b_key)
    value = (qkv[:, width + kv_width :] + nn(low_value, b_value)).astype(BF)
    query_rot = rotate(query.reshape(rows, HEADS, HEAD_DIM), cosine, sine).astype(BF)
    key_rot = rotate(key.reshape(rows, KV_HEADS, HEAD_DIM), cosine, sine).astype(BF)
    key_value = jnp.concatenate([key_rot.reshape(rows, kv_width), value], 1)
    key_value = jnp.concatenate([key_value, exchange(key_value, X, n)], 0)
    key_value, query_rot, *out_rows.near = order.point(key_value, query_rot, *out_rows.near)
    out_rows.end_plane()
    key_heads = key_value[:, :kv_width].reshape(2 * rows, KV_HEADS, HEAD_DIM)
    value_heads = key_value[:, kv_width:].reshape(2 * rows, KV_HEADS, HEAD_DIM)
    query_heads = query_rot.reshape(rows, KV_HEADS, groups, HEAD_DIM)
    scores = jnp.einsum("mkgd,tkd->kgmt", query_heads, key_heads, preferred_element_type=F32)
    scores = jnp.where(visible, scores * attn_scale, -1e30)
    peak = jnp.max(scores, -1, keepdims=True)
    weights = jnp.exp(scores - peak)
    probs = (weights / jnp.sum(weights, -1, keepdims=True)).astype(BF)
    mixed = jnp.einsum("kgmt,tkd->mkgd", probs, value_heads, preferred_element_type=F32)
    attended = mixed.reshape(rows, width).astype(BF)
    low_out = nt(attended, a_out).astype(BF)
    attended, *out_rows.near = order.point(attended, *out_rows.near)
    w_out = out_rows.place(me)
    middle = tokens + nn(attended, w_out) + nn(low_out, b_out)

    scale_two, normed_two = norm_forward(middle, gain_two)
    low_gate = nt(normed_two, a_gate).astype(BF)
    low_up = nt(normed_two, a_up).astype(BF)
    grad_low_down = nt(grad_out, b_down).astype(BF)
    spare = jnp.zeros((rows, TABLE - 3 * RANK), BF)
    normed_plane = Plane(
        jnp.concatenate([normed_two, low_gate, low_up, grad_low_down, spare], 1), n
    )
    plane_ids = ids[me ^ jnp.array([0, Y, C, C | Y], jnp.int32)]
    cot_all = cot_plane.all()
    *normed_plane.near, cot_all = order.point(*normed_plane.near, cot_all)
    normed_plane.end()
    more = True
    while more:
        feed_rows.pass_through(order)
        more = feed_rows.step()
    normed_all = normed_plane.all()
    feeds = feed_rows.parts()
    half = len(feeds) // 2
    stages = [
        hidden_stage(plane_ids, normed_all, cot_all, part, padded)
        for part in (feeds[:half], feeds[half:])
    ]
    hiddens, gates, ups = [[stage[i] for stage in stages] for i in range(3)]
    wide = width + TABLE
    block_shape = (4, rows, wide + TABLE)
    grad_far = grad_stage(gates, ups, feeds, padded, 2, 2).reshape(block_shape)
    grad_near = grad_stage(gates, ups, feeds, padded, 0, 2).reshape(block_shape)
    grad_normed = sum_plane(grad_near, grad_far, n)
    branch_two = down_stage(hiddens, feeds, padded).reshape(2, 4, rows, wide)
    branch_two = sum_plane(branch_two[0], branch_two[1], n)
    hidden_grads = jnp.concatenate([stage[3] for stage in stages], 2)
    hidden_grads = sum_outer(
        [hidden_grads[:, :, i * padded : i * padded + shard] for i in range(n // 8)], n
    )
    low_down = nn(branch_two[:, width:].astype(BF), lift.T).astype(BF)
    output = (middle + branch_two[:, :width] + nn(low_down, b_down)).astype(BF)

    grad_low_gate = nn(grad_normed[:, width:wide].astype(BF), lift.T).astype(BF)
    grad_low_up = nn(grad_normed[:, wide:].astype(BF), lift.T).astype(BF)
    grad_normed_two = (
        grad_normed[:, :width] + nn(grad_low_gate, a_gate) + nn(grad_low_up, a_up)
    )
    back_two, gain_grad_two = norm_backward(middle, scale_two, gain_two, grad_normed_two)
    grad_middle = grad_out.astype(F32) + back_two
    grad_one = grad_middle.astype(BF)
    grad_low_out = nt(grad_one, b_out).astype(BF)
    grad_attended = (
        nt(grad_one, w_out)
        + nn(grad_low_out, a_out)
    ).astype(BF)
    grad_heads = grad_attended.reshape(rows, KV_HEADS, groups, HEAD_DIM)
    grad_probs = jnp.einsum("mkgd,tkd->kgmt", grad_heads, value_heads, preferred_element_type=F32)
    probs_f = probs.astype(F32)
    inner = jnp.sum(probs_f * grad_probs, -1, keepdims=True)
    grad_scores = (probs_f * (grad_probs - inner)).astype(BF)
    grad_query = jnp.einsum("kgmt,tkd->mkgd", grad_scores, key_heads, preferred_element_type=F32)
    grad_key = jnp.einsum("kgmt,mkgd->tkd", grad_scores, query_heads, preferred_element_type=F32)
    grad_value = jnp.einsum("kgmt,mkgd->tkd", probs, grad_heads, preferred_element_type=F32)
    grad_query = grad_query.reshape(rows, HEADS, HEAD_DIM) * attn_scale
    grad_kv = jnp.concatenate(
        [
            (grad_key * attn_scale).reshape(2 * rows, kv_width),
            grad_value.reshape(2 * rows, kv_width),
        ],
        1,
    )
    grad_kv = grad_kv[:rows] + exchange(grad_kv[rows:].astype(BF), X, n).astype(F32)
    grad_query = unrotate(grad_query, cosine, sine).reshape(rows, width).astype(BF)
    grad_key = unrotate(grad_kv[:, :kv_width].reshape(rows, KV_HEADS, HEAD_DIM), cosine, sine)
    grad_key = grad_key.reshape(rows, kv_width).astype(BF)
    grad_value = grad_kv[:, kv_width:].astype(BF)
    grad_low_query = nt(grad_query, b_query).astype(BF)
    grad_low_key = nt(grad_key, b_key).astype(BF)
    grad_low_value = nt(grad_value, b_value).astype(BF)
    grad_qkv = jnp.concatenate([grad_query, grad_key, grad_value], 1)
    grad_low_att = jnp.concatenate([grad_low_query, grad_low_key, grad_low_value], 1)
    grad_normed_one = nt(grad_qkv, w_qkv) + nn(
        grad_low_att, jnp.concatenate([a_query, a_key, a_value], 0)
    )
    back_one, gain_grad_one = norm_backward(tokens, scale_one, gain_one, grad_normed_one)
    input_grad = (grad_middle + back_one).reshape(inputs.shape)

    reduce_att = tn(grad_low_att, normed_one)
    per_seq = jnp.concatenate(
        [
            reduce_att[:RANK],
            reduce_att[RANK : 2 * RANK],
            reduce_att[2 * RANK :],
            tn(low_query, grad_query),
            tn(grad_low_out, attended),
            tn(low_out, grad_one),
            tn(grad_low_gate, normed_two),
            tn(grad_low_up, normed_two),
            tn(low_down, grad_out),
            tn(low_key, grad_key),
            tn(low_value, grad_value),
            jnp.zeros((RANK, table_width - 9 * width - 2 * kv_width), F32),
        ],
        1,
    )
    per_seq = jnp.moveaxis(per_seq.reshape(RANK, n, chunk), 1, 0)
    per_seq = lax.all_to_all(per_seq, ALL, 0, 0, tiled=True)
    onehot = (ids[:, None] == jnp.arange(ADAPTERS, dtype=jnp.int32)[None, :]).astype(F32)
    summed = jnp.einsum("na,nrc->arc", onehot, per_seq, precision=lax.Precision.HIGHEST)
    hidden_grads = hidden_grads.transpose(1, 0, 2).reshape(n, own_rows, 3 * shard)
    gain_grads = jnp.concatenate(
        [gain_grad_one.reshape(n, gains), gain_grad_two.reshape(n, gains)], 1
    )
    gain_grads = jnp.broadcast_to(gain_grads[:, None], (n, own_rows, 2 * gains))
    final = jnp.concatenate([summed.reshape(n, own_rows, chunk), hidden_grads, gain_grads], -1)
    final = lax.all_to_all(final, ALL, 0, 0, tiled=True)
    gain_grads = jnp.sum(final[:, 0, used:], 0)
    tables = jnp.moveaxis(final[:, :, :chunk], 0, 1).reshape(own_rows, table_width)
    parts = [tables[:, i * width : (i + 1) * width] for i in range(9)]
    kv = tables[:, 9 * width : 9 * width + 2 * kv_width]
    hidden_grads = final[:, :, chunk:used].reshape(n, own_rows, 3, shard).transpose(2, 1, 0, 3)
    hidden_grads = hidden_grads.reshape(3, own_rows, n * shard)
    return (
        output.reshape(inputs.shape),
        input_grad,
        gain_grads[:gains],
        gain_grads[gains:],
        jnp.stack(parts[:3]),
        parts[3],
        jnp.stack([kv[:, :kv_width], kv[:, kv_width:]]),
        parts[4],
        parts[5],
        jnp.stack(parts[6:8]),
        hidden_grads[:2],
        hidden_grads[2],
        parts[8],
    )


def solution(mesh):
    n = mesh.shape["dp"] * mesh.shape["seq"]
    rows = P(("dp", "seq"), None)
    stacked = P(None, ("dp", "seq"), None)
    vector = P(("dp", "seq"))
    blocks = P("dp", "seq", None, None)
    return jax.shard_map(
        functools.partial(per_device, n),
        mesh=mesh,
        in_specs=(
            blocks,
            blocks,
            P("dp"),
            P("dp", None),
            vector,
            vector,
            rows,
            rows,
            rows,
            rows,
            P(None, None, ("dp", "seq")),
            rows,
            stacked,
            rows,
            stacked,
            rows,
            rows,
            stacked,
            stacked,
            rows,
            rows,
        ),
        out_specs=(
            blocks,
            blocks,
            vector,
            vector,
            stacked,
            rows,
            stacked,
            rows,
            rows,
            stacked,
            stacked,
            rows,
            rows,
        ),
        check_vma=False,
    )
```

time: 1400 us -> 705 us (0.50)
  blocking collectives: 434 us -> 0 us
  waiting for transfers between devices: 662 us -> 285 us
  matrix products: 192 us -> 77.9 us
  Pallas kernels: 0 us -> 95.2 us
  starting transfers between devices: 0.76 us -> 80.3 us
  local copies, waits for them, and re-layouts: 47.7 us -> 98.4 us
    all_gather x10 -> x0, waiting for transfers between devices: 415 us -> none  [the longest x1 244 us: per_device(): lax.all_gather(w_gate_up, ('dp', 'seq'), axis=2, tiled=True)]
    all_gather x7 -> x0, blocking collectives: 351 us -> none  [the longest x1 69.5 us: per_device(): lax.all_gather(raise_down, ('dp', 'seq'), axis=0, tiled=True)]
    ppermute x0 -> x82, waiting for transfers between devices: none -> 270 us  [exchange(): return lax.ppermute(value, ALL, [(i, i ^ mask) for i in range(n)])]
    unnamed x14 -> x0, waiting for transfers between devices: 242 us -> none
    dot_general x79 -> x40, matrix products: 192 us -> 68.1 us  [the longest x34 46.7 us: dot(): return lax.dot_general(a, b, (dims, ((), ())), preferred_element_type=F32)]
    pallas_call x0 -> x7, Pallas kernels: none -> 95.2 us  [the longest x2 45.3 us: hidden_stage(): pl.pallas_call(functools.partial(hidden_kernel, count, shard, width), gri...]
    unnamed x2 -> x0, blocking collectives: 82.7 us -> none
    ppermute x0 -> x82, starting transfers between devices: none -> 65.6 us  [exchange(): return lax.ppermute(value, ALL, [(i, i ^ mask) for i in range(n)])]
  transfers between devices with their start and end apart: 13 -> 86, of which waited for: 5 -> 28; matrix products, arithmetic and copies ran while one was open for 10% -> 22% of each run, Pallas kernels for 0% -> 8%
where the time goes in v1:
time: 705 us; the launch traced here: 697 us
  waiting for transfers between devices  285 us (40%)
  local copies, waits for them, and re-layouts  98.4 us (14%)
  Pallas kernels  95.2 us (14%)
  starting transfers between devices  80.3 us (11%)
  matrix products  77.9 us (11%)
  other arithmetic  55.3 us (8%)
    ppermute x82, waiting for transfers between devices, exchange(): return lax.ppermute(value, ALL, [(i, i ^ mask) for i in range(n)])  270 us
    ppermute x82, starting transfers between devices, exchange(): return lax.ppermute(value, ALL, [(i, i ^ mask) for i in range(n)])  65.6 us
    dot_general x34, matrix products, dot(): return lax.dot_general(a, b, (dims, ((), ())), preferred_element_type=F32)  46.7 us
    pallas_call x2, Pallas kernels, hidden_stage(): pl.pallas_call(functools.partial(hidden_kernel, count, shard, width), gri...  45.3 us
    unnamed x261, local copies, waits for them, and re-layouts  42.5 us
    pallas_call x2, Pallas kernels, grad_stage(): pl.pallas_call(functools.partial(grad_kernel, count, parts, shard, width)...  29.5 us
    all_to_all x1, waiting for transfers between devices, per_device(): final = lax.all_to_all(final, ALL, 0, 0, tiled=True)  14.3 us
  transfers between devices with their start and end apart: 86, of which 28 were waited for; matrix products, arithmetic and copies ran while one was open for 22% of the time, Pallas kernels for 8%

profile of v1, /device:TPU:0, one launch (start us, length us, event | category | flops | bytes accessed | tf_op | source)
XLA Modules:
  0.0 697.1 jit_solution(9016817394772567647)
XLA Ops:
  3.3 3.0 collective-permute-start
  6.3 2.6 collective-permute-start.1
  8.9 2.3 slice_bitcast_fusion.18
  17.7 2.6 all-to-all-start
  22.0 2.3 constant_dynamic-update-slice_fusion.27
  35.5 2.7 pad_maximum_fusion.1
  38.1 2.8 collective-permute-done.3
  42.3 2.9 collective-permute-done.6
  52.0 2.2 collective-permute-done.22
  58.3 3.6 all-to-all-start.1
  72.2 7.0 collective-permute-done.10.refs_10_
  83.7 9.3 %collective-permute-done.7.refs_1_ = bf16[4,64,1280]{2,1,0:T(8,128)(2,1)} collective-permute-done((bf16[4,64,1280]{2,1,0:T(8,128)(2,1)S(1)}, bf16[4,64,1280]{2,1,0:T(8,128)(2,1)}, u32[]{:S(2)}, u32[]{:S(2)}) %collective-permute-start.7) | collective-permute-done | bytes 655392 | tf_op jit(solution)/shard_map/ppermute | solution.py:43
  97.4 6.9 collective-permute-done.44
  106.7 2.3 constant_dynamic-update-slice_fusion.20
  110.4 6.6 collective-permute-done.12.refs_11_
  129.4 3.6 place.2
  133.1 2.9 fusion.74
  139.2 2.9 copy.148
  142.1 2.8 slice_negate_fusion.1
  151.7 3.0 fusion.36
  154.7 3.2 collective-permute-done.21
  161.4 9.8 %fusion.165 = (f32[4,8,256]{2,1,0:T(8,128)S(1)}, f32[4,8,256,512]{2,3,1,0:T(8,128)}) fusion(pred[256,512]{0,1:T(8,128)(4,1)} %broadcast_compare_fusion, bf16[512,4,64,1]{0,2,3,1:T(8,128)(2,1)S(1)} %bitcast.418, bf16[256,4,8,64]{0,3,2,1:T(8,128)(2,1)} %bitcast.404), kind=kOutput, calls=%fused_computation.372 | convolution fusion | flops 553648640 | bytes 18251776 | tf_op jit(solution)/shard_map/sub | solution.py:562
  171.2 6.9 divide_convert_fusion
  178.2 3.0 convolution_convert_fusion
  192.7 2.4 collective-permute-start.62
  195.1 3.3 place.3
  198.5 2.5 multiply_reduce_fusion.2
  208.0 2.6 concatenate.101
  215.0 78.1 %collective-permute-done.61.refs_1_.refs_3_.refs_5_ = bf16[528,2176]{1,0:T(8,128)(2,1)} collective-permute-done((bf16[528,2176]{1,0:T(8,128)(2,1)S(1)}, bf16[528,2176]{1,0:T(8,128)(2,1)}, u32[]{:S(2)}, u32[]{:S(2)}) %collective-permute-start.61) | collective-permute-done | bytes 2297888 | tf_op jit(solution)/shard_map/ppermute | solution.py:43
  297.0 9.9 %collective-permute-done.42 = bf16[128,2176]{1,0:T(8,128)(2,1)S(1)} collective-permute-done((bf16[128,2176]{1,0:T(8,128)(2,1)S(1)}, bf16[128,2176]{1,0:T(8,128)(2,1)S(1)}, u32[]{:S(2)}, u32[]{:S(2)}) %collective-permute-start.42) | collective-permute-done | bytes 557088 | tf_op jit(solution)/shard_map/ppermute | solution.py:43
  312.2 7.5 %collective-permute-done.52 = bf16[128,2176]{1,0:T(8,128)(2,1)S(1)} collective-permute-done((bf16[128,2176]{1,0:T(8,128)(2,1)S(1)}, bf16[128,2176]{1,0:T(8,128)(2,1)S(1)}, u32[]{:S(2)}, u32[]{:S(2)}) %collective-permute-start.52) | collective-permute-done | bytes 557088 | tf_op jit(solution)/shard_map/ppermute | solution.py:43
  320.6 3.1 collective-permute-done.53
  331.8 22.8 %hidden.2 = (bf16[2048,352]{1,0:T(8,128)(2,1)S(1)}, bf16[2048,352]{1,0:T(8,128)(2,1)S(1)}, bf16[2048,352]{1,0:T(8,128)(2,1)S(1)}, f32[3,128,352]{2,1,0:T(8,128)S(1)}) custom-call(s32[4]{0:T(128)S(1)} %gather_fusion.1, bf16[2048,2176]{1,0:T(8,128)(2,1)} %constant_dynamic-update-slice_fusion.28.normed_ref, ...), custom_call_target="tpu_custom_call" | custom-call | flops 9412018176 | bytes 26222592 | tf_op jit(solution)/shard_map/hidden/pallas_call | solution.py:308
  354.6 22.5 %hidden.3 = (bf16[2048,352]{1,0:T(8,128)(2,1)S(1)}, bf16[2048,352]{1,0:T(8,128)(2,1)S(1)}, bf16[2048,352]{1,0:T(8,128)(2,1)S(1)}, f32[3,128,352]{2,1,0:T(8,128)S(1)}) custom-call(s32[4]{0:T(128)S(1)} %gather_fusion.1, bf16[2048,2176]{1,0:T(8,128)(2,1)} %constant_dynamic-update-slice_fusion.28.normed_ref, ...), custom_call_target="tpu_custom_call" | custom-call | flops 9412018176 | bytes 26222592 | tf_op jit(solution)/shard_map/hidden/pallas_call | solution.py:308
  377.1 13.4 %down.1 = bf16[2048,2176]{1,0:T(8,128)(2,1)} custom-call(bf16[2048,352]{1,0:T(8,128)(2,1)S(1)} %get-tuple-element.140.refs_0_, bf16[2048,352]{1,0:T(8,128)(2,1)S(1)} %get-tuple-element.142.refs_1_, bf16[528,2176]{1,0:T(8,128)(2,1)S(1)} %bitcast.372, bf16[528,2176]{1,0:T(8,128)(2,1)} %collective-permute-done.61.refs_1_.refs_3_.refs_5_, ...), custom_call_target="tpu_custom_call" | custom-call | flops 6274678784 | bytes 14860288 | tf_op jit(solution)/shard_map/down/pallas_call | solution.py:410
  390.6 4.7 slice.672
  395.3 14.8 %grad.3 = bf16[1024,2304]{1,0:T(8,128)(2,1)} custom-call(bf16[2048,352]{1,0:T(8,128)(2,1)S(1)} %get-tuple-element.143.refs_0_, bf16[2048,352]{1,0:T(8,128)(2,1)S(1)} %get-tuple-element.144.refs_1_, bf16[2048,352]{1,0:T(8,128)(2,1)S(1)} %get-tuple-element.145.refs_2_, bf16[2048,352]{1,0:T(8,128)(2,1)S(1)} %get-tuple-element.146.refs_3_, ...), custom_call_target="tpu_custom_call" | custom-call | flops 6274678784 | bytes 13467648 | tf_op jit(solution)/shard_map/grad/pallas_call | solution.py:363
  410.6 14.8 %grad.2 = bf16[1024,2304]{1,0:T(8,128)(2,1)} custom-call(bf16[2048,352]{1,0:T(8,128)(2,1)S(1)} %get-tuple-element.143.refs_0_, bf16[2048,352]{1,0:T(8,128)(2,1)S(1)} %get-tuple-element.144.refs_1_, bf16[2048,352]{1,0:T(8,128)(2,1)S(1)} %get-tuple-element.145.refs_2_, bf16[2048,352]{1,0:T(8,128)(2,1)S(1)} %get-tuple-element.146.refs_3_, ...), custom_call_target="tpu_custom_call" | custom-call | flops 6274678784 | bytes 13467648 | tf_op jit(solution)/shard_map/grad/pallas_call | solution.py:363
  429.3 3.6 fusion.58
  435.1 7.7 %collective-permute-done.66 = bf16[128,2176]{1,0:T(8,128)(2,1)S(1)} collective-permute-done((bf16[128,2176]{1,0:T(8,128)(2,1)S(1)}, bf16[128,2176]{1,0:T(8,128)(2,1)S(1)}, u32[]{:S(2)}, u32[]{:S(2)}) %collective-permute-start.66) | collective-permute-done | bytes 557088 | tf_op jit(solution)/shard_map/ppermute | solution.py:43
  445.4 21.9 %collective-permute-done.73 = bf16[128,2304]{1,0:T(8,128)(2,1)S(1)} collective-permute-done((bf16[128,2304]{1,0:T(8,128)(2,1)S(1)}, bf16[128,2304]{1,0:T(8,128)(2,1)S(1)}, u32[]{:S(2)}, u32[]{:S(2)}) %collective-permute-start.73) | collective-permute-done | bytes 589856 | tf_op jit(solution)/shard_map/ppermute | solution.py:43
  468.8 2.4 fusion.72
  473.3 5.8 collective-permute-done.72
  479.1 4.8 collective-permute-done.74
  486.6 9.3 %collective-permute-done.69 = bf16[128,2176]{1,0:T(8,128)(2,1)S(1)} collective-permute-done((bf16[128,2176]{1,0:T(8,128)(2,1)S(1)}, bf16[128,2176]{1,0:T(8,128)(2,1)S(1)}, u32[]{:S(2)}, u32[]{:S(2)}) %collective-permute-start.69) | collective-permute-done | bytes 557088 | tf_op jit(solution)/shard_map/ppermute | solution.py:43
  498.4 22.1 %collective-permute-done.76 = bf16[128,2304]{1,0:T(8,128)(2,1)S(1)} collective-permute-done((bf16[128,2304]{1,0:T(8,128)(2,1)S(1)}, bf16[128,2304]{1,0:T(8,128)(2,1)S(1)}, u32[]{:S(2)}, u32[]{:S(2)}) %collective-permute-start.76) | collective-permute-done | bytes 589856 | tf_op jit(solution)/shard_map/ppermute | solution.py:43
  524.2 6.2 collective-permute-done.75
  534.0 2.5 multiply_reduce_fusion
  541.2 3.4 fusion.14
  544.6 2.3 copy.155
  546.9 5.2 fusion.1
  552.2 6.8 fusion.169
  559.0 7.6 %fusion.2 = bf16[4,8,256,512]{2,3,1,0:T(8,128)(2,1)S(1)} fusion(f32[4,512,256,8]{2,1,3,0:T(8,128)S(1)} %get-tuple-element.229, f32[4,8,256]{2,1,0:T(8,128)S(1)} %get-tuple-element.228, f32[4,8,256,512]{2,3,1,0:T(8,128)} %get-tuple-element.224, f32[4,8,256]{2,1,0:T(8,128)S(1)} %copy-done.71), kind=kLoop, calls=%fused_computation.6 | loop fusion | flops 25165824 | bytes 42008576 | tf_op jit(solution)/shard_map/convert_element_type | solution.py:626
  568.3 2.6 fusion.48
  575.8 2.9 collective-permute-done.78
  586.6 3.4 all-to-all-start.2
  592.5 30.1 %collective-permute-done.80 = f32[3,128,176]{2,1,0:T(8,128)S(1)} collective-permute-done((f32[3,128,176]{2,1,0:T(8,128)S(1)}, f32[3,128,176]{2,1,0:T(8,128)S(1)}, u32[]{:S(2)}, u32[]{:S(2)}) %collective-permute-start.80) | collective-permute-done | bytes 270368 | tf_op jit(solution)/shard_map/ppermute | solution.py:43
  622.7 2.6 collective-permute-start.81
  625.3 12.5 %collective-permute-done.79 = f32[3,128,176]{2,1,0:T(8,128)S(1)} collective-permute-done((f32[3,128,176]{2,1,0:T(8,128)S(1)}, f32[3,128,176]{2,1,0:T(8,128)S(1)}, u32[]{:S(2)}, u32[]{:S(2)}) %collective-permute-start.79) | collective-permute-done | bytes 270368 | tf_op jit(solution)/shard_map/ppermute | solution.py:43
  637.8 4.4 collective-permute-done.81
  647.9 8.6 %fusion.29 = (f32[2048]{0:T(1024)S(1)}, f32[256]{0:T(256)S(1)}, f32[256,2048]{1,0:T(8,128)}) fusion(bf16[1,1,256,2048]{3,2,1,0:T(8,128)(2,1)S(1)} %copy-done.36, f32[256]{0:T(256)S(1)} %copy-done.101, f32[2048]{0:T(1024)S(1)} %copy-done.85, f32[256,2048]{1,0:T(8,128)S(1)} %fusion.87, bf16[2048,2560]{1,0:T(8,128)(2,1)} %bitcast.368, ...), kind=kOutput, calls=%fused_computation.54 | convolution fusion | flops 2692478720 | bytes 17057792 | tf_op jit(solution)/shard_map/dot_general | solution.py:27
  663.7 5.0 all-to-all-start.3
  668.8 2.8 fusion.16
  673.6 14.3 %all-to-all-done.3 = f32[32,4,1296]{2,1,0:T(4,128)} async-done(((f32[32,4,1296]{2,1,0:T(4,128)}), f32[32,4,1296]{2,1,0:T(4,128)}, u32[]{:S(2)}, u32[]{:S(2)}) %all-to-all-start.3) | async-done | bytes 663584 | tf_op jit(solution)/shard_map/all_to_all | solution.py:682
  (558 shorter events, 191.1 us)
Async XLA Ops:
  3.3 27.8 %collective-permute-start = (bf16[64,2560]{1,0:T(8,128)(2,1)S(1)}, bf16[64,2560]{1,0:T(8,128)(2,1)}, u32[]{:S(2)}, u32[]{:S(2)}) collective-permute-start(bf16[64,2560]{1,0:T(8,128)(2,1)S(1)} %constant_dynamic-update-slice_fusion.11), channel_id=1, source_target_pairs={{0,8},{1,9},{2,10},{3,11},{4,12},{5,13},{6,14},{7,15},{8,0},{9,1},... | collective-permute-start | bytes 983048 | tf_op jit(solution)/shard_map/ppermute | solution.py:43
  6.3 26.3 %collective-permute-start.1 = (bf16[64,2560]{1,0:T(8,128)(2,1)S(1)}, bf16[64,2560]{1,0:T(8,128)(2,1)}, u32[]{:S(2)}, u32[]{:S(2)}) collective-permute-start(bf16[64,2560]{1,0:T(8,128)(2,1)S(1)} %constant_dynamic-update-slice_fusion.11), channel_id=1, source_target_pairs={{0,16},{1,17},{2,18},{3,19},{4,20},{5,21},{6,22},{7,23},{8,24},{9,... | collective-permute-start | bytes 983048 | tf_op jit(solution)/shard_map/ppermute | solution.py:43
  11.2 29.8 %collective-permute-start.4 = (bf16[128,2048]{1,0:T(8,128)(2,1)}, bf16[128,2048]{1,0:T(8,128)(2,1)}, u32[]{:S(2)}, u32[]{:S(2)}) collective-permute-start(bf16[128,2048]{1,0:T(8,128)(2,1)} %get-tuple-element.173), channel_id=1, source_target_pairs={{0,4},{1,5},{2,6},{3,7},{4,0},{5,1},{6,2},{7,3},{8,12},{9,13},{10,... | collective-permute-start | bytes 1572872 | tf_op jit(solution)/shard_map/ppermute | solution.py:43
  12.7 28.8 %collective-permute-start.5 = (bf16[128,2048]{1,0:T(8,128)(2,1)}, bf16[128,2048]{1,0:T(8,128)(2,1)}, u32[]{:S(2)}, u32[]{:S(2)}) collective-permute-start(bf16[128,2048]{1,0:T(8,128)(2,1)} %get-tuple-element.173), channel_id=1, source_target_pairs={{0,1},{1,0},{2,3},{3,2},{4,5},{5,4},{6,7},{7,6},{8,9},{9,8},{10,11... | collective-permute-start | bytes 1572872 | tf_op jit(solution)/shard_map/ppermute | solution.py:43
  17.7 16.5 %all-to-all-start = ((bf16[32,4,1408]{2,1,0:T(4,128)(2,1)}), bf16[32,4,1408]{2,1,0:T(4,128)(2,1)S(1)}, u32[]{:S(2)}, u32[]{:S(2)}) async-start(bf16[32,4,1408]{2,1,0:T(4,128)(2,1)} %concatenate.91), calls=%async_computation | async-start | bytes 720896 | tf_op jit(solution)/shard_map/all_to_all | solution.py:491
  20.3 20.7 %collective-permute-start.3 = (bf16[128,2048]{1,0:T(8,128)(2,1)}, bf16[128,2048]{1,0:T(8,128)(2,1)}, u32[]{:S(2)}, u32[]{:S(2)}) collective-permute-start(bf16[128,2048]{1,0:T(8,128)(2,1)} %get-tuple-element.174), channel_id=1, source_target_pairs={{0,1},{1,0},{2,3},{3,2},{4,5},{5,4},{6,7},{7,6},{8,9},{9,8},{10,11... | collective-permute-start | bytes 1572872 | tf_op jit(solution)/shard_map/ppermute | solution.py:43
  31.2 14.0 %collective-permute-start.6 = (bf16[128,2048]{1,0:T(8,128)(2,1)}, bf16[128,2048]{1,0:T(8,128)(2,1)}, u32[]{:S(2)}, u32[]{:S(2)}) collective-permute-start(bf16[128,2048]{1,0:T(8,128)(2,1)} %get-tuple-element.174), channel_id=1, source_target_pairs={{0,4},{1,5},{2,6},{3,7},{4,0},{5,1},{6,2},{7,3},{8,12},{9,13},{10,... | collective-permute-start | bytes 1572872 | tf_op jit(solution)/shard_map/ppermute | solution.py:43
  32.7 12.5 %collective-permute-start.2 = (bf16[64,2560]{1,0:T(8,128)(2,1)}, bf16[64,2560]{1,0:T(8,128)(2,1)S(1)}, u32[]{:S(2)}, u32[]{:S(2)}) collective-permute-start(bf16[64,2560]{1,0:T(8,128)(2,1)} %collective-permute-done.1), channel_id=1, source_target_pairs={{0,8},{1,9},{2,10},{3,11},{4,12},{5,13},{6,14},{7,15},{8,0},{9,1},... | collective-permute-start | bytes 983048 | tf_op jit(solution)/shard_map/ppermute | solution.py:43
  41.0 65.2 %collective-permute-start.45 = (bf16[256,2048]{1,0:T(8,128)(2,1)}, bf16[256,2048]{1,0:T(8,128)(2,1)}, u32[]{:S(2)}, u32[]{:S(2)}) collective-permute-start(bf16[256,2048]{1,0:T(8,128)(2,1)} %bitcast.61), channel_id=1, source_target_pairs={{0,2},{1,3},{2,0},{3,1},{4,6},{5,7},{6,4},{7,5},{8,10},{9,11},{10,... | collective-permute-start | bytes 3145736 | tf_op jit(solution)/shard_map/ppermute | solution.py:43
  41.0 13.2 %collective-permute-start.22 = (bf16[64,2048]{1,0:T(8,128)(2,1)S(1)}, bf16[64,2048]{1,0:T(8,128)(2,1)S(1)}, u32[]{:S(2)}, u32[]{:S(2)}) collective-permute-start(bf16[64,2048]{1,0:T(8,128)(2,1)S(1)} %copy-done.67), channel_id=1, source_target_pairs={{0,8},{1,9},{2,10},{3,11},{4,12},{5,13},{6,14},{7,15},{8,0},{9,1},... | collective-permute-start | bytes 786440 | tf_op jit(solution)/shard_map/ppermute | solution.py:43
  41.5 15.0 %collective-permute-start.23 = (bf16[64,2048]{1,0:T(8,128)(2,1)S(1)}, bf16[64,2048]{1,0:T(8,128)(2,1)}, u32[]{:S(2)}, u32[]{:S(2)}) collective-permute-start(bf16[64,2048]{1,0:T(8,128)(2,1)S(1)} %copy-done.67), channel_id=1, source_target_pairs={{0,16},{1,17},{2,18},{3,19},{4,20},{5,21},{6,22},{7,23},{8,24},{9,... | collective-permute-start | bytes 786440 | tf_op jit(solution)/shard_map/ppermute | solution.py:43
  45.2 49.8 %collective-permute-start.43 = (bf16[128,2048]{1,0:T(8,128)(2,1)}, bf16[128,2048]{1,0:T(8,128)(2,1)}, u32[]{:S(2)}, u32[]{:S(2)}) collective-permute-start(bf16[128,2048]{1,0:T(8,128)(2,1)} %collective-permute-done.3), channel_id=1, source_target_pairs={{0,4},{1,5},{2,6},{3,7},{4,0},{5,1},{6,2},{7,3},{8,12},{9,13},{10,... | collective-permute-start | bytes 1572872 | tf_op jit(solution)/shard_map/ppermute | solution.py:43
  49.6 29.6 %collective-permute-start.10 = (bf16[4,64,1280]{2,1,0:T(8,128)(2,1)S(1)}, bf16[4,64,1280]{2,1,0:T(8,128)(2,1)S(1)}, u32[]{:S(2)}, u32[]{:S(2)}) collective-permute-start(bf16[4,64,1280]{2,1,0:T(8,128)(2,1)S(1)} %pad_maximum_fusion.4.refs_8_), channel_id=1, source_target_pairs={{0,4},{1,5},{2,6},{3,7},{4,0},{5,1},{6,2},{7,3},{8,12},{9,13},{10,... | collective-permute-start | bytes 1966088 | tf_op jit(solution)/shard_map/ppermute | solution.py:43
  54.2 27.6 %collective-permute-start.9 = (bf16[4,64,1280]{2,1,0:T(8,128)(2,1)S(1)}, bf16[4,64,1280]{2,1,0:T(8,128)(2,1)S(1)}, u32[]{:S(2)}, u32[]{:S(2)}) collective-permute-start(bf16[4,64,1280]{2,1,0:T(8,128)(2,1)S(1)} %pad_maximum_fusion.4.refs_8_), channel_id=1, source_target_pairs={{0,1},{1,0},{2,3},{3,2},{4,5},{5,4},{6,7},{7,6},{8,9},{9,8},{10,11... | collective-permute-start | bytes 1966088 | tf_op jit(solution)/shard_map/ppermute | solution.py:43
  56.5 13.7 %collective-permute-start.24 = (bf16[64,2048]{1,0:T(8,128)(2,1)}, bf16[64,2048]{1,0:T(8,128)(2,1)}, u32[]{:S(2)}, u32[]{:S(2)}) collective-permute-start(bf16[64,2048]{1,0:T(8,128)(2,1)} %collective-permute-done.23), channel_id=1, source_target_pairs={{0,8},{1,9},{2,10},{3,11},{4,12},{5,13},{6,14},{7,15},{8,0},{9,1},... | collective-permute-start | bytes 786440 | tf_op jit(solution)/shard_map/ppermute | solution.py:43
  58.3 62.5 %all-to-all-start.1 = ((bf16[32,16,640]{2,1,0:T(8,128)(2,1)}), bf16[32,16,640]{2,1,0:T(8,128)(2,1)}, u32[]{:S(2)}, u32[]{:S(2)}) async-start(bf16[32,16,640]{2,1,0:T(8,128)(2,1)} %broadcast_select_fusion), calls=%async_computation.1 | async-start | bytes 1310720 | tf_op jit(solution)/shard_map/all_to_all | solution.py:497
  70.2 22.8 %collective-permute-start.7 = (bf16[4,64,1280]{2,1,0:T(8,128)(2,1)S(1)}, bf16[4,64,1280]{2,1,0:T(8,128)(2,1)}, u32[]{:S(2)}, u32[]{:S(2)}) collective-permute-start(bf16[4,64,1280]{2,1,0:T(8,128)(2,1)S(1)} %pad_maximum_fusion.3.refs_0_), channel_id=1, source_target_pairs={{0,1},{1,0},{2,3},{3,2},{4,5},{5,4},{6,7},{7,6},{8,9},{9,8},{10,11... | collective-permute-start | bytes 1966088 | tf_op jit(solution)/shard_map/ppermute | solution.py:43
  79.1 14.3 %collective-permute-start.8 = (bf16[4,64,1280]{2,1,0:T(8,128)(2,1)S(1)}, bf16[4,64,1280]{2,1,0:T(8,128)(2,1)}, u32[]{:S(2)}, u32[]{:S(2)}) collective-permute-start(bf16[4,64,1280]{2,1,0:T(8,128)(2,1)S(1)} %pad_maximum_fusion.3.refs_0_), channel_id=1, source_target_pairs={{0,4},{1,5},{2,6},{3,7},{4,0},{5,1},{6,2},{7,3},{8,12},{9,13},{10,... | collective-permute-start | bytes 1966088 | tf_op jit(solution)/shard_map/ppermute | solution.py:43
  81.9 22.4 %collective-permute-start.44 = (bf16[128,2048]{1,0:T(8,128)(2,1)}, bf16[128,2048]{1,0:T(8,128)(2,1)}, u32[]{:S(2)}, u32[]{:S(2)}) collective-permute-start(bf16[128,2048]{1,0:T(8,128)(2,1)} %collective-permute-done.4), channel_id=1, source_target_pairs={{0,1},{1,0},{2,3},{3,2},{4,5},{5,4},{6,7},{7,6},{8,9},{9,8},{10,11... | collective-permute-start | bytes 1572872 | tf_op jit(solution)/shard_map/ppermute | solution.py:43
  93.0 24.8 %collective-permute-start.46 = (bf16[128,2048]{1,0:T(8,128)(2,1)}, bf16[128,2048]{1,0:T(8,128)(2,1)S(1)}, u32[]{:S(2)}, u32[]{:S(2)}) collective-permute-start(bf16[128,2048]{1,0:T(8,128)(2,1)} %collective-permute-done.3), channel_id=1, source_target_pairs={{0,2},{1,3},{2,0},{3,1},{4,6},{5,7},{6,4},{7,5},{8,10},{9,11},{10,... | collective-permute-start | bytes 1572872 | tf_op jit(solution)/shard_map/ppermute | solution.py:43
  93.4 17.0 %collective-permute-start.11 = (bf16[4,64,1280]{2,1,0:T(8,128)(2,1)}, bf16[4,64,1280]{2,1,0:T(8,128)(2,1)S(1)}, u32[]{:S(2)}, u32[]{:S(2)}) collective-permute-start(bf16[4,64,1280]{2,1,0:T(8,128)(2,1)} %collective-permute-done.7.refs_1_), channel_id=1, source_target_pairs={{0,4},{1,5},{2,6},{3,7},{4,0},{5,1},{6,2},{7,3},{8,12},{9,13},{10,... | collective-permute-start | bytes 1966088 | tf_op jit(solution)/shard_map/ppermute | solution.py:43
  94.9 22.0 %collective-permute-start.12 = (bf16[4,64,1280]{2,1,0:T(8,128)(2,1)S(1)}, bf16[4,64,1280]{2,1,0:T(8,128)(2,1)S(1)}, u32[]{:S(2)}, u32[]{:S(2)}) collective-permute-start(bf16[4,64,1280]{2,1,0:T(8,128)(2,1)S(1)} %collective-permute-done.10.refs_10_), channel_id=1, source_target_pairs={{0,1},{1,0},{2,3},{3,2},{4,5},{5,4},{6,7},{7,6},{8,9},{9,8},{10,11... | collective-permute-start | bytes 1966088 | tf_op jit(solution)/shard_map/ppermute | solution.py:43
  104.3 14.9 %collective-permute-start.47 = (bf16[128,2048]{1,0:T(8,128)(2,1)}, bf16[128,2048]{1,0:T(8,128)(2,1)S(1)}, u32[]{:S(2)}, u32[]{:S(2)}) collective-permute-start(bf16[128,2048]{1,0:T(8,128)(2,1)} %collective-permute-done.5), channel_id=1, source_target_pairs={{0,2},{1,3},{2,0},{3,1},{4,6},{5,7},{6,4},{7,5},{8,10},{9,11},{10,... | collective-permute-start | bytes 1572872 | tf_op jit(solution)/shard_map/ppermute | solution.py:43
  106.2 13.9 %collective-permute-start.48 = (bf16[128,2048]{1,0:T(8,128)(2,1)}, bf16[128,2048]{1,0:T(8,128)(2,1)S(1)}, u32[]{:S(2)}, u32[]{:S(2)}) collective-permute-start(bf16[128,2048]{1,0:T(8,128)(2,1)} %collective-permute-done.6), channel_id=1, source_target_pairs={{0,2},{1,3},{2,0},{3,1},{4,6},{5,7},{6,4},{7,5},{8,10},{9,11},{10,... | collective-permute-start | bytes 1572872 | tf_op jit(solution)/shard_map/ppermute | solution.py:43
  125.2 32.8 %collective-permute-start.27 = (bf16[4,64,1024]{2,1,0:T(8,128)(2,1)S(1)}, bf16[4,64,1024]{2,1,0:T(8,128)(2,1)S(1)}, u32[]{:S(2)}, u32[]{:S(2)}) collective-permute-start(bf16[4,64,1024]{2,1,0:T(8,128)(2,1)S(1)} %pad_maximum_fusion.8.refs_8_), channel_id=1, source_target_pairs={{0,1},{1,0},{2,3},{3,2},{4,5},{5,4},{6,7},{7,6},{8,9},{9,8},{10,11... | collective-permute-start | bytes 1572872 | tf_op jit(solution)/shard_map/ppermute | solution.py:43
  126.6 32.0 %collective-permute-start.28 = (bf16[4,64,1024]{2,1,0:T(8,128)(2,1)S(1)}, bf16[4,64,1024]{2,1,0:T(8,128)(2,1)}, u32[]{:S(2)}, u32[]{:S(2)}) collective-permute-start(bf16[4,64,1024]{2,1,0:T(8,128)(2,1)S(1)} %pad_maximum_fusion.8.refs_8_), channel_id=1, source_target_pairs={{0,4},{1,5},{2,6},{3,7},{4,0},{5,1},{6,2},{7,3},{8,12},{9,13},{10,... | collective-permute-start | bytes 1572872 | tf_op jit(solution)/shard_map/ppermute | solution.py:43
  127.1 31.5 %collective-permute-start.25 = (bf16[4,64,1024]{2,1,0:T(8,128)(2,1)S(1)}, bf16[4,64,1024]{2,1,0:T(8,128)(2,1)}, u32[]{:S(2)}, u32[]{:S(2)}) collective-permute-start(bf16[4,64,1024]{2,1,0:T(8,128)(2,1)S(1)} %pad_maximum_fusion.7.refs_0_), channel_id=1, source_target_pairs={{0,1},{1,0},{2,3},{3,2},{4,5},{5,4},{6,7},{7,6},{8,9},{9,8},{10,11... | collective-permute-start | bytes 1572872 | tf_op jit(solution)/shard_map/ppermute | solution.py:43
  128.0 30.6 %collective-permute-start.26 = (bf16[4,64,1024]{2,1,0:T(8,128)(2,1)S(1)}, bf16[4,64,1024]{2,1,0:T(8,128)(2,1)}, u32[]{:S(2)}, u32[]{:S(2)}) collective-permute-start(bf16[4,64,1024]{2,1,0:T(8,128)(2,1)S(1)} %pad_maximum_fusion.7.refs_0_), channel_id=1, source_target_pairs={{0,4},{1,5},{2,6},{3,7},{4,0},{5,1},{6,2},{7,3},{8,12},{9,13},{10,... | collective-permute-start | bytes 1572872 | tf_op jit(solution)/shard_map/ppermute | solution.py:43
  150.4 7.6 %collective-permute-start.21 = (bf16[256,512]{1,0:T(8,128)(2,1)S(1)}, bf16[256,512]{1,0:T(8,128)(2,1)S(1)}, u32[]{:S(2)}, u32[]{:S(2)}) collective-permute-start(bf16[256,512]{1,0:T(8,128)(2,1)S(1)} %pad_maximum_fusion.9), channel_id=1, source_target_pairs={{0,1},{1,0},{2,3},{3,2},{4,5},{5,4},{6,7},{7,6},{8,9},{9,8},{10,11... | collective-permute-start | bytes 786440 | tf_op jit(solution)/shard_map/ppermute | solution.py:43
  157.9 24.5 %collective-permute-start.49 = (bf16[128,2048]{1,0:T(8,128)(2,1)}, bf16[128,2048]{1,0:T(8,128)(2,1)}, u32[]{:S(2)}, u32[]{:S(2)}) collective-permute-start(bf16[128,2048]{1,0:T(8,128)(2,1)} %collective-permute-done.4), channel_id=1, source_target_pairs={{0,2},{1,3},{2,0},{3,1},{4,6},{5,7},{6,4},{7,5},{8,10},{9,11},{10,... | collective-permute-start | bytes 1572872 | tf_op jit(solution)/shard_map/ppermute | solution.py:43
  158.0 26.3 %collective-permute-start.50 = (bf16[128,2048]{1,0:T(8,128)(2,1)}, bf16[128,2048]{1,0:T(8,128)(2,1)}, u32[]{:S(2)}, u32[]{:S(2)}) collective-permute-start(bf16[128,2048]{1,0:T(8,128)(2,1)} %collective-permute-done.43), channel_id=1, source_target_pairs={{0,2},{1,3},{2,0},{3,1},{4,6},{5,7},{6,4},{7,5},{8,10},{9,11},{10,... | collective-permute-start | bytes 1572872 | tf_op jit(solution)/shard_map/ppermute | solution.py:43
  159.0 22.8 %collective-permute-start.29 = (bf16[4,64,1024]{2,1,0:T(8,128)(2,1)}, bf16[4,64,1024]{2,1,0:T(8,128)(2,1)S(1)}, u32[]{:S(2)}, u32[]{:S(2)}) collective-permute-start(bf16[4,64,1024]{2,1,0:T(8,128)(2,1)} %collective-permute-done.25.refs_1_), channel_id=1, source_target_pairs={{0,4},{1,5},{2,6},{3,7},{4,0},{5,1},{6,2},{7,3},{8,12},{9,13},{10,... | collective-permute-start | bytes 1572872 | tf_op jit(solution)/shard_map/ppermute | solution.py:43
  160.1 21.7 %collective-permute-start.30 = (bf16[4,64,1024]{2,1,0:T(8,128)(2,1)}, bf16[4,64,1024]{2,1,0:T(8,128)(2,1)S(1)}, u32[]{:S(2)}, u32[]{:S(2)}) collective-permute-start(bf16[4,64,1024]{2,1,0:T(8,128)(2,1)} %collective-permute-done.28.refs_10_), channel_id=1, source_target_pairs={{0,1},{1,0},{2,3},{3,2},{4,5},{5,4},{6,7},{7,6},{8,9},{9,8},{10,11... | collective-permute-start | bytes 1572872 | tf_op jit(solution)/shard_map/ppermute | solution.py:43
  192.6 100.5 %collective-permute-start.61 = (bf16[528,2176]{1,0:T(8,128)(2,1)S(1)}, bf16[528,2176]{1,0:T(8,128)(2,1)}, u32[]{:S(2)}, u32[]{:S(2)}) collective-permute-start(bf16[528,2176]{1,0:T(8,128)(2,1)S(1)} %bitcast.369), channel_id=1, source_target_pairs={{0,8},{1,9},{2,10},{3,11},{4,12},{5,13},{6,14},{7,15},{8,0},{9,1},... | collective-permute-start | bytes 6893576 | tf_op jit(solution)/shard_map/ppermute | solution.py:43
  192.7 103.2 %collective-permute-start.62 = (bf16[528,2176]{1,0:T(8,128)(2,1)S(1)}, bf16[528,2176]{1,0:T(8,128)(2,1)}, u32[]{:S(2)}, u32[]{:S(2)}) collective-permute-start(bf16[528,2176]{1,0:T(8,128)(2,1)S(1)} %bitcast.370), channel_id=1, source_target_pairs={{0,16},{1,17},{2,18},{3,19},{4,20},{5,21},{6,22},{7,23},{8,24},{9,... | collective-permute-start | bytes 6893576 | tf_op jit(solution)/shard_map/ppermute | solution.py:43
  195.1 18.9 %collective-permute-start.51 = (bf16[128,2048]{1,0:T(8,128)(2,1)}, bf16[128,2048]{1,0:T(8,128)(2,1)}, u32[]{:S(2)}, u32[]{:S(2)}) collective-permute-start(bf16[128,2048]{1,0:T(8,128)(2,1)} %collective-permute-done.44), channel_id=1, source_target_pairs={{0,2},{1,3},{2,0},{3,1},{4,6},{5,7},{6,4},{7,5},{8,10},{9,11},{10,... | collective-permute-start | bytes 1572872 | tf_op jit(solution)/shard_map/ppermute | solution.py:43
  212.0 84.9 %collective-permute-start.40 = (bf16[128,2176]{1,0:T(8,128)(2,1)S(1)}, bf16[128,2176]{1,0:T(8,128)(2,1)S(1)}, u32[]{:S(2)}, u32[]{:S(2)}) collective-permute-start(bf16[128,2176]{1,0:T(8,128)(2,1)S(1)} %get-tuple-element.171), channel_id=1, source_target_pairs={{0,4},{1,5},{2,6},{3,7},{4,0},{5,1},{6,2},{7,3},{8,12},{9,13},{10,... | collective-permute-start | bytes 1671176 | tf_op jit(solution)/shard_map/ppermute | solution.py:43
  213.0 84.0 %collective-permute-start.41 = (bf16[128,2176]{1,0:T(8,128)(2,1)S(1)}, bf16[128,2176]{1,0:T(8,128)(2,1)S(1)}, u32[]{:S(2)}, u32[]{:S(2)}) collective-permute-start(bf16[128,2176]{1,0:T(8,128)(2,1)S(1)} %get-tuple-element.171), channel_id=1, source_target_pairs={{0,1},{1,0},{2,3},{3,2},{4,5},{5,4},{6,7},{7,6},{8,9},{9,8},{10,11... | collective-permute-start | bytes 1671176 | tf_op jit(solution)/shard_map/ppermute | solution.py:43
  214.0 83.0 %collective-permute-start.39 = (bf16[128,2176]{1,0:T(8,128)(2,1)S(1)}, bf16[128,2176]{1,0:T(8,128)(2,1)S(1)}, u32[]{:S(2)}, u32[]{:S(2)}) collective-permute-start(bf16[128,2176]{1,0:T(8,128)(2,1)S(1)} %get-tuple-element.172), channel_id=1, source_target_pairs={{0,1},{1,0},{2,3},{3,2},{4,5},{5,4},{6,7},{7,6},{8,9},{9,8},{10,11... | collective-permute-start | bytes 1671176 | tf_op jit(solution)/shard_map/ppermute | solution.py:43
  293.1 13.8 %collective-permute-start.42 = (bf16[128,2176]{1,0:T(8,128)(2,1)S(1)}, bf16[128,2176]{1,0:T(8,128)(2,1)S(1)}, u32[]{:S(2)}, u32[]{:S(2)}) collective-permute-start(bf16[128,2176]{1,0:T(8,128)(2,1)S(1)} %get-tuple-element.172), channel_id=1, source_target_pairs={{0,4},{1,5},{2,6},{3,7},{4,0},{5,1},{6,2},{7,3},{8,12},{9,13},{10,... | collective-permute-start | bytes 1671176 | tf_op jit(solution)/shard_map/ppermute | solution.py:43
  295.9 58.7 %collective-permute-start.63 = (bf16[528,2176]{1,0:T(8,128)(2,1)}, bf16[528,2176]{1,0:T(8,128)(2,1)S(1)}, u32[]{:S(2)}, u32[]{:S(2)}) collective-permute-start(bf16[528,2176]{1,0:T(8,128)(2,1)} %collective-permute-done.62.refs_0_.refs_4_.refs_6_), channel_id=1, source_target_pairs={{0,8},{1,9},{2,10},{3,11},{4,12},{5,13},{6,14},{7,15},{8,0},{9,1},... | collective-permute-start | bytes 6893576 | tf_op jit(solution)/shard_map/ppermute | solution.py:43
  297.0 27.6 %collective-permute-start.54 = (bf16[256,2176]{1,0:T(8,128)(2,1)S(1)}, bf16[256,2176]{1,0:T(8,128)(2,1)S(1)}, u32[]{:S(2)}, u32[]{:S(2)}) collective-permute-start(bf16[256,2176]{1,0:T(8,128)(2,1)S(1)} %copy-done.31), channel_id=1, source_target_pairs={{0,2},{1,3},{2,0},{3,1},{4,6},{5,7},{6,4},{7,5},{8,10},{9,11},{10,... | collective-permute-start | bytes 3342344 | tf_op jit(solution)/shard_map/ppermute | solution.py:43
  306.9 12.8 %collective-permute-start.52 = (bf16[128,2176]{1,0:T(8,128)(2,1)S(1)}, bf16[128,2176]{1,0:T(8,128)(2,1)S(1)}, u32[]{:S(2)}, u32[]{:S(2)}) collective-permute-start(bf16[128,2176]{1,0:T(8,128)(2,1)S(1)} %collective-permute-done.39), channel_id=1, source_target_pairs={{0,4},{1,5},{2,6},{3,7},{4,0},{5,1},{6,2},{7,3},{8,12},{9,13},{10,... | collective-permute-start | bytes 1671176 | tf_op jit(solution)/shard_map/ppermute | solution.py:43
  307.7 18.4 %collective-permute-start.55 = (bf16[128,2176]{1,0:T(8,128)(2,1)S(1)}, bf16[128,2176]{1,0:T(8,128)(2,1)S(1)}, u32[]{:S(2)}, u32[]{:S(2)}) collective-permute-start(bf16[128,2176]{1,0:T(8,128)(2,1)S(1)} %collective-permute-done.39), channel_id=1, source_target_pairs={{0,2},{1,3},{2,0},{3,1},{4,6},{5,7},{6,4},{7,5},{8,10},{9,11},{10,... | collective-permute-start | bytes 1671176 | tf_op jit(solution)/shard_map/ppermute | solution.py:43
  308.6 15.0 %collective-permute-start.53 = (bf16[128,2176]{1,0:T(8,128)(2,1)S(1)}, bf16[128,2176]{1,0:T(8,128)(2,1)S(1)}, u32[]{:S(2)}, u32[]{:S(2)}) collective-permute-start(bf16[128,2176]{1,0:T(8,128)(2,1)S(1)} %collective-permute-done.40), channel_id=1, source_target_pairs={{0,1},{1,0},{2,3},{3,2},{4,5},{5,4},{6,7},{7,6},{8,9},{9,8},{10,11... | collective-permute-start | bytes 1671176 | tf_op jit(solution)/shard_map/ppermute | solution.py:43
  395.3 30.1 %collective-permute-start.64 = (bf16[4,256,2176]{2,1,0:T(8,128)(2,1)}, bf16[4,256,2176]{2,1,0:T(8,128)(2,1)}, u32[]{:S(2)}, u32[]{:S(2)}) collective-permute-start(bf16[4,256,2176]{2,1,0:T(8,128)(2,1)} %bitcast.63), channel_id=1, source_target_pairs={{0,2},{1,3},{2,0},{3,1},{4,6},{5,7},{6,4},{7,5},{8,10},{9,11},{10,... | collective-permute-start | bytes 13369352 | tf_op jit(solution)/shard_map/ppermute | solution.py:43
  410.1 19.3 %collective-permute-start.71 = (bf16[4,256,2304]{2,1,0:T(8,128)(2,1)}, bf16[4,256,2304]{2,1,0:T(8,128)(2,1)S(1)}, u32[]{:S(2)}, u32[]{:S(2)}) collective-permute-start(bf16[4,256,2304]{2,1,0:T(8,128)(2,1)} %bitcast.423), channel_id=1, source_target_pairs={{0,2},{1,3},{2,0},{3,1},{4,6},{5,7},{6,4},{7,5},{8,10},{9,11},{10,... | collective-permute-start | bytes 14155784 | tf_op jit(solution)/shard_map/ppermute | solution.py:43
  427.2 15.5 %collective-permute-start.66 = (bf16[128,2176]{1,0:T(8,128)(2,1)S(1)}, bf16[128,2176]{1,0:T(8,128)(2,1)S(1)}, u32[]{:S(2)}, u32[]{:S(2)}) collective-permute-start(bf16[128,2176]{1,0:T(8,128)(2,1)S(1)} %get-tuple-element.159), channel_id=1, source_target_pairs={{0,1},{1,0},{2,3},{3,2},{4,5},{5,4},{6,7},{7,6},{8,9},{9,8},{10,11... | collective-permute-start | bytes 1671176 | tf_op jit(solution)/shard_map/ppermute | solution.py:43
  428.3 40.5 %collective-permute-start.65 = (bf16[128,2176]{1,0:T(8,128)(2,1)S(1)}, bf16[128,2176]{1,0:T(8,128)(2,1)S(1)}, u32[]{:S(2)}, u32[]{:S(2)}) collective-permute-start(bf16[128,2176]{1,0:T(8,128)(2,1)S(1)} %get-tuple-element.158), channel_id=1, source_target_pairs={{0,1},{1,0},{2,3},{3,2},{4,5},{5,4},{6,7},{7,6},{8,9},{9,8},{10,11... | collective-permute-start | bytes 1671176 | tf_op jit(solution)/shard_map/ppermute | solution.py:43
  433.0 34.4 %collective-permute-start.73 = (bf16[128,2304]{1,0:T(8,128)(2,1)S(1)}, bf16[128,2304]{1,0:T(8,128)(2,1)S(1)}, u32[]{:S(2)}, u32[]{:S(2)}) collective-permute-start(bf16[128,2304]{1,0:T(8,128)(2,1)S(1)} %get-tuple-element.164), channel_id=1, source_target_pairs={{0,1},{1,0},{2,3},{3,2},{4,5},{5,4},{6,7},{7,6},{8,9},{9,8},{10,11... | collective-permute-start | bytes 1769480 | tf_op jit(solution)/shard_map/ppermute | solution.py:43
  434.1 45.1 %collective-permute-start.72 = (bf16[128,2304]{1,0:T(8,128)(2,1)S(1)}, bf16[128,2304]{1,0:T(8,128)(2,1)S(1)}, u32[]{:S(2)}, u32[]{:S(2)}) collective-permute-start(bf16[128,2304]{1,0:T(8,128)(2,1)S(1)} %get-tuple-element.163), channel_id=1, source_target_pairs={{0,1},{1,0},{2,3},{3,2},{4,5},{5,4},{6,7},{7,6},{8,9},{9,8},{10,11... | collective-permute-start | bytes 1769480 | tf_op jit(solution)/shard_map/ppermute | solution.py:43
  444.2 24.6 %collective-permute-start.67 = (bf16[128,2176]{1,0:T(8,128)(2,1)S(1)}, bf16[128,2176]{1,0:T(8,128)(2,1)S(1)}, u32[]{:S(2)}, u32[]{:S(2)}) collective-permute-start(bf16[128,2176]{1,0:T(8,128)(2,1)S(1)} %fusion.69), channel_id=1, source_target_pairs={{0,4},{1,5},{2,6},{3,7},{4,0},{5,1},{6,2},{7,3},{8,12},{9,13},{10,... | collective-permute-start | bytes 1671176 | tf_op jit(solution)/shard_map/ppermute | solution.py:43
  467.6 16.3 %collective-permute-start.74 = (bf16[128,2304]{1,0:T(8,128)(2,1)S(1)}, bf16[128,2304]{1,0:T(8,128)(2,1)S(1)}, u32[]{:S(2)}, u32[]{:S(2)}) collective-permute-start(bf16[128,2304]{1,0:T(8,128)(2,1)S(1)} %fusion.57), channel_id=1, source_target_pairs={{0,4},{1,5},{2,6},{3,7},{4,0},{5,1},{6,2},{7,3},{8,12},{9,13},{10,... | collective-permute-start | bytes 1769480 | tf_op jit(solution)/shard_map/ppermute | solution.py:43
  471.2 24.6 %collective-permute-start.69 = (bf16[128,2176]{1,0:T(8,128)(2,1)S(1)}, bf16[128,2176]{1,0:T(8,128)(2,1)S(1)}, u32[]{:S(2)}, u32[]{:S(2)}) collective-permute-start(bf16[128,2176]{1,0:T(8,128)(2,1)S(1)} %get-tuple-element.156), channel_id=1, source_target_pairs={{0,4},{1,5},{2,6},{3,7},{4,0},{5,1},{6,2},{7,3},{8,12},{9,13},{10,... | collective-permute-start | bytes 1671176 | tf_op jit(solution)/shard_map/ppermute | solution.py:43
  472.2 49.5 %collective-permute-start.68 = (bf16[128,2176]{1,0:T(8,128)(2,1)S(1)}, bf16[128,2176]{1,0:T(8,128)(2,1)S(1)}, u32[]{:S(2)}, u32[]{:S(2)}) collective-permute-start(bf16[128,2176]{1,0:T(8,128)(2,1)S(1)} %get-tuple-element.157), channel_id=1, source_target_pairs={{0,4},{1,5},{2,6},{3,7},{4,0},{5,1},{6,2},{7,3},{8,12},{9,13},{10,... | collective-permute-start | bytes 1671176 | tf_op jit(solution)/shard_map/ppermute | solution.py:43
  484.5 36.0 %collective-permute-start.76 = (bf16[128,2304]{1,0:T(8,128)(2,1)S(1)}, bf16[128,2304]{1,0:T(8,128)(2,1)S(1)}, u32[]{:S(2)}, u32[]{:S(2)}) collective-permute-start(bf16[128,2304]{1,0:T(8,128)(2,1)S(1)} %get-tuple-element.161), channel_id=1, source_target_pairs={{0,4},{1,5},{2,6},{3,7},{4,0},{5,1},{6,2},{7,3},{8,12},{9,13},{10,... | collective-permute-start | bytes 1769480 | tf_op jit(solution)/shard_map/ppermute | solution.py:43
  485.7 44.7 %collective-permute-start.75 = (bf16[128,2304]{1,0:T(8,128)(2,1)S(1)}, bf16[128,2304]{1,0:T(8,128)(2,1)S(1)}, u32[]{:S(2)}, u32[]{:S(2)}) collective-permute-start(bf16[128,2304]{1,0:T(8,128)(2,1)S(1)} %get-tuple-element.162), channel_id=1, source_target_pairs={{0,4},{1,5},{2,6},{3,7},{4,0},{5,1},{6,2},{7,3},{8,12},{9,13},{10,... | collective-permute-start | bytes 1769480 | tf_op jit(solution)/shard_map/ppermute | solution.py:43
  497.3 24.4 %collective-permute-start.70 = (bf16[128,2176]{1,0:T(8,128)(2,1)S(1)}, bf16[128,2176]{1,0:T(8,128)(2,1)S(1)}, u32[]{:S(2)}, u32[]{:S(2)}) collective-permute-start(bf16[128,2176]{1,0:T(8,128)(2,1)S(1)} %fusion.63), channel_id=1, source_target_pairs={{0,1},{1,0},{2,3},{3,2},{4,5},{5,4},{6,7},{7,6},{8,9},{9,8},{10,11... | collective-permute-start | bytes 1671176 | tf_op jit(solution)/shard_map/ppermute | solution.py:43
  520.7 10.1 %collective-permute-start.77 = (bf16[128,2304]{1,0:T(8,128)(2,1)S(1)}, bf16[128,2304]{1,0:T(8,128)(2,1)S(1)}, u32[]{:S(2)}, u32[]{:S(2)}) collective-permute-start(bf16[128,2304]{1,0:T(8,128)(2,1)S(1)} %fusion.51), channel_id=1, source_target_pairs={{0,1},{1,0},{2,3},{3,2},{4,5},{5,4},{6,7},{7,6},{8,9},{9,8},{10,11... | collective-permute-start | bytes 1769480 | tf_op jit(solution)/shard_map/ppermute | solution.py:43
  586.6 70.2 %all-to-all-start.2 = ((f32[32,16,640]{2,1,0:T(8,128)}), f32[32,16,640]{2,1,0:T(8,128)}, u32[]{:S(2)}, u32[]{:S(2)}) async-start(f32[32,16,640]{2,1,0:T(8,128)} %bitcast.382), calls=%async_computation.2 | async-start | bytes 2621440 | tf_op jit(solution)/shard_map/all_to_all | solution.py:673
  590.2 32.5 %collective-permute-start.80 = (f32[3,128,176]{2,1,0:T(8,128)S(1)}, f32[3,128,176]{2,1,0:T(8,128)S(1)}, u32[]{:S(2)}, u32[]{:S(2)}) collective-permute-start(f32[3,128,176]{2,1,0:T(8,128)S(1)} %slice.619), channel_id=1, source_target_pairs={{0,8},{1,9},{2,10},{3,11},{4,12},{5,13},{6,14},{7,15},{8,0},{9,1},... | collective-permute-start | bytes 811016 | tf_op jit(solution)/shard_map/ppermute | solution.py:43
  592.0 45.8 %collective-permute-start.79 = (f32[3,128,176]{2,1,0:T(8,128)S(1)}, f32[3,128,176]{2,1,0:T(8,128)S(1)}, u32[]{:S(2)}, u32[]{:S(2)}) collective-permute-start(f32[3,128,176]{2,1,0:T(8,128)S(1)} %slice.617), channel_id=1, source_target_pairs={{0,8},{1,9},{2,10},{3,11},{4,12},{5,13},{6,14},{7,15},{8,0},{9,1},... | collective-permute-start | bytes 811016 | tf_op jit(solution)/shard_map/ppermute | solution.py:43
  622.7 19.5 %collective-permute-start.81 = (f32[3,128,176]{2,1,0:T(8,128)S(1)}, f32[3,128,176]{2,1,0:T(8,128)S(1)}, u32[]{:S(2)}, u32[]{:S(2)}) collective-permute-start(f32[3,128,176]{2,1,0:T(8,128)S(1)} %slice_add_fusion.1), channel_id=1, source_target_pairs={{0,16},{1,17},{2,18},{3,19},{4,20},{5,21},{6,22},{7,23},{8,24},{9,... | collective-permute-start | bytes 811016 | tf_op jit(solution)/shard_map/ppermute | solution.py:43
  663.7 24.2 %all-to-all-start.3 = ((f32[32,4,1296]{2,1,0:T(4,128)}), f32[32,4,1296]{2,1,0:T(4,128)}, u32[]{:S(2)}, u32[]{:S(2)}) async-start(f32[32,4,1296]{2,1,0:T(4,128)} %concatenate.115), calls=%async_computation.3 | async-start | bytes 1441792 | tf_op jit(solution)/shard_map/all_to_all | solution.py:682
  (132 other events, 1242.6 us)

commit v2 on v1

v2 whole, which is shorter than its diff:
```python
import functools

import jax
import jax.numpy as jnp
from jax import lax
from jax.experimental import pallas as pl
from jax.experimental.pallas import tpu as pltpu
from jax.sharding import Mesh
from jax.sharding import PartitionSpec as P

HEADS = 32
KV_HEADS = 4
HEAD_DIM = 64
ADAPTERS = 8
RANK = 16
TABLE = ADAPTERS * RANK

EPS = 1e-05
THETA = 10000.0

ALL = ("outer", "pair", "seq")
X, C, Y = 1, 2, 4
BF = jnp.bfloat16
F32 = jnp.float32
HBM = lambda value: pltpu.with_memory_space_constraint(value, pltpu.HBM)
LIGHT = pl.CostEstimate(flops=1 << 20, bytes_accessed=1 << 16, transcendentals=0)


def dot(a, b, dims):
    return lax.dot_general(a, b, (dims, ((), ())), preferred_element_type=F32)


def nn(a, b):
    return dot(a, b, ((1,), (0,)))


def nt(a, b):
    return dot(a, b, ((1,), (1,)))


def tn(a, b):
    return dot(a, b, ((0,), (0,)))


def exchange(value, mask, n):
    return lax.ppermute(value, ALL, [(i, i ^ mask) for i in range(n)])


def rotary_tables(positions):
    half = HEAD_DIM // 2
    speeds = THETA ** (-jnp.arange(half, dtype=F32) * (2.0 / HEAD_DIM))
    angles = positions.astype(F32)[:, None] * speeds
    cosine, sine = jnp.cos(angles), jnp.sin(angles)
    return jnp.tile(cosine, (1, 4)), jnp.tile(jnp.concatenate([-sine, sine], 1), (1, 2))


def outer_bits(n):
    bits, bit = [], 8
    while bit < n:
        bits.append(bit)
        bit *= 2
    return bits


class Outer:
    def __init__(self, value, n):
        self.n = n
        self.held = {0: value}
        self.offsets = sorted(range(8, n, 8), key=lambda offset: (bin(offset).count("1"), -offset))

    def step(self):
        if not self.offsets:
            return False
        level = bin(self.offsets[0]).count("1")
        while self.offsets and bin(self.offsets[0]).count("1") == level:
            offset = self.offsets.pop(0)
            low = offset & -offset
            self.held[offset] = exchange(self.held[offset ^ low], low, self.n)
        return bool(self.offsets)

    def step_all(self):
        while self.step():
            pass

    def pass_through(self, order, *others):
        keys = sorted(self.held)
        passed = order.point(*[self.held[k] for k in keys], *others)
        self.held = dict(zip(keys, passed))
        return passed[len(keys) :]

    def parts(self):
        return [self.held[offset] for offset in sorted(self.held)]


def place_copies(me, pieces, held, sems):
    z, y, c, x = me // 8, (me // 4) % 2, (me // 2) % 2, me % 2
    copies = []
    for i, piece in enumerate(pieces):
        dc, kind = i // 5, i % 5
        dy, dx = ((0, 0), (0, 1), (1, 0), (1, 1), (1, 1))[kind]
        first = piece.shape[0] if kind == 4 else 0
        for j in range(piece.shape[0]):
            dz = first + j
            block = (((z ^ dz) * 2 + (y ^ dy)) * 2 + (c ^ dc)) * 2 + (x ^ dx)
            copies.append(
                pltpu.make_async_copy(piece.at[j], held.at[block], sems.at[len(copies)])
            )
    return copies


def normed_of(values, gain):
    scale = lax.rsqrt(jnp.mean(values * values, -1, keepdims=True) + EPS)
    return (values * scale * gain).astype(BF)


class Outer:
    def __init__(self, value, n):
        self.n = n
        self.held = {0: value}
        self.offsets = sorted(range(8, n, 8), key=lambda offset: (bin(offset).count("1"), -offset))

    def step(self):
        if not self.offsets:
            return False
        level = bin(self.offsets[0]).count("1")
        while self.offsets and bin(self.offsets[0]).count("1") == level:
            offset = self.offsets.pop(0)
            low = offset & -offset
            self.held[offset] = exchange(self.held[offset ^ low], low, self.n)
        return bool(self.offsets)

    def step_all(self):
        while self.step():
            pass

    def pass_through(self, order, *others):
        keys = sorted(self.held)
        passed = order.point(*[self.held[k] for k in keys], *others)
        self.held = dict(zip(keys, passed))
        return passed[len(keys) :]

    def parts(self):
        return [self.held[offset] for offset in sorted(self.held)]


def sum_outer(parts, n):
    held = {8 * i: part for i, part in enumerate(parts)}
    for bit in outer_bits(n):
        for offset in sorted(held):
            if offset & bit:
                held[offset ^ bit] = held[offset ^ bit] + exchange(held.pop(offset), bit, n)
    return held[0]


def place_kernel(count, outer, width, me_ref, *refs):
    pieces, out, held, sems, last = refs[:count], *refs[count:]
    me = me_ref[0]
    z, y, c, x = me // 8, (me // 4) % 2, (me // 2) % 2, me % 2
    copies = []
    for i in range(count):
        part, dc, dy, dx = i // 8, (i // 4) % 2, (i // 2) % 2, i % 2
        for dz in range(outer):
            block = (((z ^ dz) * 2 + (y ^ dy)) * 2 + (c ^ dc)) * 2 + (x ^ dx)
            copies.append(
                pltpu.make_async_copy(
                    pieces[i].at[dz],
                    held.at[block, :, pl.ds(part * width, width)],
                    sems.at[len(copies)],
                )
            )
    for copy in copies:
        copy.start()
    for copy in copies:
        copy.wait()
    copy = pltpu.make_async_copy(held, out, last)
    copy.start()
    copy.wait()


class Rows:
    def __init__(self, parts, n):
        self.n = n
        self.whole = jnp.stack(parts)

    def start_plane(self):
        self.near = [exchange(self.whole, bit, self.n) for bit in (X, Y, C)]

    def end_plane(self):
        from_x, from_y, _ = self.near
        half = from_x.shape[0] // 2
        self.last = [
            exchange(from_x[:half], Y, self.n),
            exchange(from_y[half:], X, self.n),
        ]
        self.far = [exchange(v, C, self.n) for v in (from_x, from_y)]

    def pieces(self):
        last_far = [exchange(v, C, self.n) for v in self.last]
        from_x, from_y, other = self.near
        return [self.whole, from_x, from_y, *self.last, other, *self.far, *last_far]


class Plane:
    def __init__(self, value, n):
        self.n = n
        self.own = value
        self.near = [exchange(value, X, n), exchange(value, Y, n), exchange(value, C, n)]

    def end(self):
        from_x, from_y, _ = self.near
        half = from_x.shape[0] // 2
        self.last = [exchange(from_x[:half], Y, self.n), exchange(from_y[half:], X, self.n)]
        self.far = [exchange(v, C, self.n) for v in (from_x, from_y)]

    def finish(self):
        self.last_far = [exchange(v, C, self.n) for v in self.last]

    def group(self, *which):
        parts = {0: [self.own, self.near[2]], 3: self.last + self.last_far}
        for g in (1, 2):
            parts[g] = [self.near[g - 1], self.far[g - 1]]
        return [part for g in which for part in parts[g]]


class Order:
    def __init__(self):
        self.token = jnp.zeros((), F32)

    def point(self, *values):
        *values, self.token = lax.optimization_barrier((*values, self.token))
        return values[0] if len(values) == 1 else values


def half_of(block, part):
    half = block.shape[0] // 2
    return block[part * half : (part + 1) * half].astype(F32)


class PlaneSum:
    def __init__(self, n):
        self.n = n
        self.mine, self.recv = {}, {}

    def put(self, block, near, recv):
        self.mine[block], self.recv[block] = near, recv

    def held(self, block, part):
        return half_of(self.mine[block], part) + half_of(self.recv[block], part)

    def far_sends(self):
        return self.held(3, 0).astype(BF), self.held(3, 1).astype(BF)

    def near_sends(self):
        return self.held(1, 0).astype(BF), self.held(2, 1).astype(BF)

    def last_sends(self, first, second):
        return (
            (self.held(2, 0) + first.astype(F32)).astype(BF),
            (self.held(1, 1) + second.astype(F32)).astype(BF),
        )

    def hop(self, first, second):
        return exchange(first, X, self.n), exchange(second, Y, self.n)

    def last_hop(self, first, second):
        return exchange(first, Y, self.n), exchange(second, X, self.n)

    def total(self, near, last):
        return jnp.concatenate(
            [self.held(0, i) + near[i].astype(F32) + last[i].astype(F32) for i in range(2)], 0
        )


def full(value):
    shape = value.shape
    return pl.BlockSpec(shape, lambda i: (0,) * len(shape), pipeline_mode=pl.Buffered(1))


def copies_of(pieces, target, stride, sems):
    copies, row = [], 0
    for i, piece in enumerate(pieces):
        size = piece.shape[0]
        copies.append(pltpu.make_async_copy(piece, target.at[pl.ds(row, size)], sems.at[i]))
        row += stride or size
    return copies


def clear_spare(target, used, slot):
    if slot > used:
        for row in range(0, target.shape[0], slot):
            target[pl.ds(row + used, slot - used), :] = jnp.zeros(
                (slot - used, target.shape[1]), target.dtype
            )


def lift_of(adapter):
    row = lax.broadcasted_iota(jnp.int32, (TABLE, 3 * TABLE), 0)
    col = lax.broadcasted_iota(jnp.int32, (TABLE, 3 * TABLE), 1)
    goal = (row // RANK) * TABLE + adapter * RANK + row % RANK
    return ((col == goal) & (row < 3 * RANK)).astype(F32).astype(BF)


def feed_copies(feed, kind, padded, slot, target, first, columns, sems):
    start, size, to = columns
    return [
        pltpu.make_async_copy(
            feed.at[pl.ds((3 * i + kind) * padded, padded), pl.ds(start, size)],
            target.at[pl.ds(first + i * slot, padded), pl.ds(to, size)],
            sems.at[i],
        )
        for i in range(sems.shape[0])
    ]


def feed_kernel(sizes, ids_ref, feed_ref, *refs):
    parts, padded, slot, width, place = sizes
    normed_in, cot_in, refs = refs[:parts], refs[parts : 2 * parts], refs[2 * parts :]
    hidden_ref, grads_ref, near_ref, far_ref, refs = *refs[:4], refs[4:]
    w_both, w_down, normed_all, cot_all, both_all, grad_all, acts, *sems = refs
    group = pl.program_id(0)
    block, cols = hidden_ref.shape
    half = block // 2
    wide = width + TABLE
    loads = [
        copies_of(normed_in, normed_all.at[:, pl.ds(0, wide)], None, sems[0]),
        feed_copies(feed_ref, 0, padded, slot, w_both, 0, (0, wide, 0), sems[1]),
        feed_copies(feed_ref, 1, padded, slot, w_both, cols, (0, width, 0), sems[2])
        + feed_copies(feed_ref, 1, padded, slot, w_both, cols, (width, TABLE, wide), sems[3]),
        copies_of(cot_in, cot_all.at[:, pl.ds(0, width)], None, sems[4]),
        feed_copies(feed_ref, 2, padded, slot, w_down, 0, (0, wide, 0), sems[5]),
    ]

    def arrive(*which):
        @pl.when(group == 0)
        def _():
            for i in which:
                for copy in loads[i]:
                    copy.wait()

    @pl.when(group == 0)
    def _():
        for load in loads:
            for copy in load:
                copy.start()
        grads_ref[...] = jnp.zeros_like(grads_ref)
        zeros = jnp.zeros((cols, TABLE), BF)
        w_both[pl.ds(0, cols), wide:] = zeros
        w_both[pl.ds(cols, cols), width:wide] = zeros
        clear_spare(w_both, padded, slot)
        clear_spare(w_down, padded, slot)

    row = pl.multiple_of(group * block, block)
    own = pl.ds(row, block)
    arrive(0)
    for i in range(2):
        here = pl.ds(row + i * half, half)
        lows = nn(normed_all[here, width:wide], lift_of(ids_ref[place + 2 * group + i])).astype(BF)
        normed_all[here, width:] = lows[:, : 2 * TABLE]
        cot_all[here, width:] = lows[:, 2 * TABLE :]
    arrive(1, 2)
    both_all[...] = nt(normed_all[own, :], w_both[...])
    arrive(3, 4)
    grad_all[...] = nt(cot_all[own, :], w_down[...])
    step = 16

    def rows_of(i, carry):
        here = pl.ds(pl.multiple_of(i * step, step), step)
        gate, up, grad = both_all[here, :cols], both_all[here, cols:], grad_all[here, :]
        sigmoid = 0.5 * jnp.tanh(0.5 * gate) + 0.5
        silu = gate * sigmoid
        hidden_ref[here, :] = (silu * up).astype(BF)
        acts[here, :cols] = (grad * up * (sigmoid + silu * (1.0 - sigmoid))).astype(BF)
        acts[here, cols:] = (grad * silu).astype(BF)
        return carry

    lax.fori_loop(0, block // step, rows_of, 0)
    out = nn(acts[...], w_both[...]).astype(BF)
    low = nn(hidden_ref[...], w_down[:, width:]).astype(BF)
    for i, ref in enumerate((near_ref, far_ref)):
        ref[:, : wide + TABLE] = out[i * half : (i + 1) * half]
        ref[:, wide + TABLE :] = low[i * half : (i + 1) * half]
    grads_ref[0] += tn(normed_all[own, width:wide], acts[:, :cols])
    grads_ref[1] += tn(normed_all[own, wide:], acts[:, cols:])
    grads_ref[2] += tn(cot_all[own, width:], hidden_ref[...])


def feed_stage(ids, place, groups, feed, normed, cot, padded, slot):
    wide, width = normed[0].shape[1], cot[0].shape[1]
    tokens = sum(part.shape[0] for part in normed)
    block = tokens // groups
    pieces = feed.shape[0] // (3 * padded)
    cols = pieces * slot
    tile = pl.BlockSpec((block, cols), lambda i: (i, 0))
    anywhere = pl.BlockSpec(memory_space=pl.ANY)
    out = jax.ShapeDtypeStruct((tokens // 2, wide + 2 * TABLE), BF)
    out_tile = pl.BlockSpec((block // 2, wide + 2 * TABLE), lambda i: (i, 0))
    counts = (len(normed),) + (pieces,) * 3 + (len(cot), pieces)
    return pl.pallas_call(
        functools.partial(feed_kernel, (len(normed), padded, slot, width, place)),
        grid=(groups,),
        out_shape=(
            jax.ShapeDtypeStruct((tokens, cols), BF),
            jax.ShapeDtypeStruct((3, TABLE, cols), F32),
            out,
            out,
        ),
        in_specs=[pl.BlockSpec(memory_space=pltpu.SMEM)]
        + [anywhere] * (1 + len(normed) + len(cot)),
        out_specs=(
            tile,
            pl.BlockSpec((3, TABLE, cols), lambda i: (0, 0, 0)),
            out_tile,
            out_tile,
        ),
        scratch_shapes=[
            pltpu.VMEM((2 * cols, wide + TABLE), BF),
            pltpu.VMEM((cols, wide), BF),
            pltpu.VMEM((tokens, wide + TABLE), BF),
            pltpu.VMEM((tokens, wide), BF),
            pltpu.VMEM((block, 2 * cols), F32),
            pltpu.VMEM((block, cols), F32),
            pltpu.VMEM((block, 2 * cols), BF),
        ]
        + [pltpu.SemaphoreType.DMA((count,)) for count in counts],
        compiler_params=pltpu.CompilerParams(vmem_limit_bytes=44 << 20),
        cost_estimate=LIGHT,
        name="feed",
    )(ids, HBM(feed), *map(HBM, normed), *map(HBM, cot))


def down_kernel(padded, slot, *refs):
    *acts, feed_ref, near_ref, far_ref, w_down, sems = refs
    loads = feed_copies(feed_ref, 2, padded, slot, w_down, 0, (0, w_down.shape[1], 0), sems)
    for copy in loads:
        copy.start()
    clear_spare(w_down, padded, slot)
    for copy in loads:
        copy.wait()
    rows = near_ref.shape[0] // 4
    done = 0
    for act in acts:
        for i in range(act.shape[0] // (2 * rows)):
            out = nn(act[pl.ds(i * 2 * rows, 2 * rows), :], w_down[...]).astype(BF)
            near_ref[pl.ds(done, rows), :] = out[:rows]
            far_ref[pl.ds(done, rows), :] = out[rows:]
            done += rows


def down_stage(hiddens, feed, pieces, padded, slot, rows):
    width = feed.shape[1] - TABLE
    out = jax.ShapeDtypeStruct((4 * rows, width), BF)
    return pl.pallas_call(
        functools.partial(down_kernel, padded, slot),
        grid=(1,),
        out_shape=(out, out),
        in_specs=[full(v) for v in hiddens] + [pl.BlockSpec(memory_space=pl.ANY)],
        out_specs=(full(out), full(out)),
        scratch_shapes=[
            pltpu.VMEM((pieces * slot, width), BF),
            pltpu.SemaphoreType.DMA((pieces,)),
        ],
        compiler_params=pltpu.CompilerParams(vmem_limit_bytes=32 << 20),
        cost_estimate=LIGHT,
        name="down",
    )(*map(HBM, hiddens), HBM(feed))


LANES = 2 * HEAD_DIM


def swap_halves(values):
    lane = lax.broadcasted_iota(jnp.int32, values.shape, 1) % HEAD_DIM
    half = HEAD_DIM // 2
    left = pltpu.roll(values, LANES - half, 1)
    return jnp.where(lane < half, left, pltpu.roll(values, half, 1))


def rope(slab, cosine, sine):
    return slab * cosine + swap_halves(slab) * sine


def project_kernel(
    me_ref, x_ref, gain_ref, a_ref, b_ref, cos_ref, sin_ref, *refs
):
    *pieces, normed_ref, low_ref, kv_ref, w_ref, held, sems, last = refs
    copies = place_copies(me_ref[0], pieces, held, sems)
    for copy in copies:
        copy.start()
    normed = normed_of(x_ref[...].astype(F32), gain_ref[...])
    normed_ref[...] = normed
    low = nt(normed, a_ref[...]).astype(BF)
    low_ref[...] = low
    for copy in copies:
        copy.wait()
    copy = pltpu.make_async_copy(held, w_ref, last)
    copy.start()
    width = kv_ref.shape[1]
    start = held.shape[2] - width
    weights = held[:, :, start:].reshape(normed.shape[1], width)
    kv = nn(normed, weights) + nn(low, b_ref[...])
    for i in range(width // LANES):
        cols = slice(i * LANES, (i + 1) * LANES)
        slab = kv[:, cols]
        if i < width // LANES // 2:
            slab = rope(slab, cos_ref[...], sin_ref[...])
        kv_ref[:, cols] = slab.astype(BF)
    copy.wait()


def project_stage(me, x, gain, a_att, b_kv, cosine, sine, pieces, n):
    rows, width = x.shape
    outer, shard, columns = pieces[0].shape
    anywhere = pl.BlockSpec(memory_space=pl.ANY)
    outs = (
        jax.ShapeDtypeStruct((rows, width), BF),
        jax.ShapeDtypeStruct((rows, a_att.shape[0]), BF),
        jax.ShapeDtypeStruct((rows, b_kv.shape[1]), BF),
    )
    operands = (x, gain, a_att, b_kv, cosine, sine)
    normed, low, kv, weights = pl.pallas_call(
        project_kernel,
        grid=(1,),
        out_shape=(*outs, jax.ShapeDtypeStruct((n, shard, columns), BF)),
        in_specs=[pl.BlockSpec(memory_space=pltpu.SMEM)]
        + [full(v) for v in operands]
        + [anywhere] * len(pieces),
        out_specs=(*[full(v) for v in outs], anywhere),
        scratch_shapes=[
            pltpu.VMEM((n, shard, columns), BF),
            pltpu.SemaphoreType.DMA((n,)),
            pltpu.SemaphoreType.DMA(()),
        ],
        compiler_params=pltpu.CompilerParams(vmem_limit_bytes=28 << 20),
        cost_estimate=LIGHT,
        name="project",
    )(me.reshape(1), *map(HBM, operands), *map(HBM, pieces))
    return normed, low, kv, weights.reshape(n * shard, columns)


def query_kernel(normed_ref, low_ref, b_ref, w_ref, cos_ref, sin_ref, out_ref):
    query = nn(normed_ref[...], w_ref[...]) + nn(low_ref[:, :RANK], b_ref[...])
    for i in range(out_ref.shape[1] // LANES):
        cols = slice(i * LANES, (i + 1) * LANES)
        slab = rope(query[:, cols], cos_ref[...], sin_ref[...]) * HEAD_DIM ** (-0.5)
        out_ref[:, cols] = slab.astype(BF)


def query_stage(normed, low, b_query, weights, cosine, sine):
    rows, width = normed.shape
    block = width // 4
    whole = lambda v: pl.BlockSpec(v.shape, lambda i: (0, 0))
    return pl.pallas_call(
        query_kernel,
        grid=(4,),
        out_shape=jax.ShapeDtypeStruct((rows, width), BF),
        in_specs=[
            whole(normed),
            whole(low),
            pl.BlockSpec((RANK, block), lambda i: (0, i)),
            pl.BlockSpec((width, block), lambda i: (0, i)),
            whole(cosine),
            whole(sine),
        ],
        out_specs=pl.BlockSpec((rows, block), lambda i: (0, i)),
        compiler_params=pltpu.CompilerParams(vmem_limit_bytes=24 << 20),
        cost_estimate=LIGHT,
        name="query",
    )(normed, low, b_query, HBM(weights), cosine, sine)


def output_kernel(me_ref, att_ref, a_ref, b_ref, x_ref, gain_ref, a_two_ref, e_ref, *refs):
    *pieces, middle_ref, normed_ref, low_ref, ext_ref, w_ref, held, sems, last = refs
    copies = place_copies(me_ref[0], pieces, held, sems)
    for copy in copies:
        copy.start()
    attended = att_ref[...]
    low = nt(attended, a_ref[...]).astype(BF)
    low_ref[...] = low
    for copy in copies:
        copy.wait()
    copy = pltpu.make_async_copy(held, w_ref, last)
    copy.start()
    rows, width = attended.shape
    weights = held[...].reshape(width, width)
    middle = x_ref[...].astype(F32) + nn(attended, weights) + nn(low, b_ref[...])
    middle_ref[...] = middle
    normed = normed_of(middle, gain_ref[...])
    normed_ref[...] = normed
    lows = nt(normed, a_two_ref[...]).astype(BF)
    spare = jnp.zeros((rows, TABLE - 3 * RANK), BF)
    lows = jnp.concatenate([lows, e_ref[...], spare], 1)
    ext_ref[:, :width] = normed
    ext_ref[:, width:] = lows
    copy.wait()


def output_stage(me, attended, a_out, b_out, x, gain, a_two, grad_low, pieces, n):
    rows, width = attended.shape
    outer, shard, columns = pieces[0].shape
    anywhere = pl.BlockSpec(memory_space=pl.ANY)
    outs = (
        jax.ShapeDtypeStruct((rows, width), F32),
        jax.ShapeDtypeStruct((rows, width), BF),
        jax.ShapeDtypeStruct((rows, RANK), BF),
        jax.ShapeDtypeStruct((rows, width + TABLE), BF),
    )
    operands = (attended, a_out, b_out, x, gain, a_two, grad_low)
    *results, weights = pl.pallas_call(
        output_kernel,
        grid=(1,),
        out_shape=(*outs, jax.ShapeDtypeStruct((n, shard, columns), BF)),
        in_specs=[pl.BlockSpec(memory_space=pltpu.SMEM)]
        + [full(v) for v in operands]
        + [anywhere] * len(pieces),
        out_specs=(*[full(v) for v in outs], anywhere),
        scratch_shapes=[
            pltpu.VMEM((n, shard, columns), BF),
            pltpu.SemaphoreType.DMA((n,)),
            pltpu.SemaphoreType.DMA(()),
        ],
        compiler_params=pltpu.CompilerParams(vmem_limit_bytes=32 << 20),
        cost_estimate=LIGHT,
        name="output",
    )(me.reshape(1), *map(HBM, operands), *map(HBM, pieces))
    return (*results, weights.reshape(n * shard, columns))


def back_kernel(grad_ref, w_ref, low_ref, a_ref, out_ref):
    out = nt(grad_ref[...], w_ref[...]) + nn(low_ref[...], a_ref[...])
    out_ref[...] = out.astype(out_ref.dtype)


def back_stage(grad, weights, low, table, dtype):
    rows, inner = grad.shape
    width = weights.shape[0]
    block = width // 4
    whole = lambda v: pl.BlockSpec(v.shape, lambda i: (0, 0))
    return pl.pallas_call(
        back_kernel,
        grid=(4,),
        out_shape=jax.ShapeDtypeStruct((rows, width), dtype),
        in_specs=[
            whole(grad),
            pl.BlockSpec((block, inner), lambda i: (i, 0)),
            whole(low),
            pl.BlockSpec((table.shape[0], block), lambda i: (0, i)),
        ],
        out_specs=pl.BlockSpec((rows, block), lambda i: (0, i)),
        compiler_params=pltpu.CompilerParams(vmem_limit_bytes=24 << 20),
        cost_estimate=LIGHT,
        name="back",
    )(*map(HBM, (grad, weights, low, table)))


def norm_two_kernel(adapter_ref, *refs):
    mine, recv, near, last, refs = refs[0], refs[1], refs[2:4], refs[4:6], refs[6:]
    middle_ref, gain_ref, cot_ref, att_ref, low_ref, normed_ref, a_ref, b_ref, refs = *refs[:8], refs[8:]
    grad_ref, one_ref, low_out_ref, low_down_ref, gain_grad_ref, tables_ref = refs
    width = middle_ref.shape[1]
    half = middle_ref.shape[0] // 2
    came = [
        near[i][...].astype(F32) + last[i][...].astype(F32) for i in range(2)
    ]
    total = mine[...].astype(F32) + recv[...].astype(F32) + jnp.concatenate(came, 0)
    lift = lift_of(adapter_ref[0])
    lows = [
        nt(total[:, width + i * TABLE : width + (i + 1) * TABLE].astype(BF), lift[:RANK, :TABLE])
        for i in range(3)
    ]
    low_down = lows[2].astype(BF)
    low_down_ref[...] = low_down
    grad_low = jnp.concatenate(lows[:2], 1).astype(BF)
    grad = total[:, :width] + nn(grad_low, a_ref[...])
    middle = middle_ref[...]
    scale = lax.rsqrt(jnp.mean(middle * middle, -1, keepdims=True) + EPS)
    gain_grad_ref[...] = jnp.sum(grad * middle * scale, 0, keepdims=True)
    grad = grad * gain_ref[...]
    inner = jnp.mean(grad * middle, -1, keepdims=True)
    grad = cot_ref[...].astype(F32) + scale * grad - middle * (scale * scale * scale * inner)
    grad_ref[...] = grad
    one = grad.astype(BF)
    one_ref[...] = one
    low_out = nt(one, b_ref[...]).astype(BF)
    low_out_ref[...] = low_out
    tables_ref[:, :width] = tn(low_out, att_ref[...]).astype(BF)
    tables_ref[:, width : 2 * width] = tn(low_ref[...], one).astype(BF)
    both = tn(grad_low, normed_ref[...]).astype(BF)
    tables_ref[:, 2 * width : 3 * width] = both[:RANK]
    tables_ref[:, 3 * width : 4 * width] = both[RANK:]
    tables_ref[:, 4 * width :] = tn(low_down, cot_ref[...]).astype(BF)


def norm_two_stage(adapter, parts, middle, gain, cot, attended, low_out, normed, a_two, b_out):
    rows, width = middle.shape
    operands = (*parts, middle, gain, cot, attended, low_out, normed, a_two, b_out)
    outs = (
        jax.ShapeDtypeStruct((rows, width), F32),
        jax.ShapeDtypeStruct((rows, width), BF),
        jax.ShapeDtypeStruct((rows, RANK), BF),
        jax.ShapeDtypeStruct((rows, RANK), BF),
        jax.ShapeDtypeStruct((1, width), F32),
        jax.ShapeDtypeStruct((RANK, 5 * width), BF),
    )
    return pl.pallas_call(
        norm_two_kernel,
        grid=(1,),
        out_shape=outs,
        in_specs=[pl.BlockSpec(memory_space=pltpu.SMEM)] + [full(v) for v in operands],
        out_specs=tuple(full(v) for v in outs),
        compiler_params=pltpu.CompilerParams(vmem_limit_bytes=40 << 20),
        cost_estimate=LIGHT,
        name="norm_two",
    )(adapter, *map(HBM, operands))


def project_back_kernel(
    query_ref, kv_ref, came_ref, cos_ref, sin_ref, bq_ref, bkv_ref, low_ref, normed_ref, *outs
):
    grad_ref, grad_low_ref, tables_ref = outs
    width = query_ref.shape[1]
    kv_width = kv_ref.shape[1] // 2
    query = query_ref[...]
    grad_ref[:, :width] = query
    kv = kv_ref[...] + came_ref[...].astype(F32)
    for i in range(kv_ref.shape[1] // LANES):
        slab = kv[:, i * LANES : (i + 1) * LANES]
        if i < kv_width // LANES:
            slab = slab * cos_ref[...] - swap_halves(slab) * sin_ref[...]
        grad_ref[:, width + i * LANES : width + (i + 1) * LANES] = slab.astype(BF)
    kv = grad_ref[:, width:]
    grad_low = nt(kv, bkv_ref[...])
    first = lax.broadcasted_iota(jnp.int32, grad_low.shape, 1) < RANK
    table = jnp.concatenate([bq_ref[...], jnp.zeros((2 * RANK, width), BF)], 0)
    grad_low = jnp.where(first, nt(query, table), grad_low).astype(BF)
    grad_low_ref[...] = grad_low
    reduced = tn(grad_low, normed_ref[...]).astype(BF)
    for i in range(3):
        tables_ref[:, i * width : (i + 1) * width] = reduced[i * RANK : (i + 1) * RANK]
    low = low_ref[...]
    tables_ref[:, 3 * width : 4 * width] = tn(low, query)[:RANK].astype(BF)
    raised = tn(low, kv).astype(BF)
    tables_ref[:, 4 * width : 4 * width + kv_width] = raised[RANK : 2 * RANK, :kv_width]
    tables_ref[:, 4 * width + kv_width :] = raised[2 * RANK :, kv_width:]


def project_back_stage(grad_query, grad_kv, came, cosine, sine, b_query, b_kv, low, normed):
    rows, width = grad_query.shape
    kv = grad_kv.shape[1]
    operands = (grad_query, grad_kv, came, cosine, sine, b_query, b_kv, low, normed)
    outs = (
        jax.ShapeDtypeStruct((rows, width + kv), BF),
        jax.ShapeDtypeStruct(low.shape, BF),
        jax.ShapeDtypeStruct((RANK, 4 * width + kv), BF),
    )
    return pl.pallas_call(
        project_back_kernel,
        grid=(1,),
        out_shape=outs,
        in_specs=[full(v) for v in operands],
        out_specs=tuple(full(v) for v in outs),
        compiler_params=pltpu.CompilerParams(vmem_limit_bytes=32 << 20),
        cost_estimate=LIGHT,
        name="project_back",
    )(*map(HBM, operands))


def norm_one_kernel(grad_ref, w_ref, low_ref, a_ref, x_ref, gain_ref, mid_ref, out_ref, gain_grad_ref, held):
    step = pl.program_id(0)
    block = w_ref.shape[0]
    cols = pl.ds(pl.multiple_of(step * block, block), block)
    held[:, cols] = nt(grad_ref[...], w_ref[...]) + nn(low_ref[...], a_ref[...])

    @pl.when(step == pl.num_programs(0) - 1)
    def _():
        values = x_ref[...].astype(F32)
        scale = lax.rsqrt(jnp.mean(values * values, -1, keepdims=True) + EPS)
        gain_grad_ref[...] = jnp.sum(held[...] * values * scale, 0, keepdims=True)
        grad = held[...] * gain_ref[...]
        inner = jnp.mean(grad * values, -1, keepdims=True)
        out_ref[...] = mid_ref[...] + scale * grad - values * (scale * scale * scale * inner)


def norm_one_stage(grad, weights, low, table, x, gain, grad_middle):
    rows, inner = grad.shape
    width = weights.shape[0]
    block = width // 4
    whole = lambda v: pl.BlockSpec(v.shape, lambda i: (0, 0))
    return pl.pallas_call(
        norm_one_kernel,
        grid=(4,),
        out_shape=(
            jax.ShapeDtypeStruct((rows, width), F32),
            jax.ShapeDtypeStruct((1, width), F32),
        ),
        in_specs=[
            whole(grad),
            pl.BlockSpec((block, inner), lambda i: (i, 0)),
            whole(low),
            pl.BlockSpec((table.shape[0], block), lambda i: (0, i)),
            whole(x),
            whole(gain),
            whole(grad_middle),
        ],
        out_specs=(whole(grad_middle), whole(gain)),
        scratch_shapes=[pltpu.VMEM((rows, width), F32)],
        compiler_params=pltpu.CompilerParams(vmem_limit_bytes=32 << 20),
        cost_estimate=LIGHT,
        name="norm_one",
    )(*map(HBM, (grad, weights, low, table, x, gain, grad_middle)))


def head_pair(own_ref, other_ref, start, group):
    cols = pl.ds(pl.multiple_of(start + (group // 2) * LANES, LANES), LANES)
    slab = jnp.concatenate([own_ref[:, cols], other_ref[:, cols]], 0).astype(F32)
    lane = lax.broadcasted_iota(jnp.int32, slab.shape, 1)
    slab = jnp.where(group % 2 == 0, slab, pltpu.roll(slab, HEAD_DIM, 1))
    first = jnp.where(lane < HEAD_DIM, slab, 0.0)
    return first, pltpu.roll(first, HEAD_DIM, 1)


def attend_kernel(pos_ref, query_ref, own_ref, other_ref, out_ref, probs_ref):
    group = pl.program_id(0)
    rows = query_ref.shape[0]
    keys = [k.astype(BF) for k in head_pair(own_ref, other_ref, 0, group)]
    values = head_pair(own_ref, other_ref, KV_HEADS * HEAD_DIM, group)
    values = [v.T.astype(BF) for v in values]
    key_at = lax.broadcasted_iota(jnp.int32, (2 * rows, rows), 0)
    query_at = lax.broadcasted_iota(jnp.int32, (2 * rows, rows), 1)
    before = (pos_ref[1] < pos_ref[0]).astype(jnp.int32)
    visible = (key_at <= query_at) | ((key_at >= rows) & (before > 0))
    for j in range(query_ref.shape[1] // LANES):
        cols = pl.ds(j * LANES, LANES)
        query = query_ref[:, cols].astype(F32).T.astype(BF)
        mixed = 0.0
        for h in range(2):
            scores = jnp.where(visible, nn(keys[h], query), -1e30)
            weights = jnp.exp(scores - jnp.max(scores, 0, keepdims=True))
            probs = (weights * (1.0 / jnp.sum(weights, 0, keepdims=True))).astype(BF)
            probs_ref[0, 2 * j + h] = probs
            mixed += nn(values[h], probs)
        out_ref[:, cols] = mixed.T.astype(BF)


def attend_stage(blocks, query, own, other):
    rows, width = query.shape
    cols = width // KV_HEADS
    heads = HEADS // KV_HEADS
    tile = pl.BlockSpec((rows, cols), lambda i: (0, i))
    whole = pl.BlockSpec(own.shape, lambda i: (0, 0))
    return pl.pallas_call(
        attend_kernel,
        grid=(KV_HEADS,),
        out_shape=(
            jax.ShapeDtypeStruct((rows, width), BF),
            jax.ShapeDtypeStruct((KV_HEADS, heads, 2 * rows, rows), BF),
        ),
        in_specs=[pl.BlockSpec(memory_space=pltpu.SMEM), tile, whole, whole],
        out_specs=(tile, pl.BlockSpec((1, heads, 2 * rows, rows), lambda i: (i, 0, 0, 0))),
        compiler_params=pltpu.CompilerParams(vmem_limit_bytes=32 << 20),
        cost_estimate=LIGHT,
        name="attend",
    )(blocks, query, own, other)


def attend_back_kernel(
    grad_ref,
    out_ref,
    query_ref,
    own_ref,
    other_ref,
    probs_ref,
    cos_ref,
    sin_ref,
    gq_ref,
    gown_ref,
    gother_ref,
    gkv_ref,
):
    group = pl.program_id(0)
    keys = [k.T.astype(BF) for k in head_pair(own_ref, other_ref, 0, group)]
    values = head_pair(own_ref, other_ref, KV_HEADS * HEAD_DIM, group)
    values = [v.astype(BF) for v in values]
    cosine, sine = cos_ref[...], sin_ref[...]
    grad_keys, grad_values = [0.0, 0.0], [0.0, 0.0]
    for j in range(query_ref.shape[1] // LANES):
        cols = pl.ds(j * LANES, LANES)
        grad = grad_ref[:, cols]
        query = query_ref[:, cols]
        turned = grad.astype(F32).T
        product = turned * out_ref[:, cols].astype(F32).T
        turned = turned.astype(BF)
        grad_query = 0.0
        for h in range(2):
            inner = jnp.sum(product[h * HEAD_DIM : (h + 1) * HEAD_DIM], 0, keepdims=True)
            probs = probs_ref[0, 2 * j + h]
            grad_scores = (probs.astype(F32) * (nn(values[h], turned) - inner)).astype(BF)
            grad_values[h] += nn(probs, grad)
            grad_keys[h] += nn(grad_scores, query)
            grad_query += nn(keys[h], grad_scores)
        grad_query = grad_query.T * HEAD_DIM ** (-0.5)
        grad_query = grad_query * cosine - swap_halves(grad_query) * sine
        gq_ref[:, cols] = grad_query.astype(BF)

    @pl.when(group == 0)
    def _():
        gkv_ref[...] = jnp.zeros_like(gkv_ref)

    lane = lax.broadcasted_iota(jnp.int32, grad_keys[0].shape, 1)
    for start, (first, last) in ((0, grad_keys), (KV_HEADS * HEAD_DIM, grad_values)):
        total = jnp.where(lane < HEAD_DIM, first + pltpu.roll(last, HEAD_DIM, 1), 0.0)
        total = jnp.where(group % 2 == 0, total, pltpu.roll(total, HEAD_DIM, 1))
        cols = pl.ds(pl.multiple_of(start + (group // 2) * LANES, LANES), LANES)
        gkv_ref[:, cols] += total

    @pl.when(group == pl.num_programs(0) - 1)
    def _():
        rows = gown_ref.shape[0]
        gown_ref[...] = gkv_ref[pl.ds(0, rows), :]
        gother_ref[...] = gkv_ref[pl.ds(rows, rows), :].astype(BF)


def attend_back_stage(grad, out, query, own, other, probs, cosine, sine):
    rows, width = query.shape
    cols = width // KV_HEADS
    tile = pl.BlockSpec((rows, cols), lambda i: (0, i))
    whole = pl.BlockSpec(own.shape, lambda i: (0, 0))
    table = pl.BlockSpec((rows, LANES), lambda i: (0, 0))
    return pl.pallas_call(
        attend_back_kernel,
        grid=(KV_HEADS,),
        out_shape=(
            jax.ShapeDtypeStruct((rows, width), BF),
            jax.ShapeDtypeStruct(own.shape, F32),
            jax.ShapeDtypeStruct(own.shape, BF),
        ),
        scratch_shapes=[pltpu.VMEM((2 * rows, own.shape[1]), F32)],
        in_specs=[tile, tile, tile, whole, whole]
        + [pl.BlockSpec((1,) + probs.shape[1:], lambda i: (i, 0, 0, 0)), table, table],
        out_specs=(tile, whole, whole),
        compiler_params=pltpu.CompilerParams(vmem_limit_bytes=32 << 20),
        cost_estimate=LIGHT,
        name="attend_back",
    )(grad, out, query, own, other, probs, cosine, sine)


def send_columns(parts, n):
    whole = jnp.concatenate(parts, 1).astype(BF)
    whole = jnp.pad(whole, ((0, 0), (0, -whole.shape[1] % n)))
    return jnp.moveaxis(whole.reshape(RANK, n, -1), 1, 0)


def sum_columns(parts, ids, own_rows):
    n, _, chunk = parts.shape
    onehot = (ids[:, None] == jnp.arange(ADAPTERS, dtype=jnp.int32)[None, :]).astype(BF)
    summed = jnp.einsum("na,nrc->arc", onehot, parts, preferred_element_type=F32)
    return summed.reshape(n, own_rows, chunk)


def per_device(
    n,
    inputs,
    cotangent,
    adapter_ids,
    block_index,
    gain_first,
    gain_second,
    w_query,
    w_key,
    w_value,
    w_output,
    w_gate_up,
    w_down,
    reduce_attention,
    raise_query,
    raise_keyvalue,
    reduce_output,
    raise_output,
    reduce_gate_up,
    raise_gate_up,
    reduce_down,
    raise_down,
):
    width = inputs.shape[-1]
    rows = inputs.shape[-2]
    shard = w_down.shape[0]
    own_rows = raise_down.shape[0]
    gains = gain_first.shape[0]
    kv_width = KV_HEADS * HEAD_DIM
    side = lax.axis_index("seq")
    me = lax.axis_index(ALL).astype(jnp.int32)
    tokens = inputs.reshape(rows, width)
    grad_out = cotangent.reshape(rows, width)

    order = Order()
    qkv_width = width + 2 * kv_width
    att_rows = Outer(jnp.concatenate([w_query, w_key, w_value, w_output], 1), n)
    att_rows.step()
    cot_plane = Plane(grad_out, n)
    padded = -(-shard // 16) * 16
    slot = -(-(n // 8) * padded // 256) * 256 // (n // 8)
    feed = jnp.stack([w_gate_up[0].T, w_gate_up[1].T, w_down])

    table_width = 10 * width
    chunk = table_width // n
    table = jnp.concatenate(
        [reduce_attention[0], reduce_attention[1], reduce_attention[2], raise_query]
        + [reduce_output, raise_output, reduce_gate_up[0], reduce_gate_up[1], raise_down]
        + [raise_keyvalue[0], raise_keyvalue[1]],
        1,
    )
    table = jnp.pad(table, ((0, 0), (0, table_width - table.shape[1])))
    table = jnp.moveaxis(table.reshape(own_rows, n, chunk), 1, 0)
    hidden_table = jnp.stack([raise_gate_up[0], raise_gate_up[1], reduce_down])
    hidden_table = hidden_table.reshape(3, own_rows, n, shard).transpose(2, 1, 0, 3)
    hidden_table = hidden_table.reshape(n, own_rows, 3 * shard)
    small = jnp.concatenate([gain_first, gain_second, adapter_ids.astype(BF)])
    used = chunk + 3 * shard
    sent = -(-(used + small.shape[0]) // 128) * 128
    small = jnp.pad(small, (0, sent - used - small.shape[0]))
    small = jnp.broadcast_to(small, (n, own_rows, small.shape[0]))
    table = jnp.concatenate([table, hidden_table, small], -1)
    came = lax.all_to_all(table, ALL, 0, 0, tiled=True)
    cot_plane.near = att_rows.pass_through(order, *cot_plane.near)
    att_rows.step_all()
    gain_one = came[:, 0, used : used + gains].reshape(width).astype(F32)
    gain_two = came[:, 0, used + gains : used + 2 * gains].reshape(width).astype(F32)
    ids = came[:, 0, used + 2 * gains].astype(jnp.int32)
    columns = came[:, :, :chunk].reshape(ADAPTERS, RANK, chunk)
    hidden_cols = came[:, :, chunk:used].reshape(TABLE, 3, shard)
    own = lax.all_to_all(jnp.take(columns, ids, axis=0), ALL, 0, 0, tiled=True)
    feed = jnp.concatenate([feed, hidden_cols.transpose(1, 2, 0)], 2)
    feed = jnp.pad(feed, ((0, 0), (0, padded - shard), (0, 0))).reshape(3 * padded, -1)
    (feed,) = att_rows.pass_through(order, feed)
    feed = lax.all_gather(feed, "outer", axis=0, tiled=True)
    qkv_rows = Rows([part[:, :qkv_width] for part in att_rows.parts()], n)
    qkv_rows.start_plane()
    qkv_rows.near = order.point(*qkv_rows.near)
    qkv_rows.end_plane()
    own = jnp.moveaxis(own, 0, 1).reshape(RANK, table_width)
    (a_query, a_key, a_value, b_query, a_out, b_out, a_gate, a_up, b_down) = [
        own[:, i * width : (i + 1) * width] for i in range(9)
    ]
    b_key = own[:, 9 * width : 9 * width + kv_width]
    b_value = own[:, 9 * width + kv_width : 9 * width + 2 * kv_width]

    own_block = lax.dynamic_index_in_dim(block_index[0], side, 0, keepdims=False)
    other_block = lax.dynamic_index_in_dim(block_index[0], 1 - side, 0, keepdims=False)
    blocks = jnp.stack([own_block, other_block])
    cosine, sine = rotary_tables(own_block * rows + jnp.arange(rows, dtype=jnp.int32))
    a_att = jnp.concatenate([a_query, a_key, a_value], 0)
    a_two = jnp.concatenate([a_gate, a_up], 0)
    b_kv = jnp.concatenate(
        [
            jnp.zeros((RANK, 2 * kv_width), BF),
            jnp.pad(b_key, ((0, 0), (0, kv_width))),
            jnp.pad(b_value, ((0, 0), (kv_width, 0))),
        ],
        0,
    )
    grad_low_down = nt(grad_out, b_down).astype(BF)
    plane_ids = jnp.stack([ids[me], ids[me ^ C], ids[me ^ Y], ids[me ^ (Y | C)]])
    *qkv_rows.last, a_att, a_two, b_kv, cosine, sine, grad_low_down, plane_ids = order.point(
        *qkv_rows.last, a_att, a_two, b_kv, cosine, sine, grad_low_down, plane_ids
    )
    normed_one, low_att, key_value, w_qkv = project_stage(
        me, tokens, gain_one[None], a_att, b_kv, cosine, sine, qkv_rows.pieces(), n
    )
    low_query, low_key, low_value = [low_att[:, i * RANK : (i + 1) * RANK] for i in range(3)]
    (key_value,) = att_rows.pass_through(order, key_value)
    other_kv = exchange(key_value, X, n)
    out_rows = Rows([part[:, qkv_width:] for part in att_rows.parts()], n)
    query = query_stage(normed_one, low_att, b_query, w_qkv, cosine, sine)
    key_value, other_kv, query, out_rows.whole = order.point(
        key_value, other_kv, query, out_rows.whole
    )
    out_rows.start_plane()
    attended, probs = attend_stage(blocks, query, key_value, other_kv)
    probs = HBM(probs)
    attended, *out_rows.near = order.point(attended, *out_rows.near)
    out_rows.end_plane()
    attended, *out_rows.last = order.point(attended, *out_rows.last)
    cot_plane.end()
    middle, normed_two, low_out, normed_ext, w_out = output_stage(
        me,
        attended,
        a_out,
        b_out,
        tokens,
        gain_two[None],
        a_two,
        grad_low_down,
        out_rows.pieces(),
        n,
    )

    normed_ext, *cot_plane.last = order.point(normed_ext, *cot_plane.last)
    cot_plane.finish()
    normed_plane = Plane(normed_ext, n)
    normed_plane.near = order.point(*normed_plane.near)
    normed_plane.end()
    passed = order.point(
        *normed_plane.last, *normed_plane.far, *cot_plane.far, *cot_plane.last_far
    )
    normed_plane.last, normed_plane.far = passed[:2], passed[2:4]
    cot_plane.far, cot_plane.last_far = passed[4:6], passed[6:]
    normed_plane.finish()
    feed_of = lambda ids_here, place, groups: feed_stage(
        ids_here,
        place,
        len(groups),
        feed,
        normed_plane.group(*groups),
        cot_plane.group(*groups),
        padded,
        slot,
    )
    hidden_far, grads_far, near_out, far_out = feed_of(plane_ids, 2, (3,))
    normed_sum = PlaneSum(n)
    normed_sum.put(3, near_out, exchange(far_out, C, n))
    ids_mid, near_out = order.point(plane_ids, near_out)
    hidden_mid, grads_mid, near_out, far_out = feed_of(ids_mid, 0, (1, 2))
    far_sends = normed_sum.far_sends()
    near_out, far_out, *far_sends = order.point(near_out, far_out, *far_sends)
    far_came = normed_sum.hop(*far_sends)
    mid_recv = exchange(far_out, C, n)
    for j in range(2):
        part = slice(j * rows, (j + 1) * rows)
        normed_sum.put(j + 1, near_out[part], mid_recv[part])
    ids_own, *near_sends = order.point(plane_ids, *normed_sum.near_sends())
    near_came = normed_sum.hop(*near_sends)
    hidden_own, grads_own, near_out, far_out = feed_of(ids_own, 0, (0,))
    recv = exchange(far_out, C, n)
    near_out, grads_own, *came = order.point(near_out, grads_own, *far_came, *near_came)
    far_came, near_came = came[:2], came[2:]
    hidden_grads = grads_own + grads_mid + grads_far
    hidden_grads = jnp.concatenate([hidden_grads[i] for i in range(3)], 1).astype(BF)
    hidden_grads = hidden_grads.reshape(n, own_rows, -1)
    last_sends = order.point(*normed_sum.last_sends(*far_came))
    last_came = normed_sum.last_hop(*last_sends)
    hidden_own, hidden_grads = order.point(hidden_own, hidden_grads)
    hidden_grads = lax.all_to_all(hidden_grads, ALL, 0, 0, tiled=True)
    down_near, down_far = down_stage(
        [hidden_own, hidden_mid, hidden_far], feed, n // 8, padded, slot, rows
    )
    parts = order.point(recv, *near_came, *last_came, down_far)
    down_far = parts[5]
    parts = (near_out, *parts[:5])

    grad_middle, grad_one, grad_low_out, low_down, gain_grad_two, early = norm_two_stage(
        adapter_ids, parts, middle, gain_two[None], grad_out, attended, low_out, normed_two, a_two, b_out
    )
    down_recv = exchange(down_far, C, n)
    grad_attended = back_stage(grad_one, w_out, grad_low_out, a_out, BF)
    down_sum = PlaneSum(n)
    for i in range(4):
        part = slice(i * rows, (i + 1) * rows)
        down_sum.put(i, down_near[part], down_recv[part])
    grad_query, grad_kv, kv_away = attend_back_stage(
        grad_attended, attended, query, key_value, other_kv, probs, cosine, sine
    )
    grad_query, grad_kv, kv_away, hidden_grads = order.point(
        grad_query, grad_kv, kv_away, hidden_grads
    )
    kv_came = exchange(kv_away, X, n)
    grad_qkv, grad_low_att, late = project_back_stage(
        grad_query, grad_kv, kv_came, cosine, sine, b_query, b_kv, low_att, normed_one
    )

    late, down_near = order.point(send_columns([late, early], n), down_near)
    late = lax.all_to_all(late, ALL, 0, 0, tiled=True)
    for i in range(4):
        down_sum.mine[i] = down_near[i * rows : (i + 1) * rows]
    grad_qkv, *sends = order.point(
        grad_qkv, *down_sum.far_sends(), *down_sum.near_sends()
    )
    down_far = down_sum.hop(*sends[:2])
    down_near = down_sum.hop(*sends[2:])
    input_grad, gain_grad_one = norm_one_stage(
        grad_qkv, w_qkv, grad_low_att, a_att, tokens, gain_one[None], grad_middle
    )
    input_grad = input_grad.reshape(inputs.shape)
    gain_grads = jnp.concatenate(
        [gain_grad_one.reshape(n, gains), gain_grad_two.reshape(n, gains)], 1
    )
    gain_grads = jnp.broadcast_to(gain_grads[:, None], (n, own_rows, 2 * gains))
    input_grad, gain_grads, *down_far = order.point(input_grad, gain_grads, *down_far)
    down_last = down_sum.last_hop(*down_sum.last_sends(*down_far))
    late = jnp.concatenate([sum_columns(late, ids, own_rows), gain_grads], -1)
    late, hidden_grads, down_sum.mine[0] = order.point(late, hidden_grads, down_sum.mine[0])
    late = lax.all_to_all(late, ALL, 0, 0, tiled=True)
    branch_two = down_sum.total(down_near, down_last)
    output = (middle + branch_two + nn(low_down, b_down)).astype(BF)
    hidden_grads = hidden_grads.reshape(n // 8, 8, own_rows, 3, n // 8, slot)
    hidden_grads = jnp.sum(hidden_grads[..., :shard].astype(F32), 0)
    hidden_grads = hidden_grads.transpose(2, 1, 3, 0, 4).reshape(3, own_rows, -1)
    gain_grads = jnp.sum(late[:, 0, -2 * gains :], 0) + order.token
    late_rows = jnp.moveaxis(late[:, :, : -2 * gains], 0, 1).reshape(own_rows, -1)
    parts = [late_rows[:, i * width : (i + 1) * width] for i in range(4)]
    kv = late_rows[:, 4 * width : 4 * width + 2 * kv_width]
    start = 4 * width + 2 * kv_width
    parts += [late_rows[:, start + i * width : start + (i + 1) * width] for i in range(5)]
    return (
        output.reshape(inputs.shape),
        input_grad,
        gain_grads[:gains],
        gain_grads[gains:],
        jnp.stack(parts[:3]),
        parts[3],
        jnp.stack([kv[:, :kv_width], kv[:, kv_width:]]),
        parts[4],
        parts[5],
        jnp.stack(parts[6:8]),
        hidden_grads[:2],
        hidden_grads[2],
        parts[8],
    )


def solution(mesh):
    dp, seq = mesh.shape["dp"], mesh.shape["seq"]
    n = dp * seq
    dp_axes = ALL[:2]
    rows = P(ALL, None)
    stacked = P(None, ALL, None)
    vector = P(ALL)
    blocks = P(dp_axes, "seq", None, None)
    return jax.shard_map(
        functools.partial(per_device, n),
        mesh=Mesh(mesh.devices.reshape(dp // 4, 4, seq), ALL),
        in_specs=(
            (blocks, blocks, P(dp_axes), P(dp_axes, None), vector, vector)
            + (rows, rows, rows, rows, P(None, None, ALL), rows)
            + (stacked, rows, stacked, rows, rows, stacked, stacked, rows, rows)
        ),
        out_specs=(
            (blocks, blocks, vector, vector, stacked, rows, stacked, rows, rows)
            + (stacked, stacked, rows, rows)
        ),
        check_vma=False,
    )
```

time: 705 us -> 514 us (0.73)
  waiting for transfers between devices: 285 us -> 153 us
  matrix products: 77.9 us -> 2.8 us
  Pallas kernels: 95.2 us -> 160 us
  other arithmetic: 55.3 us -> 29.7 us
  local copies, waits for them, and re-layouts: 98.4 us -> 76.5 us
  between operations: 5.18 us -> 16.8 us
  starting transfers between devices: 80.3 us -> 68.9 us
    ppermute x82 -> x57, waiting for transfers between devices: 270 us -> 125 us  [exchange(): return lax.ppermute(value, ALL, [(i, i ^ mask) for i in range(n)])]
    pallas_call x7 -> x13, Pallas kernels: 95.2 us -> 160 us  [the longest x3 69.4 us: feed_stage(): pl.pallas_call(functools.partial(feed_kernel, (len(normed), padded, slot,...]
    dot_general x34 -> x2, matrix products: 46.7 us -> 2.59 us  [dot(): return lax.dot_general(a, b, (dims, ((), ())), preferred_element_type=F32)]
    all_to_all x1, waiting for transfers between devices: 0.01 us -> 26.5 us  [per_device(): own = lax.all_to_all(jnp.take(columns, ids, axis=0), ALL, 0, 0, tiled=True)]
    dot_general x6 -> x1, matrix products: 21.5 us -> 0.21 us  [sum_columns(): jnp.einsum('na,nrc->arc', onehot, parts, preferred_element_type=F32)]
    convert_element_type x13 -> x6, other arithmetic: 28.1 us -> 9.32 us  [the longest x2 4.12 us: near_sends(): return (self.held(1, 0).astype(BF), self.held(2, 1).astype(BF))]
    ppermute x82 -> x57, starting transfers between devices: 65.6 us -> 48.4 us  [exchange(): return lax.ppermute(value, ALL, [(i, i ^ mask) for i in range(n)])]
    all_to_all x3 -> x4, waiting for transfers between devices: 14.3 us -> 1.44 us  [the longest x1 1.43 us: per_device(): came = lax.all_to_all(table, ALL, 0, 0, tiled=True)]
  transfers between devices with their start and end apart: 86 -> 63, of which waited for: 28 -> 26; matrix products, arithmetic and copies ran while one was open for 22% -> 14% of each run, Pallas kernels for 8% -> 28%
where the time goes in v2:
time: 514 us; the launch traced here: 508 us
  Pallas kernels  160 us (31%)
  waiting for transfers between devices  153 us (30%)
  local copies, waits for them, and re-layouts  76.5 us (15%)
  starting transfers between devices  68.9 us (13%)
  other arithmetic  29.7 us (6%)
  between operations  16.8 us (3%)
    ppermute x57, waiting for transfers between devices, exchange(): return lax.ppermute(value, ALL, [(i, i ^ mask) for i in range(n)])  125 us
    pallas_call x3, Pallas kernels, feed_stage(): pl.pallas_call(functools.partial(feed_kernel, (len(normed), padded, slot,...  69.4 us
    ppermute x57, starting transfers between devices, exchange(): return lax.ppermute(value, ALL, [(i, i ^ mask) for i in range(n)])  48.4 us
    unnamed x156, local copies, waits for them, and re-layouts  39.4 us
    all_to_all x1, waiting for transfers between devices, per_device(): own = lax.all_to_all(jnp.take(columns, ids, axis=0), ALL, 0, 0, tiled=True)  26.5 us
    pallas_call x1, Pallas kernels, attend_back_stage(): pl.pallas_call(attend_back_kernel, grid=(KV_HEADS,), out_shape=(jax.Shape...  14.6 us
    pallas_call x1, Pallas kernels, down_stage(): pl.pallas_call(functools.partial(down_kernel, padded, slot), grid=(1,), o...  12.3 us
    pallas_call x1, Pallas kernels, attend_stage(): pl.pallas_call(attend_kernel, grid=(KV_HEADS,), out_shape=(jax.ShapeDtype...  11.8 us
  transfers between devices with their start and end apart: 63, of which 26 were waited for; matrix products, arithmetic and copies ran while one was open for 14% of the time, Pallas kernels for 28%

profile of v2, /device:TPU:0, one launch (start us, length us, event | category | flops | bytes accessed | tf_op | source)
XLA Modules:
  0.0 508.1 jit_solution(3857460411758098629)
XLA Ops:
  7.3 3.0 collective-permute-start.2
  10.3 1.5 collective-permute-start.3
  11.8 1.7 constant_dynamic-update-slice_fusion.3
  16.2 1.7 constant_dynamic-update-slice_fusion
  17.9 1.6 collective-permute-start
  19.4 2.6 collective-permute-start.1
  28.2 2.6 all-to-all-start
  30.9 15.7 %collective-permute-done = bf16[64,4608]{1,0:T(8,128)(2,1)} collective-permute-done((bf16[64,4608]{1,0:T(8,128)(2,1)}, bf16[64,4608]{1,0:T(8,128)(2,1)}, u32[]{:S(2)}, u32[]{:S(2)}) %collective-permute-start) | collective-permute-done | bytes 589856 | tf_op jit(solution)/shard_map/ppermute | solution.py:46
  46.6 4.4 collective-permute-done.1
  57.0 1.6 pad_maximum_fusion
  58.6 8.1 %collective-permute-done.5 = bf16[64,4608]{1,0:T(8,128)(2,1)} collective-permute-done((bf16[64,4608]{1,0:T(8,128)(2,1)}, bf16[64,4608]{1,0:T(8,128)(2,1)}, u32[]{:S(2)}, u32[]{:S(2)}) %collective-permute-start.5) | collective-permute-done | bytes 589856 | tf_op jit(solution)/shard_map/ppermute | solution.py:46
  70.7 4.1 all-to-all-start.1
  77.6 1.9 collective-permute-start.6
  81.7 2.7 pad_add_fusion.1.ids_ref
  84.3 26.5 %all-to-all-done.1 = bf16[32,16,640]{2,1,0:T(8,128)(2,1)S(1)} async-done(((bf16[32,16,640]{2,1,0:T(8,128)(2,1)}), bf16[32,16,640]{2,1,0:T(8,128)(2,1)S(1)}, u32[]{:S(2)}, u32[]{:S(2)}) %all-to-all-start.1) | async-done | bytes 655392 | tf_op jit(solution)/shard_map/all_to_all | solution.py:1030
  117.6 1.7 collective-permute-start.10
  119.3 1.6 collective-permute-start.9
  123.0 11.5 %collective-permute-done.10.refs_4_ = bf16[2,64,2560]{2,1,0:T(8,128)(2,1)} collective-permute-done((bf16[2,64,2560]{2,1,0:T(8,128)(2,1)S(1)}, bf16[2,64,2560]{2,1,0:T(8,128)(2,1)}, u32[]{:S(2)}, u32[]{:S(2)}) %collective-permute-start.10) | collective-permute-done | bytes 655392 | tf_op jit(solution)/shard_map/ppermute | solution.py:46
  140.4 7.8 %project.1 = (bf16[256,2048]{1,0:T(8,128)(2,1)S(1)}, bf16[256,48]{1,0:T(8,128)(2,1)S(1)}, bf16[256,512]{1,0:T(8,128)(2,1)S(1)}, bf16[32,64,2560]{2,1,0:T(8,128)(2,1)S(1)}) custom-call(s32[1]{0:T(128)} %bitcast.me_ref, bf16[256,2048]{1,0:T(8,128)(2,1)} %bitcast.114, f32[1,2048]{1,0:T(1,128)} %reshape.231.gain_ref, bf16[48,2048]{1,0:T(8,128)(2,1)} %pad_maximum_fusion.6.a_ref, ...), custom_call_target="tpu_custom_call" | custom-call | flops 1048576 | bytes 65536 | tf_op jit(solution)/shard_map/project/pallas_call | solution.py:520
  148.2 4.0 copy-done
  156.6 6.5 %query.1.query_ref = bf16[256,2048]{1,0:T(8,128)(2,1)S(1)} custom-call(bf16[256,2048]{1,0:T(8,128)(2,1)S(1)} %get-tuple-element.192.normed_ref, bf16[256,48]{1,0:T(8,128)(2,1)S(1)} %get-tuple-element.193.low_ref, bf16[16,2048]{1,0:T(8,128)(2,1)S(1)} %get-tuple-element.347.b_ref.bq_ref, bf16[2048,2560]{1,0:T(8,128)(2,1)} %bitcast.111, ...), custom_call_target="tpu_custom_call" | custom-call | flops 1048576 | bytes 65536 | tf_op jit(solution)/shard_map/query/pallas_call | solution.py:552
  163.3 1.6 collective-permute-start.16
  164.9 1.6 collective-permute-start.17
  167.9 11.8 %attend.1 = (bf16[256,2048]{1,0:T(8,128)(2,1)S(1)}, bf16[4,8,512,256]{3,2,1,0:T(8,128)(2,1)S(1)}) custom-call(s32[2]{0:T(128)S(1)} %pad_add_fusion.pos_ref, bf16[256,2048]{1,0:T(8,128)(2,1)S(1)} %query.1.query_ref, bf16[256,512]{1,0:T(8,128)(2,1)S(1)} %get-tuple-element.201.own_ref, bf16[256,512]{1,0:T(8,128)(2,1)S(1)} %collective-permute-done.15.other_ref), custom_call_target="tpu_custom_call" | custom-call | flops 1048576 | bytes 65536 | tf_op jit(solution)/shard_map/attend/pallas_call | solution.py:850
  179.8 3.3 copy-done.3
  183.1 5.5 %collective-permute-done.16.refs_1_ = bf16[4,64,2048]{2,1,0:T(8,128)(2,1)S(1)} collective-permute-done((bf16[4,64,2048]{2,1,0:T(8,128)(2,1)S(1)}, bf16[4,64,2048]{2,1,0:T(8,128)(2,1)S(1)}, u32[]{:S(2)}, u32[]{:S(2)}) %collective-permute-start.16) | collective-permute-done | bytes 1048608 | tf_op jit(solution)/shard_map/ppermute | solution.py:46
  189.7 1.7 collective-permute-start.19
  193.8 8.4 %collective-permute-done.19.refs_3_ = bf16[2,64,2048]{2,1,0:T(8,128)(2,1)S(1)} collective-permute-done((bf16[2,64,2048]{2,1,0:T(8,128)(2,1)S(1)}, bf16[2,64,2048]{2,1,0:T(8,128)(2,1)S(1)}, u32[]{:S(2)}, u32[]{:S(2)}) %collective-permute-start.19) | collective-permute-done | bytes 524320 | tf_op jit(solution)/shard_map/ppermute | solution.py:46
  202.3 2.6 collective-permute-done.20.refs_4_
  210.6 10.0 %output.1 = (f32[256,2048]{1,0:T(8,128)S(1)}, bf16[256,2048]{1,0:T(8,128)(2,1)S(1)}, bf16[256,16]{1,0:T(8,128)(2,1)S(1)}, bf16[256,2176]{1,0:T(8,128)(2,1)S(1)}, bf16[32,64,2048]{2,1,0:T(8,128)(2,1)S(1)}) custom-call(s32[1]{0:T(128)} %bitcast.me_ref, bf16[256,2048]{1,0:T(8,128)(2,1)} %copy-done.1, bf16[16,2048]{1,0:T(8,128)(2,1)} %get-tuple-element.346.a_ref, ...), custom_call_target="tpu_custom_call" | custom-call | flops 1048576 | bytes 65536 | tf_op jit(solution)/shard_map/output/pallas_call | solution.py:608
  220.5 3.2 copy-done.4
  229.5 23.1 %collective-permute-done.27.refs_0_ = bf16[256,2176]{1,0:T(8,128)(2,1)S(1)} collective-permute-done((bf16[256,2176]{1,0:T(8,128)(2,1)S(1)}, bf16[256,2176]{1,0:T(8,128)(2,1)S(1)}, u32[]{:S(2)}, u32[]{:S(2)}) %collective-permute-start.27) | collective-permute-done | bytes 1114144 | tf_op jit(solution)/shard_map/ppermute | solution.py:46
  257.3 1.6 collective-permute-done.36.refs_6_
  259.0 2.0 collective-permute-done.37.refs_7_
  261.0 9.1 %collective-permute-done.30.refs_0_ = bf16[128,2176]{1,0:T(8,128)(2,1)S(1)} collective-permute-done((bf16[128,2176]{1,0:T(8,128)(2,1)S(1)}, bf16[128,2176]{1,0:T(8,128)(2,1)S(1)}, u32[]{:S(2)}, u32[]{:S(2)}) %collective-permute-start.30) | collective-permute-done | bytes 557088 | tf_op jit(solution)/shard_map/ppermute | solution.py:46
  275.4 18.1 %feed.3 = (bf16[512,768]{1,0:T(8,128)(2,1)S(1)}, f32[3,128,768]{2,1,0:T(8,128)S(1)}, bf16[256,2432]{1,0:T(8,128)(2,1)S(1)}, bf16[256,2432]{1,0:T(8,128)(2,1)S(1)}) custom-call(s32[4]{0:T(128)S(1)} %pad_add_fusion.1.ids_ref, bf16[2112,2176]{1,0:T(8,128)(2,1)} %all-gather.2.cloned.1.call-done.feed_ref.refs_3_, bf16[128,2176]{1,0:T(8,128)(2,1)} %copy-done.53, ...), custom_call_target="tpu_custom_call" | custom-call | flops 1048576 | bytes 65536 | tf_op jit(solution)/shard_map/feed/pallas_call | solution.py:398
  294.5 32.3 %feed.4 = (bf16[1024,768]{1,0:T(8,128)(2,1)S(1)}, f32[3,128,768]{2,1,0:T(8,128)S(1)}, bf16[512,2432]{1,0:T(8,128)(2,1)S(1)}, bf16[512,2432]{1,0:T(8,128)(2,1)S(1)}) custom-call(s32[4]{0:T(128)S(1)} %pad_add_fusion.1.ids_ref, bf16[2112,2176]{1,0:T(8,128)(2,1)} %all-gather.2.cloned.1.call-done.feed_ref.refs_3_, bf16[256,2176]{1,0:T(8,128)(2,1)} %copy-done.32, ...), custom_call_target="tpu_custom_call" | custom-call | flops 1048576 | bytes 65536 | tf_op jit(solution)/shard_map/feed/pallas_call | solution.py:398
  330.2 2.5 collective-permute-done.41
  334.9 19.0 %feed.5 = (bf16[512,768]{1,0:T(8,128)(2,1)S(1)}, f32[3,128,768]{2,1,0:T(8,128)S(1)}, bf16[256,2432]{1,0:T(8,128)(2,1)S(1)}, bf16[256,2432]{1,0:T(8,128)(2,1)}) custom-call(s32[4]{0:T(128)S(1)} %pad_add_fusion.1.ids_ref, bf16[2112,2176]{1,0:T(8,128)(2,1)} %all-gather.2.cloned.1.call-done.feed_ref.refs_3_, bf16[256,2176]{1,0:T(8,128)(2,1)} %copy-done.15, ...), custom_call_target="tpu_custom_call" | custom-call | flops 1048576 | bytes 65536 | tf_op jit(solution)/shard_map/feed/pallas_call | solution.py:398
  354.0 3.7 collective-permute-done.44.refs_2_
  358.4 1.5 add_convert_fusion
  363.9 1.7 concatenate.61
  366.3 2.1 pad_maximum_fusion.4
  368.4 12.3 %down.1 = (bf16[1024,2048]{1,0:T(8,128)(2,1)S(1)}, bf16[1024,2048]{1,0:T(8,128)(2,1)}) custom-call(bf16[512,768]{1,0:T(8,128)(2,1)} %copy-done.20, bf16[1024,768]{1,0:T(8,128)(2,1)} %copy-done.12, bf16[512,768]{1,0:T(8,128)(2,1)} %copy-done.19, bf16[2112,2176]{1,0:T(8,128)(2,1)} %all-gather.2.cloned.1.call-done.feed_ref.refs_3_), custom_call_target="tpu_custom_call" | custom-call | flops 1048576 | bytes 65536 | tf_op jit(solution)/shard_map/down/pallas_call | solution.py:452
  380.7 2.0 copy-done.8
  383.8 4.1 all-to-all-start.2
  387.8 7.1 %norm_two.1 = (f32[256,2048]{1,0:T(8,128)S(1)}, bf16[256,2048]{1,0:T(8,128)(2,1)S(1)}, bf16[256,16]{1,0:T(8,128)(2,1)S(1)}, bf16[256,16]{1,0:T(8,128)(2,1)S(1)},...) custom-call(s32[1]{0:T(128)S(6)} %copy.156.adapter_ref, bf16[256,2432]{1,0:T(8,128)(2,1)} %copy-done.14, ...), custom_call_target="tpu_custom_call" | custom-call | flops 1048576 | bytes 65536 | tf_op jit(solution)/shard_map/norm_two/pallas_call | solution.py:704
  396.6 6.8 %back.1.grad_ref = bf16[256,2048]{1,0:T(8,128)(2,1)S(1)} custom-call(bf16[256,2048]{1,0:T(8,128)(2,1)} %copy-done.18, bf16[2048,2048]{1,0:T(8,128)(2,1)} %bitcast.113, bf16[256,16]{1,0:T(8,128)(2,1)} %copy-done.26, bf16[16,2048]{1,0:T(8,128)(2,1)} %get-tuple-element.346.a_ref), custom_call_target="tpu_custom_call" | custom-call | flops 1048576 | bytes 65536 | tf_op jit(solution)/shard_map/back/pallas_call | solution.py:638
  403.3 14.6 %attend_back.1 = (bf16[256,2048]{1,0:T(8,128)(2,1)S(1)}, f32[256,512]{1,0:T(8,128)S(1)}, bf16[256,512]{1,0:T(8,128)(2,1)S(1)}) custom-call(bf16[256,2048]{1,0:T(8,128)(2,1)S(1)} %back.1.grad_ref, bf16[256,2048]{1,0:T(8,128)(2,1)S(1)} %copy-done.2, bf16[256,2048]{1,0:T(8,128)(2,1)S(1)} %query.1.query_ref, bf16[256,512]{1,0:T(8,128)(2,1)S(1)} %get-tuple-element.201.own_ref, ...), custom_call_target="tpu_custom_call" | custom-call | flops 1048576 | bytes 65536 | tf_op jit(solution)/shard_map/attend_back/pallas_call | solution.py:928
  419.7 1.9 collective-permute-start.49
  421.6 6.7 %collective-permute-done.49.came_ref = bf16[256,512]{1,0:T(8,128)(2,1)S(1)} collective-permute-done((bf16[256,512]{1,0:T(8,128)(2,1)S(1)}, bf16[256,512]{1,0:T(8,128)(2,1)S(1)}, u32[]{:S(2)}, u32[]{:S(2)}) %collective-permute-start.49) | collective-permute-done | bytes 262176 | tf_op jit(solution)/shard_map/ppermute | solution.py:46
  429.0 3.2 project_back.1
  436.2 5.9 %all-to-all-start.3 = ((bf16[32,16,592]{2,1,0:T(8,128)(2,1)}), bf16[32,16,592]{2,1,0:T(8,128)(2,1)S(1)}, u32[]{:S(2)}, u32[]{:S(2)}) async-start(bf16[32,16,592]{2,1,0:T(8,128)(2,1)} %bitcast.108), calls=%async_computation.3 | async-start | bytes 1310720 | tf_op jit(solution)/shard_map/all_to_all | solution.py:1170
  442.1 3.8 add_convert_fusion.9
  445.9 1.9 collective-permute-start.51
  447.8 1.5 collective-permute-start.52
  451.8 10.7 %norm_one.1 = (f32[256,2048]{1,0:T(8,128)}, f32[1,2048]{1,0:T(1,128)S(1)}) custom-call(bf16[256,2560]{1,0:T(8,128)(2,1)} %copy-done.13, bf16[2048,2560]{1,0:T(8,128)(2,1)} %bitcast.112, bf16[256,48]{1,0:T(8,128)(2,1)} %copy-done.25, bf16[48,2048]{1,0:T(8,128)(2,1)} %pad_maximum_fusion.6.a_ref, bf16[256,2048]{1,0:T(8,128)(2,1)} %bitcast.116, ...), custom_call_target="tpu_custom_call" | custom-call | flops 1048576 | bytes 65536 | tf_op jit(solution)/shard_map/norm_one/pallas_call | solution.py:788
  464.3 3.4 add_convert_fusion.8
  467.7 1.7 collective-permute-start.54
  469.4 1.5 collective-permute-start.56
  473.3 3.7 all-to-all-start.4
  479.0 13.5 %collective-permute-done.54 = bf16[128,2048]{1,0:T(8,128)(2,1)} collective-permute-done((bf16[128,2048]{1,0:T(8,128)(2,1)}, bf16[128,2048]{1,0:T(8,128)(2,1)}, u32[]{:S(2)}, u32[]{:S(2)}) %collective-permute-start.54) | collective-permute-done | bytes 524320 | tf_op jit(solution)/shard_map/ppermute | solution.py:46
  492.5 2.6 convert_add_fusion.1
  495.1 2.2 fusion.2
  (346 shorter events, 101.0 us)
Async XLA Ops:
  7.3 43.7 %collective-permute-start.2 = (bf16[256,2048]{1,0:T(8,128)(2,1)}, bf16[256,2048]{1,0:T(8,128)(2,1)S(1)}, u32[]{:S(2)}, u32[]{:S(2)}) collective-permute-start(bf16[256,2048]{1,0:T(8,128)(2,1)} %bitcast.117), channel_id=1, source_target_pairs={{0,1},{1,0},{2,3},{3,2},{4,5},{5,4},{6,7},{7,6},{8,9},{9,8},{10,11... | collective-permute-start | bytes 3145736 | tf_op jit(solution)/shard_map/ppermute | solution.py:46
  10.3 40.7 %collective-permute-start.3 = (bf16[256,2048]{1,0:T(8,128)(2,1)}, bf16[256,2048]{1,0:T(8,128)(2,1)S(1)}, u32[]{:S(2)}, u32[]{:S(2)}) collective-permute-start(bf16[256,2048]{1,0:T(8,128)(2,1)} %bitcast.118), channel_id=1, source_target_pairs={{0,4},{1,5},{2,6},{3,7},{4,0},{5,1},{6,2},{7,3},{8,12},{9,13},{10,... | collective-permute-start | bytes 3145736 | tf_op jit(solution)/shard_map/ppermute | solution.py:46
  11.8 39.2 %collective-permute-start.4 = (bf16[256,2048]{1,0:T(8,128)(2,1)}, bf16[256,2048]{1,0:T(8,128)(2,1)}, u32[]{:S(2)}, u32[]{:S(2)}) collective-permute-start(bf16[256,2048]{1,0:T(8,128)(2,1)} %bitcast.119), channel_id=1, source_target_pairs={{0,2},{1,3},{2,0},{3,1},{4,6},{5,7},{6,4},{7,5},{8,10},{9,11},{10,... | collective-permute-start | bytes 3145736 | tf_op jit(solution)/shard_map/ppermute | solution.py:46
  17.9 28.7 %collective-permute-start = (bf16[64,4608]{1,0:T(8,128)(2,1)}, bf16[64,4608]{1,0:T(8,128)(2,1)}, u32[]{:S(2)}, u32[]{:S(2)}) collective-permute-start(bf16[64,4608]{1,0:T(8,128)(2,1)} %constant_dynamic-update-slice_fusion), channel_id=1, source_target_pairs={{0,8},{1,9},{2,10},{3,11},{4,12},{5,13},{6,14},{7,15},{8,0},{9,1},... | collective-permute-start | bytes 1769480 | tf_op jit(solution)/shard_map/ppermute | solution.py:46
  19.4 31.5 %collective-permute-start.1 = (bf16[64,4608]{1,0:T(8,128)(2,1)}, bf16[64,4608]{1,0:T(8,128)(2,1)}, u32[]{:S(2)}, u32[]{:S(2)}) collective-permute-start(bf16[64,4608]{1,0:T(8,128)(2,1)} %constant_dynamic-update-slice_fusion), channel_id=1, source_target_pairs={{0,16},{1,17},{2,18},{3,19},{4,20},{5,21},{6,22},{7,23},{8,24},{9,... | collective-permute-start | bytes 1769480 | tf_op jit(solution)/shard_map/ppermute | solution.py:46
  28.2 28.3 %all-to-all-start = ((bf16[32,4,1408]{2,1,0:T(4,128)(2,1)}), bf16[32,4,1408]{2,1,0:T(4,128)(2,1)S(1)}, u32[]{:S(2)}, u32[]{:S(2)}) async-start(bf16[32,4,1408]{2,1,0:T(4,128)(2,1)} %copy.117), calls=%async_computation | async-start | bytes 720896 | tf_op jit(solution)/shard_map/all_to_all | solution.py:1022
  30.8 244.5 %all-gather.2.cloned.1.call-start = ((), (), s32[]{:S(2)}) async-start(), calls=%async_computation.5 | async-start | bytes 11489280 | tf_op jit(solution)/shard_map/all_gather | solution.py:1034
  52.4 14.3 %collective-permute-start.5 = (bf16[64,4608]{1,0:T(8,128)(2,1)}, bf16[64,4608]{1,0:T(8,128)(2,1)}, u32[]{:S(2)}, u32[]{:S(2)}) collective-permute-start(bf16[64,4608]{1,0:T(8,128)(2,1)} %collective-permute-done.1), channel_id=1, source_target_pairs={{0,8},{1,9},{2,10},{3,11},{4,12},{5,13},{6,14},{7,15},{8,0},{9,1},... | collective-permute-start | bytes 1769480 | tf_op jit(solution)/shard_map/ppermute | solution.py:46
  70.7 40.1 %all-to-all-start.1 = ((bf16[32,16,640]{2,1,0:T(8,128)(2,1)}), bf16[32,16,640]{2,1,0:T(8,128)(2,1)S(1)}, u32[]{:S(2)}, u32[]{:S(2)}) async-start(bf16[32,16,640]{2,1,0:T(8,128)(2,1)} %broadcast_select_fusion), calls=%async_computation.1 | async-start | bytes 1310720 | tf_op jit(solution)/shard_map/all_to_all | solution.py:1030
  77.6 37.1 %collective-permute-start.6 = (bf16[4,64,2560]{2,1,0:T(8,128)(2,1)S(1)}, bf16[4,64,2560]{2,1,0:T(8,128)(2,1)}, u32[]{:S(2)}, u32[]{:S(2)}) collective-permute-start(bf16[4,64,2560]{2,1,0:T(8,128)(2,1)S(1)} %pad_maximum_fusion.1.refs_0_), channel_id=1, source_target_pairs={{0,1},{1,0},{2,3},{3,2},{4,5},{5,4},{6,7},{7,6},{8,9},{9,8},{10,11... | collective-permute-start | bytes 3932168 | tf_op jit(solution)/shard_map/ppermute | solution.py:46
  79.5 35.2 %collective-permute-start.7 = (bf16[4,64,2560]{2,1,0:T(8,128)(2,1)S(1)}, bf16[4,64,2560]{2,1,0:T(8,128)(2,1)}, u32[]{:S(2)}, u32[]{:S(2)}) collective-permute-start(bf16[4,64,2560]{2,1,0:T(8,128)(2,1)S(1)} %pad_maximum_fusion.1.refs_0_), channel_id=1, source_target_pairs={{0,4},{1,5},{2,6},{3,7},{4,0},{5,1},{6,2},{7,3},{8,12},{9,13},{10,... | collective-permute-start | bytes 3932168 | tf_op jit(solution)/shard_map/ppermute | solution.py:46
  81.0 33.7 %collective-permute-start.8 = (bf16[4,64,2560]{2,1,0:T(8,128)(2,1)S(1)}, bf16[4,64,2560]{2,1,0:T(8,128)(2,1)}, u32[]{:S(2)}, u32[]{:S(2)}) collective-permute-start(bf16[4,64,2560]{2,1,0:T(8,128)(2,1)S(1)} %pad_maximum_fusion.1.refs_0_), channel_id=1, source_target_pairs={{0,2},{1,3},{2,0},{3,1},{4,6},{5,7},{6,4},{7,5},{8,10},{9,11},{10,... | collective-permute-start | bytes 3932168 | tf_op jit(solution)/shard_map/ppermute | solution.py:46
  115.8 23.5 %collective-permute-start.11 = (bf16[4,64,2560]{2,1,0:T(8,128)(2,1)}, bf16[4,64,2560]{2,1,0:T(8,128)(2,1)S(1)}, u32[]{:S(2)}, u32[]{:S(2)}) collective-permute-start(bf16[4,64,2560]{2,1,0:T(8,128)(2,1)} %collective-permute-done.6.refs_1_), channel_id=1, source_target_pairs={{0,2},{1,3},{2,0},{3,1},{4,6},{5,7},{6,4},{7,5},{8,10},{9,11},{10,... | collective-permute-start | bytes 3932168 | tf_op jit(solution)/shard_map/ppermute | solution.py:46
  117.1 22.3 %collective-permute-start.12 = (bf16[4,64,2560]{2,1,0:T(8,128)(2,1)}, bf16[4,64,2560]{2,1,0:T(8,128)(2,1)}, u32[]{:S(2)}, u32[]{:S(2)}) collective-permute-start(bf16[4,64,2560]{2,1,0:T(8,128)(2,1)} %collective-permute-done.7.refs_2_), channel_id=1, source_target_pairs={{0,2},{1,3},{2,0},{3,1},{4,6},{5,7},{6,4},{7,5},{8,10},{9,11},{10,... | collective-permute-start | bytes 3932168 | tf_op jit(solution)/shard_map/ppermute | solution.py:46
  117.6 16.8 %collective-permute-start.10 = (bf16[2,64,2560]{2,1,0:T(8,128)(2,1)S(1)}, bf16[2,64,2560]{2,1,0:T(8,128)(2,1)}, u32[]{:S(2)}, u32[]{:S(2)}) collective-permute-start(bf16[2,64,2560]{2,1,0:T(8,128)(2,1)S(1)} %slice.335), channel_id=1, source_target_pairs={{0,1},{1,0},{2,3},{3,2},{4,5},{5,4},{6,7},{7,6},{8,9},{9,8},{10,11... | collective-permute-start | bytes 1966088 | tf_op jit(solution)/shard_map/ppermute | solution.py:46
  119.3 16.5 %collective-permute-start.9 = (bf16[2,64,2560]{2,1,0:T(8,128)(2,1)S(1)}, bf16[2,64,2560]{2,1,0:T(8,128)(2,1)}, u32[]{:S(2)}, u32[]{:S(2)}) collective-permute-start(bf16[2,64,2560]{2,1,0:T(8,128)(2,1)S(1)} %slice.334), channel_id=1, source_target_pairs={{0,4},{1,5},{2,6},{3,7},{4,0},{5,1},{6,2},{7,3},{8,12},{9,13},{10,... | collective-permute-start | bytes 1966088 | tf_op jit(solution)/shard_map/ppermute | solution.py:46
  135.9 2.9 collective-permute-start.13
  135.9 3.4 collective-permute-start.14
  152.2 11.1 %collective-permute-start.15 = (bf16[256,512]{1,0:T(8,128)(2,1)S(1)}, bf16[256,512]{1,0:T(8,128)(2,1)S(1)}, u32[]{:S(2)}, u32[]{:S(2)}) collective-permute-start(bf16[256,512]{1,0:T(8,128)(2,1)S(1)} %get-tuple-element.201.own_ref), channel_id=1, source_target_pairs={{0,1},{1,0},{2,3},{3,2},{4,5},{5,4},{6,7},{7,6},{8,9},{9,8},{10,11... | collective-permute-start | bytes 786440 | tf_op jit(solution)/shard_map/ppermute | solution.py:46
  163.3 25.3 %collective-permute-start.16 = (bf16[4,64,2048]{2,1,0:T(8,128)(2,1)S(1)}, bf16[4,64,2048]{2,1,0:T(8,128)(2,1)S(1)}, u32[]{:S(2)}, u32[]{:S(2)}) collective-permute-start(bf16[4,64,2048]{2,1,0:T(8,128)(2,1)S(1)} %pad_maximum_fusion.2.refs_0_), channel_id=1, source_target_pairs={{0,1},{1,0},{2,3},{3,2},{4,5},{5,4},{6,7},{7,6},{8,9},{9,8},{10,11... | collective-permute-start | bytes 3145736 | tf_op jit(solution)/shard_map/ppermute | solution.py:46
  164.9 24.7 %collective-permute-start.17 = (bf16[4,64,2048]{2,1,0:T(8,128)(2,1)S(1)}, bf16[4,64,2048]{2,1,0:T(8,128)(2,1)}, u32[]{:S(2)}, u32[]{:S(2)}) collective-permute-start(bf16[4,64,2048]{2,1,0:T(8,128)(2,1)S(1)} %pad_maximum_fusion.2.refs_0_), channel_id=1, source_target_pairs={{0,4},{1,5},{2,6},{3,7},{4,0},{5,1},{6,2},{7,3},{8,12},{9,13},{10,... | collective-permute-start | bytes 3145736 | tf_op jit(solution)/shard_map/ppermute | solution.py:46
  166.6 23.1 %collective-permute-start.18 = (bf16[4,64,2048]{2,1,0:T(8,128)(2,1)S(1)}, bf16[4,64,2048]{2,1,0:T(8,128)(2,1)S(1)}, u32[]{:S(2)}, u32[]{:S(2)}) collective-permute-start(bf16[4,64,2048]{2,1,0:T(8,128)(2,1)S(1)} %pad_maximum_fusion.2.refs_0_), channel_id=1, source_target_pairs={{0,2},{1,3},{2,0},{3,1},{4,6},{5,7},{6,4},{7,5},{8,10},{9,11},{10,... | collective-permute-start | bytes 3145736 | tf_op jit(solution)/shard_map/ppermute | solution.py:46
  189.7 12.6 %collective-permute-start.19 = (bf16[2,64,2048]{2,1,0:T(8,128)(2,1)S(1)}, bf16[2,64,2048]{2,1,0:T(8,128)(2,1)S(1)}, u32[]{:S(2)}, u32[]{:S(2)}) collective-permute-start(bf16[2,64,2048]{2,1,0:T(8,128)(2,1)S(1)} %slice.351), channel_id=1, source_target_pairs={{0,4},{1,5},{2,6},{3,7},{4,0},{5,1},{6,2},{7,3},{8,12},{9,13},{10,... | collective-permute-start | bytes 1572872 | tf_op jit(solution)/shard_map/ppermute | solution.py:46
  192.5 12.4 %collective-permute-start.20 = (bf16[2,64,2048]{2,1,0:T(8,128)(2,1)S(1)}, bf16[2,64,2048]{2,1,0:T(8,128)(2,1)}, u32[]{:S(2)}, u32[]{:S(2)}) collective-permute-start(bf16[2,64,2048]{2,1,0:T(8,128)(2,1)S(1)} %slice.352), channel_id=1, source_target_pairs={{0,1},{1,0},{2,3},{3,2},{4,5},{5,4},{6,7},{7,6},{8,9},{9,8},{10,11... | collective-permute-start | bytes 1572872 | tf_op jit(solution)/shard_map/ppermute | solution.py:46
  193.3 17.2 %collective-permute-start.21 = (bf16[4,64,2048]{2,1,0:T(8,128)(2,1)S(1)}, bf16[4,64,2048]{2,1,0:T(8,128)(2,1)}, u32[]{:S(2)}, u32[]{:S(2)}) collective-permute-start(bf16[4,64,2048]{2,1,0:T(8,128)(2,1)S(1)} %collective-permute-done.16.refs_1_), channel_id=1, source_target_pairs={{0,2},{1,3},{2,0},{3,1},{4,6},{5,7},{6,4},{7,5},{8,10},{9,11},{10,... | collective-permute-start | bytes 3145736 | tf_op jit(solution)/shard_map/ppermute | solution.py:46
  193.3 17.2 %collective-permute-start.22 = (bf16[4,64,2048]{2,1,0:T(8,128)(2,1)}, bf16[4,64,2048]{2,1,0:T(8,128)(2,1)}, u32[]{:S(2)}, u32[]{:S(2)}) collective-permute-start(bf16[4,64,2048]{2,1,0:T(8,128)(2,1)} %collective-permute-done.17.refs_2_), channel_id=1, source_target_pairs={{0,2},{1,3},{2,0},{3,1},{4,6},{5,7},{6,4},{7,5},{8,10},{9,11},{10,... | collective-permute-start | bytes 3145736 | tf_op jit(solution)/shard_map/ppermute | solution.py:46
  204.9 3.1 collective-permute-start.23
  204.9 5.6 %collective-permute-start.24 = (bf16[2,64,2048]{2,1,0:T(8,128)(2,1)}, bf16[2,64,2048]{2,1,0:T(8,128)(2,1)}, u32[]{:S(2)}, u32[]{:S(2)}) collective-permute-start(bf16[2,64,2048]{2,1,0:T(8,128)(2,1)} %collective-permute-done.20.refs_4_), channel_id=1, source_target_pairs={{0,2},{1,3},{2,0},{3,1},{4,6},{5,7},{6,4},{7,5},{8,10},{9,11},{10,... | collective-permute-start | bytes 1572872 | tf_op jit(solution)/shard_map/ppermute | solution.py:46
  206.3 20.4 %collective-permute-start.25 = (bf16[128,2048]{1,0:T(8,128)(2,1)}, bf16[128,2048]{1,0:T(8,128)(2,1)}, u32[]{:S(2)}, u32[]{:S(2)}) collective-permute-start(bf16[128,2048]{1,0:T(8,128)(2,1)} %slice.356), channel_id=1, source_target_pairs={{0,4},{1,5},{2,6},{3,7},{4,0},{5,1},{6,2},{7,3},{8,12},{9,13},{10,... | collective-permute-start | bytes 1572872 | tf_op jit(solution)/shard_map/ppermute | solution.py:46
  208.8 17.9 %collective-permute-start.26 = (bf16[128,2048]{1,0:T(8,128)(2,1)}, bf16[128,2048]{1,0:T(8,128)(2,1)}, u32[]{:S(2)}, u32[]{:S(2)}) collective-permute-start(bf16[128,2048]{1,0:T(8,128)(2,1)} %slice.357), channel_id=1, source_target_pairs={{0,1},{1,0},{2,3},{3,2},{4,5},{5,4},{6,7},{7,6},{8,9},{9,8},{10,11... | collective-permute-start | bytes 1572872 | tf_op jit(solution)/shard_map/ppermute | solution.py:46
  226.6 66.8 %copy-start.15 = (bf16[256,2176]{1,0:T(8,128)(2,1)}, bf16[256,2176]{1,0:T(8,128)(2,1)S(1)}, u32[]{:S(2)}) copy-start(bf16[256,2176]{1,0:T(8,128)(2,1)S(1)} %get-tuple-element.223.refs_0_) | copy-start | bytes 3342340
  226.7 26.0 %collective-permute-start.27 = (bf16[256,2176]{1,0:T(8,128)(2,1)S(1)}, bf16[256,2176]{1,0:T(8,128)(2,1)S(1)}, u32[]{:S(2)}, u32[]{:S(2)}) collective-permute-start(bf16[256,2176]{1,0:T(8,128)(2,1)S(1)} %get-tuple-element.223.refs_0_), channel_id=1, source_target_pairs={{0,1},{1,0},{2,3},{3,2},{4,5},{5,4},{6,7},{7,6},{8,9},{9,8},{10,11... | collective-permute-start | bytes 3342344 | tf_op jit(solution)/shard_map/ppermute | solution.py:46
  227.7 25.6 %collective-permute-start.28 = (bf16[256,2176]{1,0:T(8,128)(2,1)S(1)}, bf16[256,2176]{1,0:T(8,128)(2,1)S(1)}, u32[]{:S(2)}, u32[]{:S(2)}) collective-permute-start(bf16[256,2176]{1,0:T(8,128)(2,1)S(1)} %get-tuple-element.223.refs_0_), channel_id=1, source_target_pairs={{0,4},{1,5},{2,6},{3,7},{4,0},{5,1},{6,2},{7,3},{8,12},{9,13},{10,... | collective-permute-start | bytes 3342344 | tf_op jit(solution)/shard_map/ppermute | solution.py:46
  228.9 24.4 %collective-permute-start.29 = (bf16[256,2176]{1,0:T(8,128)(2,1)S(1)}, bf16[256,2176]{1,0:T(8,128)(2,1)S(1)}, u32[]{:S(2)}, u32[]{:S(2)}) collective-permute-start(bf16[256,2176]{1,0:T(8,128)(2,1)S(1)} %get-tuple-element.223.refs_0_), channel_id=1, source_target_pairs={{0,2},{1,3},{2,0},{3,1},{4,6},{5,7},{6,4},{7,5},{8,10},{9,11},{10,... | collective-permute-start | bytes 3342344 | tf_op jit(solution)/shard_map/ppermute | solution.py:46
  228.9 26.1 %collective-permute-start.34 = (bf16[256,2048]{1,0:T(8,128)(2,1)S(1)}, bf16[256,2048]{1,0:T(8,128)(2,1)S(1)}, u32[]{:S(2)}, u32[]{:S(2)}) collective-permute-start(bf16[256,2048]{1,0:T(8,128)(2,1)S(1)} %copy-done.36), channel_id=1, source_target_pairs={{0,2},{1,3},{2,0},{3,1},{4,6},{5,7},{6,4},{7,5},{8,10},{9,11},{10,... | collective-permute-start | bytes 3145736 | tf_op jit(solution)/shard_map/ppermute | solution.py:46
  229.4 26.9 %collective-permute-start.35 = (bf16[256,2048]{1,0:T(8,128)(2,1)S(1)}, bf16[256,2048]{1,0:T(8,128)(2,1)S(1)}, u32[]{:S(2)}, u32[]{:S(2)}) collective-permute-start(bf16[256,2048]{1,0:T(8,128)(2,1)S(1)} %copy-done.39), channel_id=1, source_target_pairs={{0,2},{1,3},{2,0},{3,1},{4,6},{5,7},{6,4},{7,5},{8,10},{9,11},{10,... | collective-permute-start | bytes 3145736 | tf_op jit(solution)/shard_map/ppermute | solution.py:46
  254.4 16.7 %collective-permute-start.32 = (bf16[256,2176]{1,0:T(8,128)(2,1)S(1)}, bf16[256,2176]{1,0:T(8,128)(2,1)S(1)}, u32[]{:S(2)}, u32[]{:S(2)}) collective-permute-start(bf16[256,2176]{1,0:T(8,128)(2,1)S(1)} %collective-permute-done.27.refs_0_), channel_id=1, source_target_pairs={{0,2},{1,3},{2,0},{3,1},{4,6},{5,7},{6,4},{7,5},{8,10},{9,11},{10,... | collective-permute-start | bytes 3342344 | tf_op jit(solution)/shard_map/ppermute | solution.py:46
  254.4 16.7 %collective-permute-start.33 = (bf16[256,2176]{1,0:T(8,128)(2,1)S(1)}, bf16[256,2176]{1,0:T(8,128)(2,1)S(1)}, u32[]{:S(2)}, u32[]{:S(2)}) collective-permute-start(bf16[256,2176]{1,0:T(8,128)(2,1)S(1)} %collective-permute-done.28.refs_2_), channel_id=1, source_target_pairs={{0,2},{1,3},{2,0},{3,1},{4,6},{5,7},{6,4},{7,5},{8,10},{9,11},{10,... | collective-permute-start | bytes 3342344 | tf_op jit(solution)/shard_map/ppermute | solution.py:46
  254.9 4.0 collective-permute-start.36
  255.0 15.1 %collective-permute-start.30 = (bf16[128,2176]{1,0:T(8,128)(2,1)S(1)}, bf16[128,2176]{1,0:T(8,128)(2,1)S(1)}, u32[]{:S(2)}, u32[]{:S(2)}) collective-permute-start(bf16[128,2176]{1,0:T(8,128)(2,1)S(1)} %slice.358), channel_id=1, source_target_pairs={{0,4},{1,5},{2,6},{3,7},{4,0},{5,1},{6,2},{7,3},{8,12},{9,13},{10,... | collective-permute-start | bytes 1671176 | tf_op jit(solution)/shard_map/ppermute | solution.py:46
  256.3 14.8 %collective-permute-start.31 = (bf16[128,2176]{1,0:T(8,128)(2,1)S(1)}, bf16[128,2176]{1,0:T(8,128)(2,1)S(1)}, u32[]{:S(2)}, u32[]{:S(2)}) collective-permute-start(bf16[128,2176]{1,0:T(8,128)(2,1)S(1)} %slice.359), channel_id=1, source_target_pairs={{0,1},{1,0},{2,3},{3,2},{4,5},{5,4},{6,7},{7,6},{8,9},{9,8},{10,11... | collective-permute-start | bytes 1671176 | tf_op jit(solution)/shard_map/ppermute | solution.py:46
  258.9 2.1 collective-permute-start.37
  272.3 2.0 collective-permute-start.38
  273.3 2.1 collective-permute-start.39
  294.4 32.4 %collective-permute-start.40 = (bf16[256,2432]{1,0:T(8,128)(2,1)S(1)}, bf16[256,2432]{1,0:T(8,128)(2,1)S(1)}, u32[]{:S(2)}, u32[]{:S(2)}) collective-permute-start(bf16[256,2432]{1,0:T(8,128)(2,1)S(1)} %get-tuple-element.243), channel_id=1, source_target_pairs={{0,2},{1,3},{2,0},{3,1},{4,6},{5,7},{6,4},{7,5},{8,10},{9,11},{10,... | collective-permute-start | bytes 3735560 | tf_op jit(solution)/shard_map/ppermute | solution.py:46
  327.9 4.7 collective-permute-start.41
  328.3 25.7 %collective-permute-start.42 = (bf16[128,2432]{1,0:T(8,128)(2,1)S(1)}, bf16[128,2432]{1,0:T(8,128)(2,1)S(1)}, u32[]{:S(2)}, u32[]{:S(2)}) collective-permute-start(bf16[128,2432]{1,0:T(8,128)(2,1)S(1)} %get-tuple-element.253), channel_id=1, source_target_pairs={{0,1},{1,0},{2,3},{3,2},{4,5},{5,4},{6,7},{7,6},{8,9},{9,8},{10,11... | collective-permute-start | bytes 1867784 | tf_op jit(solution)/shard_map/ppermute | solution.py:46
  329.3 24.7 %collective-permute-start.43 = (bf16[128,2432]{1,0:T(8,128)(2,1)S(1)}, bf16[128,2432]{1,0:T(8,128)(2,1)S(1)}, u32[]{:S(2)}, u32[]{:S(2)}) collective-permute-start(bf16[128,2432]{1,0:T(8,128)(2,1)S(1)} %get-tuple-element.254), channel_id=1, source_target_pairs={{0,4},{1,5},{2,6},{3,7},{4,0},{5,1},{6,2},{7,3},{8,12},{9,13},{10,... | collective-permute-start | bytes 1867784 | tf_op jit(solution)/shard_map/ppermute | solution.py:46
  332.9 24.8 %collective-permute-start.44 = (bf16[128,2432]{1,0:T(8,128)(2,1)S(1)}, bf16[128,2432]{1,0:T(8,128)(2,1)S(1)}, u32[]{:S(2)}, u32[]{:S(2)}) collective-permute-start(bf16[128,2432]{1,0:T(8,128)(2,1)S(1)} %get-tuple-element.255), channel_id=1, source_target_pairs={{0,1},{1,0},{2,3},{3,2},{4,5},{5,4},{6,7},{7,6},{8,9},{9,8},{10,11... | collective-permute-start | bytes 1867784 | tf_op jit(solution)/shard_map/ppermute | solution.py:46
  334.0 24.4 %collective-permute-start.45 = (bf16[128,2432]{1,0:T(8,128)(2,1)S(1)}, bf16[128,2432]{1,0:T(8,128)(2,1)S(1)}, u32[]{:S(2)}, u32[]{:S(2)}) collective-permute-start(bf16[128,2432]{1,0:T(8,128)(2,1)S(1)} %get-tuple-element.256), channel_id=1, source_target_pairs={{0,4},{1,5},{2,6},{3,7},{4,0},{5,1},{6,2},{7,3},{8,12},{9,13},{10,... | collective-permute-start | bytes 1867784 | tf_op jit(solution)/shard_map/ppermute | solution.py:46
  353.9 28.8 %collective-permute-start.46 = (bf16[256,2432]{1,0:T(8,128)(2,1)}, bf16[256,2432]{1,0:T(8,128)(2,1)S(1)}, u32[]{:S(2)}, u32[]{:S(2)}) collective-permute-start(bf16[256,2432]{1,0:T(8,128)(2,1)} %get-tuple-element.259), channel_id=1, source_target_pairs={{0,2},{1,3},{2,0},{3,1},{4,6},{5,7},{6,4},{7,5},{8,10},{9,11},{10,... | collective-permute-start | bytes 3735560 | tf_op jit(solution)/shard_map/ppermute | solution.py:46
  359.9 22.8 %collective-permute-start.47 = (bf16[128,2432]{1,0:T(8,128)(2,1)}, bf16[128,2432]{1,0:T(8,128)(2,1)}, u32[]{:S(2)}, u32[]{:S(2)}) collective-permute-start(bf16[128,2432]{1,0:T(8,128)(2,1)} %get-tuple-element.265), channel_id=1, source_target_pairs={{0,4},{1,5},{2,6},{3,7},{4,0},{5,1},{6,2},{7,3},{8,12},{9,13},{10,... | collective-permute-start | bytes 1867784 | tf_op jit(solution)/shard_map/ppermute | solution.py:46
  360.9 21.8 %collective-permute-start.48 = (bf16[128,2432]{1,0:T(8,128)(2,1)}, bf16[128,2432]{1,0:T(8,128)(2,1)}, u32[]{:S(2)}, u32[]{:S(2)}) collective-permute-start(bf16[128,2432]{1,0:T(8,128)(2,1)} %get-tuple-element.266), channel_id=1, source_target_pairs={{0,1},{1,0},{2,3},{3,2},{4,5},{5,4},{6,7},{7,6},{8,9},{9,8},{10,11... | collective-permute-start | bytes 1867784 | tf_op jit(solution)/shard_map/ppermute | solution.py:46
  382.7 59.4 %collective-permute-start.50 = (bf16[1024,2048]{1,0:T(8,128)(2,1)}, bf16[1024,2048]{1,0:T(8,128)(2,1)}, u32[]{:S(2)}, u32[]{:S(2)}) collective-permute-start(bf16[1024,2048]{1,0:T(8,128)(2,1)} %get-tuple-element.303), channel_id=1, source_target_pairs={{0,2},{1,3},{2,0},{3,1},{4,6},{5,7},{6,4},{7,5},{8,10},{9,11},{10,... | collective-permute-start | bytes 12582920 | tf_op jit(solution)/shard_map/ppermute | solution.py:46
  383.8 36.0 %all-to-all-start.2 = ((bf16[32,4,2304]{2,1,0:T(4,128)(2,1)}), bf16[32,4,2304]{2,1,0:T(4,128)(2,1)S(1)}, u32[]{:S(2)}, u32[]{:S(2)}) async-start(bf16[32,4,2304]{2,1,0:T(4,128)(2,1)} %pad_maximum_fusion.4), calls=%async_computation.2 | async-start | bytes 1179648 | tf_op jit(solution)/shard_map/all_to_all | solution.py:1141
  419.7 8.6 %collective-permute-start.49 = (bf16[256,512]{1,0:T(8,128)(2,1)S(1)}, bf16[256,512]{1,0:T(8,128)(2,1)S(1)}, u32[]{:S(2)}, u32[]{:S(2)}) collective-permute-start(bf16[256,512]{1,0:T(8,128)(2,1)S(1)} %get-tuple-element.295), channel_id=1, source_target_pairs={{0,1},{1,0},{2,3},{3,2},{4,5},{5,4},{6,7},{7,6},{8,9},{9,8},{10,11... | collective-permute-start | bytes 786440 | tf_op jit(solution)/shard_map/ppermute | solution.py:46
  436.2 34.7 %all-to-all-start.3 = ((bf16[32,16,592]{2,1,0:T(8,128)(2,1)}), bf16[32,16,592]{2,1,0:T(8,128)(2,1)S(1)}, u32[]{:S(2)}, u32[]{:S(2)}) async-start(bf16[32,16,592]{2,1,0:T(8,128)(2,1)} %bitcast.108), calls=%async_computation.3 | async-start | bytes 1310720 | tf_op jit(solution)/shard_map/all_to_all | solution.py:1170
  445.9 18.2 %collective-permute-start.51 = (bf16[128,2048]{1,0:T(8,128)(2,1)}, bf16[128,2048]{1,0:T(8,128)(2,1)}, u32[]{:S(2)}, u32[]{:S(2)}) collective-permute-start(bf16[128,2048]{1,0:T(8,128)(2,1)} %get-tuple-element.311), channel_id=1, source_target_pairs={{0,1},{1,0},{2,3},{3,2},{4,5},{5,4},{6,7},{7,6},{8,9},{9,8},{10,11... | collective-permute-start | bytes 1572872 | tf_op jit(solution)/shard_map/ppermute | solution.py:46
  447.8 16.5 %collective-permute-start.52 = (bf16[128,2048]{1,0:T(8,128)(2,1)S(1)}, bf16[128,2048]{1,0:T(8,128)(2,1)}, u32[]{:S(2)}, u32[]{:S(2)}) collective-permute-start(bf16[128,2048]{1,0:T(8,128)(2,1)S(1)} %get-tuple-element.312), channel_id=1, source_target_pairs={{0,4},{1,5},{2,6},{3,7},{4,0},{5,1},{6,2},{7,3},{8,12},{9,13},{10,... | collective-permute-start | bytes 1572872 | tf_op jit(solution)/shard_map/ppermute | solution.py:46
  463.3 15.7 %collective-permute-start.53 = (bf16[128,2048]{1,0:T(8,128)(2,1)}, bf16[128,2048]{1,0:T(8,128)(2,1)}, u32[]{:S(2)}, u32[]{:S(2)}) collective-permute-start(bf16[128,2048]{1,0:T(8,128)(2,1)} %get-tuple-element.318), channel_id=1, source_target_pairs={{0,1},{1,0},{2,3},{3,2},{4,5},{5,4},{6,7},{7,6},{8,9},{9,8},{10,11... | collective-permute-start | bytes 1572872 | tf_op jit(solution)/shard_map/ppermute | solution.py:46
  463.8 15.2 %collective-permute-start.55 = (bf16[128,2048]{1,0:T(8,128)(2,1)}, bf16[128,2048]{1,0:T(8,128)(2,1)}, u32[]{:S(2)}, u32[]{:S(2)}) collective-permute-start(bf16[128,2048]{1,0:T(8,128)(2,1)} %get-tuple-element.320), channel_id=1, source_target_pairs={{0,4},{1,5},{2,6},{3,7},{4,0},{5,1},{6,2},{7,3},{8,12},{9,13},{10,... | collective-permute-start | bytes 1572872 | tf_op jit(solution)/shard_map/ppermute | solution.py:46
  467.7 24.8 %collective-permute-start.54 = (bf16[128,2048]{1,0:T(8,128)(2,1)}, bf16[128,2048]{1,0:T(8,128)(2,1)}, u32[]{:S(2)}, u32[]{:S(2)}) collective-permute-start(bf16[128,2048]{1,0:T(8,128)(2,1)} %get-tuple-element.329), channel_id=1, source_target_pairs={{0,4},{1,5},{2,6},{3,7},{4,0},{5,1},{6,2},{7,3},{8,12},{9,13},{10,... | collective-permute-start | bytes 1572872 | tf_op jit(solution)/shard_map/ppermute | solution.py:46
  469.4 23.1 %collective-permute-start.56 = (bf16[128,2048]{1,0:T(8,128)(2,1)}, bf16[128,2048]{1,0:T(8,128)(2,1)}, u32[]{:S(2)}, u32[]{:S(2)}) collective-permute-start(bf16[128,2048]{1,0:T(8,128)(2,1)} %get-tuple-element.330), channel_id=1, source_target_pairs={{0,1},{1,0},{2,3},{3,2},{4,5},{5,4},{6,7},{7,6},{8,9},{9,8},{10,11... | collective-permute-start | bytes 1572872 | tf_op jit(solution)/shard_map/ppermute | solution.py:46
  473.3 24.0 %all-to-all-start.4 = ((f32[32,4,720]{2,1,0:T(4,128)}), f32[32,4,720]{2,1,0:T(4,128)S(1)}, u32[]{:S(2)}, u32[]{:S(2)}) async-start(f32[32,4,720]{2,1,0:T(4,128)} %pad_maximum_fusion.5), calls=%async_computation.4 | async-start | bytes 786432 | tf_op jit(solution)/shard_map/all_to_all | solution.py:1190
  (70 other events, 658.0 us)
Sparse Core Ops, SparseCore 0:
  66.8 174.2 all-gather.1

commit v3 on v2

--- a/solution.py
+++ b/solution.py
@@ -102,8 +102,9 @@
         for j in range(piece.shape[0]):
             dz = first + j
             block = (((z ^ dz) * 2 + (y ^ dy)) * 2 + (c ^ dc)) * 2 + (x ^ dx)
+            rows = pl.ds(pl.multiple_of(block * piece.shape[1], piece.shape[1]), piece.shape[1])
             copies.append(
-                pltpu.make_async_copy(piece.at[j], held.at[block], sems.at[len(copies)])
+                pltpu.make_async_copy(piece.at[j], held.at[rows], sems.at[len(copies)])
             )
     return copies
 
@@ -495,9 +496,7 @@
     copy = pltpu.make_async_copy(held, w_ref, last)
     copy.start()
     width = kv_ref.shape[1]
-    start = held.shape[2] - width
-    weights = held[:, :, start:].reshape(normed.shape[1], width)
-    kv = nn(normed, weights) + nn(low, b_ref[...])
+    kv = nn(normed, held[:, held.shape[1] - width :]) + nn(low, b_ref[...])
     for i in range(width // LANES):
         cols = slice(i * LANES, (i + 1) * LANES)
         slab = kv[:, cols]
@@ -520,13 +519,13 @@
     normed, low, kv, weights = pl.pallas_call(
         project_kernel,
         grid=(1,),
-        out_shape=(*outs, jax.ShapeDtypeStruct((n, shard, columns), BF)),
+        out_shape=(*outs, pltpu.HBM((n * shard, columns), BF)),
         in_specs=[pl.BlockSpec(memory_space=pltpu.SMEM)]
         + [full(v) for v in operands]
         + [anywhere] * len(pieces),
         out_specs=(*[full(v) for v in outs], anywhere),
         scratch_shapes=[
-            pltpu.VMEM((n, shard, columns), BF),
+            pltpu.VMEM((n * shard, columns), BF),
             pltpu.SemaphoreType.DMA((n,)),
             pltpu.SemaphoreType.DMA(()),
         ],
@@ -534,7 +533,7 @@
         cost_estimate=LIGHT,
         name="project",
     )(me.reshape(1), *map(HBM, operands), *map(HBM, pieces))
-    return normed, low, kv, weights.reshape(n * shard, columns)
+    return normed, low, kv, weights
 
 
 def query_kernel(normed_ref, low_ref, b_ref, w_ref, cos_ref, sin_ref, out_ref):
@@ -581,8 +580,7 @@
     copy = pltpu.make_async_copy(held, w_ref, last)
     copy.start()
     rows, width = attended.shape
-    weights = held[...].reshape(width, width)
-    middle = x_ref[...].astype(F32) + nn(attended, weights) + nn(low, b_ref[...])
+    middle = x_ref[...].astype(F32) + nn(attended, held[...]) + nn(low, b_ref[...])
     middle_ref[...] = middle
     normed = normed_of(middle, gain_ref[...])
     normed_ref[...] = normed
@@ -608,13 +606,13 @@
     *results, weights = pl.pallas_call(
         output_kernel,
         grid=(1,),
-        out_shape=(*outs, jax.ShapeDtypeStruct((n, shard, columns), BF)),
+        out_shape=(*outs, pltpu.HBM((n * shard, columns), BF)),
         in_specs=[pl.BlockSpec(memory_space=pltpu.SMEM)]
         + [full(v) for v in operands]
         + [anywhere] * len(pieces),
         out_specs=(*[full(v) for v in outs], anywhere),
         scratch_shapes=[
-            pltpu.VMEM((n, shard, columns), BF),
+            pltpu.VMEM((n * shard, columns), BF),
             pltpu.SemaphoreType.DMA((n,)),
             pltpu.SemaphoreType.DMA(()),
         ],
@@ -622,7 +620,7 @@
         cost_estimate=LIGHT,
         name="output",
     )(me.reshape(1), *map(HBM, operands), *map(HBM, pieces))
-    return (*results, weights.reshape(n * shard, columns))
+    return (*results, weights)
 
 
 def back_kernel(grad_ref, w_ref, low_ref, a_ref, out_ref):
@@ -852,7 +850,7 @@
         grid=(KV_HEADS,),
         out_shape=(
             jax.ShapeDtypeStruct((rows, width), BF),
-            jax.ShapeDtypeStruct((KV_HEADS, heads, 2 * rows, rows), BF),
+            pltpu.HBM((KV_HEADS, heads, 2 * rows, rows), BF),
         ),
         in_specs=[pl.BlockSpec(memory_space=pltpu.SMEM), tile, whole, whole],
         out_specs=(tile, pl.BlockSpec((1, heads, 2 * rows, rows), lambda i: (i, 0, 0, 0))),
@@ -1059,23 +1057,22 @@
     )
     grad_low_down = nt(grad_out, b_down).astype(BF)
     plane_ids = jnp.stack([ids[me], ids[me ^ C], ids[me ^ Y], ids[me ^ (Y | C)]])
-    *qkv_rows.last, a_att, a_two, b_kv, cosine, sine, grad_low_down, plane_ids = order.point(
-        *qkv_rows.last, a_att, a_two, b_kv, cosine, sine, grad_low_down, plane_ids
-    )
+    out_rows = Rows([part[:, qkv_width:] for part in att_rows.parts()], n)
+    passed = order.point(
+        *qkv_rows.last, a_att, a_two, b_kv, cosine, sine, grad_low_down, plane_ids, out_rows.whole
+    )
+    qkv_rows.last = passed[:2]
+    a_att, a_two, b_kv, cosine, sine, grad_low_down, plane_ids, out_rows.whole = passed[2:]
+    out_rows.start_plane()
     normed_one, low_att, key_value, w_qkv = project_stage(
         me, tokens, gain_one[None], a_att, b_kv, cosine, sine, qkv_rows.pieces(), n
     )
     low_query, low_key, low_value = [low_att[:, i * RANK : (i + 1) * RANK] for i in range(3)]
-    (key_value,) = att_rows.pass_through(order, key_value)
+    key_value = order.point(key_value)
     other_kv = exchange(key_value, X, n)
-    out_rows = Rows([part[:, qkv_width:] for part in att_rows.parts()], n)
     query = query_stage(normed_one, low_att, b_query, w_qkv, cosine, sine)
-    key_value, other_kv, query, out_rows.whole = order.point(
-        key_value, other_kv, query, out_rows.whole
-    )
-    out_rows.start_plane()
+    key_value, other_kv, query = order.point(key_value, other_kv, query)
     attended, probs = attend_stage(blocks, query, key_value, other_kv)
-    probs = HBM(probs)
     attended, *out_rows.near = order.point(attended, *out_rows.near)
     out_rows.end_plane()
     attended, *out_rows.last = order.point(attended, *out_rows.last)
@@ -1161,19 +1158,16 @@
     grad_query, grad_kv, kv_away, hidden_grads = order.point(
         grad_query, grad_kv, kv_away, hidden_grads
     )
-    kv_came = exchange(kv_away, X, n)
+    kv_came, *sends = order.point(
+        exchange(kv_away, X, n), *down_sum.far_sends(), *down_sum.near_sends()
+    )
+    down_far = down_sum.hop(*sends[:2])
     grad_qkv, grad_low_att, late = project_back_stage(
         grad_query, grad_kv, kv_came, cosine, sine, b_query, b_kv, low_att, normed_one
     )
 
-    late, down_near = order.point(send_columns([late, early], n), down_near)
+    late, grad_qkv = order.point(send_columns([late, early], n), grad_qkv)
     late = lax.all_to_all(late, ALL, 0, 0, tiled=True)
-    for i in range(4):
-        down_sum.mine[i] = down_near[i * rows : (i + 1) * rows]
-    grad_qkv, *sends = order.point(
-        grad_qkv, *down_sum.far_sends(), *down_sum.near_sends()
-    )
-    down_far = down_sum.hop(*sends[:2])
     down_near = down_sum.hop(*sends[2:])
     input_grad, gain_grad_one = norm_one_stage(
         grad_qkv, w_qkv, grad_low_att, a_att, tokens, gain_one[None], grad_middle

time: 514 us -> 497 us (0.967)
  local copies, waits for them, and re-layouts: 76.5 us -> 65.5 us
  waiting for transfers between devices: 153 us -> 145 us
    unnamed x156 -> x160, local copies, waits for them, and re-layouts: 39.4 us -> 28.7 us
    ppermute x57, waiting for transfers between devices: 125 us -> 120 us  [exchange(): return lax.ppermute(value, ALL, [(i, i ^ mask) for i in range(n)])]
  transfers between devices with their start and end apart: 63 -> 63, of which waited for: 26 -> 29; matrix products, arithmetic and copies ran while one was open for 14% -> 14% of each run, Pallas kernels for 28% -> 29%
where the time goes in v3:
time: 497 us; the launch traced here: 492 us
  Pallas kernels  162 us (33%)
  waiting for transfers between devices  145 us (29%)
  starting transfers between devices  67.1 us (14%)
  local copies, waits for them, and re-layouts  65.5 us (13%)
  other arithmetic  32 us (6%)
  between operations  17.1 us (3%)
    ppermute x57, waiting for transfers between devices, exchange(): return lax.ppermute(value, ALL, [(i, i ^ mask) for i in range(n)])  120 us
    pallas_call x3, Pallas kernels, feed_stage(): pl.pallas_call(functools.partial(feed_kernel, (len(normed), padded, slot,...  69.6 us
    ppermute x57, starting transfers between devices, exchange(): return lax.ppermute(value, ALL, [(i, i ^ mask) for i in range(n)])  45.7 us
    unnamed x160, local copies, waits for them, and re-layouts  28.7 us
    all_to_all x1, waiting for transfers between devices, per_device(): own = lax.all_to_all(jnp.take(columns, ids, axis=0), ALL, 0, 0, tiled=True)  23.6 us
    pallas_call x1, Pallas kernels, attend_stage(): pl.pallas_call(attend_kernel, grid=(KV_HEADS,), out_shape=(jax.ShapeDtype...  13.4 us
    pallas_call x1, Pallas kernels, attend_back_stage(): pl.pallas_call(attend_back_kernel, grid=(KV_HEADS,), out_shape=(jax.Shape...  13 us
    pallas_call x1, Pallas kernels, down_stage(): pl.pallas_call(functools.partial(down_kernel, padded, slot), grid=(1,), o...  12.3 us
  transfers between devices with their start and end apart: 63, of which 29 were waited for; matrix products, arithmetic and copies ran while one was open for 14% of the time, Pallas kernels for 29%

profile of v3, /device:TPU:0, one launch (start us, length us, event | category | flops | bytes accessed | tf_op | source)
XLA Modules:
  0.0 492.0 jit_solution(8093957541603026153)
XLA Ops:
  7.3 3.0 collective-permute-start.2
  10.3 1.5 collective-permute-start.3
  15.3 1.6 collective-permute-start
  16.9 2.6 collective-permute-start.1
  25.7 2.6 all-to-all-start
  28.3 15.5 %collective-permute-done = bf16[64,4608]{1,0:T(8,128)(2,1)} collective-permute-done((bf16[64,4608]{1,0:T(8,128)(2,1)S(1)}, bf16[64,4608]{1,0:T(8,128)(2,1)}, u32[]{:S(2)}, u32[]{:S(2)}) %collective-permute-start) | collective-permute-done | bytes 589856 | tf_op jit(solution)/shard_map/ppermute | solution.py:46
  43.8 4.4 collective-permute-done.1
  52.2 1.6 all-to-all-done
  54.2 2.7 pad_maximum_fusion
  56.9 7.0 %collective-permute-done.5 = bf16[64,4608]{1,0:T(8,128)(2,1)} collective-permute-done((bf16[64,4608]{1,0:T(8,128)(2,1)}, bf16[64,4608]{1,0:T(8,128)(2,1)}, u32[]{:S(2)}, u32[]{:S(2)}) %collective-permute-start.5) | collective-permute-done | bytes 589856 | tf_op jit(solution)/shard_map/ppermute | solution.py:46
  68.0 4.1 all-to-all-start.1
  72.7 2.7 pad_add_fusion.1.ids_ref
  77.8 1.9 collective-permute-start.6
  79.8 1.5 collective-permute-start.7
  84.4 23.6 %all-to-all-done.1 = bf16[32,16,640]{2,1,0:T(8,128)(2,1)S(1)} async-done(((bf16[32,16,640]{2,1,0:T(8,128)(2,1)}), bf16[32,16,640]{2,1,0:T(8,128)(2,1)S(1)}, u32[]{:S(2)}, u32[]{:S(2)}) %all-to-all-start.1) | async-done | bytes 655392 | tf_op jit(solution)/shard_map/all_to_all | solution.py:1028
  111.2 1.8 fusion.29
  114.2 2.0 collective-permute-start.10
  120.7 10.0 %collective-permute-done.10.refs_4_ = bf16[2,64,2560]{2,1,0:T(8,128)(2,1)S(1)} collective-permute-done((bf16[2,64,2560]{2,1,0:T(8,128)(2,1)S(1)}, bf16[2,64,2560]{2,1,0:T(8,128)(2,1)S(1)}, u32[]{:S(2)}, u32[]{:S(2)}) %collective-permute-start.10) | collective-permute-done | bytes 655392 | tf_op jit(solution)/shard_map/ppermute | solution.py:46
  130.7 2.6 collective-permute-done.9.refs_3_
  136.6 1.7 collective-permute-done.14.refs_9_
  142.5 10.3 %project.1 = (bf16[256,2048]{1,0:T(8,128)(2,1)S(1)}, bf16[256,48]{1,0:T(8,128)(2,1)S(1)}, bf16[256,512]{1,0:T(8,128)(2,1)S(1)}, bf16[2048,2560]{1,0:T(8,128)(2,1)}) custom-call(s32[1]{0:T(128)} %bitcast.me_ref, bf16[256,2048]{1,0:T(8,128)(2,1)} %bitcast.111, f32[1,2048]{1,0:T(1,128)} %reshape.223.gain_ref, bf16[48,2048]{1,0:T(8,128)(2,1)} %pad_maximum_fusion.6.a_ref, ...), custom_call_target="tpu_custom_call" | custom-call | flops 1048576 | bytes 65536 | tf_op jit(solution)/shard_map/project/pallas_call | solution.py:519
  154.6 6.5 %query.1.query_ref = bf16[256,2048]{1,0:T(8,128)(2,1)S(1)} custom-call(bf16[256,2048]{1,0:T(8,128)(2,1)S(1)} %get-tuple-element.188.normed_ref, bf16[256,48]{1,0:T(8,128)(2,1)S(1)} %get-tuple-element.189.low_ref, bf16[16,2048]{1,0:T(8,128)(2,1)S(1)} %get-tuple-element.339.b_ref.bq_ref, bf16[2048,2560]{1,0:T(8,128)(2,1)} %get-tuple-element.190.w_ref, ...), custom_call_target="tpu_custom_call" | custom-call | flops 1048576 | bytes 65536 | tf_op jit(solution)/shard_map/query/pallas_call | solution.py:551
  161.2 4.0 collective-permute-done.15.other_ref
  165.2 13.4 %attend.1 = (bf16[256,2048]{1,0:T(8,128)(2,1)S(1)}, bf16[4,8,512,256]{3,2,1,0:T(8,128)(2,1)}) custom-call(s32[2]{0:T(128)S(1)} %pad_add_fusion.pos_ref, bf16[256,2048]{1,0:T(8,128)(2,1)S(1)} %query.1.query_ref, bf16[256,512]{1,0:T(8,128)(2,1)S(1)} %get-tuple-element.193.own_ref, bf16[256,512]{1,0:T(8,128)(2,1)S(1)} %collective-permute-done.15.other_ref), custom_call_target="tpu_custom_call" | custom-call | flops 1048576 | bytes 65536 | tf_op jit(solution)/shard_map/attend/pallas_call | solution.py:848
  178.6 1.5 slice.351
  181.8 1.7 collective-permute-start.20
  184.0 9.3 %collective-permute-done.19.refs_3_ = bf16[2,64,2048]{2,1,0:T(8,128)(2,1)S(1)} collective-permute-done((bf16[2,64,2048]{2,1,0:T(8,128)(2,1)S(1)}, bf16[2,64,2048]{2,1,0:T(8,128)(2,1)S(1)}, u32[]{:S(2)}, u32[]{:S(2)}) %collective-permute-start.19) | collective-permute-done | bytes 524320 | tf_op jit(solution)/shard_map/ppermute | solution.py:46
  193.4 1.5 collective-permute-done.20.refs_4_
  196.2 1.5 collective-permute-start.25
  201.6 9.0 %output.1 = (f32[256,2048]{1,0:T(8,128)S(1)}, bf16[256,2048]{1,0:T(8,128)(2,1)S(1)}, bf16[256,16]{1,0:T(8,128)(2,1)S(1)}, bf16[256,2176]{1,0:T(8,128)(2,1)S(1)}, bf16[2048,2048]{1,0:T(8,128)(2,1)}) custom-call(s32[1]{0:T(128)} %bitcast.me_ref, bf16[256,2048]{1,0:T(8,128)(2,1)} %copy-done, bf16[16,2048]{1,0:T(8,128)(2,1)} %get-tuple-element.338.a_ref, ...), custom_call_target="tpu_custom_call" | custom-call | flops 1048576 | bytes 65536 | tf_op jit(solution)/shard_map/output/pallas_call | solution.py:606
  213.6 1.5 collective-permute-start.27
  216.2 23.7 %collective-permute-done.27.refs_0_ = bf16[256,2176]{1,0:T(8,128)(2,1)S(1)} collective-permute-done((bf16[256,2176]{1,0:T(8,128)(2,1)S(1)}, bf16[256,2176]{1,0:T(8,128)(2,1)S(1)}, u32[]{:S(2)}, u32[]{:S(2)}) %collective-permute-start.27) | collective-permute-done | bytes 1114144 | tf_op jit(solution)/shard_map/ppermute | solution.py:46
  244.7 1.6 collective-permute-done.36.refs_6_
  246.4 2.0 collective-permute-done.37.refs_7_
  248.4 9.1 %collective-permute-done.30.refs_0_ = bf16[128,2176]{1,0:T(8,128)(2,1)S(1)} collective-permute-done((bf16[128,2176]{1,0:T(8,128)(2,1)S(1)}, bf16[128,2176]{1,0:T(8,128)(2,1)S(1)}, u32[]{:S(2)}, u32[]{:S(2)}) %collective-permute-start.30) | collective-permute-done | bytes 557088 | tf_op jit(solution)/shard_map/ppermute | solution.py:46
  262.3 18.6 %feed.3 = (bf16[512,768]{1,0:T(8,128)(2,1)S(1)}, f32[3,128,768]{2,1,0:T(8,128)S(1)}, bf16[256,2432]{1,0:T(8,128)(2,1)S(1)}, bf16[256,2432]{1,0:T(8,128)(2,1)S(1)}) custom-call(s32[4]{0:T(128)S(1)} %pad_add_fusion.1.ids_ref, bf16[2112,2176]{1,0:T(8,128)(2,1)} %all-gather.2.cloned.1.call-done.feed_ref.refs_3_, bf16[128,2176]{1,0:T(8,128)(2,1)} %copy-done.51, ...), custom_call_target="tpu_custom_call" | custom-call | flops 1048576 | bytes 65536 | tf_op jit(solution)/shard_map/feed/pallas_call | solution.py:399
  282.0 32.3 %feed.4 = (bf16[1024,768]{1,0:T(8,128)(2,1)S(1)}, f32[3,128,768]{2,1,0:T(8,128)S(1)}, bf16[512,2432]{1,0:T(8,128)(2,1)S(1)}, bf16[512,2432]{1,0:T(8,128)(2,1)S(1)}) custom-call(s32[4]{0:T(128)S(1)} %pad_add_fusion.1.ids_ref, bf16[2112,2176]{1,0:T(8,128)(2,1)} %all-gather.2.cloned.1.call-done.feed_ref.refs_3_, bf16[256,2176]{1,0:T(8,128)(2,1)} %copy-done.29, ...), custom_call_target="tpu_custom_call" | custom-call | flops 1048576 | bytes 65536 | tf_op jit(solution)/shard_map/feed/pallas_call | solution.py:399
  317.9 2.2 collective-permute-done.41
  320.4 1.4 collective-permute-start.44
  322.7 18.8 %feed.5 = (bf16[512,768]{1,0:T(8,128)(2,1)S(1)}, f32[3,128,768]{2,1,0:T(8,128)S(1)}, bf16[256,2432]{1,0:T(8,128)(2,1)S(1)}, bf16[256,2432]{1,0:T(8,128)(2,1)}) custom-call(s32[4]{0:T(128)S(1)} %pad_add_fusion.1.ids_ref, bf16[2112,2176]{1,0:T(8,128)(2,1)} %all-gather.2.cloned.1.call-done.feed_ref.refs_3_, bf16[256,2176]{1,0:T(8,128)(2,1)} %copy-done.12, ...), custom_call_target="tpu_custom_call" | custom-call | flops 1048576 | bytes 65536 | tf_op jit(solution)/shard_map/feed/pallas_call | solution.py:399
  341.6 3.6 collective-permute-done.44.refs_2_
  346.3 1.5 add_convert_fusion
  351.7 1.7 concatenate.61
  354.1 2.1 pad_maximum_fusion.4
  356.2 12.3 %down.1 = (bf16[1024,2048]{1,0:T(8,128)(2,1)S(1)}, bf16[1024,2048]{1,0:T(8,128)(2,1)}) custom-call(bf16[512,768]{1,0:T(8,128)(2,1)} %copy-done.17, bf16[1024,768]{1,0:T(8,128)(2,1)} %copy-done.9, bf16[512,768]{1,0:T(8,128)(2,1)} %copy-done.16, bf16[2112,2176]{1,0:T(8,128)(2,1)} %all-gather.2.cloned.1.call-done.feed_ref.refs_3_), custom_call_target="tpu_custom_call" | custom-call | flops 1048576 | bytes 65536 | tf_op jit(solution)/shard_map/down/pallas_call | solution.py:453
  368.5 2.0 copy-done.5
  371.6 4.0 all-to-all-start.2
  375.6 7.2 %norm_two.1 = (f32[256,2048]{1,0:T(8,128)S(1)}, bf16[256,2048]{1,0:T(8,128)(2,1)S(1)}, bf16[256,16]{1,0:T(8,128)(2,1)S(1)}, bf16[256,16]{1,0:T(8,128)(2,1)S(1)},...) custom-call(s32[1]{0:T(128)S(6)} %copy.156.adapter_ref, bf16[256,2432]{1,0:T(8,128)(2,1)} %copy-done.11, ...), custom_call_target="tpu_custom_call" | custom-call | flops 1048576 | bytes 65536 | tf_op jit(solution)/shard_map/norm_two/pallas_call | solution.py:702
  384.4 7.1 %back.1.grad_ref = bf16[256,2048]{1,0:T(8,128)(2,1)S(1)} custom-call(bf16[256,2048]{1,0:T(8,128)(2,1)} %copy-done.15, bf16[2048,2048]{1,0:T(8,128)(2,1)} %get-tuple-element.277.w_ref, bf16[256,16]{1,0:T(8,128)(2,1)} %copy-done.23, bf16[16,2048]{1,0:T(8,128)(2,1)} %get-tuple-element.338.a_ref), custom_call_target="tpu_custom_call" | custom-call | flops 1048576 | bytes 65536 | tf_op jit(solution)/shard_map/back/pallas_call | solution.py:636
  391.5 13.0 %attend_back.1 = (bf16[256,2048]{1,0:T(8,128)(2,1)S(1)}, f32[256,512]{1,0:T(8,128)S(1)}, bf16[256,512]{1,0:T(8,128)(2,1)S(1)}) custom-call(bf16[256,2048]{1,0:T(8,128)(2,1)S(1)} %back.1.grad_ref, bf16[256,2048]{1,0:T(8,128)(2,1)S(1)} %copy-done.1, bf16[256,2048]{1,0:T(8,128)(2,1)S(1)} %query.1.query_ref, bf16[256,512]{1,0:T(8,128)(2,1)S(1)} %get-tuple-element.193.own_ref, ...), custom_call_target="tpu_custom_call" | custom-call | flops 1048576 | bytes 65536 | tf_op jit(solution)/shard_map/attend_back/pallas_call | solution.py:926
  406.4 1.9 collective-permute-start.49
  408.3 4.1 add_convert_fusion.9
  412.4 2.6 collective-permute-done.49.came_ref
  415.7 3.2 project_back.1
  423.0 6.0 %all-to-all-start.3 = ((bf16[32,16,592]{2,1,0:T(8,128)(2,1)}), bf16[32,16,592]{2,1,0:T(8,128)(2,1)S(1)}, u32[]{:S(2)}, u32[]{:S(2)}) async-start(bf16[32,16,592]{2,1,0:T(8,128)(2,1)} %bitcast.106), calls=%async_computation.3 | async-start | bytes 1310720 | tf_op jit(solution)/shard_map/all_to_all | solution.py:1170
  429.0 1.9 collective-permute-start.51
  430.9 1.5 collective-permute-start.52
  434.9 10.8 %norm_one.1 = (f32[256,2048]{1,0:T(8,128)}, f32[1,2048]{1,0:T(1,128)S(1)}) custom-call(bf16[256,2560]{1,0:T(8,128)(2,1)} %copy-done.10, bf16[2048,2560]{1,0:T(8,128)(2,1)} %get-tuple-element.190.w_ref, bf16[256,48]{1,0:T(8,128)(2,1)} %copy-done.22, bf16[48,2048]{1,0:T(8,128)(2,1)} %pad_maximum_fusion.6.a_ref, bf16[256,2048]{1,0:T(8,128)(2,1)} %bitcast.113, ...), custom_call_target="tpu_custom_call" | custom-call | flops 1048576 | bytes 65536 | tf_op jit(solution)/shard_map/norm_one/pallas_call | solution.py:786
  447.3 3.4 collective-permute-done.51
  450.9 3.4 add_convert_fusion.8
  458.6 4.7 all-to-all-start.4
  465.3 10.7 %collective-permute-done.54 = bf16[128,2048]{1,0:T(8,128)(2,1)} collective-permute-done((bf16[128,2048]{1,0:T(8,128)(2,1)}, bf16[128,2048]{1,0:T(8,128)(2,1)}, u32[]{:S(2)}, u32[]{:S(2)}) %collective-permute-start.54) | collective-permute-done | bytes 524320 | tf_op jit(solution)/shard_map/ppermute | solution.py:46
  476.2 2.6 convert_add_fusion.1
  478.8 2.2 fusion.2
  (349 shorter events, 97.0 us)
Async XLA Ops:
  7.3 41.0 %collective-permute-start.2 = (bf16[256,2048]{1,0:T(8,128)(2,1)}, bf16[256,2048]{1,0:T(8,128)(2,1)S(1)}, u32[]{:S(2)}, u32[]{:S(2)}) collective-permute-start(bf16[256,2048]{1,0:T(8,128)(2,1)} %bitcast.114), channel_id=1, source_target_pairs={{0,1},{1,0},{2,3},{3,2},{4,5},{5,4},{6,7},{7,6},{8,9},{9,8},{10,11... | collective-permute-start | bytes 3145736 | tf_op jit(solution)/shard_map/ppermute | solution.py:46
  10.3 38.0 %collective-permute-start.3 = (bf16[256,2048]{1,0:T(8,128)(2,1)}, bf16[256,2048]{1,0:T(8,128)(2,1)S(1)}, u32[]{:S(2)}, u32[]{:S(2)}) collective-permute-start(bf16[256,2048]{1,0:T(8,128)(2,1)} %bitcast.115), channel_id=1, source_target_pairs={{0,4},{1,5},{2,6},{3,7},{4,0},{5,1},{6,2},{7,3},{8,12},{9,13},{10,... | collective-permute-start | bytes 3145736 | tf_op jit(solution)/shard_map/ppermute | solution.py:46
  11.8 36.5 %collective-permute-start.4 = (bf16[256,2048]{1,0:T(8,128)(2,1)}, bf16[256,2048]{1,0:T(8,128)(2,1)}, u32[]{:S(2)}, u32[]{:S(2)}) collective-permute-start(bf16[256,2048]{1,0:T(8,128)(2,1)} %bitcast.116), channel_id=1, source_target_pairs={{0,2},{1,3},{2,0},{3,1},{4,6},{5,7},{6,4},{7,5},{8,10},{9,11},{10,... | collective-permute-start | bytes 3145736 | tf_op jit(solution)/shard_map/ppermute | solution.py:46
  15.3 28.6 %collective-permute-start = (bf16[64,4608]{1,0:T(8,128)(2,1)S(1)}, bf16[64,4608]{1,0:T(8,128)(2,1)}, u32[]{:S(2)}, u32[]{:S(2)}) collective-permute-start(bf16[64,4608]{1,0:T(8,128)(2,1)S(1)} %constant_dynamic-update-slice_fusion.11), channel_id=1, source_target_pairs={{0,8},{1,9},{2,10},{3,11},{4,12},{5,13},{6,14},{7,15},{8,0},{9,1},... | collective-permute-start | bytes 1769480 | tf_op jit(solution)/shard_map/ppermute | solution.py:46
  16.9 31.3 %collective-permute-start.1 = (bf16[64,4608]{1,0:T(8,128)(2,1)S(1)}, bf16[64,4608]{1,0:T(8,128)(2,1)}, u32[]{:S(2)}, u32[]{:S(2)}) collective-permute-start(bf16[64,4608]{1,0:T(8,128)(2,1)S(1)} %constant_dynamic-update-slice_fusion.11), channel_id=1, source_target_pairs={{0,16},{1,17},{2,18},{3,19},{4,20},{5,21},{6,22},{7,23},{8,24},{9,... | collective-permute-start | bytes 1769480 | tf_op jit(solution)/shard_map/ppermute | solution.py:46
  25.7 28.1 %all-to-all-start = ((bf16[32,4,1408]{2,1,0:T(4,128)(2,1)}), bf16[32,4,1408]{2,1,0:T(4,128)(2,1)S(1)}, u32[]{:S(2)}, u32[]{:S(2)}) async-start(bf16[32,4,1408]{2,1,0:T(4,128)(2,1)} %copy.117), calls=%async_computation | async-start | bytes 720896 | tf_op jit(solution)/shard_map/all_to_all | solution.py:1020
  28.3 234.1 %all-gather.2.cloned.1.call-start = ((), (), s32[]{:S(2)}) async-start(), calls=%async_computation.5 | async-start | bytes 11489280 | tf_op jit(solution)/shard_map/all_gather | solution.py:1032
  49.6 14.3 %collective-permute-start.5 = (bf16[64,4608]{1,0:T(8,128)(2,1)}, bf16[64,4608]{1,0:T(8,128)(2,1)}, u32[]{:S(2)}, u32[]{:S(2)}) collective-permute-start(bf16[64,4608]{1,0:T(8,128)(2,1)} %collective-permute-done.1), channel_id=1, source_target_pairs={{0,8},{1,9},{2,10},{3,11},{4,12},{5,13},{6,14},{7,15},{8,0},{9,1},... | collective-permute-start | bytes 1769480 | tf_op jit(solution)/shard_map/ppermute | solution.py:46
  68.0 40.0 %all-to-all-start.1 = ((bf16[32,16,640]{2,1,0:T(8,128)(2,1)}), bf16[32,16,640]{2,1,0:T(8,128)(2,1)S(1)}, u32[]{:S(2)}, u32[]{:S(2)}) async-start(bf16[32,16,640]{2,1,0:T(8,128)(2,1)} %broadcast_select_fusion), calls=%async_computation.1 | async-start | bytes 1310720 | tf_op jit(solution)/shard_map/all_to_all | solution.py:1028
  77.8 35.1 %collective-permute-start.6 = (bf16[4,64,2560]{2,1,0:T(8,128)(2,1)S(1)}, bf16[4,64,2560]{2,1,0:T(8,128)(2,1)}, u32[]{:S(2)}, u32[]{:S(2)}) collective-permute-start(bf16[4,64,2560]{2,1,0:T(8,128)(2,1)S(1)} %pad_maximum_fusion.1.refs_0_), channel_id=1, source_target_pairs={{0,1},{1,0},{2,3},{3,2},{4,5},{5,4},{6,7},{7,6},{8,9},{9,8},{10,11... | collective-permute-start | bytes 3932168 | tf_op jit(solution)/shard_map/ppermute | solution.py:46
  79.8 33.3 %collective-permute-start.7 = (bf16[4,64,2560]{2,1,0:T(8,128)(2,1)S(1)}, bf16[4,64,2560]{2,1,0:T(8,128)(2,1)}, u32[]{:S(2)}, u32[]{:S(2)}) collective-permute-start(bf16[4,64,2560]{2,1,0:T(8,128)(2,1)S(1)} %pad_maximum_fusion.1.refs_0_), channel_id=1, source_target_pairs={{0,4},{1,5},{2,6},{3,7},{4,0},{5,1},{6,2},{7,3},{8,12},{9,13},{10,... | collective-permute-start | bytes 3932168 | tf_op jit(solution)/shard_map/ppermute | solution.py:46
  81.2 31.8 %collective-permute-start.8 = (bf16[4,64,2560]{2,1,0:T(8,128)(2,1)S(1)}, bf16[4,64,2560]{2,1,0:T(8,128)(2,1)}, u32[]{:S(2)}, u32[]{:S(2)}) collective-permute-start(bf16[4,64,2560]{2,1,0:T(8,128)(2,1)S(1)} %pad_maximum_fusion.1.refs_0_), channel_id=1, source_target_pairs={{0,2},{1,3},{2,0},{3,1},{4,6},{5,7},{6,4},{7,5},{8,10},{9,11},{10,... | collective-permute-start | bytes 3932168 | tf_op jit(solution)/shard_map/ppermute | solution.py:46
  114.2 16.5 %collective-permute-start.10 = (bf16[2,64,2560]{2,1,0:T(8,128)(2,1)S(1)}, bf16[2,64,2560]{2,1,0:T(8,128)(2,1)S(1)}, u32[]{:S(2)}, u32[]{:S(2)}) collective-permute-start(bf16[2,64,2560]{2,1,0:T(8,128)(2,1)S(1)} %slice.335), channel_id=1, source_target_pairs={{0,1},{1,0},{2,3},{3,2},{4,5},{5,4},{6,7},{7,6},{8,9},{9,8},{10,11... | collective-permute-start | bytes 1966088 | tf_op jit(solution)/shard_map/ppermute | solution.py:46
  117.3 16.0 %collective-permute-start.9 = (bf16[2,64,2560]{2,1,0:T(8,128)(2,1)S(1)}, bf16[2,64,2560]{2,1,0:T(8,128)(2,1)S(1)}, u32[]{:S(2)}, u32[]{:S(2)}) collective-permute-start(bf16[2,64,2560]{2,1,0:T(8,128)(2,1)S(1)} %slice.334), channel_id=1, source_target_pairs={{0,4},{1,5},{2,6},{3,7},{4,0},{5,1},{6,2},{7,3},{8,12},{9,13},{10,... | collective-permute-start | bytes 1966088 | tf_op jit(solution)/shard_map/ppermute | solution.py:46
  133.4 2.2 collective-permute-start.13
  133.4 4.9 collective-permute-start.14
  133.9 7.4 %collective-permute-start.11 = (bf16[4,64,2560]{2,1,0:T(8,128)(2,1)}, bf16[4,64,2560]{2,1,0:T(8,128)(2,1)S(1)}, u32[]{:S(2)}, u32[]{:S(2)}) collective-permute-start(bf16[4,64,2560]{2,1,0:T(8,128)(2,1)} %collective-permute-done.6.refs_1_), channel_id=1, source_target_pairs={{0,2},{1,3},{2,0},{3,1},{4,6},{5,7},{6,4},{7,5},{8,10},{9,11},{10,... | collective-permute-start | bytes 3932168 | tf_op jit(solution)/shard_map/ppermute | solution.py:46
  134.0 7.4 %collective-permute-start.12 = (bf16[4,64,2560]{2,1,0:T(8,128)(2,1)}, bf16[4,64,2560]{2,1,0:T(8,128)(2,1)}, u32[]{:S(2)}, u32[]{:S(2)}) collective-permute-start(bf16[4,64,2560]{2,1,0:T(8,128)(2,1)} %collective-permute-done.7.refs_2_), channel_id=1, source_target_pairs={{0,2},{1,3},{2,0},{3,1},{4,6},{5,7},{6,4},{7,5},{8,10},{9,11},{10,... | collective-permute-start | bytes 3932168 | tf_op jit(solution)/shard_map/ppermute | solution.py:46
  134.4 44.2 %collective-permute-start.16 = (bf16[4,64,2048]{2,1,0:T(8,128)(2,1)S(1)}, bf16[4,64,2048]{2,1,0:T(8,128)(2,1)}, u32[]{:S(2)}, u32[]{:S(2)}) collective-permute-start(bf16[4,64,2048]{2,1,0:T(8,128)(2,1)S(1)} %copy-done.26), channel_id=1, source_target_pairs={{0,1},{1,0},{2,3},{3,2},{4,5},{5,4},{6,7},{7,6},{8,9},{9,8},{10,11... | collective-permute-start | bytes 3145736 | tf_op jit(solution)/shard_map/ppermute | solution.py:46
  135.5 43.1 %collective-permute-start.17 = (bf16[4,64,2048]{2,1,0:T(8,128)(2,1)S(1)}, bf16[4,64,2048]{2,1,0:T(8,128)(2,1)}, u32[]{:S(2)}, u32[]{:S(2)}) collective-permute-start(bf16[4,64,2048]{2,1,0:T(8,128)(2,1)S(1)} %copy-done.26), channel_id=1, source_target_pairs={{0,4},{1,5},{2,6},{3,7},{4,0},{5,1},{6,2},{7,3},{8,12},{9,13},{10,... | collective-permute-start | bytes 3145736 | tf_op jit(solution)/shard_map/ppermute | solution.py:46
  138.3 40.3 %collective-permute-start.18 = (bf16[4,64,2048]{2,1,0:T(8,128)(2,1)S(1)}, bf16[4,64,2048]{2,1,0:T(8,128)(2,1)}, u32[]{:S(2)}, u32[]{:S(2)}) collective-permute-start(bf16[4,64,2048]{2,1,0:T(8,128)(2,1)S(1)} %copy-done.26), channel_id=1, source_target_pairs={{0,2},{1,3},{2,0},{3,1},{4,6},{5,7},{6,4},{7,5},{8,10},{9,11},{10,... | collective-permute-start | bytes 3145736 | tf_op jit(solution)/shard_map/ppermute | solution.py:46
  152.8 12.4 %collective-permute-start.15 = (bf16[256,512]{1,0:T(8,128)(2,1)S(1)}, bf16[256,512]{1,0:T(8,128)(2,1)S(1)}, u32[]{:S(2)}, u32[]{:S(2)}) collective-permute-start(bf16[256,512]{1,0:T(8,128)(2,1)S(1)} %get-tuple-element.193.own_ref), channel_id=1, source_target_pairs={{0,1},{1,0},{2,3},{3,2},{4,5},{5,4},{6,7},{7,6},{8,9},{9,8},{10,11... | collective-permute-start | bytes 786440 | tf_op jit(solution)/shard_map/ppermute | solution.py:46
  180.1 13.2 %collective-permute-start.19 = (bf16[2,64,2048]{2,1,0:T(8,128)(2,1)S(1)}, bf16[2,64,2048]{2,1,0:T(8,128)(2,1)S(1)}, u32[]{:S(2)}, u32[]{:S(2)}) collective-permute-start(bf16[2,64,2048]{2,1,0:T(8,128)(2,1)S(1)} %slice.351), channel_id=1, source_target_pairs={{0,4},{1,5},{2,6},{3,7},{4,0},{5,1},{6,2},{7,3},{8,12},{9,13},{10,... | collective-permute-start | bytes 1572872 | tf_op jit(solution)/shard_map/ppermute | solution.py:46
  181.8 13.1 %collective-permute-start.20 = (bf16[2,64,2048]{2,1,0:T(8,128)(2,1)S(1)}, bf16[2,64,2048]{2,1,0:T(8,128)(2,1)}, u32[]{:S(2)}, u32[]{:S(2)}) collective-permute-start(bf16[2,64,2048]{2,1,0:T(8,128)(2,1)S(1)} %slice.352), channel_id=1, source_target_pairs={{0,1},{1,0},{2,3},{3,2},{4,5},{5,4},{6,7},{7,6},{8,9},{9,8},{10,11... | collective-permute-start | bytes 1572872 | tf_op jit(solution)/shard_map/ppermute | solution.py:46
  183.5 17.1 %collective-permute-start.21 = (bf16[4,64,2048]{2,1,0:T(8,128)(2,1)}, bf16[4,64,2048]{2,1,0:T(8,128)(2,1)S(1)}, u32[]{:S(2)}, u32[]{:S(2)}) collective-permute-start(bf16[4,64,2048]{2,1,0:T(8,128)(2,1)} %collective-permute-done.16.refs_1_), channel_id=1, source_target_pairs={{0,2},{1,3},{2,0},{3,1},{4,6},{5,7},{6,4},{7,5},{8,10},{9,11},{10,... | collective-permute-start | bytes 3145736 | tf_op jit(solution)/shard_map/ppermute | solution.py:46
  183.5 17.1 %collective-permute-start.22 = (bf16[4,64,2048]{2,1,0:T(8,128)(2,1)}, bf16[4,64,2048]{2,1,0:T(8,128)(2,1)}, u32[]{:S(2)}, u32[]{:S(2)}) collective-permute-start(bf16[4,64,2048]{2,1,0:T(8,128)(2,1)} %collective-permute-done.17.refs_2_), channel_id=1, source_target_pairs={{0,2},{1,3},{2,0},{3,1},{4,6},{5,7},{6,4},{7,5},{8,10},{9,11},{10,... | collective-permute-start | bytes 3145736 | tf_op jit(solution)/shard_map/ppermute | solution.py:46
  194.9 3.7 collective-permute-start.23
  194.9 5.8 %collective-permute-start.24 = (bf16[2,64,2048]{2,1,0:T(8,128)(2,1)}, bf16[2,64,2048]{2,1,0:T(8,128)(2,1)}, u32[]{:S(2)}, u32[]{:S(2)}) collective-permute-start(bf16[2,64,2048]{2,1,0:T(8,128)(2,1)} %collective-permute-done.20.refs_4_), channel_id=1, source_target_pairs={{0,2},{1,3},{2,0},{3,1},{4,6},{5,7},{6,4},{7,5},{8,10},{9,11},{10,... | collective-permute-start | bytes 1572872 | tf_op jit(solution)/shard_map/ppermute | solution.py:46
  196.2 17.4 %collective-permute-start.25 = (bf16[128,2048]{1,0:T(8,128)(2,1)}, bf16[128,2048]{1,0:T(8,128)(2,1)}, u32[]{:S(2)}, u32[]{:S(2)}) collective-permute-start(bf16[128,2048]{1,0:T(8,128)(2,1)} %slice.356), channel_id=1, source_target_pairs={{0,4},{1,5},{2,6},{3,7},{4,0},{5,1},{6,2},{7,3},{8,12},{9,13},{10,... | collective-permute-start | bytes 1572872 | tf_op jit(solution)/shard_map/ppermute | solution.py:46
  199.4 14.2 %collective-permute-start.26 = (bf16[128,2048]{1,0:T(8,128)(2,1)}, bf16[128,2048]{1,0:T(8,128)(2,1)}, u32[]{:S(2)}, u32[]{:S(2)}) collective-permute-start(bf16[128,2048]{1,0:T(8,128)(2,1)} %slice.357), channel_id=1, source_target_pairs={{0,1},{1,0},{2,3},{3,2},{4,5},{5,4},{6,7},{7,6},{8,9},{9,8},{10,11... | collective-permute-start | bytes 1572872 | tf_op jit(solution)/shard_map/ppermute | solution.py:46
  213.6 67.3 %copy-start.12 = (bf16[256,2176]{1,0:T(8,128)(2,1)}, bf16[256,2176]{1,0:T(8,128)(2,1)S(1)}, u32[]{:S(2)}) copy-start(bf16[256,2176]{1,0:T(8,128)(2,1)S(1)} %get-tuple-element.215.refs_0_) | copy-start | bytes 3342340
  213.6 26.4 %collective-permute-start.27 = (bf16[256,2176]{1,0:T(8,128)(2,1)S(1)}, bf16[256,2176]{1,0:T(8,128)(2,1)S(1)}, u32[]{:S(2)}, u32[]{:S(2)}) collective-permute-start(bf16[256,2176]{1,0:T(8,128)(2,1)S(1)} %get-tuple-element.215.refs_0_), channel_id=1, source_target_pairs={{0,1},{1,0},{2,3},{3,2},{4,5},{5,4},{6,7},{7,6},{8,9},{9,8},{10,11... | collective-permute-start | bytes 3342344 | tf_op jit(solution)/shard_map/ppermute | solution.py:46
  215.1 25.6 %collective-permute-start.28 = (bf16[256,2176]{1,0:T(8,128)(2,1)S(1)}, bf16[256,2176]{1,0:T(8,128)(2,1)S(1)}, u32[]{:S(2)}, u32[]{:S(2)}) collective-permute-start(bf16[256,2176]{1,0:T(8,128)(2,1)S(1)} %get-tuple-element.215.refs_0_), channel_id=1, source_target_pairs={{0,4},{1,5},{2,6},{3,7},{4,0},{5,1},{6,2},{7,3},{8,12},{9,13},{10,... | collective-permute-start | bytes 3342344 | tf_op jit(solution)/shard_map/ppermute | solution.py:46
  215.6 25.1 %collective-permute-start.29 = (bf16[256,2176]{1,0:T(8,128)(2,1)S(1)}, bf16[256,2176]{1,0:T(8,128)(2,1)S(1)}, u32[]{:S(2)}, u32[]{:S(2)}) collective-permute-start(bf16[256,2176]{1,0:T(8,128)(2,1)S(1)} %get-tuple-element.215.refs_0_), channel_id=1, source_target_pairs={{0,2},{1,3},{2,0},{3,1},{4,6},{5,7},{6,4},{7,5},{8,10},{9,11},{10,... | collective-permute-start | bytes 3342344 | tf_op jit(solution)/shard_map/ppermute | solution.py:46
  215.6 26.7 %collective-permute-start.34 = (bf16[256,2048]{1,0:T(8,128)(2,1)S(1)}, bf16[256,2048]{1,0:T(8,128)(2,1)S(1)}, u32[]{:S(2)}, u32[]{:S(2)}) collective-permute-start(bf16[256,2048]{1,0:T(8,128)(2,1)S(1)} %copy-done.33), channel_id=1, source_target_pairs={{0,2},{1,3},{2,0},{3,1},{4,6},{5,7},{6,4},{7,5},{8,10},{9,11},{10,... | collective-permute-start | bytes 3145736 | tf_op jit(solution)/shard_map/ppermute | solution.py:46
  216.2 27.1 %collective-permute-start.35 = (bf16[256,2048]{1,0:T(8,128)(2,1)S(1)}, bf16[256,2048]{1,0:T(8,128)(2,1)S(1)}, u32[]{:S(2)}, u32[]{:S(2)}) collective-permute-start(bf16[256,2048]{1,0:T(8,128)(2,1)S(1)} %copy-done.36), channel_id=1, source_target_pairs={{0,2},{1,3},{2,0},{3,1},{4,6},{5,7},{6,4},{7,5},{8,10},{9,11},{10,... | collective-permute-start | bytes 3145736 | tf_op jit(solution)/shard_map/ppermute | solution.py:46
  241.8 16.3 %collective-permute-start.32 = (bf16[256,2176]{1,0:T(8,128)(2,1)S(1)}, bf16[256,2176]{1,0:T(8,128)(2,1)S(1)}, u32[]{:S(2)}, u32[]{:S(2)}) collective-permute-start(bf16[256,2176]{1,0:T(8,128)(2,1)S(1)} %collective-permute-done.27.refs_0_), channel_id=1, source_target_pairs={{0,2},{1,3},{2,0},{3,1},{4,6},{5,7},{6,4},{7,5},{8,10},{9,11},{10,... | collective-permute-start | bytes 3342344 | tf_op jit(solution)/shard_map/ppermute | solution.py:46
  241.8 16.3 %collective-permute-start.33 = (bf16[256,2176]{1,0:T(8,128)(2,1)S(1)}, bf16[256,2176]{1,0:T(8,128)(2,1)S(1)}, u32[]{:S(2)}, u32[]{:S(2)}) collective-permute-start(bf16[256,2176]{1,0:T(8,128)(2,1)S(1)} %collective-permute-done.28.refs_2_), channel_id=1, source_target_pairs={{0,2},{1,3},{2,0},{3,1},{4,6},{5,7},{6,4},{7,5},{8,10},{9,11},{10,... | collective-permute-start | bytes 3342344 | tf_op jit(solution)/shard_map/ppermute | solution.py:46
  242.3 4.0 collective-permute-start.36
  242.4 15.1 %collective-permute-start.30 = (bf16[128,2176]{1,0:T(8,128)(2,1)S(1)}, bf16[128,2176]{1,0:T(8,128)(2,1)S(1)}, u32[]{:S(2)}, u32[]{:S(2)}) collective-permute-start(bf16[128,2176]{1,0:T(8,128)(2,1)S(1)} %slice.358), channel_id=1, source_target_pairs={{0,4},{1,5},{2,6},{3,7},{4,0},{5,1},{6,2},{7,3},{8,12},{9,13},{10,... | collective-permute-start | bytes 1671176 | tf_op jit(solution)/shard_map/ppermute | solution.py:46
  243.3 14.8 %collective-permute-start.31 = (bf16[128,2176]{1,0:T(8,128)(2,1)S(1)}, bf16[128,2176]{1,0:T(8,128)(2,1)S(1)}, u32[]{:S(2)}, u32[]{:S(2)}) collective-permute-start(bf16[128,2176]{1,0:T(8,128)(2,1)S(1)} %slice.359), channel_id=1, source_target_pairs={{0,1},{1,0},{2,3},{3,2},{4,5},{5,4},{6,7},{7,6},{8,9},{9,8},{10,11... | collective-permute-start | bytes 1671176 | tf_op jit(solution)/shard_map/ppermute | solution.py:46
  246.2 2.1 collective-permute-start.37
  259.3 2.0 collective-permute-start.38
  260.2 2.1 collective-permute-start.39
  281.8 32.4 %collective-permute-start.40 = (bf16[256,2432]{1,0:T(8,128)(2,1)S(1)}, bf16[256,2432]{1,0:T(8,128)(2,1)S(1)}, u32[]{:S(2)}, u32[]{:S(2)}) collective-permute-start(bf16[256,2432]{1,0:T(8,128)(2,1)S(1)} %get-tuple-element.235), channel_id=1, source_target_pairs={{0,2},{1,3},{2,0},{3,1},{4,6},{5,7},{6,4},{7,5},{8,10},{9,11},{10,... | collective-permute-start | bytes 3735560 | tf_op jit(solution)/shard_map/ppermute | solution.py:46
  315.4 4.7 collective-permute-start.41
  315.8 25.8 %collective-permute-start.42 = (bf16[128,2432]{1,0:T(8,128)(2,1)S(1)}, bf16[128,2432]{1,0:T(8,128)(2,1)S(1)}, u32[]{:S(2)}, u32[]{:S(2)}) collective-permute-start(bf16[128,2432]{1,0:T(8,128)(2,1)S(1)} %get-tuple-element.245), channel_id=1, source_target_pairs={{0,1},{1,0},{2,3},{3,2},{4,5},{5,4},{6,7},{7,6},{8,9},{9,8},{10,11... | collective-permute-start | bytes 1867784 | tf_op jit(solution)/shard_map/ppermute | solution.py:46
  317.1 24.5 %collective-permute-start.43 = (bf16[128,2432]{1,0:T(8,128)(2,1)S(1)}, bf16[128,2432]{1,0:T(8,128)(2,1)S(1)}, u32[]{:S(2)}, u32[]{:S(2)}) collective-permute-start(bf16[128,2432]{1,0:T(8,128)(2,1)S(1)} %get-tuple-element.246), channel_id=1, source_target_pairs={{0,4},{1,5},{2,6},{3,7},{4,0},{5,1},{6,2},{7,3},{8,12},{9,13},{10,... | collective-permute-start | bytes 1867784 | tf_op jit(solution)/shard_map/ppermute | solution.py:46
  320.4 24.8 %collective-permute-start.44 = (bf16[128,2432]{1,0:T(8,128)(2,1)S(1)}, bf16[128,2432]{1,0:T(8,128)(2,1)S(1)}, u32[]{:S(2)}, u32[]{:S(2)}) collective-permute-start(bf16[128,2432]{1,0:T(8,128)(2,1)S(1)} %get-tuple-element.247), channel_id=1, source_target_pairs={{0,1},{1,0},{2,3},{3,2},{4,5},{5,4},{6,7},{7,6},{8,9},{9,8},{10,11... | collective-permute-start | bytes 1867784 | tf_op jit(solution)/shard_map/ppermute | solution.py:46
  321.8 24.4 %collective-permute-start.45 = (bf16[128,2432]{1,0:T(8,128)(2,1)S(1)}, bf16[128,2432]{1,0:T(8,128)(2,1)S(1)}, u32[]{:S(2)}, u32[]{:S(2)}) collective-permute-start(bf16[128,2432]{1,0:T(8,128)(2,1)S(1)} %get-tuple-element.248), channel_id=1, source_target_pairs={{0,4},{1,5},{2,6},{3,7},{4,0},{5,1},{6,2},{7,3},{8,12},{9,13},{10,... | collective-permute-start | bytes 1867784 | tf_op jit(solution)/shard_map/ppermute | solution.py:46
  341.5 29.0 %collective-permute-start.46 = (bf16[256,2432]{1,0:T(8,128)(2,1)}, bf16[256,2432]{1,0:T(8,128)(2,1)S(1)}, u32[]{:S(2)}, u32[]{:S(2)}) collective-permute-start(bf16[256,2432]{1,0:T(8,128)(2,1)} %get-tuple-element.251), channel_id=1, source_target_pairs={{0,2},{1,3},{2,0},{3,1},{4,6},{5,7},{6,4},{7,5},{8,10},{9,11},{10,... | collective-permute-start | bytes 3735560 | tf_op jit(solution)/shard_map/ppermute | solution.py:46
  347.8 22.7 %collective-permute-start.47 = (bf16[128,2432]{1,0:T(8,128)(2,1)}, bf16[128,2432]{1,0:T(8,128)(2,1)}, u32[]{:S(2)}, u32[]{:S(2)}) collective-permute-start(bf16[128,2432]{1,0:T(8,128)(2,1)} %get-tuple-element.257), channel_id=1, source_target_pairs={{0,4},{1,5},{2,6},{3,7},{4,0},{5,1},{6,2},{7,3},{8,12},{9,13},{10,... | collective-permute-start | bytes 1867784 | tf_op jit(solution)/shard_map/ppermute | solution.py:46
  348.7 21.9 %collective-permute-start.48 = (bf16[128,2432]{1,0:T(8,128)(2,1)}, bf16[128,2432]{1,0:T(8,128)(2,1)}, u32[]{:S(2)}, u32[]{:S(2)}) collective-permute-start(bf16[128,2432]{1,0:T(8,128)(2,1)} %get-tuple-element.258), channel_id=1, source_target_pairs={{0,1},{1,0},{2,3},{3,2},{4,5},{5,4},{6,7},{7,6},{8,9},{9,8},{10,11... | collective-permute-start | bytes 1867784 | tf_op jit(solution)/shard_map/ppermute | solution.py:46
  370.5 37.7 %collective-permute-start.50 = (bf16[1024,2048]{1,0:T(8,128)(2,1)}, bf16[1024,2048]{1,0:T(8,128)(2,1)}, u32[]{:S(2)}, u32[]{:S(2)}) collective-permute-start(bf16[1024,2048]{1,0:T(8,128)(2,1)} %get-tuple-element.289), channel_id=1, source_target_pairs={{0,2},{1,3},{2,0},{3,1},{4,6},{5,7},{6,4},{7,5},{8,10},{9,11},{10,... | collective-permute-start | bytes 12582920 | tf_op jit(solution)/shard_map/ppermute | solution.py:46
  371.6 34.8 %all-to-all-start.2 = ((bf16[32,4,2304]{2,1,0:T(4,128)(2,1)}), bf16[32,4,2304]{2,1,0:T(4,128)(2,1)S(1)}, u32[]{:S(2)}, u32[]{:S(2)}) async-start(bf16[32,4,2304]{2,1,0:T(4,128)(2,1)} %pad_maximum_fusion.4), calls=%async_computation.2 | async-start | bytes 1179648 | tf_op jit(solution)/shard_map/all_to_all | solution.py:1138
  406.4 8.6 %collective-permute-start.49 = (bf16[256,512]{1,0:T(8,128)(2,1)S(1)}, bf16[256,512]{1,0:T(8,128)(2,1)S(1)}, u32[]{:S(2)}, u32[]{:S(2)}) collective-permute-start(bf16[256,512]{1,0:T(8,128)(2,1)S(1)} %get-tuple-element.287), channel_id=1, source_target_pairs={{0,1},{1,0},{2,3},{3,2},{4,5},{5,4},{6,7},{7,6},{8,9},{9,8},{10,11... | collective-permute-start | bytes 786440 | tf_op jit(solution)/shard_map/ppermute | solution.py:46
  423.0 33.1 %all-to-all-start.3 = ((bf16[32,16,592]{2,1,0:T(8,128)(2,1)}), bf16[32,16,592]{2,1,0:T(8,128)(2,1)S(1)}, u32[]{:S(2)}, u32[]{:S(2)}) async-start(bf16[32,16,592]{2,1,0:T(8,128)(2,1)} %bitcast.106), calls=%async_computation.3 | async-start | bytes 1310720 | tf_op jit(solution)/shard_map/all_to_all | solution.py:1170
  429.0 21.7 %collective-permute-start.51 = (bf16[128,2048]{1,0:T(8,128)(2,1)S(1)}, bf16[128,2048]{1,0:T(8,128)(2,1)}, u32[]{:S(2)}, u32[]{:S(2)}) collective-permute-start(bf16[128,2048]{1,0:T(8,128)(2,1)S(1)} %copy-done.55), channel_id=1, source_target_pairs={{0,1},{1,0},{2,3},{3,2},{4,5},{5,4},{6,7},{7,6},{8,9},{9,8},{10,11... | collective-permute-start | bytes 1572872 | tf_op jit(solution)/shard_map/ppermute | solution.py:46
  430.9 20.0 %collective-permute-start.52 = (bf16[128,2048]{1,0:T(8,128)(2,1)S(1)}, bf16[128,2048]{1,0:T(8,128)(2,1)}, u32[]{:S(2)}, u32[]{:S(2)}) collective-permute-start(bf16[128,2048]{1,0:T(8,128)(2,1)S(1)} %copy-done.54), channel_id=1, source_target_pairs={{0,4},{1,5},{2,6},{3,7},{4,0},{5,1},{6,2},{7,3},{8,12},{9,13},{10,... | collective-permute-start | bytes 1572872 | tf_op jit(solution)/shard_map/ppermute | solution.py:46
  446.4 18.9 %collective-permute-start.53 = (bf16[128,2048]{1,0:T(8,128)(2,1)}, bf16[128,2048]{1,0:T(8,128)(2,1)}, u32[]{:S(2)}, u32[]{:S(2)}) collective-permute-start(bf16[128,2048]{1,0:T(8,128)(2,1)} %get-tuple-element.310), channel_id=1, source_target_pairs={{0,1},{1,0},{2,3},{3,2},{4,5},{5,4},{6,7},{7,6},{8,9},{9,8},{10,11... | collective-permute-start | bytes 1572872 | tf_op jit(solution)/shard_map/ppermute | solution.py:46
  447.0 18.3 %collective-permute-start.55 = (bf16[128,2048]{1,0:T(8,128)(2,1)}, bf16[128,2048]{1,0:T(8,128)(2,1)}, u32[]{:S(2)}, u32[]{:S(2)}) collective-permute-start(bf16[128,2048]{1,0:T(8,128)(2,1)} %get-tuple-element.312), channel_id=1, source_target_pairs={{0,4},{1,5},{2,6},{3,7},{4,0},{5,1},{6,2},{7,3},{8,12},{9,13},{10,... | collective-permute-start | bytes 1572872 | tf_op jit(solution)/shard_map/ppermute | solution.py:46
  454.3 21.7 %collective-permute-start.54 = (bf16[128,2048]{1,0:T(8,128)(2,1)}, bf16[128,2048]{1,0:T(8,128)(2,1)}, u32[]{:S(2)}, u32[]{:S(2)}) collective-permute-start(bf16[128,2048]{1,0:T(8,128)(2,1)} %get-tuple-element.321), channel_id=1, source_target_pairs={{0,4},{1,5},{2,6},{3,7},{4,0},{5,1},{6,2},{7,3},{8,12},{9,13},{10,... | collective-permute-start | bytes 1572872 | tf_op jit(solution)/shard_map/ppermute | solution.py:46
  455.5 20.7 %collective-permute-start.56 = (bf16[128,2048]{1,0:T(8,128)(2,1)}, bf16[128,2048]{1,0:T(8,128)(2,1)}, u32[]{:S(2)}, u32[]{:S(2)}) collective-permute-start(bf16[128,2048]{1,0:T(8,128)(2,1)} %get-tuple-element.322), channel_id=1, source_target_pairs={{0,1},{1,0},{2,3},{3,2},{4,5},{5,4},{6,7},{7,6},{8,9},{9,8},{10,11... | collective-permute-start | bytes 1572872 | tf_op jit(solution)/shard_map/ppermute | solution.py:46
  458.6 22.5 %all-to-all-start.4 = ((f32[32,4,720]{2,1,0:T(4,128)}), f32[32,4,720]{2,1,0:T(4,128)S(1)}, u32[]{:S(2)}, u32[]{:S(2)}) async-start(f32[32,4,720]{2,1,0:T(4,128)} %pad_maximum_fusion.5), calls=%async_computation.4 | async-start | bytes 786432 | tf_op jit(solution)/shard_map/all_to_all | solution.py:1184
  (72 other events, 566.3 us)
Sparse Core Ops, SparseCore 0:
  64.1 174.2 all-gather.1

commit v4 on v3

--- a/solution.py
+++ b/solution.py
@@ -217,10 +217,13 @@
         self.last_far = [exchange(v, C, self.n) for v in self.last]
 
     def group(self, *which):
-        parts = {0: [self.own, self.near[2]], 3: self.last + self.last_far}
-        for g in (1, 2):
-            parts[g] = [self.near[g - 1], self.far[g - 1]]
-        return [part for g in which for part in parts[g]]
+        parts = []
+        for g in which:
+            if g == 3:
+                parts += [*self.last, *self.last_far]
+            else:
+                parts += [self.near[g - 1], self.far[g - 1]] if g else [self.own, self.near[2]]
+        return parts
 
 
 class Order:
@@ -1095,12 +1098,8 @@
     normed_plane = Plane(normed_ext, n)
     normed_plane.near = order.point(*normed_plane.near)
     normed_plane.end()
-    passed = order.point(
-        *normed_plane.last, *normed_plane.far, *cot_plane.far, *cot_plane.last_far
-    )
-    normed_plane.last, normed_plane.far = passed[:2], passed[2:4]
-    cot_plane.far, cot_plane.last_far = passed[4:6], passed[6:]
-    normed_plane.finish()
+    passed = order.point(*normed_plane.far, *cot_plane.far, *cot_plane.last_far)
+    normed_plane.far, cot_plane.far, cot_plane.last_far = passed[:2], passed[2:4], passed[4:]
     feed_of = lambda ids_here, place, groups: feed_stage(
         ids_here,
         place,
@@ -1111,20 +1110,18 @@
         padded,
         slot,
     )
-    hidden_far, grads_far, near_out, far_out = feed_of(plane_ids, 2, (3,))
     normed_sum = PlaneSum(n)
-    normed_sum.put(3, near_out, exchange(far_out, C, n))
-    ids_mid, near_out = order.point(plane_ids, near_out)
-    hidden_mid, grads_mid, near_out, far_out = feed_of(ids_mid, 0, (1, 2))
-    far_sends = normed_sum.far_sends()
-    near_out, far_out, *far_sends = order.point(near_out, far_out, *far_sends)
-    far_came = normed_sum.hop(*far_sends)
+    hidden_mid, grads_mid, near_out, far_out = feed_of(plane_ids, 0, (1, 2))
     mid_recv = exchange(far_out, C, n)
+    near_out, *normed_plane.last = order.point(near_out, *normed_plane.last)
     for j in range(2):
         part = slice(j * rows, (j + 1) * rows)
         normed_sum.put(j + 1, near_out[part], mid_recv[part])
-    ids_own, *near_sends = order.point(plane_ids, *normed_sum.near_sends())
-    near_came = normed_sum.hop(*near_sends)
+    normed_plane.finish()
+    hidden_far, grads_far, near_out, far_out = feed_of(plane_ids, 2, (3,))
+    normed_sum.put(3, near_out, exchange(far_out, C, n))
+    ids_own, *sends = order.point(plane_ids, *normed_sum.far_sends(), *normed_sum.near_sends())
+    far_came, near_came = normed_sum.hop(*sends[:2]), normed_sum.hop(*sends[2:])
     hidden_own, grads_own, near_out, far_out = feed_of(ids_own, 0, (0,))
     recv = exchange(far_out, C, n)
     near_out, grads_own, *came = order.point(near_out, grads_own, *far_came, *near_came)

time: 497 us -> 492 us (0.990)
  waiting for transfers between devices: 145 us -> 140 us
    unnamed x160 -> x156, local copies, waits for them, and re-layouts: 28.7 us -> 26.4 us
  transfers between devices with their start and end apart: 63 -> 63, of which waited for: 29 -> 27; matrix products, arithmetic and copies ran while one was open for 14% -> 15% of each run, Pallas kernels for 29% -> 33%
where the time goes in v4:
time: 492 us; the launch traced here: 486 us
  Pallas kernels  163 us (33%)
  waiting for transfers between devices  140 us (28%)
  starting transfers between devices  67.8 us (14%)
  local copies, waits for them, and re-layouts  64.1 us (13%)
  other arithmetic  32 us (7%)
  between operations  16.8 us (3%)
    ppermute x57, waiting for transfers between devices, exchange(): return lax.ppermute(value, ALL, [(i, i ^ mask) for i in range(n)])  115 us
    pallas_call x3, Pallas kernels, feed_stage(): pl.pallas_call(functools.partial(feed_kernel, (len(normed), padded, slot,...  69.9 us
    ppermute x57, starting transfers between devices, exchange(): return lax.ppermute(value, ALL, [(i, i ^ mask) for i in range(n)])  45.9 us
    unnamed x156, local copies, waits for them, and re-layouts  26.4 us
    all_to_all x1, waiting for transfers between devices, per_device(): own = lax.all_to_all(jnp.take(columns, ids, axis=0), ALL, 0, 0, tiled=True)  23.6 us
    pallas_call x1, Pallas kernels, attend_stage(): pl.pallas_call(attend_kernel, grid=(KV_HEADS,), out_shape=(jax.ShapeDtype...  13.4 us
    pallas_call x1, Pallas kernels, attend_back_stage(): pl.pallas_call(attend_back_kernel, grid=(KV_HEADS,), out_shape=(jax.Shape...  13 us
    pallas_call x1, Pallas kernels, down_stage(): pl.pallas_call(functools.partial(down_kernel, padded, slot), grid=(1,), o...  12.3 us
  transfers between devices with their start and end apart: 63, of which 27 were waited for; matrix products, arithmetic and copies ran while one was open for 15% of the time, Pallas kernels for 33%

profile of v4, /device:TPU:0, one launch (start us, length us, event | category | flops | bytes accessed | tf_op | source)
XLA Modules:
  0.0 486.4 jit_solution(14581271571044167266)
XLA Ops:
  7.3 3.0 collective-permute-start.2
  10.3 1.5 collective-permute-start.3
  15.3 1.6 collective-permute-start
  16.9 2.6 collective-permute-start.1
  25.7 2.6 all-to-all-start
  28.3 15.5 %collective-permute-done = bf16[64,4608]{1,0:T(8,128)(2,1)} collective-permute-done((bf16[64,4608]{1,0:T(8,128)(2,1)S(1)}, bf16[64,4608]{1,0:T(8,128)(2,1)}, u32[]{:S(2)}, u32[]{:S(2)}) %collective-permute-start) | collective-permute-done | bytes 589856 | tf_op jit(solution)/shard_map/ppermute | solution.py:46
  43.8 4.4 collective-permute-done.1
  52.1 1.6 all-to-all-done
  54.2 2.7 pad_maximum_fusion
  56.9 7.0 %collective-permute-done.5 = bf16[64,4608]{1,0:T(8,128)(2,1)} collective-permute-done((bf16[64,4608]{1,0:T(8,128)(2,1)}, bf16[64,4608]{1,0:T(8,128)(2,1)}, u32[]{:S(2)}, u32[]{:S(2)}) %collective-permute-start.5) | collective-permute-done | bytes 589856 | tf_op jit(solution)/shard_map/ppermute | solution.py:46
  68.0 4.1 all-to-all-start.1
  72.8 2.7 pad_add_fusion.1.ids_ref
  77.8 1.9 collective-permute-start.6
  79.8 1.5 collective-permute-start.7
  84.4 23.6 %all-to-all-done.1 = bf16[32,16,640]{2,1,0:T(8,128)(2,1)S(1)} async-done(((bf16[32,16,640]{2,1,0:T(8,128)(2,1)}), bf16[32,16,640]{2,1,0:T(8,128)(2,1)S(1)}, u32[]{:S(2)}, u32[]{:S(2)}) %all-to-all-start.1) | async-done | bytes 655392 | tf_op jit(solution)/shard_map/all_to_all | solution.py:1031
  111.2 1.8 fusion.29
  114.3 1.9 collective-permute-start.10
  117.3 1.4 collective-permute-start.9
  120.8 9.9 %collective-permute-done.10.refs_4_ = bf16[2,64,2560]{2,1,0:T(8,128)(2,1)S(1)} collective-permute-done((bf16[2,64,2560]{2,1,0:T(8,128)(2,1)S(1)}, bf16[2,64,2560]{2,1,0:T(8,128)(2,1)S(1)}, u32[]{:S(2)}, u32[]{:S(2)}) %collective-permute-start.10) | collective-permute-done | bytes 655392 | tf_op jit(solution)/shard_map/ppermute | solution.py:46
  130.8 2.6 collective-permute-done.9.refs_3_
  136.7 1.7 collective-permute-done.14.refs_9_
  142.4 10.3 %project.1 = (bf16[256,2048]{1,0:T(8,128)(2,1)S(1)}, bf16[256,48]{1,0:T(8,128)(2,1)S(1)}, bf16[256,512]{1,0:T(8,128)(2,1)S(1)}, bf16[2048,2560]{1,0:T(8,128)(2,1)}) custom-call(s32[1]{0:T(128)} %bitcast.me_ref, bf16[256,2048]{1,0:T(8,128)(2,1)} %bitcast.111, f32[1,2048]{1,0:T(1,128)} %reshape.223.gain_ref, bf16[48,2048]{1,0:T(8,128)(2,1)} %pad_maximum_fusion.6.a_ref, ...), custom_call_target="tpu_custom_call" | custom-call | flops 1048576 | bytes 65536 | tf_op jit(solution)/shard_map/project/pallas_call | solution.py:522
  154.6 6.5 %query.1.query_ref = bf16[256,2048]{1,0:T(8,128)(2,1)S(1)} custom-call(bf16[256,2048]{1,0:T(8,128)(2,1)S(1)} %get-tuple-element.185.normed_ref, bf16[256,48]{1,0:T(8,128)(2,1)S(1)} %get-tuple-element.186.low_ref, bf16[16,2048]{1,0:T(8,128)(2,1)S(1)} %get-tuple-element.333.b_ref.bq_ref, bf16[2048,2560]{1,0:T(8,128)(2,1)} %get-tuple-element.187.w_ref, ...), custom_call_target="tpu_custom_call" | custom-call | flops 1048576 | bytes 65536 | tf_op jit(solution)/shard_map/query/pallas_call | solution.py:554
  161.2 4.0 collective-permute-done.15.other_ref
  165.2 13.4 %attend.1 = (bf16[256,2048]{1,0:T(8,128)(2,1)S(1)}, bf16[4,8,512,256]{3,2,1,0:T(8,128)(2,1)}) custom-call(s32[2]{0:T(128)S(1)} %pad_add_fusion.pos_ref, bf16[256,2048]{1,0:T(8,128)(2,1)S(1)} %query.1.query_ref, bf16[256,512]{1,0:T(8,128)(2,1)S(1)} %get-tuple-element.190.own_ref, bf16[256,512]{1,0:T(8,128)(2,1)S(1)} %collective-permute-done.15.other_ref), custom_call_target="tpu_custom_call" | custom-call | flops 1048576 | bytes 65536 | tf_op jit(solution)/shard_map/attend/pallas_call | solution.py:851
  178.7 1.5 slice.351
  182.0 1.7 collective-permute-start.20
  184.1 9.3 %collective-permute-done.19.refs_3_ = bf16[2,64,2048]{2,1,0:T(8,128)(2,1)S(1)} collective-permute-done((bf16[2,64,2048]{2,1,0:T(8,128)(2,1)S(1)}, bf16[2,64,2048]{2,1,0:T(8,128)(2,1)S(1)}, u32[]{:S(2)}, u32[]{:S(2)}) %collective-permute-start.19) | collective-permute-done | bytes 524320 | tf_op jit(solution)/shard_map/ppermute | solution.py:46
  193.4 1.6 collective-permute-done.20.refs_4_
  201.7 9.0 %output.1 = (f32[256,2048]{1,0:T(8,128)S(1)}, bf16[256,2048]{1,0:T(8,128)(2,1)S(1)}, bf16[256,16]{1,0:T(8,128)(2,1)S(1)}, bf16[256,2176]{1,0:T(8,128)(2,1)S(1)}, bf16[2048,2048]{1,0:T(8,128)(2,1)}) custom-call(s32[1]{0:T(128)} %bitcast.me_ref, bf16[256,2048]{1,0:T(8,128)(2,1)} %copy-done, bf16[16,2048]{1,0:T(8,128)(2,1)} %get-tuple-element.332.a_ref, ...), custom_call_target="tpu_custom_call" | custom-call | flops 1048576 | bytes 65536 | tf_op jit(solution)/shard_map/output/pallas_call | solution.py:609
  213.7 1.5 collective-permute-start.27
  216.4 23.7 %collective-permute-done.27.refs_0_ = bf16[256,2176]{1,0:T(8,128)(2,1)S(1)} collective-permute-done((bf16[256,2176]{1,0:T(8,128)(2,1)S(1)}, bf16[256,2176]{1,0:T(8,128)(2,1)S(1)}, u32[]{:S(2)}, u32[]{:S(2)}) %collective-permute-start.27) | collective-permute-done | bytes 1114144 | tf_op jit(solution)/shard_map/ppermute | solution.py:46
  245.5 1.6 collective-permute-done.34.refs_6_
  247.2 2.0 collective-permute-done.35.refs_7_
  251.0 32.9 %feed.3 = (bf16[1024,768]{1,0:T(8,128)(2,1)S(1)}, f32[3,128,768]{2,1,0:T(8,128)S(1)}, bf16[512,2432]{1,0:T(8,128)(2,1)S(1)}, bf16[512,2432]{1,0:T(8,128)(2,1)S(1)}) custom-call(s32[4]{0:T(128)S(1)} %pad_add_fusion.1.ids_ref, bf16[2112,2176]{1,0:T(8,128)(2,1)} %all-gather.2.cloned.1.call-done.feed_ref.refs_3_, bf16[256,2176]{1,0:T(8,128)(2,1)} %copy-done.29, ...), custom_call_target="tpu_custom_call" | custom-call | flops 1048576 | bytes 65536 | tf_op jit(solution)/shard_map/feed/pallas_call | solution.py:402
  284.7 1.5 collective-permute-done.38.refs_2_
  286.2 1.6 collective-permute-done.39.refs_3_
  288.6 18.1 %feed.4 = (bf16[512,768]{1,0:T(8,128)(2,1)S(1)}, f32[3,128,768]{2,1,0:T(8,128)S(1)}, bf16[256,2432]{1,0:T(8,128)(2,1)S(1)}, bf16[256,2432]{1,0:T(8,128)(2,1)S(1)}) custom-call(s32[4]{0:T(128)S(1)} %pad_add_fusion.1.ids_ref, bf16[2112,2176]{1,0:T(8,128)(2,1)} %all-gather.2.cloned.1.call-done.feed_ref.refs_3_, ...), custom_call_target="tpu_custom_call" | custom-call | flops 1048576 | bytes 65536 | tf_op jit(solution)/shard_map/feed/pallas_call | solution.py:402
  306.9 2.8 collective-permute-done.40
  314.4 18.9 %feed.5 = (bf16[512,768]{1,0:T(8,128)(2,1)S(1)}, f32[3,128,768]{2,1,0:T(8,128)S(1)}, bf16[256,2432]{1,0:T(8,128)(2,1)S(1)}, bf16[256,2432]{1,0:T(8,128)(2,1)}) custom-call(s32[4]{0:T(128)S(1)} %pad_add_fusion.1.ids_ref, bf16[2112,2176]{1,0:T(8,128)(2,1)} %all-gather.2.cloned.1.call-done.feed_ref.refs_3_, bf16[256,2176]{1,0:T(8,128)(2,1)} %copy-done.12, ...), custom_call_target="tpu_custom_call" | custom-call | flops 1048576 | bytes 65536 | tf_op jit(solution)/shard_map/feed/pallas_call | solution.py:402
  333.5 6.3 %collective-permute-done.44.refs_2_ = bf16[128,2432]{1,0:T(8,128)(2,1)S(1)} collective-permute-done((bf16[128,2432]{1,0:T(8,128)(2,1)S(1)}, bf16[128,2432]{1,0:T(8,128)(2,1)S(1)}, u32[]{:S(2)}, u32[]{:S(2)}) %collective-permute-start.44) | collective-permute-done | bytes 622624 | tf_op jit(solution)/shard_map/ppermute | solution.py:46
  340.6 1.5 add_convert_fusion
  346.0 1.7 concatenate.61
  348.4 2.1 pad_maximum_fusion.4
  350.5 12.3 %down.1 = (bf16[1024,2048]{1,0:T(8,128)(2,1)S(1)}, bf16[1024,2048]{1,0:T(8,128)(2,1)}) custom-call(bf16[512,768]{1,0:T(8,128)(2,1)} %copy-done.17, bf16[1024,768]{1,0:T(8,128)(2,1)} %copy-done.9, bf16[512,768]{1,0:T(8,128)(2,1)} %copy-done.16, bf16[2112,2176]{1,0:T(8,128)(2,1)} %all-gather.2.cloned.1.call-done.feed_ref.refs_3_), custom_call_target="tpu_custom_call" | custom-call | flops 1048576 | bytes 65536 | tf_op jit(solution)/shard_map/down/pallas_call | solution.py:456
  362.8 1.9 copy-done.5
  365.8 4.5 all-to-all-start.2
  370.3 7.2 %norm_two.1 = (f32[256,2048]{1,0:T(8,128)S(1)}, bf16[256,2048]{1,0:T(8,128)(2,1)S(1)}, bf16[256,16]{1,0:T(8,128)(2,1)S(1)}, bf16[256,16]{1,0:T(8,128)(2,1)S(1)},...) custom-call(s32[1]{0:T(128)S(6)} %copy.156.adapter_ref, bf16[256,2432]{1,0:T(8,128)(2,1)} %copy-done.11, ...), custom_call_target="tpu_custom_call" | custom-call | flops 1048576 | bytes 65536 | tf_op jit(solution)/shard_map/norm_two/pallas_call | solution.py:705
  379.1 7.1 %back.1.grad_ref = bf16[256,2048]{1,0:T(8,128)(2,1)S(1)} custom-call(bf16[256,2048]{1,0:T(8,128)(2,1)} %copy-done.15, bf16[2048,2048]{1,0:T(8,128)(2,1)} %get-tuple-element.271.w_ref, bf16[256,16]{1,0:T(8,128)(2,1)} %copy-done.23, bf16[16,2048]{1,0:T(8,128)(2,1)} %get-tuple-element.332.a_ref), custom_call_target="tpu_custom_call" | custom-call | flops 1048576 | bytes 65536 | tf_op jit(solution)/shard_map/back/pallas_call | solution.py:639
  386.2 13.0 %attend_back.1 = (bf16[256,2048]{1,0:T(8,128)(2,1)S(1)}, f32[256,512]{1,0:T(8,128)S(1)}, bf16[256,512]{1,0:T(8,128)(2,1)S(1)}) custom-call(bf16[256,2048]{1,0:T(8,128)(2,1)S(1)} %back.1.grad_ref, bf16[256,2048]{1,0:T(8,128)(2,1)S(1)} %copy-done.1, bf16[256,2048]{1,0:T(8,128)(2,1)S(1)} %query.1.query_ref, bf16[256,512]{1,0:T(8,128)(2,1)S(1)} %get-tuple-element.190.own_ref, ...), custom_call_target="tpu_custom_call" | custom-call | flops 1048576 | bytes 65536 | tf_op jit(solution)/shard_map/attend_back/pallas_call | solution.py:929
  401.1 1.9 collective-permute-start.49
  402.9 4.1 add_convert_fusion.9
  407.0 2.6 collective-permute-done.49.came_ref
  410.3 3.2 project_back.1
  417.6 5.9 %all-to-all-start.3 = ((bf16[32,16,592]{2,1,0:T(8,128)(2,1)}), bf16[32,16,592]{2,1,0:T(8,128)(2,1)S(1)}, u32[]{:S(2)}, u32[]{:S(2)}) async-start(bf16[32,16,592]{2,1,0:T(8,128)(2,1)} %bitcast.106), calls=%async_computation.3 | async-start | bytes 1310720 | tf_op jit(solution)/shard_map/all_to_all | solution.py:1167
  423.6 1.9 collective-permute-start.51
  425.5 1.5 collective-permute-start.52
  429.5 10.7 %norm_one.1 = (f32[256,2048]{1,0:T(8,128)}, f32[1,2048]{1,0:T(1,128)S(1)}) custom-call(bf16[256,2560]{1,0:T(8,128)(2,1)} %copy-done.10, bf16[2048,2560]{1,0:T(8,128)(2,1)} %get-tuple-element.187.w_ref, bf16[256,48]{1,0:T(8,128)(2,1)} %copy-done.22, bf16[48,2048]{1,0:T(8,128)(2,1)} %pad_maximum_fusion.6.a_ref, bf16[256,2048]{1,0:T(8,128)(2,1)} %bitcast.113, ...), custom_call_target="tpu_custom_call" | custom-call | flops 1048576 | bytes 65536 | tf_op jit(solution)/shard_map/norm_one/pallas_call | solution.py:789
  441.8 3.5 collective-permute-done.51
  445.5 3.4 add_convert_fusion.8
  453.2 4.7 all-to-all-start.4
  459.9 10.7 %collective-permute-done.54 = bf16[128,2048]{1,0:T(8,128)(2,1)} collective-permute-done((bf16[128,2048]{1,0:T(8,128)(2,1)}, bf16[128,2048]{1,0:T(8,128)(2,1)}, u32[]{:S(2)}, u32[]{:S(2)}) %collective-permute-start.54) | collective-permute-done | bytes 524320 | tf_op jit(solution)/shard_map/ppermute | solution.py:46
  470.8 2.6 convert_add_fusion.1
  473.4 2.2 fusion.2
  (345 shorter events, 95.4 us)
Async XLA Ops:
  7.3 41.0 %collective-permute-start.2 = (bf16[256,2048]{1,0:T(8,128)(2,1)}, bf16[256,2048]{1,0:T(8,128)(2,1)S(1)}, u32[]{:S(2)}, u32[]{:S(2)}) collective-permute-start(bf16[256,2048]{1,0:T(8,128)(2,1)} %bitcast.114), channel_id=1, source_target_pairs={{0,1},{1,0},{2,3},{3,2},{4,5},{5,4},{6,7},{7,6},{8,9},{9,8},{10,11... | collective-permute-start | bytes 3145736 | tf_op jit(solution)/shard_map/ppermute | solution.py:46
  10.3 38.0 %collective-permute-start.3 = (bf16[256,2048]{1,0:T(8,128)(2,1)}, bf16[256,2048]{1,0:T(8,128)(2,1)S(1)}, u32[]{:S(2)}, u32[]{:S(2)}) collective-permute-start(bf16[256,2048]{1,0:T(8,128)(2,1)} %bitcast.115), channel_id=1, source_target_pairs={{0,4},{1,5},{2,6},{3,7},{4,0},{5,1},{6,2},{7,3},{8,12},{9,13},{10,... | collective-permute-start | bytes 3145736 | tf_op jit(solution)/shard_map/ppermute | solution.py:46
  11.8 36.5 %collective-permute-start.4 = (bf16[256,2048]{1,0:T(8,128)(2,1)}, bf16[256,2048]{1,0:T(8,128)(2,1)}, u32[]{:S(2)}, u32[]{:S(2)}) collective-permute-start(bf16[256,2048]{1,0:T(8,128)(2,1)} %bitcast.116), channel_id=1, source_target_pairs={{0,2},{1,3},{2,0},{3,1},{4,6},{5,7},{6,4},{7,5},{8,10},{9,11},{10,... | collective-permute-start | bytes 3145736 | tf_op jit(solution)/shard_map/ppermute | solution.py:46
  15.3 28.6 %collective-permute-start = (bf16[64,4608]{1,0:T(8,128)(2,1)S(1)}, bf16[64,4608]{1,0:T(8,128)(2,1)}, u32[]{:S(2)}, u32[]{:S(2)}) collective-permute-start(bf16[64,4608]{1,0:T(8,128)(2,1)S(1)} %constant_dynamic-update-slice_fusion.11), channel_id=1, source_target_pairs={{0,8},{1,9},{2,10},{3,11},{4,12},{5,13},{6,14},{7,15},{8,0},{9,1},... | collective-permute-start | bytes 1769480 | tf_op jit(solution)/shard_map/ppermute | solution.py:46
  16.9 31.3 %collective-permute-start.1 = (bf16[64,4608]{1,0:T(8,128)(2,1)S(1)}, bf16[64,4608]{1,0:T(8,128)(2,1)}, u32[]{:S(2)}, u32[]{:S(2)}) collective-permute-start(bf16[64,4608]{1,0:T(8,128)(2,1)S(1)} %constant_dynamic-update-slice_fusion.11), channel_id=1, source_target_pairs={{0,16},{1,17},{2,18},{3,19},{4,20},{5,21},{6,22},{7,23},{8,24},{9,... | collective-permute-start | bytes 1769480 | tf_op jit(solution)/shard_map/ppermute | solution.py:46
  25.7 28.0 %all-to-all-start = ((bf16[32,4,1408]{2,1,0:T(4,128)(2,1)}), bf16[32,4,1408]{2,1,0:T(4,128)(2,1)S(1)}, u32[]{:S(2)}, u32[]{:S(2)}) async-start(bf16[32,4,1408]{2,1,0:T(4,128)(2,1)} %copy.117), calls=%async_computation | async-start | bytes 720896 | tf_op jit(solution)/shard_map/all_to_all | solution.py:1023
  28.3 222.8 %all-gather.2.cloned.1.call-start = ((), (), s32[]{:S(2)}) async-start(), calls=%async_computation.5 | async-start | bytes 11489280 | tf_op jit(solution)/shard_map/all_gather | solution.py:1035
  49.5 14.4 %collective-permute-start.5 = (bf16[64,4608]{1,0:T(8,128)(2,1)}, bf16[64,4608]{1,0:T(8,128)(2,1)}, u32[]{:S(2)}, u32[]{:S(2)}) collective-permute-start(bf16[64,4608]{1,0:T(8,128)(2,1)} %collective-permute-done.1), channel_id=1, source_target_pairs={{0,8},{1,9},{2,10},{3,11},{4,12},{5,13},{6,14},{7,15},{8,0},{9,1},... | collective-permute-start | bytes 1769480 | tf_op jit(solution)/shard_map/ppermute | solution.py:46
  68.0 40.0 %all-to-all-start.1 = ((bf16[32,16,640]{2,1,0:T(8,128)(2,1)}), bf16[32,16,640]{2,1,0:T(8,128)(2,1)S(1)}, u32[]{:S(2)}, u32[]{:S(2)}) async-start(bf16[32,16,640]{2,1,0:T(8,128)(2,1)} %broadcast_select_fusion), calls=%async_computation.1 | async-start | bytes 1310720 | tf_op jit(solution)/shard_map/all_to_all | solution.py:1031
  77.8 35.1 %collective-permute-start.6 = (bf16[4,64,2560]{2,1,0:T(8,128)(2,1)S(1)}, bf16[4,64,2560]{2,1,0:T(8,128)(2,1)}, u32[]{:S(2)}, u32[]{:S(2)}) collective-permute-start(bf16[4,64,2560]{2,1,0:T(8,128)(2,1)S(1)} %pad_maximum_fusion.1.refs_0_), channel_id=1, source_target_pairs={{0,1},{1,0},{2,3},{3,2},{4,5},{5,4},{6,7},{7,6},{8,9},{9,8},{10,11... | collective-permute-start | bytes 3932168 | tf_op jit(solution)/shard_map/ppermute | solution.py:46
  79.8 33.4 %collective-permute-start.7 = (bf16[4,64,2560]{2,1,0:T(8,128)(2,1)S(1)}, bf16[4,64,2560]{2,1,0:T(8,128)(2,1)}, u32[]{:S(2)}, u32[]{:S(2)}) collective-permute-start(bf16[4,64,2560]{2,1,0:T(8,128)(2,1)S(1)} %pad_maximum_fusion.1.refs_0_), channel_id=1, source_target_pairs={{0,4},{1,5},{2,6},{3,7},{4,0},{5,1},{6,2},{7,3},{8,12},{9,13},{10,... | collective-permute-start | bytes 3932168 | tf_op jit(solution)/shard_map/ppermute | solution.py:46
  81.3 31.9 %collective-permute-start.8 = (bf16[4,64,2560]{2,1,0:T(8,128)(2,1)S(1)}, bf16[4,64,2560]{2,1,0:T(8,128)(2,1)}, u32[]{:S(2)}, u32[]{:S(2)}) collective-permute-start(bf16[4,64,2560]{2,1,0:T(8,128)(2,1)S(1)} %pad_maximum_fusion.1.refs_0_), channel_id=1, source_target_pairs={{0,2},{1,3},{2,0},{3,1},{4,6},{5,7},{6,4},{7,5},{8,10},{9,11},{10,... | collective-permute-start | bytes 3932168 | tf_op jit(solution)/shard_map/ppermute | solution.py:46
  114.3 16.4 %collective-permute-start.10 = (bf16[2,64,2560]{2,1,0:T(8,128)(2,1)S(1)}, bf16[2,64,2560]{2,1,0:T(8,128)(2,1)S(1)}, u32[]{:S(2)}, u32[]{:S(2)}) collective-permute-start(bf16[2,64,2560]{2,1,0:T(8,128)(2,1)S(1)} %slice.335), channel_id=1, source_target_pairs={{0,1},{1,0},{2,3},{3,2},{4,5},{5,4},{6,7},{7,6},{8,9},{9,8},{10,11... | collective-permute-start | bytes 1966088 | tf_op jit(solution)/shard_map/ppermute | solution.py:46
  117.3 16.0 %collective-permute-start.9 = (bf16[2,64,2560]{2,1,0:T(8,128)(2,1)S(1)}, bf16[2,64,2560]{2,1,0:T(8,128)(2,1)S(1)}, u32[]{:S(2)}, u32[]{:S(2)}) collective-permute-start(bf16[2,64,2560]{2,1,0:T(8,128)(2,1)S(1)} %slice.334), channel_id=1, source_target_pairs={{0,4},{1,5},{2,6},{3,7},{4,0},{5,1},{6,2},{7,3},{8,12},{9,13},{10,... | collective-permute-start | bytes 1966088 | tf_op jit(solution)/shard_map/ppermute | solution.py:46
  133.3 2.2 collective-permute-start.13
  133.4 4.9 %collective-permute-start.14 = (bf16[2,64,2560]{2,1,0:T(8,128)(2,1)S(1)}, bf16[2,64,2560]{2,1,0:T(8,128)(2,1)S(1)}, u32[]{:S(2)}, u32[]{:S(2)}) collective-permute-start(bf16[2,64,2560]{2,1,0:T(8,128)(2,1)S(1)} %collective-permute-done.10.refs_4_), channel_id=1, source_target_pairs={{0,2},{1,3},{2,0},{3,1},{4,6},{5,7},{6,4},{7,5},{8,10},{9,11},{10,... | collective-permute-start | bytes 1966088 | tf_op jit(solution)/shard_map/ppermute | solution.py:46
  133.9 7.4 %collective-permute-start.11 = (bf16[4,64,2560]{2,1,0:T(8,128)(2,1)}, bf16[4,64,2560]{2,1,0:T(8,128)(2,1)S(1)}, u32[]{:S(2)}, u32[]{:S(2)}) collective-permute-start(bf16[4,64,2560]{2,1,0:T(8,128)(2,1)} %collective-permute-done.6.refs_1_), channel_id=1, source_target_pairs={{0,2},{1,3},{2,0},{3,1},{4,6},{5,7},{6,4},{7,5},{8,10},{9,11},{10,... | collective-permute-start | bytes 3932168 | tf_op jit(solution)/shard_map/ppermute | solution.py:46
  134.0 7.4 %collective-permute-start.12 = (bf16[4,64,2560]{2,1,0:T(8,128)(2,1)}, bf16[4,64,2560]{2,1,0:T(8,128)(2,1)}, u32[]{:S(2)}, u32[]{:S(2)}) collective-permute-start(bf16[4,64,2560]{2,1,0:T(8,128)(2,1)} %collective-permute-done.7.refs_2_), channel_id=1, source_target_pairs={{0,2},{1,3},{2,0},{3,1},{4,6},{5,7},{6,4},{7,5},{8,10},{9,11},{10,... | collective-permute-start | bytes 3932168 | tf_op jit(solution)/shard_map/ppermute | solution.py:46
  134.4 44.2 %collective-permute-start.16 = (bf16[4,64,2048]{2,1,0:T(8,128)(2,1)S(1)}, bf16[4,64,2048]{2,1,0:T(8,128)(2,1)}, u32[]{:S(2)}, u32[]{:S(2)}) collective-permute-start(bf16[4,64,2048]{2,1,0:T(8,128)(2,1)S(1)} %copy-done.26), channel_id=1, source_target_pairs={{0,1},{1,0},{2,3},{3,2},{4,5},{5,4},{6,7},{7,6},{8,9},{9,8},{10,11... | collective-permute-start | bytes 3145736 | tf_op jit(solution)/shard_map/ppermute | solution.py:46
  135.5 43.2 %collective-permute-start.17 = (bf16[4,64,2048]{2,1,0:T(8,128)(2,1)S(1)}, bf16[4,64,2048]{2,1,0:T(8,128)(2,1)}, u32[]{:S(2)}, u32[]{:S(2)}) collective-permute-start(bf16[4,64,2048]{2,1,0:T(8,128)(2,1)S(1)} %copy-done.26), channel_id=1, source_target_pairs={{0,4},{1,5},{2,6},{3,7},{4,0},{5,1},{6,2},{7,3},{8,12},{9,13},{10,... | collective-permute-start | bytes 3145736 | tf_op jit(solution)/shard_map/ppermute | solution.py:46
  138.3 40.4 %collective-permute-start.18 = (bf16[4,64,2048]{2,1,0:T(8,128)(2,1)S(1)}, bf16[4,64,2048]{2,1,0:T(8,128)(2,1)}, u32[]{:S(2)}, u32[]{:S(2)}) collective-permute-start(bf16[4,64,2048]{2,1,0:T(8,128)(2,1)S(1)} %copy-done.26), channel_id=1, source_target_pairs={{0,2},{1,3},{2,0},{3,1},{4,6},{5,7},{6,4},{7,5},{8,10},{9,11},{10,... | collective-permute-start | bytes 3145736 | tf_op jit(solution)/shard_map/ppermute | solution.py:46
  152.8 12.4 %collective-permute-start.15 = (bf16[256,512]{1,0:T(8,128)(2,1)S(1)}, bf16[256,512]{1,0:T(8,128)(2,1)S(1)}, u32[]{:S(2)}, u32[]{:S(2)}) collective-permute-start(bf16[256,512]{1,0:T(8,128)(2,1)S(1)} %get-tuple-element.190.own_ref), channel_id=1, source_target_pairs={{0,1},{1,0},{2,3},{3,2},{4,5},{5,4},{6,7},{7,6},{8,9},{9,8},{10,11... | collective-permute-start | bytes 786440 | tf_op jit(solution)/shard_map/ppermute | solution.py:46
  180.2 13.3 %collective-permute-start.19 = (bf16[2,64,2048]{2,1,0:T(8,128)(2,1)S(1)}, bf16[2,64,2048]{2,1,0:T(8,128)(2,1)S(1)}, u32[]{:S(2)}, u32[]{:S(2)}) collective-permute-start(bf16[2,64,2048]{2,1,0:T(8,128)(2,1)S(1)} %slice.351), channel_id=1, source_target_pairs={{0,4},{1,5},{2,6},{3,7},{4,0},{5,1},{6,2},{7,3},{8,12},{9,13},{10,... | collective-permute-start | bytes 1572872 | tf_op jit(solution)/shard_map/ppermute | solution.py:46
  182.0 13.1 %collective-permute-start.20 = (bf16[2,64,2048]{2,1,0:T(8,128)(2,1)S(1)}, bf16[2,64,2048]{2,1,0:T(8,128)(2,1)}, u32[]{:S(2)}, u32[]{:S(2)}) collective-permute-start(bf16[2,64,2048]{2,1,0:T(8,128)(2,1)S(1)} %slice.352), channel_id=1, source_target_pairs={{0,1},{1,0},{2,3},{3,2},{4,5},{5,4},{6,7},{7,6},{8,9},{9,8},{10,11... | collective-permute-start | bytes 1572872 | tf_op jit(solution)/shard_map/ppermute | solution.py:46
  183.6 17.1 %collective-permute-start.21 = (bf16[4,64,2048]{2,1,0:T(8,128)(2,1)}, bf16[4,64,2048]{2,1,0:T(8,128)(2,1)S(1)}, u32[]{:S(2)}, u32[]{:S(2)}) collective-permute-start(bf16[4,64,2048]{2,1,0:T(8,128)(2,1)} %collective-permute-done.16.refs_1_), channel_id=1, source_target_pairs={{0,2},{1,3},{2,0},{3,1},{4,6},{5,7},{6,4},{7,5},{8,10},{9,11},{10,... | collective-permute-start | bytes 3145736 | tf_op jit(solution)/shard_map/ppermute | solution.py:46
  183.6 17.1 %collective-permute-start.22 = (bf16[4,64,2048]{2,1,0:T(8,128)(2,1)}, bf16[4,64,2048]{2,1,0:T(8,128)(2,1)}, u32[]{:S(2)}, u32[]{:S(2)}) collective-permute-start(bf16[4,64,2048]{2,1,0:T(8,128)(2,1)} %collective-permute-done.17.refs_2_), channel_id=1, source_target_pairs={{0,2},{1,3},{2,0},{3,1},{4,6},{5,7},{6,4},{7,5},{8,10},{9,11},{10,... | collective-permute-start | bytes 3145736 | tf_op jit(solution)/shard_map/ppermute | solution.py:46
  195.0 3.6 collective-permute-start.23
  195.0 5.7 %collective-permute-start.24 = (bf16[2,64,2048]{2,1,0:T(8,128)(2,1)}, bf16[2,64,2048]{2,1,0:T(8,128)(2,1)}, u32[]{:S(2)}, u32[]{:S(2)}) collective-permute-start(bf16[2,64,2048]{2,1,0:T(8,128)(2,1)} %collective-permute-done.20.refs_4_), channel_id=1, source_target_pairs={{0,2},{1,3},{2,0},{3,1},{4,6},{5,7},{6,4},{7,5},{8,10},{9,11},{10,... | collective-permute-start | bytes 1572872 | tf_op jit(solution)/shard_map/ppermute | solution.py:46
  196.4 17.3 %collective-permute-start.25 = (bf16[128,2048]{1,0:T(8,128)(2,1)}, bf16[128,2048]{1,0:T(8,128)(2,1)}, u32[]{:S(2)}, u32[]{:S(2)}) collective-permute-start(bf16[128,2048]{1,0:T(8,128)(2,1)} %slice.356), channel_id=1, source_target_pairs={{0,4},{1,5},{2,6},{3,7},{4,0},{5,1},{6,2},{7,3},{8,12},{9,13},{10,... | collective-permute-start | bytes 1572872 | tf_op jit(solution)/shard_map/ppermute | solution.py:46
  199.4 14.2 %collective-permute-start.26 = (bf16[128,2048]{1,0:T(8,128)(2,1)}, bf16[128,2048]{1,0:T(8,128)(2,1)}, u32[]{:S(2)}, u32[]{:S(2)}) collective-permute-start(bf16[128,2048]{1,0:T(8,128)(2,1)} %slice.357), channel_id=1, source_target_pairs={{0,1},{1,0},{2,3},{3,2},{4,5},{5,4},{6,7},{7,6},{8,9},{9,8},{10,11... | collective-permute-start | bytes 1572872 | tf_op jit(solution)/shard_map/ppermute | solution.py:46
  213.7 70.2 %copy-start.12 = (bf16[256,2176]{1,0:T(8,128)(2,1)}, bf16[256,2176]{1,0:T(8,128)(2,1)S(1)}, u32[]{:S(2)}) copy-start(bf16[256,2176]{1,0:T(8,128)(2,1)S(1)} %get-tuple-element.212.refs_0_) | copy-start | bytes 3342340
  213.7 26.4 %collective-permute-start.27 = (bf16[256,2176]{1,0:T(8,128)(2,1)S(1)}, bf16[256,2176]{1,0:T(8,128)(2,1)S(1)}, u32[]{:S(2)}, u32[]{:S(2)}) collective-permute-start(bf16[256,2176]{1,0:T(8,128)(2,1)S(1)} %get-tuple-element.212.refs_0_), channel_id=1, source_target_pairs={{0,1},{1,0},{2,3},{3,2},{4,5},{5,4},{6,7},{7,6},{8,9},{9,8},{10,11... | collective-permute-start | bytes 3342344 | tf_op jit(solution)/shard_map/ppermute | solution.py:46
  215.1 25.6 %collective-permute-start.28 = (bf16[256,2176]{1,0:T(8,128)(2,1)S(1)}, bf16[256,2176]{1,0:T(8,128)(2,1)S(1)}, u32[]{:S(2)}, u32[]{:S(2)}) collective-permute-start(bf16[256,2176]{1,0:T(8,128)(2,1)S(1)} %get-tuple-element.212.refs_0_), channel_id=1, source_target_pairs={{0,4},{1,5},{2,6},{3,7},{4,0},{5,1},{6,2},{7,3},{8,12},{9,13},{10,... | collective-permute-start | bytes 3342344 | tf_op jit(solution)/shard_map/ppermute | solution.py:46
  215.8 25.0 %collective-permute-start.29 = (bf16[256,2176]{1,0:T(8,128)(2,1)S(1)}, bf16[256,2176]{1,0:T(8,128)(2,1)S(1)}, u32[]{:S(2)}, u32[]{:S(2)}) collective-permute-start(bf16[256,2176]{1,0:T(8,128)(2,1)S(1)} %get-tuple-element.212.refs_0_), channel_id=1, source_target_pairs={{0,2},{1,3},{2,0},{3,1},{4,6},{5,7},{6,4},{7,5},{8,10},{9,11},{10,... | collective-permute-start | bytes 3342344 | tf_op jit(solution)/shard_map/ppermute | solution.py:46
  215.8 27.5 %collective-permute-start.32 = (bf16[256,2048]{1,0:T(8,128)(2,1)S(1)}, bf16[256,2048]{1,0:T(8,128)(2,1)S(1)}, u32[]{:S(2)}, u32[]{:S(2)}) collective-permute-start(bf16[256,2048]{1,0:T(8,128)(2,1)S(1)} %copy-done.33), channel_id=1, source_target_pairs={{0,2},{1,3},{2,0},{3,1},{4,6},{5,7},{6,4},{7,5},{8,10},{9,11},{10,... | collective-permute-start | bytes 3145736 | tf_op jit(solution)/shard_map/ppermute | solution.py:46
  216.3 27.9 %collective-permute-start.33 = (bf16[256,2048]{1,0:T(8,128)(2,1)S(1)}, bf16[256,2048]{1,0:T(8,128)(2,1)S(1)}, u32[]{:S(2)}, u32[]{:S(2)}) collective-permute-start(bf16[256,2048]{1,0:T(8,128)(2,1)S(1)} %copy-done.36), channel_id=1, source_target_pairs={{0,2},{1,3},{2,0},{3,1},{4,6},{5,7},{6,4},{7,5},{8,10},{9,11},{10,... | collective-permute-start | bytes 3145736 | tf_op jit(solution)/shard_map/ppermute | solution.py:46
  241.8 7.4 %collective-permute-start.30 = (bf16[256,2176]{1,0:T(8,128)(2,1)S(1)}, bf16[256,2176]{1,0:T(8,128)(2,1)S(1)}, u32[]{:S(2)}, u32[]{:S(2)}) collective-permute-start(bf16[256,2176]{1,0:T(8,128)(2,1)S(1)} %collective-permute-done.27.refs_0_), channel_id=1, source_target_pairs={{0,2},{1,3},{2,0},{3,1},{4,6},{5,7},{6,4},{7,5},{8,10},{9,11},{10,... | collective-permute-start | bytes 3342344 | tf_op jit(solution)/shard_map/ppermute | solution.py:46
  241.8 9.2 %collective-permute-start.31 = (bf16[256,2176]{1,0:T(8,128)(2,1)S(1)}, bf16[256,2176]{1,0:T(8,128)(2,1)}, u32[]{:S(2)}, u32[]{:S(2)}) collective-permute-start(bf16[256,2176]{1,0:T(8,128)(2,1)S(1)} %collective-permute-done.28.refs_2_), channel_id=1, source_target_pairs={{0,2},{1,3},{2,0},{3,1},{4,6},{5,7},{6,4},{7,5},{8,10},{9,11},{10,... | collective-permute-start | bytes 3342344 | tf_op jit(solution)/shard_map/ppermute | solution.py:46
  242.3 4.8 collective-permute-start.34
  243.3 40.7 %collective-permute-start.36 = (bf16[128,2176]{1,0:T(8,128)(2,1)}, bf16[128,2176]{1,0:T(8,128)(2,1)}, u32[]{:S(2)}, u32[]{:S(2)}) collective-permute-start(bf16[128,2176]{1,0:T(8,128)(2,1)} %slice.358), channel_id=1, source_target_pairs={{0,4},{1,5},{2,6},{3,7},{4,0},{5,1},{6,2},{7,3},{8,12},{9,13},{10,... | collective-permute-start | bytes 1671176 | tf_op jit(solution)/shard_map/ppermute | solution.py:46
  244.2 39.8 %collective-permute-start.37 = (bf16[128,2176]{1,0:T(8,128)(2,1)S(1)}, bf16[128,2176]{1,0:T(8,128)(2,1)}, u32[]{:S(2)}, u32[]{:S(2)}) collective-permute-start(bf16[128,2176]{1,0:T(8,128)(2,1)S(1)} %slice.359), channel_id=1, source_target_pairs={{0,1},{1,0},{2,3},{3,2},{4,5},{5,4},{6,7},{7,6},{8,9},{9,8},{10,11... | collective-permute-start | bytes 1671176 | tf_op jit(solution)/shard_map/ppermute | solution.py:46
  247.1 2.1 collective-permute-start.35
  283.9 2.2 collective-permute-start.38
  284.1 3.6 collective-permute-start.39
  284.5 25.5 %collective-permute-start.41 = (bf16[512,2432]{1,0:T(8,128)(2,1)S(1)}, bf16[512,2432]{1,0:T(8,128)(2,1)S(1)}, u32[]{:S(2)}, u32[]{:S(2)}) collective-permute-start(bf16[512,2432]{1,0:T(8,128)(2,1)S(1)} %get-tuple-element.232), channel_id=1, source_target_pairs={{0,2},{1,3},{2,0},{3,1},{4,6},{5,7},{6,4},{7,5},{8,10},{9,11},{10,... | collective-permute-start | bytes 7471112 | tf_op jit(solution)/shard_map/ppermute | solution.py:46
  306.7 3.0 collective-permute-start.40
  310.3 23.2 %collective-permute-start.42 = (bf16[128,2432]{1,0:T(8,128)(2,1)S(1)}, bf16[128,2432]{1,0:T(8,128)(2,1)S(1)}, u32[]{:S(2)}, u32[]{:S(2)}) collective-permute-start(bf16[128,2432]{1,0:T(8,128)(2,1)S(1)} %get-tuple-element.239), channel_id=1, source_target_pairs={{0,1},{1,0},{2,3},{3,2},{4,5},{5,4},{6,7},{7,6},{8,9},{9,8},{10,11... | collective-permute-start | bytes 1867784 | tf_op jit(solution)/shard_map/ppermute | solution.py:46
  311.4 22.1 %collective-permute-start.43 = (bf16[128,2432]{1,0:T(8,128)(2,1)S(1)}, bf16[128,2432]{1,0:T(8,128)(2,1)S(1)}, u32[]{:S(2)}, u32[]{:S(2)}) collective-permute-start(bf16[128,2432]{1,0:T(8,128)(2,1)S(1)} %get-tuple-element.240), channel_id=1, source_target_pairs={{0,4},{1,5},{2,6},{3,7},{4,0},{5,1},{6,2},{7,3},{8,12},{9,13},{10,... | collective-permute-start | bytes 1867784 | tf_op jit(solution)/shard_map/ppermute | solution.py:46
  312.6 27.2 %collective-permute-start.44 = (bf16[128,2432]{1,0:T(8,128)(2,1)S(1)}, bf16[128,2432]{1,0:T(8,128)(2,1)S(1)}, u32[]{:S(2)}, u32[]{:S(2)}) collective-permute-start(bf16[128,2432]{1,0:T(8,128)(2,1)S(1)} %get-tuple-element.241), channel_id=1, source_target_pairs={{0,1},{1,0},{2,3},{3,2},{4,5},{5,4},{6,7},{7,6},{8,9},{9,8},{10,11... | collective-permute-start | bytes 1867784 | tf_op jit(solution)/shard_map/ppermute | solution.py:46
  313.3 27.3 %collective-permute-start.45 = (bf16[128,2432]{1,0:T(8,128)(2,1)S(1)}, bf16[128,2432]{1,0:T(8,128)(2,1)S(1)}, u32[]{:S(2)}, u32[]{:S(2)}) collective-permute-start(bf16[128,2432]{1,0:T(8,128)(2,1)S(1)} %get-tuple-element.242), channel_id=1, source_target_pairs={{0,4},{1,5},{2,6},{3,7},{4,0},{5,1},{6,2},{7,3},{8,12},{9,13},{10,... | collective-permute-start | bytes 1867784 | tf_op jit(solution)/shard_map/ppermute | solution.py:46
  333.4 31.4 %collective-permute-start.46 = (bf16[256,2432]{1,0:T(8,128)(2,1)}, bf16[256,2432]{1,0:T(8,128)(2,1)S(1)}, u32[]{:S(2)}, u32[]{:S(2)}) collective-permute-start(bf16[256,2432]{1,0:T(8,128)(2,1)} %get-tuple-element.245), channel_id=1, source_target_pairs={{0,2},{1,3},{2,0},{3,1},{4,6},{5,7},{6,4},{7,5},{8,10},{9,11},{10,... | collective-permute-start | bytes 3735560 | tf_op jit(solution)/shard_map/ppermute | solution.py:46
  342.1 22.7 %collective-permute-start.47 = (bf16[128,2432]{1,0:T(8,128)(2,1)}, bf16[128,2432]{1,0:T(8,128)(2,1)}, u32[]{:S(2)}, u32[]{:S(2)}) collective-permute-start(bf16[128,2432]{1,0:T(8,128)(2,1)} %get-tuple-element.251), channel_id=1, source_target_pairs={{0,4},{1,5},{2,6},{3,7},{4,0},{5,1},{6,2},{7,3},{8,12},{9,13},{10,... | collective-permute-start | bytes 1867784 | tf_op jit(solution)/shard_map/ppermute | solution.py:46
  343.3 21.4 %collective-permute-start.48 = (bf16[128,2432]{1,0:T(8,128)(2,1)}, bf16[128,2432]{1,0:T(8,128)(2,1)}, u32[]{:S(2)}, u32[]{:S(2)}) collective-permute-start(bf16[128,2432]{1,0:T(8,128)(2,1)} %get-tuple-element.252), channel_id=1, source_target_pairs={{0,1},{1,0},{2,3},{3,2},{4,5},{5,4},{6,7},{7,6},{8,9},{9,8},{10,11... | collective-permute-start | bytes 1867784 | tf_op jit(solution)/shard_map/ppermute | solution.py:46
  364.8 38.2 %collective-permute-start.50 = (bf16[1024,2048]{1,0:T(8,128)(2,1)}, bf16[1024,2048]{1,0:T(8,128)(2,1)}, u32[]{:S(2)}, u32[]{:S(2)}) collective-permute-start(bf16[1024,2048]{1,0:T(8,128)(2,1)} %get-tuple-element.283), channel_id=1, source_target_pairs={{0,2},{1,3},{2,0},{3,1},{4,6},{5,7},{6,4},{7,5},{8,10},{9,11},{10,... | collective-permute-start | bytes 12582920 | tf_op jit(solution)/shard_map/ppermute | solution.py:46
  365.8 35.3 %all-to-all-start.2 = ((bf16[32,4,2304]{2,1,0:T(4,128)(2,1)}), bf16[32,4,2304]{2,1,0:T(4,128)(2,1)S(1)}, u32[]{:S(2)}, u32[]{:S(2)}) async-start(bf16[32,4,2304]{2,1,0:T(4,128)(2,1)} %pad_maximum_fusion.4), calls=%async_computation.2 | async-start | bytes 1179648 | tf_op jit(solution)/shard_map/all_to_all | solution.py:1135
  401.1 8.6 %collective-permute-start.49 = (bf16[256,512]{1,0:T(8,128)(2,1)S(1)}, bf16[256,512]{1,0:T(8,128)(2,1)S(1)}, u32[]{:S(2)}, u32[]{:S(2)}) collective-permute-start(bf16[256,512]{1,0:T(8,128)(2,1)S(1)} %get-tuple-element.281), channel_id=1, source_target_pairs={{0,1},{1,0},{2,3},{3,2},{4,5},{5,4},{6,7},{7,6},{8,9},{9,8},{10,11... | collective-permute-start | bytes 786440 | tf_op jit(solution)/shard_map/ppermute | solution.py:46
  417.6 33.1 %all-to-all-start.3 = ((bf16[32,16,592]{2,1,0:T(8,128)(2,1)}), bf16[32,16,592]{2,1,0:T(8,128)(2,1)S(1)}, u32[]{:S(2)}, u32[]{:S(2)}) async-start(bf16[32,16,592]{2,1,0:T(8,128)(2,1)} %bitcast.106), calls=%async_computation.3 | async-start | bytes 1310720 | tf_op jit(solution)/shard_map/all_to_all | solution.py:1167
  423.6 21.7 %collective-permute-start.51 = (bf16[128,2048]{1,0:T(8,128)(2,1)S(1)}, bf16[128,2048]{1,0:T(8,128)(2,1)}, u32[]{:S(2)}, u32[]{:S(2)}) collective-permute-start(bf16[128,2048]{1,0:T(8,128)(2,1)S(1)} %copy-done.53), channel_id=1, source_target_pairs={{0,1},{1,0},{2,3},{3,2},{4,5},{5,4},{6,7},{7,6},{8,9},{9,8},{10,11... | collective-permute-start | bytes 1572872 | tf_op jit(solution)/shard_map/ppermute | solution.py:46
  425.5 20.0 %collective-permute-start.52 = (bf16[128,2048]{1,0:T(8,128)(2,1)S(1)}, bf16[128,2048]{1,0:T(8,128)(2,1)}, u32[]{:S(2)}, u32[]{:S(2)}) collective-permute-start(bf16[128,2048]{1,0:T(8,128)(2,1)S(1)} %copy-done.52), channel_id=1, source_target_pairs={{0,4},{1,5},{2,6},{3,7},{4,0},{5,1},{6,2},{7,3},{8,12},{9,13},{10,... | collective-permute-start | bytes 1572872 | tf_op jit(solution)/shard_map/ppermute | solution.py:46
  441.0 18.9 %collective-permute-start.53 = (bf16[128,2048]{1,0:T(8,128)(2,1)}, bf16[128,2048]{1,0:T(8,128)(2,1)}, u32[]{:S(2)}, u32[]{:S(2)}) collective-permute-start(bf16[128,2048]{1,0:T(8,128)(2,1)} %get-tuple-element.304), channel_id=1, source_target_pairs={{0,1},{1,0},{2,3},{3,2},{4,5},{5,4},{6,7},{7,6},{8,9},{9,8},{10,11... | collective-permute-start | bytes 1572872 | tf_op jit(solution)/shard_map/ppermute | solution.py:46
  441.5 18.4 %collective-permute-start.55 = (bf16[128,2048]{1,0:T(8,128)(2,1)}, bf16[128,2048]{1,0:T(8,128)(2,1)}, u32[]{:S(2)}, u32[]{:S(2)}) collective-permute-start(bf16[128,2048]{1,0:T(8,128)(2,1)} %get-tuple-element.306), channel_id=1, source_target_pairs={{0,4},{1,5},{2,6},{3,7},{4,0},{5,1},{6,2},{7,3},{8,12},{9,13},{10,... | collective-permute-start | bytes 1572872 | tf_op jit(solution)/shard_map/ppermute | solution.py:46
  448.9 21.7 %collective-permute-start.54 = (bf16[128,2048]{1,0:T(8,128)(2,1)}, bf16[128,2048]{1,0:T(8,128)(2,1)}, u32[]{:S(2)}, u32[]{:S(2)}) collective-permute-start(bf16[128,2048]{1,0:T(8,128)(2,1)} %get-tuple-element.315), channel_id=1, source_target_pairs={{0,4},{1,5},{2,6},{3,7},{4,0},{5,1},{6,2},{7,3},{8,12},{9,13},{10,... | collective-permute-start | bytes 1572872 | tf_op jit(solution)/shard_map/ppermute | solution.py:46
  450.1 20.6 %collective-permute-start.56 = (bf16[128,2048]{1,0:T(8,128)(2,1)}, bf16[128,2048]{1,0:T(8,128)(2,1)}, u32[]{:S(2)}, u32[]{:S(2)}) collective-permute-start(bf16[128,2048]{1,0:T(8,128)(2,1)} %get-tuple-element.316), channel_id=1, source_target_pairs={{0,1},{1,0},{2,3},{3,2},{4,5},{5,4},{6,7},{7,6},{8,9},{9,8},{10,11... | collective-permute-start | bytes 1572872 | tf_op jit(solution)/shard_map/ppermute | solution.py:46
  453.2 22.4 %all-to-all-start.4 = ((f32[32,4,720]{2,1,0:T(4,128)}), f32[32,4,720]{2,1,0:T(4,128)S(1)}, u32[]{:S(2)}, u32[]{:S(2)}) async-start(f32[32,4,720]{2,1,0:T(4,128)} %pad_maximum_fusion.5), calls=%async_computation.4 | async-start | bytes 786432 | tf_op jit(solution)/shard_map/all_to_all | solution.py:1181
  (70 other events, 531.9 us)
Sparse Core Ops, SparseCore 0:
  64.0 174.3 all-gather.1

commit v5 on v4

--- a/solution.py
+++ b/solution.py
@@ -1124,12 +1124,12 @@
     far_came, near_came = normed_sum.hop(*sends[:2]), normed_sum.hop(*sends[2:])
     hidden_own, grads_own, near_out, far_out = feed_of(ids_own, 0, (0,))
     recv = exchange(far_out, C, n)
-    near_out, grads_own, *came = order.point(near_out, grads_own, *far_came, *near_came)
-    far_came, near_came = came[:2], came[2:]
+    near_out, grads_own, *far_came = order.point(near_out, grads_own, *far_came)
     hidden_grads = grads_own + grads_mid + grads_far
     hidden_grads = jnp.concatenate([hidden_grads[i] for i in range(3)], 1).astype(BF)
     hidden_grads = hidden_grads.reshape(n, own_rows, -1)
-    last_sends = order.point(*normed_sum.last_sends(*far_came))
+    passed = order.point(*normed_sum.last_sends(*far_came), *near_came)
+    last_sends, near_came = passed[:2], passed[2:]
     last_came = normed_sum.last_hop(*last_sends)
     hidden_own, hidden_grads = order.point(hidden_own, hidden_grads)
     hidden_grads = lax.all_to_all(hidden_grads, ALL, 0, 0, tiled=True)

time: 492 us -> 490 us (level)
  no operation moved by 1% of the time
where the time goes in v5:
time: 490 us; the launch traced here: 485 us
  Pallas kernels  163 us (33%)
  waiting for transfers between devices  138 us (28%)
  starting transfers between devices  67.7 us (14%)
  local copies, waits for them, and re-layouts  64.1 us (13%)
  other arithmetic  32.1 us (7%)
  between operations  16.8 us (3%)
    ppermute x57, waiting for transfers between devices, exchange(): return lax.ppermute(value, ALL, [(i, i ^ mask) for i in range(n)])  113 us
    pallas_call x3, Pallas kernels, feed_stage(): pl.pallas_call(functools.partial(feed_kernel, (len(normed), padded, slot,...  69.9 us
    ppermute x57, starting transfers between devices, exchange(): return lax.ppermute(value, ALL, [(i, i ^ mask) for i in range(n)])  45.9 us
    unnamed x156, local copies, waits for them, and re-layouts  26.4 us
    all_to_all x1, waiting for transfers between devices, per_device(): own = lax.all_to_all(jnp.take(columns, ids, axis=0), ALL, 0, 0, tiled=True)  23.6 us
    pallas_call x1, Pallas kernels, attend_stage(): pl.pallas_call(attend_kernel, grid=(KV_HEADS,), out_shape=(jax.ShapeDtype...  13.4 us
    pallas_call x1, Pallas kernels, attend_back_stage(): pl.pallas_call(attend_back_kernel, grid=(KV_HEADS,), out_shape=(jax.Shape...  13 us
    pallas_call x1, Pallas kernels, down_stage(): pl.pallas_call(functools.partial(down_kernel, padded, slot), grid=(1,), o...  12.3 us
  transfers between devices with their start and end apart: 63, of which 27 were waited for; matrix products, arithmetic and copies ran while one was open for 15% of the time, Pallas kernels for 33%

profile of v5, /device:TPU:0, one launch (start us, length us, event | category | flops | bytes accessed | tf_op | source)
XLA Modules:
  0.0 484.8 jit_solution(6061345180305878814)
XLA Ops:
  7.3 3.0 collective-permute-start.2
  10.3 1.5 collective-permute-start.3
  15.3 1.6 collective-permute-start
  16.9 2.6 collective-permute-start.1
  25.7 2.6 all-to-all-start
  28.3 15.5 %collective-permute-done = bf16[64,4608]{1,0:T(8,128)(2,1)} collective-permute-done((bf16[64,4608]{1,0:T(8,128)(2,1)S(1)}, bf16[64,4608]{1,0:T(8,128)(2,1)}, u32[]{:S(2)}, u32[]{:S(2)}) %collective-permute-start) | collective-permute-done | bytes 589856 | tf_op jit(solution)/shard_map/ppermute | solution.py:46
  43.8 4.4 collective-permute-done.1
  52.1 1.6 all-to-all-done
  54.2 2.7 pad_maximum_fusion
  56.9 7.0 %collective-permute-done.5 = bf16[64,4608]{1,0:T(8,128)(2,1)} collective-permute-done((bf16[64,4608]{1,0:T(8,128)(2,1)}, bf16[64,4608]{1,0:T(8,128)(2,1)}, u32[]{:S(2)}, u32[]{:S(2)}) %collective-permute-start.5) | collective-permute-done | bytes 589856 | tf_op jit(solution)/shard_map/ppermute | solution.py:46
  68.0 4.1 all-to-all-start.1
  72.8 2.7 pad_add_fusion.1.ids_ref
  77.8 1.9 collective-permute-start.6
  79.8 1.5 collective-permute-start.7
  84.4 23.6 %all-to-all-done.1 = bf16[32,16,640]{2,1,0:T(8,128)(2,1)S(1)} async-done(((bf16[32,16,640]{2,1,0:T(8,128)(2,1)}), bf16[32,16,640]{2,1,0:T(8,128)(2,1)S(1)}, u32[]{:S(2)}, u32[]{:S(2)}) %all-to-all-start.1) | async-done | bytes 655392 | tf_op jit(solution)/shard_map/all_to_all | solution.py:1031
  111.2 1.8 fusion.29
  114.3 1.9 collective-permute-start.10
  117.3 1.4 collective-permute-start.9
  120.8 9.9 %collective-permute-done.10.refs_4_ = bf16[2,64,2560]{2,1,0:T(8,128)(2,1)S(1)} collective-permute-done((bf16[2,64,2560]{2,1,0:T(8,128)(2,1)S(1)}, bf16[2,64,2560]{2,1,0:T(8,128)(2,1)S(1)}, u32[]{:S(2)}, u32[]{:S(2)}) %collective-permute-start.10) | collective-permute-done | bytes 655392 | tf_op jit(solution)/shard_map/ppermute | solution.py:46
  130.8 2.5 collective-permute-done.9.refs_3_
  136.7 1.6 collective-permute-done.14.refs_9_
  142.4 10.3 %project.1 = (bf16[256,2048]{1,0:T(8,128)(2,1)S(1)}, bf16[256,48]{1,0:T(8,128)(2,1)S(1)}, bf16[256,512]{1,0:T(8,128)(2,1)S(1)}, bf16[2048,2560]{1,0:T(8,128)(2,1)}) custom-call(s32[1]{0:T(128)} %bitcast.me_ref, bf16[256,2048]{1,0:T(8,128)(2,1)} %bitcast.111, f32[1,2048]{1,0:T(1,128)} %reshape.223.gain_ref, bf16[48,2048]{1,0:T(8,128)(2,1)} %pad_maximum_fusion.6.a_ref, ...), custom_call_target="tpu_custom_call" | custom-call | flops 1048576 | bytes 65536 | tf_op jit(solution)/shard_map/project/pallas_call | solution.py:522
  154.6 6.5 %query.1.query_ref = bf16[256,2048]{1,0:T(8,128)(2,1)S(1)} custom-call(bf16[256,2048]{1,0:T(8,128)(2,1)S(1)} %get-tuple-element.185.normed_ref, bf16[256,48]{1,0:T(8,128)(2,1)S(1)} %get-tuple-element.186.low_ref, bf16[16,2048]{1,0:T(8,128)(2,1)S(1)} %get-tuple-element.333.b_ref.bq_ref, bf16[2048,2560]{1,0:T(8,128)(2,1)} %get-tuple-element.187.w_ref, ...), custom_call_target="tpu_custom_call" | custom-call | flops 1048576 | bytes 65536 | tf_op jit(solution)/shard_map/query/pallas_call | solution.py:554
  161.2 4.0 collective-permute-done.15.other_ref
  165.2 13.4 %attend.1 = (bf16[256,2048]{1,0:T(8,128)(2,1)S(1)}, bf16[4,8,512,256]{3,2,1,0:T(8,128)(2,1)}) custom-call(s32[2]{0:T(128)S(1)} %pad_add_fusion.pos_ref, bf16[256,2048]{1,0:T(8,128)(2,1)S(1)} %query.1.query_ref, bf16[256,512]{1,0:T(8,128)(2,1)S(1)} %get-tuple-element.190.own_ref, bf16[256,512]{1,0:T(8,128)(2,1)S(1)} %collective-permute-done.15.other_ref), custom_call_target="tpu_custom_call" | custom-call | flops 1048576 | bytes 65536 | tf_op jit(solution)/shard_map/attend/pallas_call | solution.py:851
  178.7 1.5 slice.351
  182.0 1.7 collective-permute-start.20
  184.1 9.3 %collective-permute-done.19.refs_3_ = bf16[2,64,2048]{2,1,0:T(8,128)(2,1)S(1)} collective-permute-done((bf16[2,64,2048]{2,1,0:T(8,128)(2,1)S(1)}, bf16[2,64,2048]{2,1,0:T(8,128)(2,1)S(1)}, u32[]{:S(2)}, u32[]{:S(2)}) %collective-permute-start.19) | collective-permute-done | bytes 524320 | tf_op jit(solution)/shard_map/ppermute | solution.py:46
  193.4 1.6 collective-permute-done.20.refs_4_
  201.7 9.0 %output.1 = (f32[256,2048]{1,0:T(8,128)S(1)}, bf16[256,2048]{1,0:T(8,128)(2,1)S(1)}, bf16[256,16]{1,0:T(8,128)(2,1)S(1)}, bf16[256,2176]{1,0:T(8,128)(2,1)S(1)}, bf16[2048,2048]{1,0:T(8,128)(2,1)}) custom-call(s32[1]{0:T(128)} %bitcast.me_ref, bf16[256,2048]{1,0:T(8,128)(2,1)} %copy-done, bf16[16,2048]{1,0:T(8,128)(2,1)} %get-tuple-element.332.a_ref, ...), custom_call_target="tpu_custom_call" | custom-call | flops 1048576 | bytes 65536 | tf_op jit(solution)/shard_map/output/pallas_call | solution.py:609
  213.7 1.5 collective-permute-start.27
  216.4 23.7 %collective-permute-done.27.refs_0_ = bf16[256,2176]{1,0:T(8,128)(2,1)S(1)} collective-permute-done((bf16[256,2176]{1,0:T(8,128)(2,1)S(1)}, bf16[256,2176]{1,0:T(8,128)(2,1)S(1)}, u32[]{:S(2)}, u32[]{:S(2)}) %collective-permute-start.27) | collective-permute-done | bytes 1114144 | tf_op jit(solution)/shard_map/ppermute | solution.py:46
  245.6 1.5 collective-permute-done.34.refs_6_
  247.2 2.0 collective-permute-done.35.refs_7_
  251.0 32.9 %feed.3 = (bf16[1024,768]{1,0:T(8,128)(2,1)S(1)}, f32[3,128,768]{2,1,0:T(8,128)S(1)}, bf16[512,2432]{1,0:T(8,128)(2,1)S(1)}, bf16[512,2432]{1,0:T(8,128)(2,1)S(1)}) custom-call(s32[4]{0:T(128)S(1)} %pad_add_fusion.1.ids_ref, bf16[2112,2176]{1,0:T(8,128)(2,1)} %all-gather.2.cloned.1.call-done.feed_ref.refs_3_, bf16[256,2176]{1,0:T(8,128)(2,1)} %copy-done.29, ...), custom_call_target="tpu_custom_call" | custom-call | flops 1048576 | bytes 65536 | tf_op jit(solution)/shard_map/feed/pallas_call | solution.py:402
  284.7 1.5 collective-permute-done.38.refs_2_
  286.2 1.6 collective-permute-done.39.refs_3_
  288.6 18.1 %feed.4 = (bf16[512,768]{1,0:T(8,128)(2,1)S(1)}, f32[3,128,768]{2,1,0:T(8,128)S(1)}, bf16[256,2432]{1,0:T(8,128)(2,1)S(1)}, bf16[256,2432]{1,0:T(8,128)(2,1)S(1)}) custom-call(s32[4]{0:T(128)S(1)} %pad_add_fusion.1.ids_ref, bf16[2112,2176]{1,0:T(8,128)(2,1)} %all-gather.2.cloned.1.call-done.feed_ref.refs_3_, ...), custom_call_target="tpu_custom_call" | custom-call | flops 1048576 | bytes 65536 | tf_op jit(solution)/shard_map/feed/pallas_call | solution.py:402
  306.9 2.8 collective-permute-done.40
  314.4 18.9 %feed.5 = (bf16[512,768]{1,0:T(8,128)(2,1)S(1)}, f32[3,128,768]{2,1,0:T(8,128)S(1)}, bf16[256,2432]{1,0:T(8,128)(2,1)S(1)}, bf16[256,2432]{1,0:T(8,128)(2,1)}) custom-call(s32[4]{0:T(128)S(1)} %pad_add_fusion.1.ids_ref, bf16[2112,2176]{1,0:T(8,128)(2,1)} %all-gather.2.cloned.1.call-done.feed_ref.refs_3_, bf16[256,2176]{1,0:T(8,128)(2,1)} %copy-done.12, ...), custom_call_target="tpu_custom_call" | custom-call | flops 1048576 | bytes 65536 | tf_op jit(solution)/shard_map/feed/pallas_call | solution.py:402
  333.5 1.7 add_convert_fusion
  335.2 4.6 collective-permute-done.45.refs_2_
  344.4 1.7 concatenate.61
  346.8 2.1 pad_maximum_fusion.4
  348.9 12.3 %down.1 = (bf16[1024,2048]{1,0:T(8,128)(2,1)S(1)}, bf16[1024,2048]{1,0:T(8,128)(2,1)}) custom-call(bf16[512,768]{1,0:T(8,128)(2,1)} %copy-done.17, bf16[1024,768]{1,0:T(8,128)(2,1)} %copy-done.9, bf16[512,768]{1,0:T(8,128)(2,1)} %copy-done.16, bf16[2112,2176]{1,0:T(8,128)(2,1)} %all-gather.2.cloned.1.call-done.feed_ref.refs_3_), custom_call_target="tpu_custom_call" | custom-call | flops 1048576 | bytes 65536 | tf_op jit(solution)/shard_map/down/pallas_call | solution.py:456
  361.2 1.9 copy-done.5
  364.2 4.5 all-to-all-start.2
  368.7 7.2 %norm_two.1 = (f32[256,2048]{1,0:T(8,128)S(1)}, bf16[256,2048]{1,0:T(8,128)(2,1)S(1)}, bf16[256,16]{1,0:T(8,128)(2,1)S(1)}, bf16[256,16]{1,0:T(8,128)(2,1)S(1)},...) custom-call(s32[1]{0:T(128)S(6)} %copy.156.adapter_ref, bf16[256,2432]{1,0:T(8,128)(2,1)} %copy-done.11, ...), custom_call_target="tpu_custom_call" | custom-call | flops 1048576 | bytes 65536 | tf_op jit(solution)/shard_map/norm_two/pallas_call | solution.py:705
  377.5 7.1 %back.1.grad_ref = bf16[256,2048]{1,0:T(8,128)(2,1)S(1)} custom-call(bf16[256,2048]{1,0:T(8,128)(2,1)} %copy-done.15, bf16[2048,2048]{1,0:T(8,128)(2,1)} %get-tuple-element.271.w_ref, bf16[256,16]{1,0:T(8,128)(2,1)} %copy-done.23, bf16[16,2048]{1,0:T(8,128)(2,1)} %get-tuple-element.332.a_ref), custom_call_target="tpu_custom_call" | custom-call | flops 1048576 | bytes 65536 | tf_op jit(solution)/shard_map/back/pallas_call | solution.py:639
  384.7 13.0 %attend_back.1 = (bf16[256,2048]{1,0:T(8,128)(2,1)S(1)}, f32[256,512]{1,0:T(8,128)S(1)}, bf16[256,512]{1,0:T(8,128)(2,1)S(1)}) custom-call(bf16[256,2048]{1,0:T(8,128)(2,1)S(1)} %back.1.grad_ref, bf16[256,2048]{1,0:T(8,128)(2,1)S(1)} %copy-done.1, bf16[256,2048]{1,0:T(8,128)(2,1)S(1)} %query.1.query_ref, bf16[256,512]{1,0:T(8,128)(2,1)S(1)} %get-tuple-element.190.own_ref, ...), custom_call_target="tpu_custom_call" | custom-call | flops 1048576 | bytes 65536 | tf_op jit(solution)/shard_map/attend_back/pallas_call | solution.py:929
  399.5 1.9 collective-permute-start.49
  401.4 4.1 add_convert_fusion.9
  405.5 2.6 collective-permute-done.49.came_ref
  408.8 3.2 project_back.1
  416.1 5.9 %all-to-all-start.3 = ((bf16[32,16,592]{2,1,0:T(8,128)(2,1)}), bf16[32,16,592]{2,1,0:T(8,128)(2,1)S(1)}, u32[]{:S(2)}, u32[]{:S(2)}) async-start(bf16[32,16,592]{2,1,0:T(8,128)(2,1)} %bitcast.106), calls=%async_computation.3 | async-start | bytes 1310720 | tf_op jit(solution)/shard_map/all_to_all | solution.py:1167
  422.0 1.9 collective-permute-start.51
  423.9 1.5 collective-permute-start.52
  428.0 10.7 %norm_one.1 = (f32[256,2048]{1,0:T(8,128)}, f32[1,2048]{1,0:T(1,128)S(1)}) custom-call(bf16[256,2560]{1,0:T(8,128)(2,1)} %copy-done.10, bf16[2048,2560]{1,0:T(8,128)(2,1)} %get-tuple-element.187.w_ref, bf16[256,48]{1,0:T(8,128)(2,1)} %copy-done.22, bf16[48,2048]{1,0:T(8,128)(2,1)} %pad_maximum_fusion.6.a_ref, bf16[256,2048]{1,0:T(8,128)(2,1)} %bitcast.113, ...), custom_call_target="tpu_custom_call" | custom-call | flops 1048576 | bytes 65536 | tf_op jit(solution)/shard_map/norm_one/pallas_call | solution.py:789
  440.2 3.5 collective-permute-done.51
  443.9 3.4 add_convert_fusion.8
  451.6 4.7 all-to-all-start.4
  458.3 10.7 %collective-permute-done.54 = bf16[128,2048]{1,0:T(8,128)(2,1)} collective-permute-done((bf16[128,2048]{1,0:T(8,128)(2,1)}, bf16[128,2048]{1,0:T(8,128)(2,1)}, u32[]{:S(2)}, u32[]{:S(2)}) %collective-permute-start.54) | collective-permute-done | bytes 524320 | tf_op jit(solution)/shard_map/ppermute | solution.py:46
  469.2 2.6 convert_add_fusion.1
  471.8 2.2 fusion.2
  (345 shorter events, 95.4 us)
Async XLA Ops:
  7.3 41.0 %collective-permute-start.2 = (bf16[256,2048]{1,0:T(8,128)(2,1)}, bf16[256,2048]{1,0:T(8,128)(2,1)S(1)}, u32[]{:S(2)}, u32[]{:S(2)}) collective-permute-start(bf16[256,2048]{1,0:T(8,128)(2,1)} %bitcast.114), channel_id=1, source_target_pairs={{0,1},{1,0},{2,3},{3,2},{4,5},{5,4},{6,7},{7,6},{8,9},{9,8},{10,11... | collective-permute-start | bytes 3145736 | tf_op jit(solution)/shard_map/ppermute | solution.py:46
  10.3 38.0 %collective-permute-start.3 = (bf16[256,2048]{1,0:T(8,128)(2,1)}, bf16[256,2048]{1,0:T(8,128)(2,1)S(1)}, u32[]{:S(2)}, u32[]{:S(2)}) collective-permute-start(bf16[256,2048]{1,0:T(8,128)(2,1)} %bitcast.115), channel_id=1, source_target_pairs={{0,4},{1,5},{2,6},{3,7},{4,0},{5,1},{6,2},{7,3},{8,12},{9,13},{10,... | collective-permute-start | bytes 3145736 | tf_op jit(solution)/shard_map/ppermute | solution.py:46
  11.8 36.5 %collective-permute-start.4 = (bf16[256,2048]{1,0:T(8,128)(2,1)}, bf16[256,2048]{1,0:T(8,128)(2,1)}, u32[]{:S(2)}, u32[]{:S(2)}) collective-permute-start(bf16[256,2048]{1,0:T(8,128)(2,1)} %bitcast.116), channel_id=1, source_target_pairs={{0,2},{1,3},{2,0},{3,1},{4,6},{5,7},{6,4},{7,5},{8,10},{9,11},{10,... | collective-permute-start | bytes 3145736 | tf_op jit(solution)/shard_map/ppermute | solution.py:46
  15.3 28.6 %collective-permute-start = (bf16[64,4608]{1,0:T(8,128)(2,1)S(1)}, bf16[64,4608]{1,0:T(8,128)(2,1)}, u32[]{:S(2)}, u32[]{:S(2)}) collective-permute-start(bf16[64,4608]{1,0:T(8,128)(2,1)S(1)} %constant_dynamic-update-slice_fusion.11), channel_id=1, source_target_pairs={{0,8},{1,9},{2,10},{3,11},{4,12},{5,13},{6,14},{7,15},{8,0},{9,1},... | collective-permute-start | bytes 1769480 | tf_op jit(solution)/shard_map/ppermute | solution.py:46
  16.9 31.3 %collective-permute-start.1 = (bf16[64,4608]{1,0:T(8,128)(2,1)S(1)}, bf16[64,4608]{1,0:T(8,128)(2,1)}, u32[]{:S(2)}, u32[]{:S(2)}) collective-permute-start(bf16[64,4608]{1,0:T(8,128)(2,1)S(1)} %constant_dynamic-update-slice_fusion.11), channel_id=1, source_target_pairs={{0,16},{1,17},{2,18},{3,19},{4,20},{5,21},{6,22},{7,23},{8,24},{9,... | collective-permute-start | bytes 1769480 | tf_op jit(solution)/shard_map/ppermute | solution.py:46
  25.7 28.0 %all-to-all-start = ((bf16[32,4,1408]{2,1,0:T(4,128)(2,1)}), bf16[32,4,1408]{2,1,0:T(4,128)(2,1)S(1)}, u32[]{:S(2)}, u32[]{:S(2)}) async-start(bf16[32,4,1408]{2,1,0:T(4,128)(2,1)} %copy.117), calls=%async_computation | async-start | bytes 720896 | tf_op jit(solution)/shard_map/all_to_all | solution.py:1023
  28.3 222.8 %all-gather.2.cloned.1.call-start = ((), (), s32[]{:S(2)}) async-start(), calls=%async_computation.5 | async-start | bytes 11489280 | tf_op jit(solution)/shard_map/all_gather | solution.py:1035
  49.5 14.4 %collective-permute-start.5 = (bf16[64,4608]{1,0:T(8,128)(2,1)}, bf16[64,4608]{1,0:T(8,128)(2,1)}, u32[]{:S(2)}, u32[]{:S(2)}) collective-permute-start(bf16[64,4608]{1,0:T(8,128)(2,1)} %collective-permute-done.1), channel_id=1, source_target_pairs={{0,8},{1,9},{2,10},{3,11},{4,12},{5,13},{6,14},{7,15},{8,0},{9,1},... | collective-permute-start | bytes 1769480 | tf_op jit(solution)/shard_map/ppermute | solution.py:46
  68.0 40.0 %all-to-all-start.1 = ((bf16[32,16,640]{2,1,0:T(8,128)(2,1)}), bf16[32,16,640]{2,1,0:T(8,128)(2,1)S(1)}, u32[]{:S(2)}, u32[]{:S(2)}) async-start(bf16[32,16,640]{2,1,0:T(8,128)(2,1)} %broadcast_select_fusion), calls=%async_computation.1 | async-start | bytes 1310720 | tf_op jit(solution)/shard_map/all_to_all | solution.py:1031
  77.8 35.1 %collective-permute-start.6 = (bf16[4,64,2560]{2,1,0:T(8,128)(2,1)S(1)}, bf16[4,64,2560]{2,1,0:T(8,128)(2,1)}, u32[]{:S(2)}, u32[]{:S(2)}) collective-permute-start(bf16[4,64,2560]{2,1,0:T(8,128)(2,1)S(1)} %pad_maximum_fusion.1.refs_0_), channel_id=1, source_target_pairs={{0,1},{1,0},{2,3},{3,2},{4,5},{5,4},{6,7},{7,6},{8,9},{9,8},{10,11... | collective-permute-start | bytes 3932168 | tf_op jit(solution)/shard_map/ppermute | solution.py:46
  79.8 33.4 %collective-permute-start.7 = (bf16[4,64,2560]{2,1,0:T(8,128)(2,1)S(1)}, bf16[4,64,2560]{2,1,0:T(8,128)(2,1)}, u32[]{:S(2)}, u32[]{:S(2)}) collective-permute-start(bf16[4,64,2560]{2,1,0:T(8,128)(2,1)S(1)} %pad_maximum_fusion.1.refs_0_), channel_id=1, source_target_pairs={{0,4},{1,5},{2,6},{3,7},{4,0},{5,1},{6,2},{7,3},{8,12},{9,13},{10,... | collective-permute-start | bytes 3932168 | tf_op jit(solution)/shard_map/ppermute | solution.py:46
  81.3 31.9 %collective-permute-start.8 = (bf16[4,64,2560]{2,1,0:T(8,128)(2,1)S(1)}, bf16[4,64,2560]{2,1,0:T(8,128)(2,1)}, u32[]{:S(2)}, u32[]{:S(2)}) collective-permute-start(bf16[4,64,2560]{2,1,0:T(8,128)(2,1)S(1)} %pad_maximum_fusion.1.refs_0_), channel_id=1, source_target_pairs={{0,2},{1,3},{2,0},{3,1},{4,6},{5,7},{6,4},{7,5},{8,10},{9,11},{10,... | collective-permute-start | bytes 3932168 | tf_op jit(solution)/shard_map/ppermute | solution.py:46
  114.3 16.4 %collective-permute-start.10 = (bf16[2,64,2560]{2,1,0:T(8,128)(2,1)S(1)}, bf16[2,64,2560]{2,1,0:T(8,128)(2,1)S(1)}, u32[]{:S(2)}, u32[]{:S(2)}) collective-permute-start(bf16[2,64,2560]{2,1,0:T(8,128)(2,1)S(1)} %slice.335), channel_id=1, source_target_pairs={{0,1},{1,0},{2,3},{3,2},{4,5},{5,4},{6,7},{7,6},{8,9},{9,8},{10,11... | collective-permute-start | bytes 1966088 | tf_op jit(solution)/shard_map/ppermute | solution.py:46
  117.3 16.0 %collective-permute-start.9 = (bf16[2,64,2560]{2,1,0:T(8,128)(2,1)S(1)}, bf16[2,64,2560]{2,1,0:T(8,128)(2,1)S(1)}, u32[]{:S(2)}, u32[]{:S(2)}) collective-permute-start(bf16[2,64,2560]{2,1,0:T(8,128)(2,1)S(1)} %slice.334), channel_id=1, source_target_pairs={{0,4},{1,5},{2,6},{3,7},{4,0},{5,1},{6,2},{7,3},{8,12},{9,13},{10,... | collective-permute-start | bytes 1966088 | tf_op jit(solution)/shard_map/ppermute | solution.py:46
  133.3 2.2 collective-permute-start.13
  133.4 4.9 %collective-permute-start.14 = (bf16[2,64,2560]{2,1,0:T(8,128)(2,1)S(1)}, bf16[2,64,2560]{2,1,0:T(8,128)(2,1)S(1)}, u32[]{:S(2)}, u32[]{:S(2)}) collective-permute-start(bf16[2,64,2560]{2,1,0:T(8,128)(2,1)S(1)} %collective-permute-done.10.refs_4_), channel_id=1, source_target_pairs={{0,2},{1,3},{2,0},{3,1},{4,6},{5,7},{6,4},{7,5},{8,10},{9,11},{10,... | collective-permute-start | bytes 1966088 | tf_op jit(solution)/shard_map/ppermute | solution.py:46
  133.9 7.4 %collective-permute-start.11 = (bf16[4,64,2560]{2,1,0:T(8,128)(2,1)}, bf16[4,64,2560]{2,1,0:T(8,128)(2,1)S(1)}, u32[]{:S(2)}, u32[]{:S(2)}) collective-permute-start(bf16[4,64,2560]{2,1,0:T(8,128)(2,1)} %collective-permute-done.6.refs_1_), channel_id=1, source_target_pairs={{0,2},{1,3},{2,0},{3,1},{4,6},{5,7},{6,4},{7,5},{8,10},{9,11},{10,... | collective-permute-start | bytes 3932168 | tf_op jit(solution)/shard_map/ppermute | solution.py:46
  134.0 7.4 %collective-permute-start.12 = (bf16[4,64,2560]{2,1,0:T(8,128)(2,1)}, bf16[4,64,2560]{2,1,0:T(8,128)(2,1)}, u32[]{:S(2)}, u32[]{:S(2)}) collective-permute-start(bf16[4,64,2560]{2,1,0:T(8,128)(2,1)} %collective-permute-done.7.refs_2_), channel_id=1, source_target_pairs={{0,2},{1,3},{2,0},{3,1},{4,6},{5,7},{6,4},{7,5},{8,10},{9,11},{10,... | collective-permute-start | bytes 3932168 | tf_op jit(solution)/shard_map/ppermute | solution.py:46
  134.4 44.2 %collective-permute-start.16 = (bf16[4,64,2048]{2,1,0:T(8,128)(2,1)S(1)}, bf16[4,64,2048]{2,1,0:T(8,128)(2,1)}, u32[]{:S(2)}, u32[]{:S(2)}) collective-permute-start(bf16[4,64,2048]{2,1,0:T(8,128)(2,1)S(1)} %copy-done.26), channel_id=1, source_target_pairs={{0,1},{1,0},{2,3},{3,2},{4,5},{5,4},{6,7},{7,6},{8,9},{9,8},{10,11... | collective-permute-start | bytes 3145736 | tf_op jit(solution)/shard_map/ppermute | solution.py:46
  135.5 43.2 %collective-permute-start.17 = (bf16[4,64,2048]{2,1,0:T(8,128)(2,1)S(1)}, bf16[4,64,2048]{2,1,0:T(8,128)(2,1)}, u32[]{:S(2)}, u32[]{:S(2)}) collective-permute-start(bf16[4,64,2048]{2,1,0:T(8,128)(2,1)S(1)} %copy-done.26), channel_id=1, source_target_pairs={{0,4},{1,5},{2,6},{3,7},{4,0},{5,1},{6,2},{7,3},{8,12},{9,13},{10,... | collective-permute-start | bytes 3145736 | tf_op jit(solution)/shard_map/ppermute | solution.py:46
  138.3 40.4 %collective-permute-start.18 = (bf16[4,64,2048]{2,1,0:T(8,128)(2,1)S(1)}, bf16[4,64,2048]{2,1,0:T(8,128)(2,1)}, u32[]{:S(2)}, u32[]{:S(2)}) collective-permute-start(bf16[4,64,2048]{2,1,0:T(8,128)(2,1)S(1)} %copy-done.26), channel_id=1, source_target_pairs={{0,2},{1,3},{2,0},{3,1},{4,6},{5,7},{6,4},{7,5},{8,10},{9,11},{10,... | collective-permute-start | bytes 3145736 | tf_op jit(solution)/shard_map/ppermute | solution.py:46
  152.8 12.4 %collective-permute-start.15 = (bf16[256,512]{1,0:T(8,128)(2,1)S(1)}, bf16[256,512]{1,0:T(8,128)(2,1)S(1)}, u32[]{:S(2)}, u32[]{:S(2)}) collective-permute-start(bf16[256,512]{1,0:T(8,128)(2,1)S(1)} %get-tuple-element.190.own_ref), channel_id=1, source_target_pairs={{0,1},{1,0},{2,3},{3,2},{4,5},{5,4},{6,7},{7,6},{8,9},{9,8},{10,11... | collective-permute-start | bytes 786440 | tf_op jit(solution)/shard_map/ppermute | solution.py:46
  180.2 13.3 %collective-permute-start.19 = (bf16[2,64,2048]{2,1,0:T(8,128)(2,1)S(1)}, bf16[2,64,2048]{2,1,0:T(8,128)(2,1)S(1)}, u32[]{:S(2)}, u32[]{:S(2)}) collective-permute-start(bf16[2,64,2048]{2,1,0:T(8,128)(2,1)S(1)} %slice.351), channel_id=1, source_target_pairs={{0,4},{1,5},{2,6},{3,7},{4,0},{5,1},{6,2},{7,3},{8,12},{9,13},{10,... | collective-permute-start | bytes 1572872 | tf_op jit(solution)/shard_map/ppermute | solution.py:46
  182.0 13.1 %collective-permute-start.20 = (bf16[2,64,2048]{2,1,0:T(8,128)(2,1)S(1)}, bf16[2,64,2048]{2,1,0:T(8,128)(2,1)}, u32[]{:S(2)}, u32[]{:S(2)}) collective-permute-start(bf16[2,64,2048]{2,1,0:T(8,128)(2,1)S(1)} %slice.352), channel_id=1, source_target_pairs={{0,1},{1,0},{2,3},{3,2},{4,5},{5,4},{6,7},{7,6},{8,9},{9,8},{10,11... | collective-permute-start | bytes 1572872 | tf_op jit(solution)/shard_map/ppermute | solution.py:46
  183.6 17.1 %collective-permute-start.21 = (bf16[4,64,2048]{2,1,0:T(8,128)(2,1)}, bf16[4,64,2048]{2,1,0:T(8,128)(2,1)S(1)}, u32[]{:S(2)}, u32[]{:S(2)}) collective-permute-start(bf16[4,64,2048]{2,1,0:T(8,128)(2,1)} %collective-permute-done.16.refs_1_), channel_id=1, source_target_pairs={{0,2},{1,3},{2,0},{3,1},{4,6},{5,7},{6,4},{7,5},{8,10},{9,11},{10,... | collective-permute-start | bytes 3145736 | tf_op jit(solution)/shard_map/ppermute | solution.py:46
  183.6 17.1 %collective-permute-start.22 = (bf16[4,64,2048]{2,1,0:T(8,128)(2,1)}, bf16[4,64,2048]{2,1,0:T(8,128)(2,1)}, u32[]{:S(2)}, u32[]{:S(2)}) collective-permute-start(bf16[4,64,2048]{2,1,0:T(8,128)(2,1)} %collective-permute-done.17.refs_2_), channel_id=1, source_target_pairs={{0,2},{1,3},{2,0},{3,1},{4,6},{5,7},{6,4},{7,5},{8,10},{9,11},{10,... | collective-permute-start | bytes 3145736 | tf_op jit(solution)/shard_map/ppermute | solution.py:46
  195.0 3.6 collective-permute-start.23
  195.0 5.7 %collective-permute-start.24 = (bf16[2,64,2048]{2,1,0:T(8,128)(2,1)}, bf16[2,64,2048]{2,1,0:T(8,128)(2,1)}, u32[]{:S(2)}, u32[]{:S(2)}) collective-permute-start(bf16[2,64,2048]{2,1,0:T(8,128)(2,1)} %collective-permute-done.20.refs_4_), channel_id=1, source_target_pairs={{0,2},{1,3},{2,0},{3,1},{4,6},{5,7},{6,4},{7,5},{8,10},{9,11},{10,... | collective-permute-start | bytes 1572872 | tf_op jit(solution)/shard_map/ppermute | solution.py:46
  196.4 17.3 %collective-permute-start.25 = (bf16[128,2048]{1,0:T(8,128)(2,1)}, bf16[128,2048]{1,0:T(8,128)(2,1)}, u32[]{:S(2)}, u32[]{:S(2)}) collective-permute-start(bf16[128,2048]{1,0:T(8,128)(2,1)} %slice.356), channel_id=1, source_target_pairs={{0,4},{1,5},{2,6},{3,7},{4,0},{5,1},{6,2},{7,3},{8,12},{9,13},{10,... | collective-permute-start | bytes 1572872 | tf_op jit(solution)/shard_map/ppermute | solution.py:46
  199.4 14.3 %collective-permute-start.26 = (bf16[128,2048]{1,0:T(8,128)(2,1)}, bf16[128,2048]{1,0:T(8,128)(2,1)}, u32[]{:S(2)}, u32[]{:S(2)}) collective-permute-start(bf16[128,2048]{1,0:T(8,128)(2,1)} %slice.357), channel_id=1, source_target_pairs={{0,1},{1,0},{2,3},{3,2},{4,5},{5,4},{6,7},{7,6},{8,9},{9,8},{10,11... | collective-permute-start | bytes 1572872 | tf_op jit(solution)/shard_map/ppermute | solution.py:46
  213.7 70.2 %copy-start.12 = (bf16[256,2176]{1,0:T(8,128)(2,1)}, bf16[256,2176]{1,0:T(8,128)(2,1)S(1)}, u32[]{:S(2)}) copy-start(bf16[256,2176]{1,0:T(8,128)(2,1)S(1)} %get-tuple-element.212.refs_0_) | copy-start | bytes 3342340
  213.7 26.4 %collective-permute-start.27 = (bf16[256,2176]{1,0:T(8,128)(2,1)S(1)}, bf16[256,2176]{1,0:T(8,128)(2,1)S(1)}, u32[]{:S(2)}, u32[]{:S(2)}) collective-permute-start(bf16[256,2176]{1,0:T(8,128)(2,1)S(1)} %get-tuple-element.212.refs_0_), channel_id=1, source_target_pairs={{0,1},{1,0},{2,3},{3,2},{4,5},{5,4},{6,7},{7,6},{8,9},{9,8},{10,11... | collective-permute-start | bytes 3342344 | tf_op jit(solution)/shard_map/ppermute | solution.py:46
  215.1 25.6 %collective-permute-start.28 = (bf16[256,2176]{1,0:T(8,128)(2,1)S(1)}, bf16[256,2176]{1,0:T(8,128)(2,1)S(1)}, u32[]{:S(2)}, u32[]{:S(2)}) collective-permute-start(bf16[256,2176]{1,0:T(8,128)(2,1)S(1)} %get-tuple-element.212.refs_0_), channel_id=1, source_target_pairs={{0,4},{1,5},{2,6},{3,7},{4,0},{5,1},{6,2},{7,3},{8,12},{9,13},{10,... | collective-permute-start | bytes 3342344 | tf_op jit(solution)/shard_map/ppermute | solution.py:46
  215.8 25.0 %collective-permute-start.29 = (bf16[256,2176]{1,0:T(8,128)(2,1)S(1)}, bf16[256,2176]{1,0:T(8,128)(2,1)S(1)}, u32[]{:S(2)}, u32[]{:S(2)}) collective-permute-start(bf16[256,2176]{1,0:T(8,128)(2,1)S(1)} %get-tuple-element.212.refs_0_), channel_id=1, source_target_pairs={{0,2},{1,3},{2,0},{3,1},{4,6},{5,7},{6,4},{7,5},{8,10},{9,11},{10,... | collective-permute-start | bytes 3342344 | tf_op jit(solution)/shard_map/ppermute | solution.py:46
  215.8 27.5 %collective-permute-start.32 = (bf16[256,2048]{1,0:T(8,128)(2,1)S(1)}, bf16[256,2048]{1,0:T(8,128)(2,1)S(1)}, u32[]{:S(2)}, u32[]{:S(2)}) collective-permute-start(bf16[256,2048]{1,0:T(8,128)(2,1)S(1)} %copy-done.33), channel_id=1, source_target_pairs={{0,2},{1,3},{2,0},{3,1},{4,6},{5,7},{6,4},{7,5},{8,10},{9,11},{10,... | collective-permute-start | bytes 3145736 | tf_op jit(solution)/shard_map/ppermute | solution.py:46
  216.3 27.9 %collective-permute-start.33 = (bf16[256,2048]{1,0:T(8,128)(2,1)S(1)}, bf16[256,2048]{1,0:T(8,128)(2,1)S(1)}, u32[]{:S(2)}, u32[]{:S(2)}) collective-permute-start(bf16[256,2048]{1,0:T(8,128)(2,1)S(1)} %copy-done.36), channel_id=1, source_target_pairs={{0,2},{1,3},{2,0},{3,1},{4,6},{5,7},{6,4},{7,5},{8,10},{9,11},{10,... | collective-permute-start | bytes 3145736 | tf_op jit(solution)/shard_map/ppermute | solution.py:46
  241.8 7.4 %collective-permute-start.30 = (bf16[256,2176]{1,0:T(8,128)(2,1)S(1)}, bf16[256,2176]{1,0:T(8,128)(2,1)S(1)}, u32[]{:S(2)}, u32[]{:S(2)}) collective-permute-start(bf16[256,2176]{1,0:T(8,128)(2,1)S(1)} %collective-permute-done.27.refs_0_), channel_id=1, source_target_pairs={{0,2},{1,3},{2,0},{3,1},{4,6},{5,7},{6,4},{7,5},{8,10},{9,11},{10,... | collective-permute-start | bytes 3342344 | tf_op jit(solution)/shard_map/ppermute | solution.py:46
  241.8 9.2 %collective-permute-start.31 = (bf16[256,2176]{1,0:T(8,128)(2,1)S(1)}, bf16[256,2176]{1,0:T(8,128)(2,1)}, u32[]{:S(2)}, u32[]{:S(2)}) collective-permute-start(bf16[256,2176]{1,0:T(8,128)(2,1)S(1)} %collective-permute-done.28.refs_2_), channel_id=1, source_target_pairs={{0,2},{1,3},{2,0},{3,1},{4,6},{5,7},{6,4},{7,5},{8,10},{9,11},{10,... | collective-permute-start | bytes 3342344 | tf_op jit(solution)/shard_map/ppermute | solution.py:46
  242.3 4.8 collective-permute-start.34
  243.2 40.7 %collective-permute-start.36 = (bf16[128,2176]{1,0:T(8,128)(2,1)}, bf16[128,2176]{1,0:T(8,128)(2,1)}, u32[]{:S(2)}, u32[]{:S(2)}) collective-permute-start(bf16[128,2176]{1,0:T(8,128)(2,1)} %slice.358), channel_id=1, source_target_pairs={{0,4},{1,5},{2,6},{3,7},{4,0},{5,1},{6,2},{7,3},{8,12},{9,13},{10,... | collective-permute-start | bytes 1671176 | tf_op jit(solution)/shard_map/ppermute | solution.py:46
  244.2 39.8 %collective-permute-start.37 = (bf16[128,2176]{1,0:T(8,128)(2,1)S(1)}, bf16[128,2176]{1,0:T(8,128)(2,1)}, u32[]{:S(2)}, u32[]{:S(2)}) collective-permute-start(bf16[128,2176]{1,0:T(8,128)(2,1)S(1)} %slice.359), channel_id=1, source_target_pairs={{0,1},{1,0},{2,3},{3,2},{4,5},{5,4},{6,7},{7,6},{8,9},{9,8},{10,11... | collective-permute-start | bytes 1671176 | tf_op jit(solution)/shard_map/ppermute | solution.py:46
  247.1 2.1 collective-permute-start.35
  283.9 2.2 collective-permute-start.38
  284.1 3.6 collective-permute-start.39
  284.5 25.5 %collective-permute-start.41 = (bf16[512,2432]{1,0:T(8,128)(2,1)S(1)}, bf16[512,2432]{1,0:T(8,128)(2,1)S(1)}, u32[]{:S(2)}, u32[]{:S(2)}) collective-permute-start(bf16[512,2432]{1,0:T(8,128)(2,1)S(1)} %get-tuple-element.232), channel_id=1, source_target_pairs={{0,2},{1,3},{2,0},{3,1},{4,6},{5,7},{6,4},{7,5},{8,10},{9,11},{10,... | collective-permute-start | bytes 7471112 | tf_op jit(solution)/shard_map/ppermute | solution.py:46
  306.7 3.0 collective-permute-start.40
  310.3 23.2 %collective-permute-start.42 = (bf16[128,2432]{1,0:T(8,128)(2,1)S(1)}, bf16[128,2432]{1,0:T(8,128)(2,1)S(1)}, u32[]{:S(2)}, u32[]{:S(2)}) collective-permute-start(bf16[128,2432]{1,0:T(8,128)(2,1)S(1)} %get-tuple-element.239), channel_id=1, source_target_pairs={{0,1},{1,0},{2,3},{3,2},{4,5},{5,4},{6,7},{7,6},{8,9},{9,8},{10,11... | collective-permute-start | bytes 1867784 | tf_op jit(solution)/shard_map/ppermute | solution.py:46
  311.4 22.0 %collective-permute-start.43 = (bf16[128,2432]{1,0:T(8,128)(2,1)S(1)}, bf16[128,2432]{1,0:T(8,128)(2,1)S(1)}, u32[]{:S(2)}, u32[]{:S(2)}) collective-permute-start(bf16[128,2432]{1,0:T(8,128)(2,1)S(1)} %get-tuple-element.240), channel_id=1, source_target_pairs={{0,4},{1,5},{2,6},{3,7},{4,0},{5,1},{6,2},{7,3},{8,12},{9,13},{10,... | collective-permute-start | bytes 1867784 | tf_op jit(solution)/shard_map/ppermute | solution.py:46
  312.6 27.2 %collective-permute-start.45 = (bf16[128,2432]{1,0:T(8,128)(2,1)S(1)}, bf16[128,2432]{1,0:T(8,128)(2,1)S(1)}, u32[]{:S(2)}, u32[]{:S(2)}) collective-permute-start(bf16[128,2432]{1,0:T(8,128)(2,1)S(1)} %get-tuple-element.246), channel_id=1, source_target_pairs={{0,1},{1,0},{2,3},{3,2},{4,5},{5,4},{6,7},{7,6},{8,9},{9,8},{10,11... | collective-permute-start | bytes 1867784 | tf_op jit(solution)/shard_map/ppermute | solution.py:46
  313.3 27.3 %collective-permute-start.46 = (bf16[128,2432]{1,0:T(8,128)(2,1)S(1)}, bf16[128,2432]{1,0:T(8,128)(2,1)S(1)}, u32[]{:S(2)}, u32[]{:S(2)}) collective-permute-start(bf16[128,2432]{1,0:T(8,128)(2,1)S(1)} %get-tuple-element.247), channel_id=1, source_target_pairs={{0,4},{1,5},{2,6},{3,7},{4,0},{5,1},{6,2},{7,3},{8,12},{9,13},{10,... | collective-permute-start | bytes 1867784 | tf_op jit(solution)/shard_map/ppermute | solution.py:46
  333.4 29.8 %collective-permute-start.44 = (bf16[256,2432]{1,0:T(8,128)(2,1)}, bf16[256,2432]{1,0:T(8,128)(2,1)S(1)}, u32[]{:S(2)}, u32[]{:S(2)}) collective-permute-start(bf16[256,2432]{1,0:T(8,128)(2,1)} %get-tuple-element.243), channel_id=1, source_target_pairs={{0,2},{1,3},{2,0},{3,1},{4,6},{5,7},{6,4},{7,5},{8,10},{9,11},{10,... | collective-permute-start | bytes 3735560 | tf_op jit(solution)/shard_map/ppermute | solution.py:46
  340.6 22.6 %collective-permute-start.47 = (bf16[128,2432]{1,0:T(8,128)(2,1)}, bf16[128,2432]{1,0:T(8,128)(2,1)}, u32[]{:S(2)}, u32[]{:S(2)}) collective-permute-start(bf16[128,2432]{1,0:T(8,128)(2,1)} %get-tuple-element.251), channel_id=1, source_target_pairs={{0,4},{1,5},{2,6},{3,7},{4,0},{5,1},{6,2},{7,3},{8,12},{9,13},{10,... | collective-permute-start | bytes 1867784 | tf_op jit(solution)/shard_map/ppermute | solution.py:46
  341.8 21.4 %collective-permute-start.48 = (bf16[128,2432]{1,0:T(8,128)(2,1)}, bf16[128,2432]{1,0:T(8,128)(2,1)}, u32[]{:S(2)}, u32[]{:S(2)}) collective-permute-start(bf16[128,2432]{1,0:T(8,128)(2,1)} %get-tuple-element.252), channel_id=1, source_target_pairs={{0,1},{1,0},{2,3},{3,2},{4,5},{5,4},{6,7},{7,6},{8,9},{9,8},{10,11... | collective-permute-start | bytes 1867784 | tf_op jit(solution)/shard_map/ppermute | solution.py:46
  363.2 38.2 %collective-permute-start.50 = (bf16[1024,2048]{1,0:T(8,128)(2,1)}, bf16[1024,2048]{1,0:T(8,128)(2,1)}, u32[]{:S(2)}, u32[]{:S(2)}) collective-permute-start(bf16[1024,2048]{1,0:T(8,128)(2,1)} %get-tuple-element.283), channel_id=1, source_target_pairs={{0,2},{1,3},{2,0},{3,1},{4,6},{5,7},{6,4},{7,5},{8,10},{9,11},{10,... | collective-permute-start | bytes 12582920 | tf_op jit(solution)/shard_map/ppermute | solution.py:46
  364.2 35.3 %all-to-all-start.2 = ((bf16[32,4,2304]{2,1,0:T(4,128)(2,1)}), bf16[32,4,2304]{2,1,0:T(4,128)(2,1)S(1)}, u32[]{:S(2)}, u32[]{:S(2)}) async-start(bf16[32,4,2304]{2,1,0:T(4,128)(2,1)} %pad_maximum_fusion.4), calls=%async_computation.2 | async-start | bytes 1179648 | tf_op jit(solution)/shard_map/all_to_all | solution.py:1135
  399.5 8.6 %collective-permute-start.49 = (bf16[256,512]{1,0:T(8,128)(2,1)S(1)}, bf16[256,512]{1,0:T(8,128)(2,1)S(1)}, u32[]{:S(2)}, u32[]{:S(2)}) collective-permute-start(bf16[256,512]{1,0:T(8,128)(2,1)S(1)} %get-tuple-element.281), channel_id=1, source_target_pairs={{0,1},{1,0},{2,3},{3,2},{4,5},{5,4},{6,7},{7,6},{8,9},{9,8},{10,11... | collective-permute-start | bytes 786440 | tf_op jit(solution)/shard_map/ppermute | solution.py:46
  416.1 33.1 %all-to-all-start.3 = ((bf16[32,16,592]{2,1,0:T(8,128)(2,1)}), bf16[32,16,592]{2,1,0:T(8,128)(2,1)S(1)}, u32[]{:S(2)}, u32[]{:S(2)}) async-start(bf16[32,16,592]{2,1,0:T(8,128)(2,1)} %bitcast.106), calls=%async_computation.3 | async-start | bytes 1310720 | tf_op jit(solution)/shard_map/all_to_all | solution.py:1167
  422.0 21.7 %collective-permute-start.51 = (bf16[128,2048]{1,0:T(8,128)(2,1)S(1)}, bf16[128,2048]{1,0:T(8,128)(2,1)}, u32[]{:S(2)}, u32[]{:S(2)}) collective-permute-start(bf16[128,2048]{1,0:T(8,128)(2,1)S(1)} %copy-done.53), channel_id=1, source_target_pairs={{0,1},{1,0},{2,3},{3,2},{4,5},{5,4},{6,7},{7,6},{8,9},{9,8},{10,11... | collective-permute-start | bytes 1572872 | tf_op jit(solution)/shard_map/ppermute | solution.py:46
  423.9 20.0 %collective-permute-start.52 = (bf16[128,2048]{1,0:T(8,128)(2,1)S(1)}, bf16[128,2048]{1,0:T(8,128)(2,1)}, u32[]{:S(2)}, u32[]{:S(2)}) collective-permute-start(bf16[128,2048]{1,0:T(8,128)(2,1)S(1)} %copy-done.52), channel_id=1, source_target_pairs={{0,4},{1,5},{2,6},{3,7},{4,0},{5,1},{6,2},{7,3},{8,12},{9,13},{10,... | collective-permute-start | bytes 1572872 | tf_op jit(solution)/shard_map/ppermute | solution.py:46
  439.4 18.9 %collective-permute-start.53 = (bf16[128,2048]{1,0:T(8,128)(2,1)}, bf16[128,2048]{1,0:T(8,128)(2,1)}, u32[]{:S(2)}, u32[]{:S(2)}) collective-permute-start(bf16[128,2048]{1,0:T(8,128)(2,1)} %get-tuple-element.304), channel_id=1, source_target_pairs={{0,1},{1,0},{2,3},{3,2},{4,5},{5,4},{6,7},{7,6},{8,9},{9,8},{10,11... | collective-permute-start | bytes 1572872 | tf_op jit(solution)/shard_map/ppermute | solution.py:46
  440.0 18.4 %collective-permute-start.55 = (bf16[128,2048]{1,0:T(8,128)(2,1)}, bf16[128,2048]{1,0:T(8,128)(2,1)}, u32[]{:S(2)}, u32[]{:S(2)}) collective-permute-start(bf16[128,2048]{1,0:T(8,128)(2,1)} %get-tuple-element.306), channel_id=1, source_target_pairs={{0,4},{1,5},{2,6},{3,7},{4,0},{5,1},{6,2},{7,3},{8,12},{9,13},{10,... | collective-permute-start | bytes 1572872 | tf_op jit(solution)/shard_map/ppermute | solution.py:46
  447.3 21.7 %collective-permute-start.54 = (bf16[128,2048]{1,0:T(8,128)(2,1)}, bf16[128,2048]{1,0:T(8,128)(2,1)}, u32[]{:S(2)}, u32[]{:S(2)}) collective-permute-start(bf16[128,2048]{1,0:T(8,128)(2,1)} %get-tuple-element.315), channel_id=1, source_target_pairs={{0,4},{1,5},{2,6},{3,7},{4,0},{5,1},{6,2},{7,3},{8,12},{9,13},{10,... | collective-permute-start | bytes 1572872 | tf_op jit(solution)/shard_map/ppermute | solution.py:46
  448.6 20.6 %collective-permute-start.56 = (bf16[128,2048]{1,0:T(8,128)(2,1)}, bf16[128,2048]{1,0:T(8,128)(2,1)}, u32[]{:S(2)}, u32[]{:S(2)}) collective-permute-start(bf16[128,2048]{1,0:T(8,128)(2,1)} %get-tuple-element.316), channel_id=1, source_target_pairs={{0,1},{1,0},{2,3},{3,2},{4,5},{5,4},{6,7},{7,6},{8,9},{9,8},{10,11... | collective-permute-start | bytes 1572872 | tf_op jit(solution)/shard_map/ppermute | solution.py:46
  451.6 22.4 %all-to-all-start.4 = ((f32[32,4,720]{2,1,0:T(4,128)}), f32[32,4,720]{2,1,0:T(4,128)S(1)}, u32[]{:S(2)}, u32[]{:S(2)}) async-start(f32[32,4,720]{2,1,0:T(4,128)} %pad_maximum_fusion.5), calls=%async_computation.4 | async-start | bytes 786432 | tf_op jit(solution)/shard_map/all_to_all | solution.py:1181
  (70 other events, 519.1 us)
Sparse Core Ops, SparseCore 0:
  64.0 174.3 all-gather.1
